TPU v7x, 32 devices: a whole 2x2x4 slice. The times are simulated.
32 devices in a mesh: ctx: 8 (over y, x, core), fsdp: 4 (over z).
Axes of the slice: x: 2, y: 2, z: 4, core: 2. Of those that a mesh axis runs over, the one named last changes fastest.
Arguments:
- tokens: bfloat16 [4, 1024, 2048], P('fsdp', 'ctx'), may hold values from -6 to 6
- per_layer: bfloat16 [4, 1024, 256], P('fsdp', 'ctx'), may hold values from -6 to 6
- out_grad: bfloat16 [4, 1024, 2048], P('fsdp', 'ctx'), may hold values from -6 to 6
- segment_ids: int32 [4, 1024], P('fsdp'), may hold values from 0 to 8, as said below
- query_weight: bfloat16 [2048, 2048], P('fsdp'), may hold values from -0.125 to 0.125
- key_weight: bfloat16 [2048, 512], P('fsdp'), may hold values from -0.125 to 0.125
- value_weight: bfloat16 [2048, 512], P('fsdp'), may hold values from -0.125 to 0.125
- out_weight: bfloat16 [2048, 2048], P('fsdp'), may hold values from -0.125 to 0.125
- left_weight: bfloat16 [2048, 64], P('fsdp'), may hold values from -0.125 to 0.125
- right_weight: bfloat16 [64, 2048], P(None, 'fsdp'), may hold values from -0.75 to 0.75
- gate_weight: bfloat16 [2048, 8192], P(None, 'fsdp'), may hold values from -0.125 to 0.125
- up_weight: bfloat16 [2048, 8192], P(None, 'fsdp'), may hold values from -0.125 to 0.125
- down_weight: bfloat16 [8192, 2048], P('fsdp'), may hold values from -0.0625 to 0.0625
- side_gate: bfloat16 [2048, 256], P('fsdp'), may hold values from -0.125 to 0.125
- side_out: bfloat16 [256, 2048], P('fsdp'), may hold values from -0.375 to 0.375
- input_gain: float32 [2048], replicated, may hold values from 0.25 to 1.75
- laurel_gain: float32 [2048], replicated, may hold values from 0.25 to 1.75
- attn_gain: float32 [2048], replicated, may hold values from 0.25 to 1.75
- pre_gain: float32 [2048], replicated, may hold values from 0.25 to 1.75
- post_gain: float32 [2048], replicated, may hold values from 0.25 to 1.75
- side_gain: float32 [2048], replicated, may hold values from 0.25 to 1.75
- query_gain: float32 [256], replicated, may hold values from 0.25 to 0.5
- key_gain: float32 [256], replicated, may hold values from 0.25 to 0.5
Outputs:
- block_out: bfloat16 [4, 1024, 2048], P('fsdp', 'ctx')
- tokens_grad: bfloat16 [4, 1024, 2048], P('fsdp', 'ctx')
- per_layer_grad: bfloat16 [4, 1024, 256], P('fsdp', 'ctx')
- query_weight_grad: float32 [2048, 2048], P('ctx', 'fsdp')
- key_weight_grad: float32 [2048, 512], P('ctx', 'fsdp')
- value_weight_grad: float32 [2048, 512], P('ctx', 'fsdp')
- out_weight_grad: float32 [2048, 2048], P('ctx', 'fsdp')
- left_weight_grad: float32 [2048, 64], P(('ctx', 'fsdp'))
- right_weight_grad: float32 [64, 2048], P(None, ('ctx', 'fsdp'))
- gate_weight_grad: float32 [2048, 8192], P('ctx', 'fsdp')
- up_weight_grad: float32 [2048, 8192], P('ctx', 'fsdp')
- down_weight_grad: float32 [8192, 2048], P('fsdp', 'ctx')
- side_gate_grad: float32 [2048, 256], P('ctx', 'fsdp')
- side_out_grad: float32 [256, 2048], P('ctx', 'fsdp')
- input_gain_grad: float32 [2048], P(('ctx', 'fsdp'))
- laurel_gain_grad: float32 [2048], P(('ctx', 'fsdp'))
- attn_gain_grad: float32 [2048], P(('ctx', 'fsdp'))
- pre_gain_grad: float32 [2048], P(('ctx', 'fsdp'))
- post_gain_grad: float32 [2048], P(('ctx', 'fsdp'))
- side_gain_grad: float32 [2048], P(('ctx', 'fsdp'))
- query_gain_grad: float32 [256], P(('ctx', 'fsdp'))
- key_gain_grad: float32 [256], P(('ctx', 'fsdp'))
Inputs may be any that keep to these rules, and one draw needn't show every extreme that they name: `segment_ids`: within a sequence the ids never fall; one document of each sequence begins within the first 128 tokens and ends within the last 128; every other document lies wholly within the first 128 or the last 128 tokens.
All inputs are finite; a program needn't handle non-finite values.
Results may differ from a plain program's by a relative error of at most 0.034.
Values may be sent and summed in bfloat16 or wider, within the bound.
A program may use at most 448 MiB of HBM per device.

v0:
```python
import math

import jax
import jax.numpy as jnp
from jax import lax
from jax.sharding import PartitionSpec as P

HEADS = 8
KV_HEADS = 2
HD = 256


epsilon = 1e-06
rope_theta = 1000000.0
masked_score = -1e30
inverse_root = 1.0 / math.sqrt(2.0)


def from_behind(shard, axis, by):
    length = lax.axis_size(axis)
    return lax.ppermute(shard, axis, [(i, (i + by) % length) for i in range(length)])


def passed_along(shard, axis, by):
    length = lax.axis_size(axis)
    pairs = [(i, i + by) for i in range(length) if 0 <= i + by < length]
    return lax.ppermute(shard, axis, pairs)


def rms_norm(v, factor):
    return v * lax.rsqrt(jnp.mean(v * v, axis=-1, keepdims=True) + epsilon) * factor


def rotate(v, positions):
    halfway = v.shape[-1] // 2
    frequency = jnp.exp(
        jnp.arange(halfway).astype(jnp.float32) * (-2.0 * math.log(rope_theta) / v.shape[-1])
    )
    angles = positions.astype(jnp.float32)[:, None] * frequency[None, :]
    cosine = jnp.cos(angles)[:, None, :]
    sine_part = jnp.sin(angles)[:, None, :]
    leading = v[..., :halfway]
    trailing = v[..., halfway:]
    return jnp.concatenate(
        [leading * cosine - trailing * sine_part, trailing * cosine + leading * sine_part], axis=-1
    )


def forward_product(a, b):
    return jnp.dot(a, b, preferred_element_type=jnp.float32)


def across(a, b):
    return lax.dot_general(a, b, (((1,), (1,)), ((), ())), preferred_element_type=jnp.float32)


def over_rows(a, b):
    return lax.dot_general(a, b, (((0,), (0,)), ((), ())), preferred_element_type=jnp.float32)


def hidden_piece(gate_in, up_in):
    return jax.nn.gelu(gate_in, approximate=True) * up_in


def middle_piece(mixed_in, ffn_in_rows, factor):
    return mixed_in + rms_norm(ffn_in_rows, factor)


def send_grads(key_grad, value_grad):
    return (
        from_behind(key_grad.astype(jnp.bfloat16), "ctx", 1).astype(key_grad.dtype),
        from_behind(value_grad.astype(jnp.bfloat16), "ctx", 1).astype(value_grad.dtype),
    )


def body(
    tokens,
    per_layer,
    out_grad,
    segment_ids,
    query_weight,
    key_weight,
    value_weight,
    out_weight,
    left_weight,
    right_weight,
    gate_weight,
    up_weight,
    down_weight,
    side_gate,
    side_out,
    input_gain,
    laurel_gain,
    attn_gain,
    pre_gain,
    post_gain,
    side_gain,
    query_gain,
    key_gain,
):
    inputs = tokens[0].astype(jnp.float32)
    extra_rows = per_layer[0].astype(jnp.float32)
    cotangent = out_grad[0].astype(jnp.float32)
    sequence_ids = segment_ids[0]
    rows_here = inputs.shape[0]
    axis_count = lax.axis_size("ctx")
    axis_place = lax.axis_index("ctx")
    groups = HEADS // KV_HEADS
    local_rows = jnp.arange(rows_here, dtype=jnp.int32)
    query_pos = axis_place * rows_here + local_rows
    query_ids = lax.dynamic_slice_in_dim(sequence_ids, axis_place * rows_here, rows_here)
    row_ids = jnp.tile(query_ids, groups)
    row_pos = jnp.tile(query_pos, groups)

    def block_mask(first, count):
        key_ids = lax.dynamic_slice_in_dim(sequence_ids, jnp.maximum(first, 0), count)
        key_pos = first + jnp.arange(count, dtype=jnp.int32)
        allowed = (
            (row_ids[:, None] == key_ids[None, :])
            & (key_pos[None, :] <= row_pos[:, None])
            & (first >= 0)
        )
        return allowed[None]

    (
        full_query,
        full_key,
        full_value,
        full_out,
        full_left,
        full_right,
        full_side_gate,
        full_side_out,
    ) = (
        lax.all_gather(query_weight, "fsdp", axis=0, tiled=True),
        lax.all_gather(key_weight, "fsdp", axis=0, tiled=True),
        lax.all_gather(value_weight, "fsdp", axis=0, tiled=True),
        lax.all_gather(out_weight, "fsdp", axis=0, tiled=True),
        lax.all_gather(left_weight, "fsdp", axis=0, tiled=True),
        lax.all_gather(right_weight, "fsdp", axis=1, tiled=True),
        lax.all_gather(side_gate, "fsdp", axis=0, tiled=True),
        lax.all_gather(side_out, "fsdp", axis=0, tiled=True),
    )
    normed, input_pull = jax.vjp(rms_norm, inputs, input_gain)
    normed_low = normed.astype(jnp.bfloat16)
    query_raw = forward_product(normed_low, full_query)
    key_raw = forward_product(normed_low, full_key)
    value_raw = forward_product(normed_low, full_value)
    left_low = forward_product(normed_low, full_left).astype(jnp.bfloat16)
    right_out = forward_product(left_low, full_right)

    def heads_piece(query_in, key_in, value_in, gain_one, gain_two):
        query_heads = rotate(rms_norm(query_in.reshape(rows_here, HEADS, HD), gain_one), query_pos)
        key_heads = rotate(rms_norm(key_in.reshape(rows_here, KV_HEADS, HD), gain_two), query_pos)
        value_heads = rms_norm(value_in.reshape(rows_here, KV_HEADS, HD), 1.0)
        return (query_heads, key_heads, value_heads)

    (query_heads, key_heads, value_heads), heads_pull = jax.vjp(
        heads_piece, query_raw, key_raw, value_raw, query_gain, key_gain
    )
    query_low = query_heads.astype(jnp.bfloat16).reshape(rows_here, KV_HEADS, groups, HD)
    query_low = query_low.transpose(1, 2, 0, 3).reshape(KV_HEADS, groups * rows_here, HD)
    key_low = key_heads.astype(jnp.bfloat16).transpose(1, 0, 2)
    value_low = value_heads.astype(jnp.bfloat16).transpose(1, 0, 2)

    def forward_block(state, key_block, value_block, first):
        row_max, row_total, partial_value = state
        scores = jnp.einsum(
            "kqd,kjd->kqj", query_low, key_block, preferred_element_type=jnp.float32
        )
        allowed = block_mask(first, key_block.shape[1])
        scores = jnp.where(allowed, scores, masked_score)
        new_max = jnp.maximum(row_max, jnp.max(scores, axis=-1))
        weights = jnp.where(allowed, jnp.exp(scores - new_max[..., None]), 0.0)
        shrink = jnp.exp(row_max - new_max)
        row_total = row_total * shrink + jnp.sum(weights, axis=-1)
        partial_value = partial_value * shrink[..., None] + jnp.einsum(
            "kqj,kjd->kqd",
            weights.astype(jnp.bfloat16),
            value_block,
            preferred_element_type=jnp.float32,
        )
        return (new_max, row_total, partial_value)

    start_state = (
        jnp.full((KV_HEADS, groups * rows_here), masked_score, jnp.float32),
        jnp.zeros((KV_HEADS, groups * rows_here), jnp.float32),
        jnp.zeros((KV_HEADS, groups * rows_here, HD), jnp.float32),
    )
    first_state = forward_block(start_state, key_low, value_low, axis_place * rows_here)

    def forward_step(turn_index, carry):
        key_block, value_block, state = carry
        key_block, value_block = passed_along((key_block, value_block), "ctx", 1)
        source = axis_place - turn_index
        state = forward_block(state, key_block, value_block, source * rows_here)
        return (key_block, value_block, state)

    final_carry = lax.fori_loop(1, axis_count, forward_step, (key_low, value_low, first_state))
    row_max, row_total, partial_value = final_carry[2]
    attended_rows = partial_value / row_total[..., None]
    log_total = row_max + jnp.log(row_total)
    attended = attended_rows.reshape(KV_HEADS, groups, rows_here, HD).transpose(2, 0, 1, 3)
    attended_low = attended.reshape(rows_here, HEADS * HD).astype(jnp.bfloat16)
    attn_raw = forward_product(attended_low, full_out)

    def mix_piece(x, normed_in, attn_in, right_in, gain_one, gain_two, gain_three):
        mixed = (
            x + rms_norm(attn_in, gain_one) + normed_in + rms_norm(right_in, gain_two)
        ) * inverse_root
        return (mixed, rms_norm(mixed, gain_three))

    (mixed, ffn_in), mix_pull = jax.vjp(
        mix_piece, inputs, normed, attn_raw, right_out, attn_gain, laurel_gain, pre_gain
    )
    ffn_low = ffn_in.astype(jnp.bfloat16)
    gate_full, up_full, down_full = (
        lax.all_gather(gate_weight, "fsdp", axis=1, tiled=True),
        lax.all_gather(up_weight, "fsdp", axis=1, tiled=True),
        lax.all_gather(down_weight, "fsdp", axis=0, tiled=True),
    )
    gate_raw = forward_product(ffn_low, gate_full)
    up_raw = forward_product(ffn_low, up_full)
    hidden, hidden_pull = jax.vjp(hidden_piece, gate_raw, up_raw)
    hidden_low = hidden.astype(jnp.bfloat16)
    ffn_out = forward_product(hidden_low, down_full)
    middle, middle_pull = jax.vjp(middle_piece, mixed, ffn_out, post_gain)
    middle_low = middle.astype(jnp.bfloat16)
    layer_gate = forward_product(middle_low, full_side_gate)
    layer_act, extra_pull = jax.vjp(hidden_piece, layer_gate, extra_rows)
    layer_low = layer_act.astype(jnp.bfloat16)
    layer_out = forward_product(layer_low, full_side_out)
    result, out_pull = jax.vjp(middle_piece, middle, layer_out, side_gain)
    middle_grad_one, layer_out_grad, side_gain_grad = out_pull(cotangent)
    layer_grad_low = layer_out_grad.astype(jnp.bfloat16)
    side_out_grad = over_rows(layer_low, layer_grad_low)
    layer_gate_grad, extra_grad = extra_pull(across(layer_grad_low, full_side_out))
    gate_grad_low = layer_gate_grad.astype(jnp.bfloat16)
    side_gate_grad = over_rows(middle_low, gate_grad_low)
    mixed_grad_one, ffn_out_grad, post_gain_grad = middle_pull(
        middle_grad_one + across(gate_grad_low, full_side_gate)
    )
    ffn_grad_low = ffn_out_grad.astype(jnp.bfloat16)
    down_weight_grad = over_rows(hidden_low, ffn_grad_low)
    gate_raw_grad, up_raw_grad = hidden_pull(across(ffn_grad_low, down_full))
    gate_back_low = gate_raw_grad.astype(jnp.bfloat16)
    up_back_low = up_raw_grad.astype(jnp.bfloat16)
    gate_weight_grad = over_rows(ffn_low, gate_back_low)
    up_weight_grad = over_rows(ffn_low, up_back_low)
    ffn_in_grad = across(gate_back_low, gate_full) + across(up_back_low, up_full)
    (
        inputs_grad_one,
        normed_grad_one,
        attn_raw_grad,
        right_out_grad,
        attn_gain_grad,
        laurel_gain_grad,
        pre_gain_grad,
    ) = mix_pull((mixed_grad_one, ffn_in_grad))
    attn_grad_low = attn_raw_grad.astype(jnp.bfloat16)
    out_weight_grad = over_rows(attended_low, attn_grad_low)
    attended_grad_low = across(attn_grad_low, full_out).astype(jnp.bfloat16)
    right_grad_low = right_out_grad.astype(jnp.bfloat16)
    right_weight_grad = over_rows(left_low, right_grad_low)
    left_grad_low = across(right_grad_low, full_right).astype(jnp.bfloat16)
    grad_rows = attended_grad_low.reshape(rows_here, KV_HEADS, groups, HD).transpose(1, 2, 0, 3)
    grad_rows = grad_rows.reshape(KV_HEADS, groups * rows_here, HD)
    correction = jnp.sum(grad_rows.astype(jnp.float32) * attended_rows, axis=-1)

    def backward_block(query_grad, key_block, value_block, key_grad, value_grad, first):
        scores = jnp.einsum(
            "kqd,kjd->kqj", query_low, key_block, preferred_element_type=jnp.float32
        )
        allowed = block_mask(first, key_block.shape[1])
        weights = jnp.where(allowed, jnp.exp(scores - log_total[..., None]), 0.0)
        value_grad = value_grad + jnp.einsum(
            "kqj,kqd->kjd",
            weights.astype(jnp.bfloat16),
            grad_rows,
            preferred_element_type=jnp.float32,
        )
        weight_grad = jnp.einsum(
            "kqd,kjd->kqj", grad_rows, value_block, preferred_element_type=jnp.float32
        )
        score_grad = (weights * (weight_grad - correction[..., None])).astype(jnp.bfloat16)
        query_grad = query_grad + jnp.einsum(
            "kqj,kjd->kqd", score_grad, key_block, preferred_element_type=jnp.float32
        )
        key_grad = key_grad + jnp.einsum(
            "kqj,kqd->kjd", score_grad, query_low, preferred_element_type=jnp.float32
        )
        return (query_grad, key_grad, value_grad)

    query_start = jnp.zeros((KV_HEADS, groups * rows_here, HD), jnp.float32)
    empty_grad = jnp.zeros((KV_HEADS, rows_here, HD), jnp.float32)
    query_grad, key_grad, value_grad = backward_block(
        query_start, key_low, value_low, empty_grad, empty_grad, axis_place * rows_here
    )
    key_grad, value_grad = send_grads(key_grad, value_grad)

    def backward_step(turn_index, carry):
        query_grad, key_block, value_block, key_grad, value_grad = carry
        key_block, value_block = passed_along((key_block, value_block), "ctx", 1)
        source = axis_place - turn_index
        query_grad, key_grad, value_grad = backward_block(
            query_grad, key_block, value_block, key_grad, value_grad, source * rows_here
        )
        key_grad, value_grad = send_grads(key_grad, value_grad)
        return (query_grad, key_block, value_block, key_grad, value_grad)

    back_carry = lax.fori_loop(
        1, axis_count, backward_step, (query_grad, key_low, value_low, key_grad, value_grad)
    )
    query_grad = back_carry[0]
    key_grad = back_carry[3]
    value_grad = back_carry[4]
    query_heads_grad = query_grad.reshape(KV_HEADS, groups, rows_here, HD).transpose(2, 0, 1, 3)
    query_heads_grad = query_heads_grad.reshape(rows_here, HEADS, HD)
    query_raw_grad, key_raw_grad, value_raw_grad, query_gain_grad, key_gain_grad = heads_pull(
        (query_heads_grad, key_grad.transpose(1, 0, 2), value_grad.transpose(1, 0, 2))
    )
    query_back_low = query_raw_grad.astype(jnp.bfloat16)
    key_back_low = key_raw_grad.astype(jnp.bfloat16)
    value_back_low = value_raw_grad.astype(jnp.bfloat16)
    query_weight_grad = over_rows(normed_low, query_back_low)
    key_weight_grad = over_rows(normed_low, key_back_low)
    value_weight_grad = over_rows(normed_low, value_back_low)
    left_weight_grad = over_rows(normed_low, left_grad_low)
    normed_grad_two = (
        across(query_back_low, full_query)
        + across(key_back_low, full_key)
        + across(value_back_low, full_value)
        + across(left_grad_low, full_left)
    )
    inputs_grad_two, input_gain_grad = input_pull(normed_grad_one + normed_grad_two)
    block_out = result.astype(jnp.bfloat16)[None]
    tokens_grad = (inputs_grad_one + inputs_grad_two).astype(jnp.bfloat16)[None]
    per_layer_grad = extra_grad.astype(jnp.bfloat16)[None]
    (
        query_weight_grad,
        key_weight_grad,
        value_weight_grad,
        out_weight_grad,
        left_weight_grad,
        right_weight_grad,
        gate_weight_grad,
        up_weight_grad,
        down_weight_grad,
        side_gate_grad,
        side_out_grad,
        input_gain_grad,
        laurel_gain_grad,
        attn_gain_grad,
        pre_gain_grad,
        post_gain_grad,
        side_gain_grad,
        query_gain_grad,
        key_gain_grad,
    ) = (
        lax.psum_scatter(
            query_weight_grad.astype(jnp.bfloat16), "ctx", scatter_dimension=0, tiled=True
        ).astype(jnp.float32),
        lax.psum_scatter(
            key_weight_grad.astype(jnp.bfloat16), "ctx", scatter_dimension=0, tiled=True
        ).astype(jnp.float32),
        lax.psum_scatter(
            value_weight_grad.astype(jnp.bfloat16), "ctx", scatter_dimension=0, tiled=True
        ).astype(jnp.float32),
        lax.psum_scatter(
            out_weight_grad.astype(jnp.bfloat16), "ctx", scatter_dimension=0, tiled=True
        ).astype(jnp.float32),
        lax.psum_scatter(
            left_weight_grad.astype(jnp.bfloat16), "ctx", scatter_dimension=0, tiled=True
        ).astype(jnp.float32),
        lax.psum_scatter(
            right_weight_grad.astype(jnp.bfloat16), "ctx", scatter_dimension=1, tiled=True
        ).astype(jnp.float32),
        lax.psum_scatter(
            gate_weight_grad.astype(jnp.bfloat16), "ctx", scatter_dimension=0, tiled=True
        ).astype(jnp.float32),
        lax.psum_scatter(
            up_weight_grad.astype(jnp.bfloat16), "ctx", scatter_dimension=0, tiled=True
        ).astype(jnp.float32),
        lax.psum_scatter(
            down_weight_grad.astype(jnp.bfloat16), "ctx", scatter_dimension=1, tiled=True
        ).astype(jnp.float32),
        lax.psum_scatter(
            side_gate_grad.astype(jnp.bfloat16), "ctx", scatter_dimension=0, tiled=True
        ).astype(jnp.float32),
        lax.psum_scatter(
            side_out_grad.astype(jnp.bfloat16), "ctx", scatter_dimension=0, tiled=True
        ).astype(jnp.float32),
        lax.psum_scatter(
            input_gain_grad.astype(jnp.bfloat16), "ctx", scatter_dimension=0, tiled=True
        ).astype(jnp.float32),
        lax.psum_scatter(
            laurel_gain_grad.astype(jnp.bfloat16), "ctx", scatter_dimension=0, tiled=True
        ).astype(jnp.float32),
        lax.psum_scatter(
            attn_gain_grad.astype(jnp.bfloat16), "ctx", scatter_dimension=0, tiled=True
        ).astype(jnp.float32),
        lax.psum_scatter(
            pre_gain_grad.astype(jnp.bfloat16), "ctx", scatter_dimension=0, tiled=True
        ).astype(jnp.float32),
        lax.psum_scatter(
            post_gain_grad.astype(jnp.bfloat16), "ctx", scatter_dimension=0, tiled=True
        ).astype(jnp.float32),
        lax.psum_scatter(
            side_gain_grad.astype(jnp.bfloat16), "ctx", scatter_dimension=0, tiled=True
        ).astype(jnp.float32),
        lax.psum_scatter(
            query_gain_grad.astype(jnp.bfloat16), "ctx", scatter_dimension=0, tiled=True
        ).astype(jnp.float32),
        lax.psum_scatter(
            key_gain_grad.astype(jnp.bfloat16), "ctx", scatter_dimension=0, tiled=True
        ).astype(jnp.float32),
    )
    gate_weight_grad, up_weight_grad, down_weight_grad = (
        lax.psum_scatter(
            gate_weight_grad.astype(jnp.bfloat16), "fsdp", scatter_dimension=1, tiled=True
        ).astype(jnp.float32),
        lax.psum_scatter(
            up_weight_grad.astype(jnp.bfloat16), "fsdp", scatter_dimension=1, tiled=True
        ).astype(jnp.float32),
        lax.psum_scatter(
            down_weight_grad.astype(jnp.bfloat16), "fsdp", scatter_dimension=0, tiled=True
        ).astype(jnp.float32),
    )
    (
        query_weight_grad,
        key_weight_grad,
        value_weight_grad,
        out_weight_grad,
        left_weight_grad,
        right_weight_grad,
        side_gate_grad,
        side_out_grad,
        input_gain_grad,
        laurel_gain_grad,
        attn_gain_grad,
        pre_gain_grad,
        post_gain_grad,
        side_gain_grad,
        query_gain_grad,
        key_gain_grad,
    ) = (
        lax.psum_scatter(
            query_weight_grad.astype(jnp.bfloat16), "fsdp", scatter_dimension=1, tiled=True
        ).astype(jnp.float32),
        lax.psum_scatter(
            key_weight_grad.astype(jnp.bfloat16), "fsdp", scatter_dimension=1, tiled=True
        ).astype(jnp.float32),
        lax.psum_scatter(
            value_weight_grad.astype(jnp.bfloat16), "fsdp", scatter_dimension=1, tiled=True
        ).astype(jnp.float32),
        lax.psum_scatter(
            out_weight_grad.astype(jnp.bfloat16), "fsdp", scatter_dimension=1, tiled=True
        ).astype(jnp.float32),
        lax.psum_scatter(
            left_weight_grad.astype(jnp.bfloat16), "fsdp", scatter_dimension=0, tiled=True
        ).astype(jnp.float32),
        lax.psum_scatter(
            right_weight_grad.astype(jnp.bfloat16), "fsdp", scatter_dimension=1, tiled=True
        ).astype(jnp.float32),
        lax.psum_scatter(
            side_gate_grad.astype(jnp.bfloat16), "fsdp", scatter_dimension=1, tiled=True
        ).astype(jnp.float32),
        lax.psum_scatter(
            side_out_grad.astype(jnp.bfloat16), "fsdp", scatter_dimension=1, tiled=True
        ).astype(jnp.float32),
        lax.psum_scatter(
            input_gain_grad.astype(jnp.bfloat16), "fsdp", scatter_dimension=0, tiled=True
        ).astype(jnp.float32),
        lax.psum_scatter(
            laurel_gain_grad.astype(jnp.bfloat16), "fsdp", scatter_dimension=0, tiled=True
        ).astype(jnp.float32),
        lax.psum_scatter(
            attn_gain_grad.astype(jnp.bfloat16), "fsdp", scatter_dimension=0, tiled=True
        ).astype(jnp.float32),
        lax.psum_scatter(
            pre_gain_grad.astype(jnp.bfloat16), "fsdp", scatter_dimension=0, tiled=True
        ).astype(jnp.float32),
        lax.psum_scatter(
            post_gain_grad.astype(jnp.bfloat16), "fsdp", scatter_dimension=0, tiled=True
        ).astype(jnp.float32),
        lax.psum_scatter(
            side_gain_grad.astype(jnp.bfloat16), "fsdp", scatter_dimension=0, tiled=True
        ).astype(jnp.float32),
        lax.psum_scatter(
            query_gain_grad.astype(jnp.bfloat16), "fsdp", scatter_dimension=0, tiled=True
        ).astype(jnp.float32),
        lax.psum_scatter(
            key_gain_grad.astype(jnp.bfloat16), "fsdp", scatter_dimension=0, tiled=True
        ).astype(jnp.float32),
    )
    return (
        block_out,
        tokens_grad,
        per_layer_grad,
        query_weight_grad,
        key_weight_grad,
        value_weight_grad,
        out_weight_grad,
        left_weight_grad,
        right_weight_grad,
        gate_weight_grad,
        up_weight_grad,
        down_weight_grad,
        side_gate_grad,
        side_out_grad,
        input_gain_grad,
        laurel_gain_grad,
        attn_gain_grad,
        pre_gain_grad,
        post_gain_grad,
        side_gain_grad,
        query_gain_grad,
        key_gain_grad,
    )


def solution(mesh):
    placed = (
        P("fsdp", "ctx", None),
        P("fsdp", "ctx", None),
        P("fsdp", "ctx", None),
        P("fsdp", None),
        P("fsdp", None),
        P("fsdp", None),
        P("fsdp", None),
        P("fsdp", None),
        P("fsdp", None),
        P(None, "fsdp"),
        P(None, "fsdp"),
        P(None, "fsdp"),
        P("fsdp", None),
        P("fsdp", None),
        P("fsdp", None),
        P(),
        P(),
        P(),
        P(),
        P(),
        P(),
        P(),
        P(),
    )
    return jax.shard_map(
        body,
        mesh=mesh,
        in_specs=placed,
        out_specs=(
            P("fsdp", "ctx", None),
            P("fsdp", "ctx", None),
            P("fsdp", "ctx", None),
            P("ctx", "fsdp"),
            P("ctx", "fsdp"),
            P("ctx", "fsdp"),
            P("ctx", "fsdp"),
            P(("ctx", "fsdp"), None),
            P(None, ("ctx", "fsdp")),
            P("ctx", "fsdp"),
            P("ctx", "fsdp"),
            P("fsdp", "ctx"),
            P("ctx", "fsdp"),
            P("ctx", "fsdp"),
            P(("ctx", "fsdp")),
            P(("ctx", "fsdp")),
            P(("ctx", "fsdp")),
            P(("ctx", "fsdp")),
            P(("ctx", "fsdp")),
            P(("ctx", "fsdp")),
            P(("ctx", "fsdp")),
            P(("ctx", "fsdp")),
        ),
        check_vma=False,
    )
```

profile of v0, /device:TPU:0, one launch (start us, length us, event | category | flops | bytes accessed | tf_op | source)
XLA Modules:
  0.0 3679.8 jit_solution(6663124356101454462)
XLA Ops:
  15.1 17.9 all_gather.37
  33.1 16.3 all_gather.38
  52.7 12.1 all-gather.12.cloned.1.call-done
  70.2 42.1 %all-gather.10.cloned.1.call-done = bf16[2048,512]{1,0:T(8,128)(2,1)} async-done(((bf16[512,512]{1,0:T(8,128)(2,1)}), bf16[2048,512]{1,0:T(8,128)(2,1)}) %all-gather.10.cloned.1.call-update) | async-done | bytes 2097168 | tf_op jit(solution)/shard_map/all_gather | solution.py:136
  117.8 144.5 %all-gather.14.cloned.1.call-done = bf16[2048,2048]{1,0:T(8,128)(2,1)} async-done(((bf16[512,2048]{1,0:T(8,128)(2,1)}), bf16[2048,2048]{1,0:T(8,128)(2,1)}) %all-gather.14.cloned.1.call-update) | async-done | bytes 8388624 | tf_op jit(solution)/shard_map/all_gather | solution.py:135
  262.2 12.5 copy.93
  274.8 6.5 multiply_reduce_fusion.16
  283.5 77.8 %while.44 = (s32[]{:T(128)}, bf16[2,128,256]{2,1,0:T(8,128)(2,1)}, bf16[2,128,256]{2,1,0:T(8,128)(2,1)}, f32[2,512]{1,0:T(2,128)S(1)}, f32[2,512]{1,0:T(2,128)S(...) while((s32[]{:T(128)}, bf16[2,128,256]{2,1,0:T(8,128)(2,1)}, ...), condition=%wide.region_9.10_spmd.clone, body=%wide.region_6.9_spmd.clone.sunk | while | flops 136054912 | bytes 6369035 | solution.py:199
  329.1 4.5 collective-permute-start
  361.8 49.7 %all-gather.16.cloned.1.call-done = bf16[2048,2048]{1,0:T(8,128)(2,1)} async-done(((bf16[512,2048]{1,0:T(8,128)(2,1)}), bf16[2048,2048]{1,0:T(8,128)(2,1)}) %all-gather.16.cloned.1.call-update) | async-done | bytes 8388624 | tf_op jit(solution)/shard_map/all_gather | solution.py:138
  411.6 4.8 multiply_reduce_fusion.15
  419.2 553.4 %all-gather.18.cloned.1.call-done = bf16[2048,8192]{1,0:T(8,128)(2,1)} async-done(((bf16[2048,2048]{1,0:T(8,128)(2,1)}), bf16[2048,8192]{1,0:T(8,128)(2,1)}) %all-gather.18.cloned.1.call-update) | async-done | bytes 33554448 | tf_op jit(solution)/shard_map/all_gather | solution.py:218
  972.6 21.2 fusion.128
  993.9 539.8 %all-gather.20.cloned.1.call-done = bf16[2048,8192]{1,0:T(8,128)(2,1)} async-done(((bf16[2048,2048]{1,0:T(8,128)(2,1)}), bf16[2048,8192]{1,0:T(8,128)(2,1)}) %all-gather.20.cloned.1.call-update) | async-done | bytes 33554448 | tf_op jit(solution)/shard_map/all_gather | solution.py:219
  1533.7 21.8 multiply_convert_fusion.1
  1555.5 539.4 %all-gather.22.cloned.1.call-done = bf16[8192,2048]{1,0:T(8,128)(2,1)} async-done(((bf16[2048,2048]{1,0:T(8,128)(2,1)}), bf16[8192,2048]{1,0:T(8,128)(2,1)}) %all-gather.22.cloned.1.call-update) | async-done | bytes 33554448 | tf_op jit(solution)/shard_map/all_gather | solution.py:220
  2094.9 14.2 multiply_reduce_fusion.12
  2111.4 11.2 all-gather.24.cloned.1.call-done
  2125.1 26.5 all-gather.26.cloned.1.call-done
  2160.7 20.6 multiply_convert_fusion
  2181.4 17.4 fusion.129
  2198.8 18.7 multiply_reduce_fusion.2
  2230.1 7.2 convolution_convert_fusion.9
  2251.4 130.1 %while.45 = (s32[]{:T(128)}, f32[2,512,256]{2,1,0:T(8,128)S(1)}, bf16[2,128,256]{2,1,0:T(8,128)(2,1)}, bf16[2,128,256]{2,1,0:T(8,128)(2,1)}, f32[2,128,256]{2,1,...) while((s32[]{:T(128)}, f32[2,512,256]{2,1,0:T(8,128)S(1)}, ...), condition=%wide.region_21.22_spmd.clone, body=%wide.region_20.21_spmd.clone.sunk | while | flops 337248384 | bytes 12373959 | solution.py:311
  2288.3 4.5 collective-permute-start.2
  2361.0 5.1 collective-permute-start.3
  2393.0 6.7 convolution_convert_fusion.3
  2402.8 5.8 convolution_convert_fusion.4
  2410.2 15.0 convolution_convert_fusion.2
  2426.8 13.8 convolution_convert_fusion
  2442.3 13.8 convolution_convert_fusion.1
  2463.6 13.9 reduce-scatter.37.cloned.1.call-done
  2479.3 72.7 %reduce-scatter.41.cloned.1.call-done = bf16[256,2048]{1,0:T(8,128)(2,1)} async-done(((bf16[2048,2048]{1,0:T(8,128)(2,1)}), bf16[256,2048]{1,0:T(8,128)(2,1)}) %reduce-scatter.41.cloned.1.call-update) | async-done | bytes 1048592 | tf_op jit(solution)/shard_map/reduce_scatter | solution.py:369
  2552.1 75.0 %reduce-scatter.33.cloned.1.call-done = bf16[256,2048]{1,0:T(8,128)(2,1)} async-done(((bf16[2048,2048]{1,0:T(8,128)(2,1)}), bf16[256,2048]{1,0:T(8,128)(2,1)}) %reduce-scatter.33.cloned.1.call-update) | async-done | bytes 1048592 | tf_op jit(solution)/shard_map/reduce_scatter | solution.py:360
  2627.1 208.6 %reduce-scatter.57.cloned.1.call-done = bf16[8192,256]{1,0:T(8,128)(2,1)} async-done(((bf16[8192,2048]{1,0:T(8,128)(2,1)}), bf16[8192,256]{1,0:T(8,128)(2,1)}) %reduce-scatter.57.cloned.1.call-update) | async-done | bytes 4194320 | tf_op jit(solution)/shard_map/reduce_scatter | solution.py:384
  2835.8 209.2 %reduce-scatter.53.cloned.1.call-done = bf16[256,8192]{1,0:T(8,128)(2,1)} async-done(((bf16[2048,8192]{1,0:T(8,128)(2,1)}), bf16[256,8192]{1,0:T(8,128)(2,1)}) %reduce-scatter.53.cloned.1.call-update) | async-done | bytes 4194320 | tf_op jit(solution)/shard_map/reduce_scatter | solution.py:381
  3045.1 208.6 %reduce-scatter.49.cloned.1.call-done = bf16[256,8192]{1,0:T(8,128)(2,1)} async-done(((bf16[2048,8192]{1,0:T(8,128)(2,1)}), bf16[256,8192]{1,0:T(8,128)(2,1)}) %reduce-scatter.49.cloned.1.call-update) | async-done | bytes 4194320 | tf_op jit(solution)/shard_map/reduce_scatter | solution.py:378
  3257.6 6.4 fusion.130
  3267.3 23.3 all-reduce.20
  3291.2 11.8 all-reduce.21
  3317.6 17.9 reduce-scatter.65.cloned.1.call-done
  3337.0 19.3 reduce-scatter.69.cloned.1.call-done
  3357.9 19.1 reduce-scatter.67.cloned.1.call-done
  3378.6 26.0 reduce-scatter.43.cloned.1.call-done
  3406.4 26.3 reduce-scatter.35.cloned.1.call-done
  3434.6 76.0 %reduce-scatter.59.cloned.1.call-done = bf16[2048,256]{1,0:T(8,128)(2,1)} async-done(((bf16[8192,256]{1,0:T(8,128)(2,1)}), bf16[2048,256]{1,0:T(8,128)(2,1)}) %reduce-scatter.59.cloned.1.call-update) | async-done | bytes 1048592 | tf_op jit(solution)/shard_map/reduce_scatter | solution.py:425
  3513.3 76.7 %reduce-scatter.55.cloned.1.call-done = bf16[256,2048]{1,0:T(8,128)(2,1)} async-done(((bf16[256,8192]{1,0:T(8,128)(2,1)}), bf16[256,2048]{1,0:T(8,128)(2,1)}) %reduce-scatter.55.cloned.1.call-update) | async-done | bytes 1048592 | tf_op jit(solution)/shard_map/reduce_scatter | solution.py:422
  3592.8 76.9 %reduce-scatter.51.cloned.1.call-done = bf16[256,2048]{1,0:T(8,128)(2,1)} async-done(((bf16[256,8192]{1,0:T(8,128)(2,1)}), bf16[256,2048]{1,0:T(8,128)(2,1)}) %reduce-scatter.51.cloned.1.call-update) | async-done | bytes 1048592 | tf_op jit(solution)/shard_map/reduce_scatter | solution.py:419
  (740 shorter events, 324.0 us)
Async XLA Ops:
  7.2 57.6 %all-gather.12.cloned.1.call-start = ((), (), s32[]{:S(2)}) async-start(), calls=%async_computation.23 | async-start | bytes 2621440 | tf_op jit(solution)/shard_map/all_gather | solution.py:137
  7.9 104.3 %all-gather.10.cloned.1.call-start = ((), (), s32[]{:S(2)}) async-start(), calls=%async_computation.22 | async-start | bytes 2621440 | tf_op jit(solution)/shard_map/all_gather | solution.py:136
  8.7 253.6 %all-gather.14.cloned.1.call-start = ((), (), s32[]{:S(2)}) async-start(), calls=%async_computation.24 | async-start | bytes 10485760 | tf_op jit(solution)/shard_map/all_gather | solution.py:135
  9.4 402.1 %all-gather.16.cloned.1.call-start = ((), (), s32[]{:S(2)}) async-start(), calls=%async_computation.25 | async-start | bytes 10485760 | tf_op jit(solution)/shard_map/all_gather | solution.py:138
  10.0 962.7 %all-gather.18.cloned.1.call-start = ((), (), s32[]{:S(2)}) async-start(), calls=%async_computation.26 | async-start | bytes 41943040 | tf_op jit(solution)/shard_map/all_gather | solution.py:218
  10.6 1523.1 %all-gather.20.cloned.1.call-start = ((), (), s32[]{:S(2)}) async-start(), calls=%async_computation.27 | async-start | bytes 41943040 | tf_op jit(solution)/shard_map/all_gather | solution.py:219
  11.2 2083.7 %all-gather.22.cloned.1.call-start = ((), (), s32[]{:S(2)}) async-start(), calls=%async_computation.28 | async-start | bytes 41943040 | tf_op jit(solution)/shard_map/all_gather | solution.py:220
  12.0 2110.7 %all-gather.24.cloned.1.call-start = ((), (), s32[]{:S(2)}) async-start(), calls=%async_computation.29 | async-start | bytes 1310720 | tf_op jit(solution)/shard_map/all_gather | solution.py:141
  12.7 2138.9 %all-gather.26.cloned.1.call-start = ((), (), s32[]{:S(2)}) async-start(), calls=%async_computation.30 | async-start | bytes 1310720 | tf_op jit(solution)/shard_map/all_gather | solution.py:142
  13.4 2442.7 %reduce-scatter.47.cloned.1.call-start = ((), (), s32[]{:S(2)}) async-start(), calls=%async_computation.38 | async-start | bytes 294912 | tf_op jit(solution)/shard_map/reduce_scatter | solution.py:375
  283.5 8.2 collective-permute-start.1
  293.0 9.7 collective-permute-start.1
  303.9 9.6 collective-permute-start.1
  314.7 10.0 collective-permute-start.1
  325.9 10.5 collective-permute-start.1
  337.6 10.5 collective-permute-start.1
  349.4 10.5 collective-permute-start.1
  2223.8 233.9 %reduce-scatter.45.cloned.1.call-start = ((), (), s32[]{:S(2)}) async-start(), calls=%async_computation.37 | async-start | bytes 294912 | tf_op jit(solution)/shard_map/reduce_scatter | solution.py:372
  2226.6 232.7 %reduce-scatter.61.cloned.1.call-start = ((), (), s32[]{:S(2)}) async-start(), calls=%async_computation.45 | async-start | bytes 1179648 | tf_op jit(solution)/shard_map/reduce_scatter | solution.py:387
  2230.0 231.1 %reduce-scatter.63.cloned.1.call-start = ((), (), s32[]{:S(2)}) async-start(), calls=%async_computation.46 | async-start | bytes 1179648 | tf_op jit(solution)/shard_map/reduce_scatter | solution.py:390
  2247.4 214.3 %reduce-scatter.39.cloned.1.call-start = ((), (), s32[]{:S(2)}) async-start(), calls=%async_computation.34 | async-start | bytes 2359296 | tf_op jit(solution)/shard_map/reduce_scatter | solution.py:366
  2251.4 7.5 collective-permute-start.3
  2267.2 9.6 collective-permute-start.3
  2279.0 6.8 collective-permute-start.5
  2285.9 9.9 collective-permute-start.3
  2304.1 10.6 collective-permute-start.3
  2316.2 7.5 collective-permute-start.4
  2316.9 8.9 collective-permute-start.5
  2325.9 7.8 collective-permute-start.3
  2342.3 10.3 collective-permute-start.3
  2361.0 11.9 collective-permute-start.3
  2387.4 90.0 %reduce-scatter.37.cloned.1.call-start = ((), (), s32[]{:S(2)}) async-start(), calls=%async_computation.33 | async-start | bytes 2359296 | tf_op jit(solution)/shard_map/reduce_scatter | solution.py:363
  2393.0 159.1 %reduce-scatter.41.cloned.1.call-start = ((), (), s32[]{:S(2)}) async-start(), calls=%async_computation.35 | async-start | bytes 9437184 | tf_op jit(solution)/shard_map/reduce_scatter | solution.py:369
  2399.7 227.3 %reduce-scatter.33.cloned.1.call-start = ((), (), s32[]{:S(2)}) async-start(), calls=%async_computation.31 | async-start | bytes 9437184 | tf_op jit(solution)/shard_map/reduce_scatter | solution.py:360
  2408.6 427.1 %reduce-scatter.57.cloned.1.call-start = ((), (), s32[]{:S(2)}) async-start(), calls=%async_computation.43 | async-start | bytes 37748736 | tf_op jit(solution)/shard_map/reduce_scatter | solution.py:384
  2425.2 619.8 %reduce-scatter.53.cloned.1.call-start = ((), (), s32[]{:S(2)}) async-start(), calls=%async_computation.41 | async-start | bytes 37748736 | tf_op jit(solution)/shard_map/reduce_scatter | solution.py:381
  2440.5 813.2 %reduce-scatter.49.cloned.1.call-start = ((), (), s32[]{:S(2)}) async-start(), calls=%async_computation.39 | async-start | bytes 37748736 | tf_op jit(solution)/shard_map/reduce_scatter | solution.py:378
  2456.1 852.8 %reduce-scatter.73.cloned.1.call-start = ((), (), s32[]{:S(2)}) async-start(), calls=%async_computation.51 | async-start | bytes 81920
  2457.7 852.7 %reduce-scatter.71.cloned.1.call-start = ((), (), s32[]{:S(2)}) async-start(), calls=%async_computation.50 | async-start | bytes 81920
  2459.3 856.8 %reduce-scatter.75.cloned.1.call-start = ((), (), s32[]{:S(2)}) async-start(), calls=%async_computation.52 | async-start | bytes 163840
  2461.0 874.5 %reduce-scatter.65.cloned.1.call-start = ((), (), s32[]{:S(2)}) async-start(), calls=%async_computation.47 | async-start | bytes 163840 | tf_op jit(solution)/shard_map/reduce_scatter | solution.py:468
  2461.6 894.7 %reduce-scatter.69.cloned.1.call-start = ((), (), s32[]{:S(2)}) async-start(), calls=%async_computation.49 | async-start | bytes 327680
  2463.5 913.5 %reduce-scatter.67.cloned.1.call-start = ((), (), s32[]{:S(2)}) async-start(), calls=%async_computation.48 | async-start | bytes 327680
  2479.3 925.4 %reduce-scatter.43.cloned.1.call-start = ((), (), s32[]{:S(2)}) async-start(), calls=%async_computation.36 | async-start | bytes 1310720 | tf_op jit(solution)/shard_map/reduce_scatter | solution.py:456
  2552.1 880.7 %reduce-scatter.35.cloned.1.call-start = ((), (), s32[]{:S(2)}) async-start(), calls=%async_computation.32 | async-start | bytes 1310720 | tf_op jit(solution)/shard_map/reduce_scatter | solution.py:447
  2627.1 883.5 %reduce-scatter.59.cloned.1.call-start = ((), (), s32[]{:S(2)}) async-start(), calls=%async_computation.44 | async-start | bytes 5242880 | tf_op jit(solution)/shard_map/reduce_scatter | solution.py:425
  2835.8 754.2 %reduce-scatter.55.cloned.1.call-start = ((), (), s32[]{:S(2)}) async-start(), calls=%async_computation.42 | async-start | bytes 5242880 | tf_op jit(solution)/shard_map/reduce_scatter | solution.py:422
  3045.1 624.7 %reduce-scatter.51.cloned.1.call-start = ((), (), s32[]{:S(2)}) async-start(), calls=%async_computation.40 | async-start | bytes 5242880 | tf_op jit(solution)/shard_map/reduce_scatter | solution.py:419
  (166 other events, 3866.6 us)
Sparse Core Ops, SparseCore 0:
  9.6 55.1 all-gather.11
  66.4 45.8 all-gather.9
  113.8 148.3 all-gather.13
  263.7 147.8 all-gather.15
  413.0 559.6 all-gather.17
  974.1 559.5 all-gather.19
  1535.3 559.5 all-gather.21
  2096.5 26.1 all-gather.23
  2124.2 27.4 all-gather.25
  2224.0 33.1 reduce-scatter.46
  2260.5 33.6 reduce-scatter.44
  2297.2 37.3 reduce-scatter.60
  2337.8 36.8 reduce-scatter.62
  2387.5 45.1 reduce-scatter.38
  2436.2 41.2 reduce-scatter.36
  2480.8 71.2 reduce-scatter.40
  2555.7 71.2 reduce-scatter.32
  2630.5 205.2 reduce-scatter.56
  2839.7 205.2 reduce-scatter.52
  3048.4 205.2 reduce-scatter.48
  3256.6 18.9 reduce-scatter.72
  3278.5 17.1 reduce-scatter.70
  3298.6 17.3 reduce-scatter.74
  3318.1 17.3 reduce-scatter.64
  3338.5 17.7 reduce-scatter.68
  3359.0 17.9 reduce-scatter.66
  3379.2 25.3 reduce-scatter.42
  3406.9 25.7 reduce-scatter.34
  3435.1 75.4 reduce-scatter.58
  3512.7 77.2 reduce-scatter.54
  3592.4 77.2 reduce-scatter.50
where the time goes:
time: 3690 us; the launch traced here: 3680 us
  waiting for transfers between devices  3060 us (83%)
  matrix products  251 us (7%)
  starting transfers between devices  124 us (3%)
  local copies, waits for them, and re-layouts  97.6 us (3%)
  blocking collectives  69.4 us (2%)
  other arithmetic  55.6 us (2%)
    all_gather x1, waiting for transfers between devices, body(): lax.all_gather(gate_weight, 'fsdp', axis=1, tiled=True)  553 us
    all_gather x1, waiting for transfers between devices, body(): lax.all_gather(up_weight, 'fsdp', axis=1, tiled=True)  540 us
    all_gather x1, waiting for transfers between devices, body(): lax.all_gather(down_weight, 'fsdp', axis=0, tiled=True)  539 us
    reduce_scatter x1, waiting for transfers between devices, body(): lax.psum_scatter(up_weight_grad.astype(jnp.bfloat16), 'ctx', scatter_dime...  209 us
    reduce_scatter x1, waiting for transfers between devices, body(): lax.psum_scatter(gate_weight_grad.astype(jnp.bfloat16), 'ctx', scatter_di...  209 us
    reduce_scatter x1, waiting for transfers between devices, body(): lax.psum_scatter(down_weight_grad.astype(jnp.bfloat16), 'ctx', scatter_di...  209 us
    all_gather x1, waiting for transfers between devices, body(): lax.all_gather(query_weight, 'fsdp', axis=0, tiled=True)  144 us
    ppermute x28, starting transfers between devices, passed_along(): return lax.ppermute(shard, axis, pairs)  95.9 us
  transfers between devices with their start and end apart: 75, of which 31 were waited for; matrix products, arithmetic and copies ran while one was open for 9% of the time, Pallas kernels for 0%

commit v1 on v0

v1 whole, which is shorter than its diff:
```python
import math

import jax
import jax.numpy as jnp
from jax import lax
from jax.sharding import PartitionSpec as P

HEADS = 8
KV_HEADS = 2
HD = 256


epsilon = 1e-06
rope_theta = 1000000.0
masked_score = -1e30
inverse_root = 1.0 / math.sqrt(2.0)


def rms_norm(v, factor):
    return v * lax.rsqrt(jnp.mean(v * v, axis=-1, keepdims=True) + epsilon) * factor


def rotate(v, positions):
    halfway = v.shape[-1] // 2
    frequency = jnp.exp(
        jnp.arange(halfway).astype(jnp.float32) * (-2.0 * math.log(rope_theta) / v.shape[-1])
    )
    angles = positions.astype(jnp.float32)[:, None] * frequency[None, :]
    cosine = jnp.cos(angles)[:, None, :]
    sine_part = jnp.sin(angles)[:, None, :]
    leading = v[..., :halfway]
    trailing = v[..., halfway:]
    return jnp.concatenate(
        [leading * cosine - trailing * sine_part, trailing * cosine + leading * sine_part], axis=-1
    )


def forward_product(a, b):
    return jnp.dot(a, b, preferred_element_type=jnp.float32)


def across(a, b):
    return lax.dot_general(a, b, (((1,), (1,)), ((), ())), preferred_element_type=jnp.float32)


def over_rows(a, b):
    return lax.dot_general(a, b, (((0,), (0,)), ((), ())), preferred_element_type=jnp.float32)


def hidden_piece(gate_in, up_in):
    return jax.nn.gelu(gate_in, approximate=True) * up_in


def middle_piece(mixed_in, ffn_in_rows, factor):
    return mixed_in + rms_norm(ffn_in_rows, factor)


def gather(x, axis):
    return lax.all_gather(x, axis, axis=0, tiled=True)


def scatter_sum(x, axis):
    return lax.psum_scatter(x, axis, scatter_dimension=0, tiled=True)


def blocks_of(grad, rows, columns):
    tall = grad.reshape(rows, grad.shape[0] // rows, columns, grad.shape[1] // columns)
    return tall.transpose(0, 2, 1, 3).reshape(rows * columns, -1)


def body(
    tokens,
    per_layer,
    out_grad,
    segment_ids,
    query_weight,
    key_weight,
    value_weight,
    out_weight,
    left_weight,
    right_weight,
    gate_weight,
    up_weight,
    down_weight,
    side_gate,
    side_out,
    input_gain,
    laurel_gain,
    attn_gain,
    pre_gain,
    post_gain,
    side_gain,
    query_gain,
    key_gain,
):
    low = jnp.bfloat16
    inputs = tokens[0].astype(jnp.float32)
    extra_rows = per_layer[0].astype(jnp.float32)
    cotangent = out_grad[0].astype(jnp.float32)
    sequence_ids = segment_ids[0]
    rows_here, width = inputs.shape
    ctx_count = lax.axis_size("ctx")
    fsdp_count = lax.axis_size("fsdp")
    count = ctx_count * fsdp_count
    ctx_place = lax.axis_index("ctx")
    groups = HEADS // KV_HEADS
    rank = left_weight.shape[1]
    side = side_gate.shape[1]
    length = sequence_ids.shape[0]
    query_width = HEADS * HD
    kv_width = KV_HEADS * HD
    query_pos = ctx_place * rows_here + jnp.arange(rows_here, dtype=jnp.int32)

    piece = width // count

    def own_rows(weight):
        step = weight.shape[0] // ctx_count
        return lax.dynamic_slice_in_dim(weight, ctx_place * step, step)

    first_set = jnp.concatenate(
        [own_rows(w) for w in (query_weight, key_weight, value_weight, left_weight)], axis=1
    )
    second_set = jnp.concatenate(
        [
            own_rows(out_weight),
            own_rows(side_gate),
            own_rows(side_out).reshape(piece, -1),
            own_rows(right_weight).reshape(piece, -1),
        ],
        axis=1,
    )
    full_first = gather(first_set, ("fsdp", "ctx"))
    full_second = gather(second_set, ("fsdp", "ctx"))
    qkv_width = query_width + 2 * kv_width
    full_qkv = full_first[:, :qkv_width]
    full_left = full_first[:, qkv_width:]
    full_out = full_second[:, :width]
    full_side_gate = full_second[:, width : width + side]
    full_side_out = full_second[:, width + side : width + 2 * side].reshape(side, width)
    full_right = full_second[:, width + 2 * side :]
    full_right = full_right.reshape(fsdp_count, rank, width // fsdp_count)
    full_right = full_right.transpose(1, 0, 2).reshape(rank, width)

    normed, input_pull = jax.vjp(rms_norm, inputs, input_gain)
    normed_low = normed.astype(low)
    normed_all = gather(normed_low, "fsdp")
    qkv_raw = forward_product(normed_low, full_qkv)
    left_low = forward_product(normed_low, full_left).astype(low)
    right_out = forward_product(left_low, full_right)

    def heads_piece(qkv_in, gain_one, gain_two):
        query_in = qkv_in[:, :query_width].reshape(rows_here, HEADS, HD)
        key_in = qkv_in[:, query_width : query_width + kv_width].reshape(rows_here, KV_HEADS, HD)
        value_in = qkv_in[:, query_width + kv_width :].reshape(rows_here, KV_HEADS, HD)
        query_heads = rotate(rms_norm(query_in, gain_one), query_pos)
        key_heads = rotate(rms_norm(key_in, gain_two), query_pos)
        value_heads = rms_norm(value_in, 1.0)
        return (query_heads, key_heads, value_heads)

    (query_heads, key_heads, value_heads), heads_pull = jax.vjp(
        heads_piece, qkv_raw, query_gain, key_gain
    )
    query_low = query_heads.astype(low).reshape(rows_here, KV_HEADS, groups, HD)
    query_low = query_low.transpose(1, 2, 0, 3).reshape(KV_HEADS, groups * rows_here, HD)
    kv_low = jnp.concatenate(
        [key_heads.astype(low).reshape(rows_here, -1), value_heads.astype(low).reshape(rows_here, -1)],
        axis=1,
    )
    kv_all = gather(kv_low, "ctx")
    key_all = kv_all[:, :kv_width].reshape(length, KV_HEADS, HD).transpose(1, 0, 2)
    value_all = kv_all[:, kv_width:].reshape(length, KV_HEADS, HD).transpose(1, 0, 2)

    query_ids = lax.dynamic_slice_in_dim(sequence_ids, ctx_place * rows_here, rows_here)
    key_pos = jnp.arange(length, dtype=jnp.int32)
    allowed = (query_ids[:, None] == sequence_ids[None, :]) & (
        key_pos[None, :] <= query_pos[:, None]
    )
    allowed = jnp.tile(allowed, (groups, 1))[None]
    scores = jnp.einsum("kqd,kjd->kqj", query_low, key_all, preferred_element_type=jnp.float32)
    scores = jnp.where(allowed, scores, masked_score)
    row_max = jnp.max(scores, axis=-1, keepdims=True)
    weights = jnp.where(allowed, jnp.exp(scores - row_max), 0.0)
    weights = weights / jnp.sum(weights, axis=-1, keepdims=True)
    weights_low = weights.astype(low)
    attended_rows = jnp.einsum(
        "kqj,kjd->kqd", weights_low, value_all, preferred_element_type=jnp.float32
    )
    attended = attended_rows.reshape(KV_HEADS, groups, rows_here, HD).transpose(2, 0, 1, 3)
    attended_low = attended.reshape(rows_here, query_width).astype(low)
    attended_all = gather(attended_low, "fsdp")
    attn_raw = forward_product(attended_low, full_out)

    def mix_piece(x, normed_in, attn_in, right_in, gain_one, gain_two, gain_three):
        mixed = (
            x + rms_norm(attn_in, gain_one) + normed_in + rms_norm(right_in, gain_two)
        ) * inverse_root
        return (mixed, rms_norm(mixed, gain_three))

    (mixed, ffn_in), mix_pull = jax.vjp(
        mix_piece, inputs, normed, attn_raw, right_out, attn_gain, laurel_gain, pre_gain
    )

    ffn_all = gather(ffn_in.astype(low), "fsdp")
    gate_raw = forward_product(ffn_all, gate_weight)
    up_raw = forward_product(ffn_all, up_weight)
    hidden, hidden_pull = jax.vjp(hidden_piece, gate_raw, up_raw)
    hidden_low = hidden.astype(low)
    ffn_out = scatter_sum(forward_product(hidden_low, down_weight).astype(low), "fsdp")
    ffn_out = ffn_out.astype(jnp.float32)
    middle, middle_pull = jax.vjp(middle_piece, mixed, ffn_out, post_gain)
    middle_low = middle.astype(low)
    layer_gate = forward_product(middle_low, full_side_gate)
    layer_act, extra_pull = jax.vjp(hidden_piece, layer_gate, extra_rows)
    layer_low = layer_act.astype(low)
    layer_out = forward_product(layer_low, full_side_out)
    result, out_pull = jax.vjp(middle_piece, middle, layer_out, side_gain)

    middle_grad_one, layer_out_grad, side_gain_grad = out_pull(cotangent)
    layer_grad_low = layer_out_grad.astype(low)
    side_out_grad = over_rows(layer_low, layer_grad_low)
    layer_gate_grad, extra_grad = extra_pull(across(layer_grad_low, full_side_out))
    gate_grad_low = layer_gate_grad.astype(low)
    side_gate_grad = over_rows(middle_low, gate_grad_low)
    mixed_grad_one, ffn_out_grad, post_gain_grad = middle_pull(
        middle_grad_one + across(gate_grad_low, full_side_gate)
    )
    ffn_grad_all = gather(ffn_out_grad.astype(low), "fsdp")
    down_weight_grad = over_rows(ffn_grad_all, hidden_low)
    gate_raw_grad, up_raw_grad = hidden_pull(across(ffn_grad_all, down_weight))
    gate_back_low = gate_raw_grad.astype(low)
    up_back_low = up_raw_grad.astype(low)
    ffn_in_grad = scatter_sum(
        (across(gate_back_low, gate_weight) + across(up_back_low, up_weight)).astype(low), "fsdp"
    )
    gate_weight_grad = over_rows(ffn_all, gate_back_low)
    up_weight_grad = over_rows(ffn_all, up_back_low)
    (
        inputs_grad_one,
        normed_grad_one,
        attn_raw_grad,
        right_out_grad,
        attn_gain_grad,
        laurel_gain_grad,
        pre_gain_grad,
    ) = mix_pull((mixed_grad_one, ffn_in_grad.astype(jnp.float32)))
    attn_grad_low = attn_raw_grad.astype(low)
    attended_grad_low = across(attn_grad_low, full_out).astype(low)
    right_grad_low = right_out_grad.astype(low)
    right_weight_grad = over_rows(right_grad_low, left_low)
    left_grad_low = across(right_grad_low, full_right).astype(low)
    left_weight_grad = over_rows(normed_low, left_grad_low)
    grad_rows = attended_grad_low.reshape(rows_here, KV_HEADS, groups, HD).transpose(1, 2, 0, 3)
    grad_rows = grad_rows.reshape(KV_HEADS, groups * rows_here, HD)
    correction = jnp.sum(
        grad_rows.astype(jnp.float32) * attended_rows, axis=-1, keepdims=True
    )
    weight_grad = jnp.einsum(
        "kqd,kjd->kqj", grad_rows, value_all, preferred_element_type=jnp.float32
    )
    score_grad = (weights * (weight_grad - correction)).astype(low)
    query_grad = jnp.einsum(
        "kqj,kjd->kqd", score_grad, key_all, preferred_element_type=jnp.float32
    )
    key_grad = jnp.einsum(
        "kqj,kqd->kjd", score_grad, query_low, preferred_element_type=jnp.float32
    )
    value_grad = jnp.einsum(
        "kqj,kqd->kjd", weights_low, grad_rows, preferred_element_type=jnp.float32
    )
    kv_grad = jnp.concatenate([key_grad.astype(low), value_grad.astype(low)], axis=0)
    kv_grad = kv_grad.transpose(1, 0, 2).reshape(length, 2 * kv_width)
    kv_grad = scatter_sum(kv_grad, "ctx").astype(jnp.float32)
    kv_grad = kv_grad.reshape(rows_here, 2, KV_HEADS, HD)
    query_heads_grad = query_grad.reshape(KV_HEADS, groups, rows_here, HD).transpose(2, 0, 1, 3)
    query_heads_grad = query_heads_grad.reshape(rows_here, HEADS, HD)
    qkv_grad, query_gain_grad, key_gain_grad = heads_pull(
        (query_heads_grad, kv_grad[:, 0], kv_grad[:, 1])
    )
    qkv_back_low = qkv_grad.astype(low)
    normed_grad_two = across(qkv_back_low, full_qkv) + across(left_grad_low, full_left)
    inputs_grad_two, input_gain_grad = input_pull(normed_grad_one + normed_grad_two)
    block_out = result.astype(low)[None]
    tokens_grad = (inputs_grad_one + inputs_grad_two).astype(low)[None]
    per_layer_grad = extra_grad.astype(low)[None]

    def columns_to_owner(x):
        parts = x.reshape(rows_here, fsdp_count, -1).transpose(1, 0, 2)
        return lax.all_to_all(parts, "fsdp", 0, 0, tiled=True).reshape(fsdp_count * rows_here, -1)

    out_columns = columns_to_owner(attn_grad_low)
    out_weight_grad = scatter_sum(over_rows(attended_all, out_columns).astype(low), "ctx")
    qkv_parts = jnp.concatenate(
        [
            part.reshape(rows_here, fsdp_count, -1)
            for part in (
                qkv_back_low[:, :query_width],
                qkv_back_low[:, query_width : query_width + kv_width],
                qkv_back_low[:, query_width + kv_width :],
            )
        ],
        axis=2,
    )
    qkv_columns = columns_to_owner(qkv_parts.reshape(rows_here, -1))
    qkv_weight_grad = scatter_sum(over_rows(normed_all, qkv_columns).astype(low), "ctx")
    query_part = query_width // fsdp_count
    kv_part = kv_width // fsdp_count
    query_weight_grad = qkv_weight_grad[:, :query_part]
    key_weight_grad = qkv_weight_grad[:, query_part : query_part + kv_part]
    value_weight_grad = qkv_weight_grad[:, query_part + kv_part :]
    down_weight_grad = scatter_sum(down_weight_grad.astype(low), "ctx").T
    gate_weight_grad = scatter_sum(gate_weight_grad.astype(low), "ctx")
    up_weight_grad = scatter_sum(up_weight_grad.astype(low), "ctx")

    small = [
        left_weight_grad.reshape(count, -1),
        right_weight_grad.reshape(count, -1),
        blocks_of(side_gate_grad, ctx_count, fsdp_count),
        blocks_of(side_out_grad, ctx_count, fsdp_count),
        input_gain_grad.reshape(count, -1),
        laurel_gain_grad.reshape(count, -1),
        attn_gain_grad.reshape(count, -1),
        pre_gain_grad.reshape(count, -1),
        post_gain_grad.reshape(count, -1),
        side_gain_grad.reshape(count, -1),
        query_gain_grad.reshape(count, -1),
        key_gain_grad.reshape(count, -1),
    ]
    sizes = [part.shape[1] for part in small]
    packed = jnp.concatenate([part.astype(low) for part in small], axis=1)
    packed = jnp.pad(packed, ((0, 0), (0, -packed.shape[1] % 128)))
    packed = scatter_sum(packed.reshape(-1, 128), ("ctx", "fsdp")).reshape(-1)
    shares = []
    start = 0
    for size in sizes:
        shares.append(packed[start : start + size].astype(jnp.float32))
        start += size
    left_weight_grad = shares[0].reshape(-1, rank)
    right_weight_grad = shares[1].reshape(-1, rank).T
    side_gate_grad = shares[2].reshape(width // ctx_count, -1)
    side_out_grad = shares[3].reshape(side // ctx_count, -1)
    wide = jnp.float32
    return (
        block_out,
        tokens_grad,
        per_layer_grad,
        query_weight_grad.astype(wide),
        key_weight_grad.astype(wide),
        value_weight_grad.astype(wide),
        out_weight_grad.astype(wide),
        left_weight_grad,
        right_weight_grad,
        gate_weight_grad.astype(wide),
        up_weight_grad.astype(wide),
        down_weight_grad.astype(wide),
        side_gate_grad,
        side_out_grad,
        *shares[4:],
    )


def solution(mesh):
    placed = (
        P("fsdp", "ctx", None),
        P("fsdp", "ctx", None),
        P("fsdp", "ctx", None),
        P("fsdp", None),
        P("fsdp", None),
        P("fsdp", None),
        P("fsdp", None),
        P("fsdp", None),
        P("fsdp", None),
        P(None, "fsdp"),
        P(None, "fsdp"),
        P(None, "fsdp"),
        P("fsdp", None),
        P("fsdp", None),
        P("fsdp", None),
        P(),
        P(),
        P(),
        P(),
        P(),
        P(),
        P(),
        P(),
    )
    return jax.shard_map(
        body,
        mesh=mesh,
        in_specs=placed,
        out_specs=(
            P("fsdp", "ctx", None),
            P("fsdp", "ctx", None),
            P("fsdp", "ctx", None),
            P("ctx", "fsdp"),
            P("ctx", "fsdp"),
            P("ctx", "fsdp"),
            P("ctx", "fsdp"),
            P(("ctx", "fsdp"), None),
            P(None, ("ctx", "fsdp")),
            P("ctx", "fsdp"),
            P("ctx", "fsdp"),
            P("fsdp", "ctx"),
            P("ctx", "fsdp"),
            P("ctx", "fsdp"),
            P(("ctx", "fsdp")),
            P(("ctx", "fsdp")),
            P(("ctx", "fsdp")),
            P(("ctx", "fsdp")),
            P(("ctx", "fsdp")),
            P(("ctx", "fsdp")),
            P(("ctx", "fsdp")),
            P(("ctx", "fsdp")),
        ),
        check_vma=False,
    )
```

time: 3690 us -> 1110 us (0.30)
  waiting for transfers between devices: 3060 us -> 781 us
  starting transfers between devices: 124 us -> 11.8 us
  matrix products: 251 us -> 148 us
  blocking collectives: 69.4 us -> 0 us
    all_gather x9 -> x7, waiting for transfers between devices: 1920 us -> 287 us  [gather(): return lax.all_gather(x, axis, axis=0, tiled=True)]
    reduce_scatter x17 -> x7, waiting for transfers between devices: 1090 us -> 335 us  [scatter_sum(): return lax.psum_scatter(x, axis, scatter_dimension=0, tiled=True)]
    ppermute x44 -> x0, starting transfers between devices: 122 us -> none  [the longest x28 95.9 us: passed_along(): return lax.ppermute(shard, axis, pairs)]
    unnamed x36 -> x18, waiting for transfers between devices: 49.1 us -> 139 us
    dot_general x11 -> x9, matrix products: 76.5 us -> 40.3 us  [forward_product(): return jnp.dot(a, b, preferred_element_type=jnp.float32)]
    dot_general x11 -> x9, matrix products: 75.2 us -> 52.5 us  [across(): lax.dot_general(a, b, (((1,), (1,)), ((), ())), preferred_element_type=jn...]
  transfers between devices with their start and end apart: 75 -> 18, of which waited for: 31 -> 14; matrix products, arithmetic and copies ran while one was open for 9% -> 18% of each run, Pallas kernels for 0% -> 0%
where the time goes in v1:
time: 1110 us
  waiting for transfers between devices  781 us (70%)
  matrix products  148 us (13%)
  local copies, waits for them, and re-layouts  97 us (9%)
  other arithmetic  52.3 us (5%)
  between operations  15.9 us (1%)
  starting transfers between devices  11.8 us (1%)
    reduce_scatter x7, waiting for transfers between devices, scatter_sum(): return lax.psum_scatter(x, axis, scatter_dimension=0, tiled=True)  335 us
    all_gather x7, waiting for transfers between devices, gather(): return lax.all_gather(x, axis, axis=0, tiled=True)  287 us
    unnamed x18, waiting for transfers between devices  139 us
    dot_general x9, matrix products, across(): lax.dot_general(a, b, (((1,), (1,)), ((), ())), preferred_element_type=jn...  52.5 us
    dot_general x9, matrix products, over_rows(): lax.dot_general(a, b, (((0,), (0,)), ((), ())), preferred_element_type=jn...  45.9 us
    dot_general x9, matrix products, forward_product(): return jnp.dot(a, b, preferred_element_type=jnp.float32)  40.3 us
    unnamed x244, local copies, waits for them, and re-layouts  38.4 us
    convert_element_type x17, local copies, waits for them, and re-layouts, body(): packed = jnp.concatenate([part.astype(low) for part in small], axis=1)  23 us
  transfers between devices with their start and end apart: 18, of which 14 were waited for; matrix products, arithmetic and copies ran while one was open for 18% of the time, Pallas kernels for 0%

profile of v1, /device:TPU:0, one launch (start us, length us, event | category | flops | bytes accessed | tf_op | source)
XLA Modules:
  0.0 1105.3 jit_solution(3513125268636216237)
XLA Ops:
  15.5 97.2 %all-gather.8.cloned.1.call-done = bf16[2048,3136]{1,0:T(8,128)(2,1)} async-done(((bf16[64,3136]{1,0:T(8,128)(2,1)}), bf16[2048,3136]{1,0:T(8,128)(2,1)}) %all-gather.8.cloned.1.call-update) | async-done | bytes 12845072 | tf_op jit(solution)/shard_map/all_gather | solution.py:59
  112.7 5.6 fusion.3
  126.6 76.8 %all-gather.12.cloned.1.call-done = bf16[2048,2624]{1,0:T(8,128)(2,1)} async-done(((bf16[64,2624]{1,0:T(8,128)(2,1)}), bf16[2048,2624]{1,0:T(8,128)(2,1)}) %all-gather.12.cloned.1.call-update) | async-done | bytes 10747920 | tf_op jit(solution)/shard_map/all_gather | solution.py:59
  209.8 22.4 %all-gather.10.cloned.1.call-done = bf16[1024,1024]{1,0:T(8,128)(2,1)} async-done(((bf16[128,1024]{1,0:T(8,128)(2,1)}), bf16[1024,1024]{1,0:T(8,128)(2,1)}) %all-gather.10.cloned.1.call-update) | async-done | bytes 2097168 | tf_op jit(solution)/shard_map/all_gather | solution.py:59
  241.3 5.0 multiply_reduce_fusion.10
  250.1 45.5 %all-gather.14.cloned.1.call-done = bf16[512,2048]{1,0:T(8,128)(2,1)} async-done(((bf16[128,2048]{1,0:T(8,128)(2,1)}), bf16[512,2048]{1,0:T(8,128)(2,1)}) %all-gather.14.cloned.1.call-update) | async-done | bytes 2097168 | tf_op jit(solution)/shard_map/all_gather | solution.py:59
  295.6 8.5 fusion.104
  304.1 11.6 %multiply_convert_fusion.2 = (bf16[512,2048]{1,0:T(8,128)(2,1)S(1)}, f32[512,2048]{1,0:T(8,128)}) fusion(f32[512,2048]{1,0:T(8,128)S(1)} %fusion.104, bf16[512,2048]{1,0:T(8,128)(2,1)S(1)} %copy-done.102, bf16[2048,2048]{1,0:T(8,128)(2,1)} %param.34), kind=kOutput, calls=%fused_computation.24 | convolution fusion | flops 4305453056 | bytes 20971520 | tf_op jit(solution)/shard_map/dot_general | solution.py:39
  317.1 5.7 convolution_convert_fusion.5
  322.8 2.3 slice.158
  325.1 2.3 reshape.512
  327.4 38.1 %reduce-scatter.11.cloned.1.call-done = bf16[128,2048]{1,0:T(8,128)(2,1)} async-done(((bf16[512,2048]{1,0:T(8,128)(2,1)}), bf16[128,2048]{1,0:T(8,128)(2,1)}) %reduce-scatter.11.cloned.1.call-update) | async-done | bytes 524304 | tf_op jit(solution)/shard_map/reduce_scatter | solution.py:63
  374.6 2.5 fusion.39
  379.4 45.2 %all-gather.16.cloned.1.call-done = bf16[512,2048]{1,0:T(8,128)(2,1)} async-done(((bf16[128,2048]{1,0:T(8,128)(2,1)}), bf16[512,2048]{1,0:T(8,128)(2,1)}) %all-gather.16.cloned.1.call-update) | async-done | bytes 2097168 | tf_op jit(solution)/shard_map/all_gather | solution.py:59
  424.6 12.0 %multiply_convert_fusion.1 = (bf16[512,2048]{1,0:T(8,128)(2,1)S(1)}, bf16[512,2048]{1,0:T(8,128)(2,1)S(1)}) fusion(f32[512,2048]{1,0:T(8,128)} %copy-done.105, f32[512,2048]{1,0:T(8,128)} %get-tuple-element.226, bf16[512,2048]{1,0:T(8,128)(2,1)} %all-gather.16.cloned.1.call-done, bf16[2048,2048]{1,0:T(8,128)(2,1)} %param.35), kind=kOutput, calls=%fused_computation.23 | convolution fusion | flops 4320133120 | bytes 23068672 | tf_op jit(solution)/shard_map/dot_general | solution.py:43
  436.6 8.5 fusion.105
  445.1 9.4 add_convert_fusion
  456.2 41.1 %reduce-scatter.13.cloned.1.call-done = bf16[128,2048]{1,0:T(8,128)(2,1)} async-done(((bf16[512,2048]{1,0:T(8,128)(2,1)}), bf16[128,2048]{1,0:T(8,128)(2,1)}) %reduce-scatter.13.cloned.1.call-update) | async-done | bytes 524304 | tf_op jit(solution)/shard_map/reduce_scatter | solution.py:63
  500.1 3.4 multiply_reduce_fusion.1
  504.6 6.7 fusion.20
  513.4 2.5 convolution_convert_fusion.10
  519.3 4.0 copy.245
  526.3 2.5 convolution_convert_fusion.6
  533.8 2.8 convert_element_type.372
  536.6 2.6 convert_element_type.374
  543.6 2.6 fusion.56
  551.0 4.2 all-to-all-start.1
  576.3 4.3 convolution_convert_fusion.4
  581.1 6.7 reduce-scatter.25.cloned.1.call-done
  591.9 7.7 fusion.1
  599.8 2.6 fusion.37
  613.8 3.5 pad.32
  617.2 6.4 reshape.528
  623.7 10.2 convolution_convert_fusion
  634.1 10.1 convolution_convert_fusion.2
  644.3 10.3 convolution_convert_fusion.1
  656.8 4.6 all-to-all-start
  661.6 19.8 %all-to-all-done = bf16[4,128,768]{2,1,0:T(8,128)(2,1)S(1)} async-done(((bf16[4,128,768]{2,1,0:T(8,128)(2,1)}), bf16[4,128,768]{2,1,0:T(8,128)(2,1)S(1)}, u32[]{:S(2)}, u32[]{:S(2)}) %all-to-all-start) | async-done | bytes 786464 | tf_op jit(solution)/shard_map/all_to_all | solution.py:288
  681.4 5.2 convolution_convert_fusion.3
  689.7 131.4 %all-reduce.11.cloned.1.call-done = bf16[10368,128]{1,0:T(8,128)(2,1)} async-done(((bf16[10368,128]{1,0:T(8,128)(2,1)}), bf16[10368,128]{1,0:T(8,128)(2,1)}) %all-reduce.11.cloned.1.call-update) | async-done | bytes 2654224
  827.7 68.2 %reduce-scatter.23.cloned.1.call-done = bf16[256,2048]{1,0:T(8,128)(2,1)} async-done(((bf16[2048,2048]{1,0:T(8,128)(2,1)}), bf16[256,2048]{1,0:T(8,128)(2,1)}) %reduce-scatter.23.cloned.1.call-update) | async-done | bytes 1048592 | tf_op jit(solution)/shard_map/reduce_scatter | solution.py:63
  895.9 2.8 convert_bitcast_fusion
  898.7 3.0 copy.237
  901.8 68.8 %reduce-scatter.19.cloned.1.call-done = bf16[256,2048]{1,0:T(8,128)(2,1)} async-done(((bf16[2048,2048]{1,0:T(8,128)(2,1)}), bf16[256,2048]{1,0:T(8,128)(2,1)}) %reduce-scatter.19.cloned.1.call-update) | async-done | bytes 1048592 | tf_op jit(solution)/shard_map/reduce_scatter | solution.py:63
  970.6 2.8 convert_element_type.397
  973.4 72.2 %reduce-scatter.21.cloned.1.call-done = bf16[256,2048]{1,0:T(8,128)(2,1)} async-done(((bf16[2048,2048]{1,0:T(8,128)(2,1)}), bf16[256,2048]{1,0:T(8,128)(2,1)}) %reduce-scatter.21.cloned.1.call-update) | async-done | bytes 1048592 | tf_op jit(solution)/shard_map/reduce_scatter | solution.py:63
  1045.6 2.8 convert_element_type.399
  1048.4 46.7 %reduce-scatter.15.cloned.1.call-done = bf16[256,768]{1,0:T(8,128)(2,1)} async-done(((bf16[2048,768]{1,0:T(8,128)(2,1)}), bf16[256,768]{1,0:T(8,128)(2,1)}) %reduce-scatter.15.cloned.1.call-update) | async-done | bytes 393232 | tf_op jit(solution)/shard_map/reduce_scatter | solution.py:63
  (435 shorter events, 128.4 us)
Async XLA Ops:
  7.2 8.1 copy-start.53
  7.2 105.5 %all-gather.8.cloned.1.call-start = ((), (), s32[]{:S(2)}) async-start(), calls=%async_computation.10 | async-start | bytes 13516800 | tf_op jit(solution)/shard_map/all_gather | solution.py:59
  10.5 192.9 %all-gather.12.cloned.1.call-start = ((), (), s32[]{:S(2)}) async-start(), calls=%async_computation.12 | async-start | bytes 11354112 | tf_op jit(solution)/shard_map/all_gather | solution.py:59
  14.7 217.5 %all-gather.10.cloned.1.call-start = ((), (), s32[]{:S(2)}) async-start(), calls=%async_computation.11 | async-start | bytes 2359296 | tf_op jit(solution)/shard_map/all_gather | solution.py:59
  15.0 103.4 %copy-start.99 = (f32[128]{0:T(128)}, f32[128]{0:T(128)S(1)}, u32[]{:S(2)}) copy-start(f32[128]{0:T(128)S(1)} %fusion.53) | copy-start | bytes 1540
  15.0 103.4 %copy-start.85 = (f32[128]{0:T(128)}, f32[128]{0:T(128)S(1)}, u32[]{:S(2)}) copy-start(f32[128]{0:T(128)S(1)} %fusion.87) | copy-start | bytes 1540
  15.3 109.0 %copy-start.39 = (f32[128,128]{0,1:T(8,128)}, f32[128,128]{0,1:T(8,128)S(1)}, u32[]{:S(2)}) copy-start(f32[128,128]{0,1:T(8,128)S(1)} %get-tuple-element.214) | copy-start | bytes 196612
  15.5 191.8 %copy-start.11 = (bf16[128,2048]{1,0:T(8,128)(2,1)}, bf16[128,2048]{1,0:T(8,128)(2,1)S(1)}, u32[]{:S(2)}) copy-start(bf16[128,2048]{1,0:T(8,128)(2,1)S(1)} %fusion.35) | copy-start | bytes 1572868
  119.7 85.1 %copy-start.24 = (f32[128,2,256]{2,1,0:T(2,128)}, f32[128,2,256]{2,1,0:T(2,128)S(1)}, u32[]{:S(2)}) copy-start(f32[128,2,256]{2,1,0:T(2,128)S(1)} %reshape.505) | copy-start | bytes 786436
  122.0 83.6 %slice-start = ((f32[128,3072]{1,0:T(8,128)}), f32[128,2048]{1,0:T(8,128)S(1)}, s32[]{:S(2)}) async-start(f32[128,3072]{1,0:T(8,128)} %copy-done.19), calls=%async_computation.26 | async-start | bytes 2097152 | tf_op jit(solution)/shard_map/jvp()/slice | solution.py:152
  123.9 82.9 %copy-start.78 = (f32[256]{0:T(256)S(1)}, f32[256]{0:T(256)}, u32[]{:S(2)}) copy-start(f32[256]{0:T(256)} %param.44) | copy-start | bytes 3076
  123.9 171.7 %all-gather.14.cloned.1.call-start = ((), (), s32[]{:S(2)}) async-start(), calls=%async_computation.13 | async-start | bytes 2621440 | tf_op jit(solution)/shard_map/all_gather | solution.py:59
  207.3 27.4 %copy-start.13 = (bf16[128,2,4,256]{3,0,2,1:T(8,128)(2,1)}, bf16[128,2,4,256]{3,0,2,1:T(8,128)(2,1)S(1)}, u32[]{:S(2)}) copy-start(bf16[128,2,4,256]{3,0,2,1:T(8,128)(2,1)S(1)} %pad_maximum_fusion.1) | copy-start | bytes 1572868
  209.3 24.6 %copy-start.97 = (f32[128]{0:T(128)}, f32[128]{0:T(128)S(1)}, u32[]{:S(2)}) copy-start(f32[128]{0:T(128)S(1)} %get-tuple-element.217) | copy-start | bytes 1540
  249.5 116.0 %reduce-scatter.11.cloned.1.call-start = ((), (), s32[]{:S(2)}) async-start(), calls=%async_computation.14 | async-start | bytes 2621440 | tf_op jit(solution)/shard_map/reduce_scatter | solution.py:63
  295.6 8.5 copy-start.102
  295.6 21.5 %slice-start.1 = ((s8[8388608]{0:T(1024)(128)(4,1)}), s8[4194304]{0:T(1024)(128)(4,1)S(1)}, s32[]{:S(2)}) async-start(s8[8388608]{0:T(1024)(128)(4,1)} %bitcast.244), calls=%async_computation.27 | async-start | bytes 8388608
  304.1 11.6 %copy-start.105 = (f32[512,2048]{1,0:T(8,128)}, f32[512,2048]{1,0:T(8,128)S(1)}, u32[]{:S(2)}) copy-start(f32[512,2048]{1,0:T(8,128)S(1)} %fusion.104) | copy-start | bytes 12582916
  304.1 12.9 %slice-start.2 = ((s8[8388608]{0:T(1024)(128)(4,1)}), s8[4194304]{0:T(1024)(128)(4,1)S(1)}, s32[]{:S(2)}) async-start(s8[8388608]{0:T(1024)(128)(4,1)} %bitcast.244), calls=%async_computation.28 | async-start | bytes 8388608
  322.8 101.8 %all-gather.16.cloned.1.call-start = ((), (), s32[]{:S(2)}) async-start(), calls=%async_computation.15 | async-start | bytes 2621440 | tf_op jit(solution)/shard_map/all_gather | solution.py:59
  379.2 118.1 %reduce-scatter.13.cloned.1.call-start = ((), (), s32[]{:S(2)}) async-start(), calls=%async_computation.16 | async-start | bytes 2621440 | tf_op jit(solution)/shard_map/reduce_scatter | solution.py:63
  436.6 8.5 copy-start.108
  436.6 8.5 copy-start.107
  454.5 121.8 %all-gather.20.cloned.1.call-start = ((), (), s32[]{:S(2)}) async-start(), calls=%async_computation.19 | async-start | bytes 2621440 | tf_op jit(solution)/shard_map/all_gather | solution.py:59
  455.9 131.9 %reduce-scatter.25.cloned.1.call-start = ((), (), s32[]{:S(2)}) async-start(), calls=%async_computation.24 | async-start | bytes 2359296
  523.3 138.3 %all-gather.18.cloned.1.call-start = ((), (), s32[]{:S(2)}) async-start(), calls=%async_computation.17 | async-start | bytes 2621440 | tf_op jit(solution)/shard_map/all_gather | solution.py:59
  533.8 8.5 copy-start.93
  533.8 9.2 copy-start.75
  543.6 11.6 %copy-start.12 = (bf16[128,2048]{1,0:T(8,128)(2,1)S(1)}, bf16[128,2048]{1,0:T(8,128)(2,1)}, u32[]{:S(2)}) copy-start(bf16[128,2048]{1,0:T(8,128)(2,1)} %copy-done.11) | copy-start | bytes 1572868
  551.0 25.3 %all-to-all-start.1 = ((bf16[4,128,512]{2,1,0:T(8,128)(2,1)}), bf16[4,128,512]{2,1,0:T(8,128)(2,1)}, u32[]{:S(2)}, u32[]{:S(2)}) async-start(bf16[4,128,512]{2,1,0:T(8,128)(2,1)} %bitcast.194), calls=%async_computation.4 | async-start | bytes 1048576 | tf_op jit(solution)/shard_map/all_to_all | solution.py:288
  555.2 132.7 %reduce-scatter.17.cloned.1.call-start = ((), (), s32[]{:S(2)}) async-start(), calls=%async_computation.20 | async-start | bytes 2359296 | tf_op jit(solution)/shard_map/reduce_scatter | solution.py:63
  556.2 12.9 %copy-start.18 = (bf16[4,8,32,512]{3,1,2,0:T(8,128)(2,1)S(1)}, bf16[4,8,32,512]{3,1,2,0:T(8,128)(2,1)}, u32[]{:S(2)}) copy-start(bf16[4,8,32,512]{3,1,2,0:T(8,128)(2,1)} %copy.261) | copy-start | bytes 3145732
  576.3 12.7 %copy-start.40 = (f32[128,128]{0,1:T(8,128)S(1)}, f32[128,128]{0,1:T(8,128)}, u32[]{:S(2)}) copy-start(f32[128,128]{0,1:T(8,128)} %copy-done.39) | copy-start | bytes 196612
  580.6 8.5 copy-start.73
  580.6 8.5 copy-start.81
  580.6 8.7 copy-start.84
  580.6 8.9 copy-start.38
  580.6 10.1 copy-start.27
  580.6 240.4 %all-reduce.11.cloned.1.call-start = ((), (), s32[]{:S(2)}) async-start(), calls=%async_computation.25 | async-start | bytes 5308416
  599.7 8.5 copy-start.67
  599.8 9.8 copy-start.66
  599.8 11.3 %copy-start.68 = (bf16[32,8]{1,0:T(8,128)(2,1)S(1)}, bf16[32,8]{1,0:T(8,128)(2,1)}, u32[]{:S(2)}) copy-start(bf16[32,8]{1,0:T(8,128)(2,1)} %convert_element_type.390) | copy-start | bytes 1540
  623.6 272.3 %reduce-scatter.23.cloned.1.call-start = ((), (), s32[]{:S(2)}) async-start(), calls=%async_computation.23 | async-start | bytes 9437184 | tf_op jit(solution)/shard_map/reduce_scatter | solution.py:63
  633.9 336.7 %reduce-scatter.19.cloned.1.call-start = ((), (), s32[]{:S(2)}) async-start(), calls=%async_computation.21 | async-start | bytes 9437184 | tf_op jit(solution)/shard_map/reduce_scatter | solution.py:63
  644.2 401.4 %reduce-scatter.21.cloned.1.call-start = ((), (), s32[]{:S(2)}) async-start(), calls=%async_computation.22 | async-start | bytes 9437184 | tf_op jit(solution)/shard_map/reduce_scatter | solution.py:63
  656.8 24.6 %all-to-all-start = ((bf16[4,128,768]{2,1,0:T(8,128)(2,1)}), bf16[4,128,768]{2,1,0:T(8,128)(2,1)S(1)}, u32[]{:S(2)}, u32[]{:S(2)}) async-start(bf16[4,128,768]{2,1,0:T(8,128)(2,1)} %maximum_bitcast_fusion), calls=%async_computation.2 | async-start | bytes 1572864 | tf_op jit(solution)/shard_map/all_to_all | solution.py:288
  661.4 433.7 %reduce-scatter.15.cloned.1.call-start = ((), (), s32[]{:S(2)}) async-start(), calls=%async_computation.18 | async-start | bytes 3538944 | tf_op jit(solution)/shard_map/reduce_scatter | solution.py:63
  898.7 199.8 %copy-start.1 = (bf16[512,2048]{1,0:T(8,128)(2,1)S(1)}, bf16[512,2048]{1,0:T(8,128)(2,1)}, u32[]{:S(2)}) copy-start(bf16[512,2048]{1,0:T(8,128)(2,1)} %param.27) | copy-start | bytes 6291460
  (82 other events, 343.0 us)
Sparse Core Ops, SparseCore 0:
  11.5 101.1 all-gather.7
  116.2 87.1 all-gather.11
  205.9 26.2 all-gather.9
  249.6 45.9 all-gather.13
  322.9 42.5 reduce-scatter.10
  379.3 45.2 all-gather.15
  454.7 42.5 reduce-scatter.12
  498.8 45.5 all-gather.19
  548.3 39.4 reduce-scatter.24
  589.9 45.9 all-gather.17
  640.1 39.9 reduce-scatter.16
  685.4 135.6 all-reduce.10
  824.9 70.9 reduce-scatter.22
  899.3 71.2 reduce-scatter.18
  974.3 71.2 reduce-scatter.20
  1048.8 46.2 reduce-scatter.14

commit v2 on v1

--- a/solution.py
+++ b/solution.py
@@ -1,13 +1,17 @@
+import functools
 import math
 
 import jax
 import jax.numpy as jnp
 from jax import lax
+from jax.experimental import pallas as pl
+from jax.experimental.pallas import tpu as pltpu
 from jax.sharding import PartitionSpec as P
 
 HEADS = 8
 KV_HEADS = 2
 HD = 256
+MESH = pl.DeviceIdType.MESH
 
 
 epsilon = 1e-06
@@ -61,6 +65,187 @@
 
 def scatter_sum(x, axis):
     return lax.psum_scatter(x, axis, scatter_dimension=0, tiled=True)
+
+
+def partner_barrier(partners):
+    barrier = pltpu.get_barrier_semaphore()
+    for partner in partners:
+        pl.semaphore_signal(barrier, inc=1, device_id=partner, device_id_type=MESH)
+    pl.semaphore_wait(barrier, len(partners))
+
+
+def add_rows(target, source, first, rows):
+    tile = 16
+
+    def one(step, carry):
+        at = pl.ds(pl.multiple_of(first + step * tile, tile), tile)
+        from_at = pl.ds(pl.multiple_of(step * tile, tile), tile)
+        total = target[at].astype(jnp.float32) + source[from_at].astype(jnp.float32)
+        target[at] = total.astype(target.dtype)
+        return carry
+
+    lax.fori_loop(0, rows // tile, one, 0)
+
+
+def owner_sum_kernel(ctx_count, fsdp_count, shapes, *refs):
+    many = len(shapes)
+    ins, outs = refs[:many], refs[many : 2 * many]
+    rest = refs[2 * many :]
+    held, first_in = rest[:many], rest[many : 2 * many]
+    later_in = rest[2 * many : 3 * many]
+    across_in, own_sem, send_zero, recv_zero, send_sem, recv_sem, send_z, recv_z = rest[3 * many :]
+    bits = ctx_count.bit_length() - 1
+    pairs = ctx_count // 2
+    place = lax.axis_index("ctx")
+    along = lax.axis_index("fsdp")
+    mine = [lax.rem(place // (1 << t), 2) for t in range(bits)]
+    partners = [(place + (1 - 2 * mine[t]) * (1 << t), along) for t in range(bits)]
+    across = [(place, lax.rem(along + d, fsdp_count)) for d in range(1, fsdp_count)]
+    partner_barrier(partners + across)
+
+    own_copies = []
+    zero_copies = []
+    for i, (rows, _) in enumerate(shapes):
+        for b in range(pairs):
+            keep = pl.ds(pl.multiple_of((2 * b + mine[0]) * rows, 16), rows)
+            give = pl.ds(pl.multiple_of((2 * b + 1 - mine[0]) * rows, 16), rows)
+            copy = pltpu.make_async_remote_copy(
+                src_ref=ins[i].at[give],
+                dst_ref=first_in[i].at[b],
+                send_sem=send_zero.at[i, b],
+                recv_sem=recv_zero.at[i, b],
+                device_id=partners[0],
+                device_id_type=MESH,
+            )
+            copy.start()
+            zero_copies.append(copy)
+            own = pltpu.make_async_copy(ins[i].at[keep], held[i].at[b], own_sem.at[i, b])
+            own.start()
+            own_copies.append(own)
+
+    orders = [list(range(1, bits)), list(range(bits - 1, 0, -1))]
+
+    def block_sets(half, stage):
+        order = orders[half]
+        bit = order[stage]
+        free = order[stage + 1 :]
+        fixed = sum(mine[t] * (1 << (t - 1)) for t in order[:stage])
+        sent, kept = [], []
+        for combo in range(1 << len(free)):
+            value = sum(((combo >> n) & 1) << (t - 1) for n, t in enumerate(free))
+            sent.append(fixed + (1 - mine[bit]) * (1 << (bit - 1)) + value)
+            kept.append(fixed + mine[bit] * (1 << (bit - 1)) + value)
+        return bit, sent, kept
+
+    def start_stage(i, stage):
+        rows = shapes[i][0] // 2
+        copies = []
+        for half in range(2):
+            bit, sent, _ = block_sets(half, stage)
+            for n, block in enumerate(sent):
+                copy = pltpu.make_async_remote_copy(
+                    src_ref=held[i].at[block, pl.ds(half * rows, rows)],
+                    dst_ref=later_in[i].at[half, slot_of(stage) + n],
+                    send_sem=send_sem.at[i, half, slot_of(stage) + n],
+                    recv_sem=recv_sem.at[i, half, slot_of(stage) + n],
+                    device_id=partners[bit],
+                    device_id_type=MESH,
+                )
+                copy.start()
+                copies.append(copy)
+        return copies
+
+    def slot_of(stage):
+        return sum(1 << (bits - 2 - s) for s in range(stage))
+
+    def add_stage(i, stage):
+        rows = shapes[i][0] // 2
+        for half in range(2):
+            _, _, kept = block_sets(half, stage)
+            for n, block in enumerate(kept):
+                add_rows(held[i].at[block], later_in[i].at[half, slot_of(stage) + n], half * rows, rows)
+
+    flying = {}
+    for i in range(many):
+        for b in range(pairs):
+            zero_copies[i * pairs + b].wait()
+            own_copies[i * pairs + b].wait()
+            add_rows(held[i].at[b], first_in[i].at[b], 0, shapes[i][0])
+        flying[i] = start_stage(i, 0)
+    for stage in range(1, bits - 1):
+        for i in range(many):
+            for copy in flying[i]:
+                copy.wait()
+            add_stage(i, stage - 1)
+            flying[i] = start_stage(i, stage)
+    block = place // 2
+    for i in range(many):
+        for copy in flying[i]:
+            copy.wait()
+        add_stage(i, bits - 2)
+        if i < many - 1:
+            outs[i][...] = held[i][block]
+    last = many - 1
+    share = shapes[last][0] // fsdp_count
+    copies = []
+    for d, peer in enumerate(across):
+        part = pl.ds(pl.multiple_of(peer[1] * share, 16), share)
+        copy = pltpu.make_async_remote_copy(
+            src_ref=held[last].at[block, part],
+            dst_ref=across_in.at[d],
+            send_sem=send_z.at[d],
+            recv_sem=recv_z.at[d],
+            device_id=peer,
+            device_id_type=MESH,
+        )
+        copy.start()
+        copies.append(copy)
+    for copy in copies:
+        copy.wait()
+    part = pl.ds(pl.multiple_of(along * share, 16), share)
+    total = held[last][block, part].astype(jnp.float32)
+    for d in range(fsdp_count - 1):
+        total = total + across_in[d].astype(jnp.float32)
+    outs[last][...] = total.astype(outs[last].dtype)
+
+
+def owner_sums(arrays):
+    ctx_count = lax.axis_size("ctx")
+    fsdp_count = lax.axis_size("fsdp")
+    bits = ctx_count.bit_length() - 1
+    pairs = ctx_count // 2
+    many = len(arrays)
+    shapes = [(a.shape[0] // ctx_count, a.shape[1]) for a in arrays]
+    low = jnp.bfloat16
+    slots = pairs - 1
+    last_share = (shapes[-1][0] // fsdp_count, shapes[-1][1])
+    out_shapes = shapes[:-1] + [last_share]
+    scratch = [pltpu.VMEM((pairs,) + s, low) for s in shapes]
+    scratch += [pltpu.VMEM((pairs,) + s, low) for s in shapes]
+    scratch += [pltpu.VMEM((2, slots, s[0] // 2, s[1]), low) for s in shapes]
+    scratch += [
+        pltpu.VMEM((fsdp_count - 1,) + last_share, low),
+        pltpu.SemaphoreType.DMA((many, pairs)),
+        pltpu.SemaphoreType.DMA((many, pairs)),
+        pltpu.SemaphoreType.DMA((many, pairs)),
+        pltpu.SemaphoreType.DMA((many, 2, slots)),
+        pltpu.SemaphoreType.DMA((many, 2, slots)),
+        pltpu.SemaphoreType.DMA((fsdp_count - 1,)),
+        pltpu.SemaphoreType.DMA((fsdp_count - 1,)),
+    ]
+    total = sum(a.size for a in arrays)
+    return pl.pallas_call(
+        functools.partial(owner_sum_kernel, ctx_count, fsdp_count, shapes),
+        out_shape=[jax.ShapeDtypeStruct(s, low) for s in out_shapes],
+        in_specs=[pl.BlockSpec(memory_space=pl.ANY)] * many,
+        out_specs=[pl.BlockSpec(memory_space=pltpu.VMEM)] * many,
+        scratch_shapes=scratch,
+        compiler_params=pltpu.CompilerParams(
+            collective_id=0, has_side_effects=True, vmem_limit_bytes=58 << 20
+        ),
+        cost_estimate=pl.CostEstimate(flops=total, bytes_accessed=4 * total, transcendentals=0),
+        name="owner_sums",
+    )(*arrays)
 
 
 def blocks_of(grad, rows, columns):
@@ -288,7 +473,7 @@
         return lax.all_to_all(parts, "fsdp", 0, 0, tiled=True).reshape(fsdp_count * rows_here, -1)
 
     out_columns = columns_to_owner(attn_grad_low)
-    out_weight_grad = scatter_sum(over_rows(attended_all, out_columns).astype(low), "ctx")
+    out_weight_grad = over_rows(attended_all, out_columns)
     qkv_parts = jnp.concatenate(
         [
             part.reshape(rows_here, fsdp_count, -1)
@@ -301,15 +486,7 @@
         axis=2,
     )
     qkv_columns = columns_to_owner(qkv_parts.reshape(rows_here, -1))
-    qkv_weight_grad = scatter_sum(over_rows(normed_all, qkv_columns).astype(low), "ctx")
-    query_part = query_width // fsdp_count
-    kv_part = kv_width // fsdp_count
-    query_weight_grad = qkv_weight_grad[:, :query_part]
-    key_weight_grad = qkv_weight_grad[:, query_part : query_part + kv_part]
-    value_weight_grad = qkv_weight_grad[:, query_part + kv_part :]
-    down_weight_grad = scatter_sum(down_weight_grad.astype(low), "ctx").T
-    gate_weight_grad = scatter_sum(gate_weight_grad.astype(low), "ctx")
-    up_weight_grad = scatter_sum(up_weight_grad.astype(low), "ctx")
+    qkv_weight_grad = over_rows(normed_all, qkv_columns)
 
     small = [
         left_weight_grad.reshape(count, -1),
@@ -327,8 +504,28 @@
     ]
     sizes = [part.shape[1] for part in small]
     packed = jnp.concatenate([part.astype(low) for part in small], axis=1)
-    packed = jnp.pad(packed, ((0, 0), (0, -packed.shape[1] % 128)))
-    packed = scatter_sum(packed.reshape(-1, 128), ("ctx", "fsdp")).reshape(-1)
+    packed = jnp.pad(packed, ((0, 0), (0, -packed.shape[1] % (16 * 128))))
+    sums = owner_sums(
+        [
+            grad.astype(low)
+            for grad in (
+                down_weight_grad,
+                gate_weight_grad,
+                up_weight_grad,
+                out_weight_grad,
+                qkv_weight_grad,
+                packed.reshape(count * 16, -1),
+            )
+        ]
+    )
+    down_weight_grad, gate_weight_grad, up_weight_grad, out_weight_grad, qkv_weight_grad = sums[:5]
+    down_weight_grad = down_weight_grad.T
+    packed = sums[5].reshape(-1)
+    query_part = query_width // fsdp_count
+    kv_part = kv_width // fsdp_count
+    query_weight_grad = qkv_weight_grad[:, :query_part]
+    key_weight_grad = qkv_weight_grad[:, query_part : query_part + kv_part]
+    value_weight_grad = qkv_weight_grad[:, query_part + kv_part :]
     shares = []
     start = 0
     for size in sizes:

time: 1110 us -> 848 us (0.76)
  waiting for transfers between devices: 781 us -> 383 us
  Pallas kernels: 0 us -> 157 us
    reduce_scatter x7 -> x2, waiting for transfers between devices: 335 us -> 79.2 us  [scatter_sum(): return lax.psum_scatter(x, axis, scatter_dimension=0, tiled=True)]
    pallas_call x0 -> x1, Pallas kernels: none -> 157 us  [owner_sums(): pl.pallas_call(functools.partial(owner_sum_kernel, ctx_count, fsdp_count,...]
    unnamed x18 -> x11, waiting for transfers between devices: 139 us -> 0.68 us
    all_to_all x2, waiting for transfers between devices: 19.8 us -> 7.21 us  [columns_to_owner(): lax.all_to_all(parts, 'fsdp', 0, 0, tiled=True)]
    unnamed x244 -> x260, local copies, waits for them, and re-layouts: 38.4 us -> 38.6 us
  transfers between devices with their start and end apart: 18 -> 12, of which waited for: 14 -> 9; matrix products, arithmetic and copies ran while one was open for 18% -> 18% of each run, Pallas kernels for 0% -> 0%
where the time goes in v2:
time: 848 us; the launch traced here: 843 us
  waiting for transfers between devices  383 us (45%)
  Pallas kernels  157 us (19%)
  matrix products  137 us (16%)
  local copies, waits for them, and re-layouts  91.6 us (11%)
  other arithmetic  47.8 us (6%)
  between operations  16.1 us (2%)
  starting transfers between devices  10.3 us (1%)
    all_gather x7, waiting for transfers between devices, gather(): return lax.all_gather(x, axis, axis=0, tiled=True)  296 us
    pallas_call x1, Pallas kernels, owner_sums(): pl.pallas_call(functools.partial(owner_sum_kernel, ctx_count, fsdp_count,...  157 us
    reduce_scatter x2, waiting for transfers between devices, scatter_sum(): return lax.psum_scatter(x, axis, scatter_dimension=0, tiled=True)  79.2 us
    dot_general x9, matrix products, across(): lax.dot_general(a, b, (((1,), (1,)), ((), ())), preferred_element_type=jn...  49.7 us
    dot_general x9, matrix products, forward_product(): return jnp.dot(a, b, preferred_element_type=jnp.float32)  40.3 us
    dot_general x9, matrix products, over_rows(): lax.dot_general(a, b, (((0,), (0,)), ((), ())), preferred_element_type=jn...  39 us
    unnamed x260, local copies, waits for them, and re-layouts  38.6 us
    convert_element_type x17, local copies, waits for them, and re-layouts, body(): packed = jnp.concatenate([part.astype(low) for part in small], axis=1)  17.4 us
  transfers between devices with their start and end apart: 12, of which 9 were waited for; matrix products, arithmetic and copies ran while one was open for 18% of the time, Pallas kernels for 0%

profile of v2, /device:TPU:0, one launch (start us, length us, event | category | flops | bytes accessed | tf_op | source)
XLA Modules:
  0.0 842.9 jit_solution(4184908922227801824)
XLA Ops:
  16.4 96.3 %all-gather.8.cloned.1.call-done = bf16[2048,3136]{1,0:T(8,128)(2,1)} async-done(((bf16[64,3136]{1,0:T(8,128)(2,1)}), bf16[2048,3136]{1,0:T(8,128)(2,1)}) %all-gather.8.cloned.1.call-update) | async-done | bytes 12845072 | tf_op jit(solution)/shard_map/all_gather | solution.py:63
  112.8 5.6 fusion.3
  126.6 76.7 %all-gather.12.cloned.1.call-done = bf16[2048,2624]{1,0:T(8,128)(2,1)} async-done(((bf16[64,2624]{1,0:T(8,128)(2,1)}), bf16[2048,2624]{1,0:T(8,128)(2,1)}) %all-gather.12.cloned.1.call-update) | async-done | bytes 10747920 | tf_op jit(solution)/shard_map/all_gather | solution.py:63
  209.8 22.4 %all-gather.10.cloned.1.call-done = bf16[1024,1024]{1,0:T(8,128)(2,1)} async-done(((bf16[128,1024]{1,0:T(8,128)(2,1)}), bf16[1024,1024]{1,0:T(8,128)(2,1)}) %all-gather.10.cloned.1.call-update) | async-done | bytes 2097168 | tf_op jit(solution)/shard_map/all_gather | solution.py:63
  234.9 2.1 fusion.102
  241.4 5.0 multiply_reduce_fusion.10
  250.1 45.5 %all-gather.14.cloned.1.call-done = bf16[512,2048]{1,0:T(8,128)(2,1)} async-done(((bf16[128,2048]{1,0:T(8,128)(2,1)}), bf16[512,2048]{1,0:T(8,128)(2,1)}) %all-gather.14.cloned.1.call-update) | async-done | bytes 2097168 | tf_op jit(solution)/shard_map/all_gather | solution.py:63
  295.6 8.5 %fusion.104 = f32[512,2048]{1,0:T(8,128)S(1)} fusion(bf16[512,2048]{1,0:T(8,128)(2,1)} %all-gather.14.cloned.1.call-done, bf16[2048,2048]{1,0:T(8,128)(2,1)} %param.33), kind=kOutput, calls=%fused_computation.256 | convolution fusion | flops 4294967296 | bytes 14680064 | tf_op jit(solution)/shard_map/dot_general | solution.py:43
  304.2 11.6 %multiply_convert_fusion.2 = (bf16[512,2048]{1,0:T(8,128)(2,1)S(1)}, f32[512,2048]{1,0:T(8,128)}) fusion(f32[512,2048]{1,0:T(8,128)S(1)} %fusion.104, bf16[512,2048]{1,0:T(8,128)(2,1)S(1)} %copy-done.106, bf16[2048,2048]{1,0:T(8,128)(2,1)} %param.34), kind=kOutput, calls=%fused_computation.24 | convolution fusion | flops 4305453056 | bytes 20971520 | tf_op jit(solution)/shard_map/dot_general | solution.py:43
  317.0 5.7 convolution_convert_fusion.5
  322.8 2.3 slice.164
  325.1 2.3 reshape.504
  327.4 38.1 %reduce-scatter.6.cloned.1.call-done = bf16[128,2048]{1,0:T(8,128)(2,1)} async-done(((bf16[512,2048]{1,0:T(8,128)(2,1)}), bf16[128,2048]{1,0:T(8,128)(2,1)}) %reduce-scatter.6.cloned.1.call-update) | async-done | bytes 524304 | tf_op jit(solution)/shard_map/reduce_scatter | solution.py:67
  374.6 2.5 fusion.39
  379.4 45.2 %all-gather.16.cloned.1.call-done = bf16[512,2048]{1,0:T(8,128)(2,1)} async-done(((bf16[128,2048]{1,0:T(8,128)(2,1)}), bf16[512,2048]{1,0:T(8,128)(2,1)}) %all-gather.16.cloned.1.call-update) | async-done | bytes 2097168 | tf_op jit(solution)/shard_map/all_gather | solution.py:63
  424.6 12.0 %multiply_convert_fusion.1 = (bf16[512,2048]{1,0:T(8,128)(2,1)S(1)}, bf16[512,2048]{1,0:T(8,128)(2,1)S(1)}) fusion(f32[512,2048]{1,0:T(8,128)} %copy-done.111, f32[512,2048]{1,0:T(8,128)} %get-tuple-element.236, bf16[512,2048]{1,0:T(8,128)(2,1)} %all-gather.16.cloned.1.call-done, bf16[2048,2048]{1,0:T(8,128)(2,1)} %param.35), kind=kOutput, calls=%fused_computation.23 | convolution fusion | flops 4320133120 | bytes 23068672 | tf_op jit(solution)/shard_map/dot_general | solution.py:47
  436.6 8.5 %fusion.105 = f32[512,2048]{1,0:T(8,128)S(1)} fusion(bf16[512,2048]{1,0:T(8,128)(2,1)S(1)} %get-tuple-element.188, bf16[2048,2048]{1,0:T(8,128)(2,1)} %param.33), kind=kOutput, calls=%fused_computation.257 | convolution fusion | flops 4294967296 | bytes 14680064 | tf_op jit(solution)/shard_map/dot_general | solution.py:47
  445.1 9.4 %add_convert_fusion = bf16[512,2048]{1,0:T(8,128)(2,1)} fusion(f32[512,2048]{1,0:T(8,128)S(1)} %fusion.105, bf16[512,2048]{1,0:T(8,128)(2,1)S(1)} %get-tuple-element.187, bf16[2048,2048]{1,0:T(8,128)(2,1)} %param.34), kind=kOutput, calls=%fused_computation.22 | convolution fusion | flops 4297064448 | bytes 16777216 | tf_op jit(solution)/shard_map/dot_general | solution.py:47
  456.2 41.1 %reduce-scatter.8.cloned.1.call-done = bf16[128,2048]{1,0:T(8,128)(2,1)} async-done(((bf16[512,2048]{1,0:T(8,128)(2,1)}), bf16[128,2048]{1,0:T(8,128)(2,1)}) %reduce-scatter.8.cloned.1.call-update) | async-done | bytes 524304 | tf_op jit(solution)/shard_map/reduce_scatter | solution.py:67
  497.4 2.1 fusion.43
  500.1 3.4 multiply_reduce_fusion.1
  504.6 6.8 fusion.20
  513.5 2.5 convolution_convert_fusion.10
  519.4 4.0 copy.249
  526.4 2.5 convolution_convert_fusion.6
  532.1 2.0 copy.238
  534.1 3.7 convert_element_type.359
  537.7 1.8 convert_element_type.361
  542.7 10.2 %convolution_convert_fusion.refs_2_ = bf16[2048,2048]{1,0:T(8,128)(2,1)} fusion(bf16[512,2048]{1,0:T(8,128)(2,1)} %all-gather.14.cloned.1.call-done, bf16[512,2048]{1,0:T(8,128)(2,1)} %copy-done.116), kind=kOutput, calls=%fused_computation.5 | convolution fusion | flops 4299161600 | bytes 12582912 | tf_op jit(solution)/shard_map/dot_general | solution.py:51
  553.0 6.8 convolution_convert_fusion.1.refs_1_
  559.8 7.3 convolution_convert_fusion.2.refs_0_
  571.8 2.0 copy.236
  573.8 2.2 convert_element_type.355
  576.0 2.3 fusion.101
  578.3 1.9 copy.293
  580.2 4.3 all-to-all-start
  592.0 7.2 all-to-all-done
  599.2 4.3 convolution_convert_fusion.4.refs_3_
  608.2 4.4 all-to-all-start.1
  612.6 7.4 fusion.1
  633.4 3.4 pad.32
  636.8 4.6 reshape.520.refs_5_
  642.6 10.0 %all-gather.20.cloned.1.call-done = bf16[512,2048]{1,0:T(8,128)(2,1)} async-done(((bf16[128,2048]{1,0:T(8,128)(2,1)}), bf16[512,2048]{1,0:T(8,128)(2,1)}) %all-gather.20.cloned.1.call-update) | async-done | bytes 2097168 | tf_op jit(solution)/shard_map/all_gather | solution.py:63
  652.6 5.2 convolution_convert_fusion.3.refs_4_
  657.8 156.7 %owner_sums.1 = (bf16[256,2048]{1,0:T(8,128)(2,1)}, bf16[256,2048]{1,0:T(8,128)(2,1)}, bf16[256,2048]{1,0:T(8,128)(2,1)}, bf16[256,512]{1,0:T(8,128)(2,1)}, bf16...) custom-call(bf16[2048,2048]{1,0:T(8,128)(2,1)} %convolution_convert_fusion.2.refs_0_, ...), custom_call_target="tpu_custom_call" | custom-call | flops 16580608 | bytes 66322432 | tf_op jit(solution)/shard_map/owner_sums/pallas_call | solution.py:237
  822.8 2.8 convert_bitcast_fusion
  825.6 3.0 copy.241
  828.6 2.8 convert_element_type.385
  (433 shorter events, 108.3 us)
Async XLA Ops:
  7.2 8.4 %copy-start.4 = (bf16[1,128,2048]{2,1,0:T(8,128)(2,1)S(1)}, bf16[1,128,2048]{2,1,0:T(8,128)(2,1)}, u32[]{:S(2)}) copy-start(bf16[1,128,2048]{2,1,0:T(8,128)(2,1)} %param.23) | copy-start | bytes 1572868
  7.2 9.0 %copy-start.57 = (f32[2048]{0:T(1024)S(1)}, f32[2048]{0:T(1024)}, u32[]{:S(2)}) copy-start(f32[2048]{0:T(1024)} %param.38) | copy-start | bytes 24580
  7.2 105.5 %all-gather.8.cloned.1.call-start = ((), (), s32[]{:S(2)}) async-start(), calls=%async_computation.5 | async-start | bytes 13516800 | tf_op jit(solution)/shard_map/all_gather | solution.py:63
  11.4 192.0 %all-gather.12.cloned.1.call-start = ((), (), s32[]{:S(2)}) async-start(), calls=%async_computation.7 | async-start | bytes 11354112 | tf_op jit(solution)/shard_map/all_gather | solution.py:63
  15.6 216.6 %all-gather.10.cloned.1.call-start = ((), (), s32[]{:S(2)}) async-start(), calls=%async_computation.6 | async-start | bytes 2359296 | tf_op jit(solution)/shard_map/all_gather | solution.py:63
  15.8 102.6 %copy-start.103 = (f32[128]{0:T(128)}, f32[128]{0:T(128)S(1)}, u32[]{:S(2)}) copy-start(f32[128]{0:T(128)S(1)} %fusion.53) | copy-start | bytes 1540
  15.9 102.6 %copy-start.89 = (f32[128]{0:T(128)}, f32[128]{0:T(128)S(1)}, u32[]{:S(2)}) copy-start(f32[128]{0:T(128)S(1)} %fusion.87) | copy-start | bytes 1540
  16.2 108.8 %copy-start.41 = (f32[128,128]{0,1:T(8,128)}, f32[128,128]{0,1:T(8,128)S(1)}, u32[]{:S(2)}) copy-start(f32[128,128]{0,1:T(8,128)S(1)} %get-tuple-element.224) | copy-start | bytes 196612
  16.4 190.9 %copy-start.11 = (bf16[128,2048]{1,0:T(8,128)(2,1)}, bf16[128,2048]{1,0:T(8,128)(2,1)S(1)}, u32[]{:S(2)}) copy-start(bf16[128,2048]{1,0:T(8,128)(2,1)S(1)} %fusion.35) | copy-start | bytes 1572868
  119.8 85.0 %copy-start.26 = (f32[128,2,256]{2,1,0:T(2,128)}, f32[128,2,256]{2,1,0:T(2,128)S(1)}, u32[]{:S(2)}) copy-start(f32[128,2,256]{2,1,0:T(2,128)S(1)} %reshape.497) | copy-start | bytes 786436
  122.0 83.5 %slice-start = ((f32[128,3072]{1,0:T(8,128)}), f32[128,2048]{1,0:T(8,128)S(1)}, s32[]{:S(2)}) async-start(f32[128,3072]{1,0:T(8,128)} %copy-done.20), calls=%async_computation.15 | async-start | bytes 2097152 | tf_op jit(solution)/shard_map/jvp()/slice | solution.py:337
  123.9 82.8 %copy-start.81 = (f32[256]{0:T(256)S(1)}, f32[256]{0:T(256)}, u32[]{:S(2)}) copy-start(f32[256]{0:T(256)} %param.44) | copy-start | bytes 3076
  124.0 171.7 %all-gather.14.cloned.1.call-start = ((), (), s32[]{:S(2)}) async-start(), calls=%async_computation.8 | async-start | bytes 2621440 | tf_op jit(solution)/shard_map/all_gather | solution.py:63
  207.3 27.4 %copy-start.13 = (bf16[128,2,4,256]{3,0,2,1:T(8,128)(2,1)}, bf16[128,2,4,256]{3,0,2,1:T(8,128)(2,1)S(1)}, u32[]{:S(2)}) copy-start(bf16[128,2,4,256]{3,0,2,1:T(8,128)(2,1)S(1)} %pad_maximum_fusion.1) | copy-start | bytes 1572868
  209.3 24.6 %copy-start.101 = (f32[128]{0:T(128)}, f32[128]{0:T(128)S(1)}, u32[]{:S(2)}) copy-start(f32[128]{0:T(128)S(1)} %get-tuple-element.227) | copy-start | bytes 1540
  249.6 116.0 %reduce-scatter.6.cloned.1.call-start = ((), (), s32[]{:S(2)}) async-start(), calls=%async_computation.9 | async-start | bytes 2621440 | tf_op jit(solution)/shard_map/reduce_scatter | solution.py:67
  295.6 8.5 %copy-start.106 = (bf16[512,2048]{1,0:T(8,128)(2,1)S(1)}, bf16[512,2048]{1,0:T(8,128)(2,1)}, u32[]{:S(2)}) copy-start(bf16[512,2048]{1,0:T(8,128)(2,1)} %all-gather.14.cloned.1.call-done) | copy-start | bytes 6291460
  295.6 21.4 %slice-start.1 = ((s8[8388608]{0:T(1024)(128)(4,1)}), s8[4194304]{0:T(1024)(128)(4,1)S(1)}, s32[]{:S(2)}) async-start(s8[8388608]{0:T(1024)(128)(4,1)} %bitcast.243), calls=%async_computation.16 | async-start | bytes 8388608
  304.1 11.6 %copy-start.111 = (f32[512,2048]{1,0:T(8,128)}, f32[512,2048]{1,0:T(8,128)S(1)}, u32[]{:S(2)}) copy-start(f32[512,2048]{1,0:T(8,128)S(1)} %fusion.104) | copy-start | bytes 12582916
  304.2 12.9 %slice-start.2 = ((s8[8388608]{0:T(1024)(128)(4,1)}), s8[4194304]{0:T(1024)(128)(4,1)S(1)}, s32[]{:S(2)}) async-start(s8[8388608]{0:T(1024)(128)(4,1)} %bitcast.243), calls=%async_computation.17 | async-start | bytes 8388608
  322.8 101.9 %all-gather.16.cloned.1.call-start = ((), (), s32[]{:S(2)}) async-start(), calls=%async_computation.10 | async-start | bytes 2621440 | tf_op jit(solution)/shard_map/all_gather | solution.py:63
  379.2 118.1 %reduce-scatter.8.cloned.1.call-start = ((), (), s32[]{:S(2)}) async-start(), calls=%async_computation.11 | async-start | bytes 2621440 | tf_op jit(solution)/shard_map/reduce_scatter | solution.py:67
  436.6 8.5 %copy-start.114 = (bf16[512,2048]{1,0:T(8,128)(2,1)}, bf16[512,2048]{1,0:T(8,128)(2,1)S(1)}, u32[]{:S(2)}) copy-start(bf16[512,2048]{1,0:T(8,128)(2,1)S(1)} %get-tuple-element.188) | copy-start | bytes 6291460
  436.6 8.5 %copy-start.116 = (bf16[512,2048]{1,0:T(8,128)(2,1)}, bf16[512,2048]{1,0:T(8,128)(2,1)S(1)}, u32[]{:S(2)}) copy-start(bf16[512,2048]{1,0:T(8,128)(2,1)S(1)} %get-tuple-element.187) | copy-start | bytes 6291460
  454.6 137.4 %all-gather.18.cloned.1.call-start = ((), (), s32[]{:S(2)}) async-start(), calls=%async_computation.12 | async-start | bytes 2621440 | tf_op jit(solution)/shard_map/all_gather | solution.py:63
  456.0 147.5 %reduce-scatter.10.cloned.1.call-start = ((), (), s32[]{:S(2)}) async-start(), calls=%async_computation.14 | async-start | bytes 2359296
  523.4 129.2 %all-gather.20.cloned.1.call-start = ((), (), s32[]{:S(2)}) async-start(), calls=%async_computation.13 | async-start | bytes 2621440 | tf_op jit(solution)/shard_map/all_gather | solution.py:63
  534.1 7.3 copy-start.97
  534.1 8.0 copy-start.78
  542.7 10.2 %copy-start.107 = (bf16[512,2048]{1,0:T(8,128)(2,1)S(1)}, bf16[512,2048]{1,0:T(8,128)(2,1)}, u32[]{:S(2)}) copy-start(bf16[512,2048]{1,0:T(8,128)(2,1)} %all-gather.14.cloned.1.call-done) | copy-start | bytes 6291460
  542.7 10.2 %copy-start.115 = (bf16[512,2048]{1,0:T(8,128)(2,1)S(1)}, bf16[512,2048]{1,0:T(8,128)(2,1)}, u32[]{:S(2)}) copy-start(bf16[512,2048]{1,0:T(8,128)(2,1)} %copy-done.114) | copy-start | bytes 6291460
  559.8 7.3 copy-start.25
  559.8 8.6 %copy-start.23 = (bf16[1024,512]{1,0:T(8,128)(2,1)S(1)}, bf16[1024,512]{1,0:T(8,128)(2,1)}, u32[]{:S(2)}) copy-start(bf16[1024,512]{1,0:T(8,128)(2,1)} %copy-done.22) | copy-start | bytes 3145732
  559.8 8.6 %copy-start.33 = (bf16[2,512,1024]{2,1,0:T(8,128)(2,1)S(1)}, bf16[2,512,1024]{2,1,0:T(8,128)(2,1)}, u32[]{:S(2)}) copy-start(bf16[2,512,1024]{2,1,0:T(8,128)(2,1)} %copy-done.32) | copy-start | bytes 6291460
  570.3 16.0 %copy-start.15 = (bf16[32,16384]{1,0:T(8,128)(2,1)S(1)}, bf16[32,16384]{1,0:T(8,128)(2,1)}, u32[]{:S(2)}) copy-start(bf16[32,16384]{1,0:T(8,128)(2,1)} %convert_element_type.359) | copy-start | bytes 3145732
  571.8 15.6 %copy-start.19 = (bf16[4,8,32,512]{3,1,2,0:T(8,128)(2,1)S(1)}, bf16[4,8,32,512]{3,1,2,0:T(8,128)(2,1)}, u32[]{:S(2)}) copy-start(bf16[4,8,32,512]{3,1,2,0:T(8,128)(2,1)} %copy.265) | copy-start | bytes 3145732
  580.2 8.9 %copy-start.82 = (f32[256]{0:T(256)S(1)}, f32[256]{0:T(256)}, u32[]{:S(2)}) copy-start(f32[256]{0:T(256)} %param.44) | copy-start | bytes 3076
  580.2 19.0 %all-to-all-start = ((bf16[4,128,512]{2,1,0:T(8,128)(2,1)}), bf16[4,128,512]{2,1,0:T(8,128)(2,1)}, u32[]{:S(2)}, u32[]{:S(2)}) async-start(bf16[4,128,512]{2,1,0:T(8,128)(2,1)} %bitcast.223), calls=%async_computation.2 | async-start | bytes 1048576 | tf_op jit(solution)/shard_map/all_to_all | solution.py:473
  608.2 44.4 %all-to-all-start.1 = ((bf16[4,128,768]{2,1,0:T(8,128)(2,1)}), bf16[4,128,768]{2,1,0:T(8,128)(2,1)}, u32[]{:S(2)}, u32[]{:S(2)}) async-start(bf16[4,128,768]{2,1,0:T(8,128)(2,1)} %maximum_bitcast_fusion), calls=%async_computation.3 | async-start | bytes 1572864 | tf_op jit(solution)/shard_map/all_to_all | solution.py:473
  612.5 7.5 copy-start.3
  612.5 7.5 copy-start.6
  612.6 7.5 copy-start.56
  612.6 7.5 copy-start.59
  612.6 7.5 copy-start.91
  620.1 7.7 copy-start.72
  620.1 9.0 %copy-start.71 = (bf16[32,64]{1,0:T(8,128)(2,1)S(1)}, bf16[32,64]{1,0:T(8,128)(2,1)}, u32[]{:S(2)}) copy-start(bf16[32,64]{1,0:T(8,128)(2,1)} %convert_element_type.375) | copy-start | bytes 12292
  633.4 8.0 copy-start.104
  825.6 10.3 %copy-start.1 = (bf16[512,2048]{1,0:T(8,128)(2,1)S(1)}, bf16[512,2048]{1,0:T(8,128)(2,1)}, u32[]{:S(2)}) copy-start(bf16[512,2048]{1,0:T(8,128)(2,1)} %param.27) | copy-start | bytes 6291460
  (84 other events, 324.0 us)
Sparse Core Ops, SparseCore 0:
  11.5 101.1 all-gather.7
  116.2 87.1 all-gather.11
  205.8 26.3 all-gather.9
  249.7 45.9 all-gather.13
  322.9 42.6 reduce-scatter.5
  379.3 45.2 all-gather.15
  454.7 42.5 reduce-scatter.7
  499.4 45.5 all-gather.17
  548.9 39.4 reduce-scatter.9
  589.9 62.6 all-gather.19

commit v3 on v2

--- a/solution.py
+++ b/solution.py
@@ -87,20 +87,16 @@
     lax.fori_loop(0, rows // tile, one, 0)
 
 
-def owner_sum_kernel(ctx_count, fsdp_count, shapes, *refs):
+def owner_sum_kernel(ctx_count, fsdp_count, shapes, shared, *refs):
     many = len(shapes)
     ins, outs = refs[:many], refs[many : 2 * many]
     rest = refs[2 * many :]
     held, first_in = rest[:many], rest[many : 2 * many]
     later_in = rest[2 * many : 3 * many]
     across_in, own_sem, send_zero, recv_zero, send_sem, recv_sem, send_z, recv_z = rest[3 * many :]
-    bits = ctx_count.bit_length() - 1
     pairs = ctx_count // 2
-    place = lax.axis_index("ctx")
-    along = lax.axis_index("fsdp")
-    mine = [lax.rem(place // (1 << t), 2) for t in range(bits)]
-    partners = [(place + (1 - 2 * mine[t]) * (1 << t), along) for t in range(bits)]
-    across = [(place, lax.rem(along + d, fsdp_count)) for d in range(1, fsdp_count)]
+    bits, place, along, mine, partners, orders = ctx_position(ctx_count)
+    across = [(place, lax.rem(along + d, fsdp_count)) for d in range(1, fsdp_count) if shared]
     partner_barrier(partners + across)
 
     own_copies = []
@@ -123,8 +119,6 @@
             own.start()
             own_copies.append(own)
 
-    orders = [list(range(1, bits)), list(range(bits - 1, 0, -1))]
-
     def block_sets(half, stage):
         order = orders[half]
         bit = order[stage]
@@ -183,8 +177,10 @@
         for copy in flying[i]:
             copy.wait()
         add_stage(i, bits - 2)
-        if i < many - 1:
+        if i < many - 1 or not shared:
             outs[i][...] = held[i][block]
+    if not shared:
+        return
     last = many - 1
     share = shapes[last][0] // fsdp_count
     copies = []
@@ -209,7 +205,7 @@
     outs[last][...] = total.astype(outs[last].dtype)
 
 
-def owner_sums(arrays):
+def owner_sums(arrays, shared, collective_id):
     ctx_count = lax.axis_size("ctx")
     fsdp_count = lax.axis_size("fsdp")
     bits = ctx_count.bit_length() - 1
@@ -218,7 +214,7 @@
     shapes = [(a.shape[0] // ctx_count, a.shape[1]) for a in arrays]
     low = jnp.bfloat16
     slots = pairs - 1
-    last_share = (shapes[-1][0] // fsdp_count, shapes[-1][1])
+    last_share = (shapes[-1][0] // (fsdp_count if shared else 1), shapes[-1][1])
     out_shapes = shapes[:-1] + [last_share]
     scratch = [pltpu.VMEM((pairs,) + s, low) for s in shapes]
     scratch += [pltpu.VMEM((pairs,) + s, low) for s in shapes]
@@ -235,17 +231,276 @@
     ]
     total = sum(a.size for a in arrays)
     return pl.pallas_call(
-        functools.partial(owner_sum_kernel, ctx_count, fsdp_count, shapes),
+        functools.partial(owner_sum_kernel, ctx_count, fsdp_count, shapes, shared),
         out_shape=[jax.ShapeDtypeStruct(s, low) for s in out_shapes],
         in_specs=[pl.BlockSpec(memory_space=pl.ANY)] * many,
         out_specs=[pl.BlockSpec(memory_space=pltpu.VMEM)] * many,
         scratch_shapes=scratch,
         compiler_params=pltpu.CompilerParams(
-            collective_id=0, has_side_effects=True, vmem_limit_bytes=58 << 20
+            collective_id=collective_id, has_side_effects=True, vmem_limit_bytes=58 << 20
         ),
         cost_estimate=pl.CostEstimate(flops=total, bytes_accessed=4 * total, transcendentals=0),
         name="owner_sums",
     )(*arrays)
+
+
+def held_index(mine, done, bits):
+    return tuple(slice(None) if t in done else mine[t] for t in reversed(range(bits)))
+
+
+def ctx_position(ctx_count):
+    bits = ctx_count.bit_length() - 1
+    place = lax.axis_index("ctx")
+    along = lax.axis_index("fsdp")
+    mine = [lax.rem(place // (1 << t), 2) for t in range(bits)]
+    partners = [(place + (1 - 2 * mine[t]) * (1 << t), along) for t in range(bits)]
+    orders = [list(range(1, bits)), list(range(bits - 1, 0, -1))]
+    return bits, place, along, mine, partners, orders
+
+
+def spread_copy(out, lead, half, stage, position, send_sem, recv_sem):
+    bits, _, _, mine, partners, orders = position
+    order = orders[half]
+    rows = out.shape[-2] // 2
+    at = lead + held_index(mine, order[:stage], bits) + (pl.ds(half * rows, rows),)
+    return pltpu.make_async_remote_copy(
+        src_ref=out.at[at],
+        dst_ref=out.at[at],
+        send_sem=send_sem.at[half, stage],
+        recv_sem=recv_sem.at[half, stage],
+        device_id=partners[order[stage]],
+        device_id_type=MESH,
+    )
+
+
+def sibling_copy(out, lead, position, send_sem, recv_sem):
+    bits, _, _, mine, partners, orders = position
+    at = lead + held_index(mine, orders[0], bits)
+    return pltpu.make_async_remote_copy(
+        src_ref=out.at[at],
+        dst_ref=out.at[at],
+        send_sem=send_sem,
+        recv_sem=recv_sem,
+        device_id=partners[0],
+        device_id_type=MESH,
+    )
+
+
+def weight_gather_kernel(ctx_count, fsdp_count, members, *refs):
+    sets = len(members)
+    locals_count = sum(members)
+    pieces, own = refs[:sets], refs[sets : sets + locals_count]
+    outs = refs[sets + locals_count : 2 * sets + locals_count]
+    rest = refs[2 * sets + locals_count :]
+    passing = rest[:locals_count]
+    own_sem, line_send, line_recv, send_sem, recv_sem, core_send, core_recv = rest[locals_count:]
+    position = ctx_position(ctx_count)
+    bits, place, along, mine, partners, _ = position
+    steps = fsdp_count - 1
+    here = held_index(mine, (), bits)
+    loads = []
+    for n in range(locals_count):
+        loads.append(pltpu.make_async_copy(own[n], passing[n], own_sem.at[0, n]))
+        loads[-1].start()
+    partner_barrier(
+        partners
+        + [(place, lax.rem(along + 1, fsdp_count)), (place, lax.rem(along + steps, fsdp_count))]
+    )
+
+    def line_copy(i, way, step, origin):
+        toward = along + 1 if way == 0 else along - 1
+        return pltpu.make_async_remote_copy(
+            src_ref=pieces[i] if step == 1 else outs[i].at[(origin,) + here],
+            dst_ref=outs[i].at[(origin,) + here],
+            send_sem=line_send.at[i, way, step - 1],
+            recv_sem=line_recv.at[i, way, step - 1],
+            device_id=(place, toward),
+            device_id_type=MESH,
+        )
+
+    def comes(way, step):
+        return along >= step if way == 0 else along + step < fsdp_count
+
+    def goes(way, step):
+        if way == 0:
+            return (along + 1 < fsdp_count) & (along >= step - 1)
+        return (along >= 1) & (along + step - 1 < fsdp_count)
+
+    def origin_of(way, step):
+        return along - step if way == 0 else along + step
+
+    def each(flag, action):
+        pl.when(flag)(action)
+
+    def forward(i, step):
+        for way in range(2):
+            each(goes(way, step), lambda: line_copy(i, way, step, origin_of(way, step - 1)).start())
+
+    for i in range(sets):
+        forward(i, 1)
+    copies = []
+    n = 0
+    for i in range(sets):
+        column = 0
+        for _ in range(members[i]):
+            wide = own[n].shape[-1]
+            target = outs[i].at[
+                (along,) + (slice(None),) * (bits + 1) + (pl.ds(column, wide),)
+            ]
+            loads[n].wait()
+            copies.append(pltpu.make_async_copy(passing[n], target, own_sem.at[1, n]))
+            copies[-1].start()
+            column += wide
+            n += 1
+
+    def stage_copies(i, way, step, stage):
+        lead = (origin_of(way, step),)
+        at = (i, way, step - 1)
+        return [
+            spread_copy(outs[i], lead, half, stage, position, send_sem.at[at], recv_sem.at[at])
+            for half in range(2)
+        ]
+
+    def core_copy(i, way, step):
+        at = (i, way, step - 1)
+        return sibling_copy(
+            outs[i], (origin_of(way, step),), position, core_send.at[at], core_recv.at[at]
+        )
+
+    def arrive(i, step):
+        for way in range(2):
+
+            def landed():
+                line_copy(i, way, step, origin_of(way, step)).wait_recv()
+
+            each(comes(way, step), landed)
+        if step < steps:
+            forward(i, step + 1)
+        for way in range(2):
+
+            def begin():
+                for copy in stage_copies(i, way, step, 0):
+                    copy.start()
+
+            each(comes(way, step), begin)
+
+    def advance(i, step, stage):
+        for way in range(2):
+
+            def proceed():
+                for copy in stage_copies(i, way, step, stage):
+                    copy.wait_recv()
+                if stage < bits - 2:
+                    for copy in stage_copies(i, way, step, stage + 1):
+                        copy.start()
+                else:
+                    core_copy(i, way, step).start()
+
+            each(comes(way, step), proceed)
+
+    order = [(i, step) for i in range(sets) for step in range(1, steps + 1)]
+    for tick in range(len(order) + bits - 1):
+        if tick < len(order):
+            arrive(*order[tick])
+        for stage in range(bits - 1):
+            at = tick - 1 - stage
+            if 0 <= at < len(order):
+                advance(*order[at], stage)
+    for copy in copies:
+        copy.wait()
+    for i, step in order:
+        for way in range(2):
+
+            def leave():
+                line_copy(i, way, step, origin_of(way, step - 1)).wait_send()
+
+            def finish():
+                for stage in range(bits - 1):
+                    for copy in stage_copies(i, way, step, stage):
+                        copy.wait_send()
+                core_copy(i, way, step).wait()
+
+            each(goes(way, step), leave)
+            each(comes(way, step), finish)
+
+
+def weight_gather(pieces, own):
+    ctx_count = lax.axis_size("ctx")
+    fsdp_count = lax.axis_size("fsdp")
+    bits = ctx_count.bit_length() - 1
+    steps = fsdp_count - 1
+    sets = len(pieces)
+    cut = (2,) * bits
+    flat = [w.reshape(cut + (w.shape[0] // ctx_count, w.shape[1])) for group in own for w in group]
+    out_shapes = [(fsdp_count,) + cut + p.shape for p in pieces]
+    total = sum(p.size for p in pieces) * ctx_count * fsdp_count
+    outs = pl.pallas_call(
+        functools.partial(weight_gather_kernel, ctx_count, fsdp_count, [len(g) for g in own]),
+        out_shape=[jax.ShapeDtypeStruct(s, jnp.bfloat16) for s in out_shapes],
+        in_specs=[pl.BlockSpec(memory_space=pl.ANY)] * (sets + len(flat)),
+        out_specs=[pl.BlockSpec(memory_space=pl.ANY)] * sets,
+        scratch_shapes=[pltpu.VMEM(w.shape, w.dtype) for w in flat]
+        + [
+            pltpu.SemaphoreType.DMA((2, len(flat))),
+            pltpu.SemaphoreType.DMA((sets, 2, steps)),
+            pltpu.SemaphoreType.DMA((sets, 2, steps)),
+            pltpu.SemaphoreType.DMA((sets, 2, steps, 2, bits - 1)),
+            pltpu.SemaphoreType.DMA((sets, 2, steps, 2, bits - 1)),
+            pltpu.SemaphoreType.DMA((sets, 2, steps)),
+            pltpu.SemaphoreType.DMA((sets, 2, steps)),
+        ],
+        compiler_params=pltpu.CompilerParams(
+            collective_id=1, has_side_effects=True, vmem_limit_bytes=16 << 20
+        ),
+        cost_estimate=pl.CostEstimate(flops=0, bytes_accessed=4 * total, transcendentals=0),
+        name="weight_gather",
+    )(*pieces, *flat)
+    return [o.reshape(-1, o.shape[-1]) for o in outs]
+
+
+def sequence_gather_kernel(ctx_count, own, out, own_sem, send_sem, recv_sem, core_send, core_recv):
+    position = ctx_position(ctx_count)
+    bits, _, _, mine, partners, _ = position
+    copy = pltpu.make_async_copy(own, out.at[held_index(mine, (), bits)], own_sem)
+    copy.start()
+    partner_barrier(partners)
+    copy.wait()
+    for stage in range(bits - 1):
+        copies = [spread_copy(out, (), h, stage, position, send_sem, recv_sem) for h in range(2)]
+        for copy in copies:
+            copy.start()
+        for copy in copies:
+            copy.wait()
+    last = sibling_copy(out, (), position, core_send, core_recv)
+    last.start()
+    last.wait()
+
+
+def sequence_gather(own):
+    ctx_count = lax.axis_size("ctx")
+    bits = ctx_count.bit_length() - 1
+    out_shape = (2,) * bits + own.shape
+    out = pl.pallas_call(
+        functools.partial(sequence_gather_kernel, ctx_count),
+        out_shape=jax.ShapeDtypeStruct(out_shape, own.dtype),
+        in_specs=[pl.BlockSpec(memory_space=pltpu.VMEM)],
+        out_specs=pl.BlockSpec(memory_space=pltpu.VMEM),
+        scratch_shapes=[
+            pltpu.SemaphoreType.DMA,
+            pltpu.SemaphoreType.DMA((2, bits - 1)),
+            pltpu.SemaphoreType.DMA((2, bits - 1)),
+            pltpu.SemaphoreType.DMA,
+            pltpu.SemaphoreType.DMA,
+        ],
+        compiler_params=pltpu.CompilerParams(
+            collective_id=2, has_side_effects=True, vmem_limit_bytes=32 << 20
+        ),
+        cost_estimate=pl.CostEstimate(
+            flops=0, bytes_accessed=4 * own.size * ctx_count, transcendentals=0
+        ),
+        name="sequence_gather",
+    )(own)
+    return out.reshape(-1, own.shape[-1])
 
 
 def blocks_of(grad, rows, columns):
@@ -296,33 +551,34 @@
     kv_width = KV_HEADS * HD
     query_pos = ctx_place * rows_here + jnp.arange(rows_here, dtype=jnp.int32)
 
-    piece = width // count
 
     def own_rows(weight):
         step = weight.shape[0] // ctx_count
         return lax.dynamic_slice_in_dim(weight, ctx_place * step, step)
 
-    first_set = jnp.concatenate(
-        [own_rows(w) for w in (query_weight, key_weight, value_weight, left_weight)], axis=1
-    )
-    second_set = jnp.concatenate(
-        [
-            own_rows(out_weight),
-            own_rows(side_gate),
-            own_rows(side_out).reshape(piece, -1),
-            own_rows(right_weight).reshape(piece, -1),
-        ],
-        axis=1,
-    )
-    full_first = gather(first_set, ("fsdp", "ctx"))
-    full_second = gather(second_set, ("fsdp", "ctx"))
+    def widened(parts, columns):
+        return jnp.pad(jnp.concatenate(parts, axis=1), ((0, 0), (0, columns)))
+
+    shard = width // fsdp_count
+    spare = -rank % 128
+    first_own = [query_weight, key_weight, value_weight, widened([left_weight], spare)]
+    second_own = [
+        out_weight,
+        side_gate,
+        widened([side_out.reshape(shard, -1), right_weight.reshape(shard, -1)], spare),
+    ]
+    first_piece = jnp.concatenate([own_rows(w) for w in first_own], axis=1)
+    second_piece = jnp.concatenate([own_rows(w) for w in second_own], axis=1)
+    full_first, full_second = weight_gather(
+        [first_piece, second_piece], [first_own, second_own]
+    )
     qkv_width = query_width + 2 * kv_width
     full_qkv = full_first[:, :qkv_width]
-    full_left = full_first[:, qkv_width:]
+    full_left = full_first[:, qkv_width : qkv_width + rank]
     full_out = full_second[:, :width]
     full_side_gate = full_second[:, width : width + side]
     full_side_out = full_second[:, width + side : width + 2 * side].reshape(side, width)
-    full_right = full_second[:, width + 2 * side :]
+    full_right = full_second[:, width + 2 * side : width + 2 * side + rank]
     full_right = full_right.reshape(fsdp_count, rank, width // fsdp_count)
     full_right = full_right.transpose(1, 0, 2).reshape(rank, width)
 
@@ -351,7 +607,7 @@
         [key_heads.astype(low).reshape(rows_here, -1), value_heads.astype(low).reshape(rows_here, -1)],
         axis=1,
     )
-    kv_all = gather(kv_low, "ctx")
+    kv_all = sequence_gather(kv_low)
     key_all = kv_all[:, :kv_width].reshape(length, KV_HEADS, HD).transpose(1, 0, 2)
     value_all = kv_all[:, kv_width:].reshape(length, KV_HEADS, HD).transpose(1, 0, 2)
 
@@ -454,7 +710,7 @@
     )
     kv_grad = jnp.concatenate([key_grad.astype(low), value_grad.astype(low)], axis=0)
     kv_grad = kv_grad.transpose(1, 0, 2).reshape(length, 2 * kv_width)
-    kv_grad = scatter_sum(kv_grad, "ctx").astype(jnp.float32)
+    kv_grad = owner_sums([kv_grad], False, 3)[0].astype(jnp.float32)
     kv_grad = kv_grad.reshape(rows_here, 2, KV_HEADS, HD)
     query_heads_grad = query_grad.reshape(KV_HEADS, groups, rows_here, HD).transpose(2, 0, 1, 3)
     query_heads_grad = query_heads_grad.reshape(rows_here, HEADS, HD)
@@ -516,7 +772,9 @@
                 qkv_weight_grad,
                 packed.reshape(count * 16, -1),
             )
-        ]
+        ],
+        True,
+        0,
     )
     down_weight_grad, gate_weight_grad, up_weight_grad, out_weight_grad, qkv_weight_grad = sums[:5]
     down_weight_grad = down_weight_grad.T

time: 848 us -> 791 us (0.933)
  waiting for transfers between devices: 383 us -> 130 us
  Pallas kernels: 157 us -> 295 us
  local copies, waits for them, and re-layouts: 91.6 us -> 128 us
  other arithmetic: 47.8 us -> 63.9 us
    all_gather x7 -> x4, waiting for transfers between devices: 296 us -> 90.6 us  [gather(): return lax.all_gather(x, axis, axis=0, tiled=True)]
    pallas_call x0 -> x2, Pallas kernels: none -> 120 us  [the longest x1 104 us: weight_gather(): pl.pallas_call(functools.partial(weight_gather_kernel, ctx_count, fsdp_co...]
    reduce_scatter x2, waiting for transfers between devices: 79.2 us -> 38.1 us  [scatter_sum(): return lax.psum_scatter(x, axis, scatter_dimension=0, tiled=True)]
    pallas_call x1 -> x2, Pallas kernels: 157 us -> 175 us  [owner_sums(): pl.pallas_call(functools.partial(owner_sum_kernel, ctx_count, fsdp_count,...]
    unnamed x260 -> x238, local copies, waits for them, and re-layouts: 38.6 us -> 51.9 us
    reshape x2 -> x6, local copies, waits for them, and re-layouts: 0.11 us -> 11.8 us  [the longest x1 2.79 us: body(): kv_all[:, kv_width:].reshape(length, KV_HEADS, HD).transpose(1, 0, 2)]
  transfers between devices with their start and end apart: 12 -> 8, of which waited for: 9 -> 3; matrix products, arithmetic and copies ran while one was open for 18% -> 20% of each run, Pallas kernels for 0% -> 2%
where the time goes in v3:
time: 791 us; the launch traced here: 782 us
  Pallas kernels  295 us (37%)
  matrix products  139 us (18%)
  waiting for transfers between devices  130 us (16%)
  local copies, waits for them, and re-layouts  128 us (16%)
  other arithmetic  63.9 us (8%)
  between operations  16 us (2%)
  starting transfers between devices  9.8 us (1%)
    pallas_call x2, Pallas kernels, owner_sums(): pl.pallas_call(functools.partial(owner_sum_kernel, ctx_count, fsdp_count,...  175 us
    pallas_call x1, Pallas kernels, weight_gather(): pl.pallas_call(functools.partial(weight_gather_kernel, ctx_count, fsdp_co...  104 us
    all_gather x4, waiting for transfers between devices, gather(): return lax.all_gather(x, axis, axis=0, tiled=True)  90.6 us
    dot_general x9, matrix products, across(): lax.dot_general(a, b, (((1,), (1,)), ((), ())), preferred_element_type=jn...  54.9 us
    unnamed x238, local copies, waits for them, and re-layouts  51.9 us
    dot_general x9, matrix products, over_rows(): lax.dot_general(a, b, (((0,), (0,)), ((), ())), preferred_element_type=jn...  40.3 us
    reduce_scatter x2, waiting for transfers between devices, scatter_sum(): return lax.psum_scatter(x, axis, scatter_dimension=0, tiled=True)  38.1 us
    dot_general x9, matrix products, forward_product(): return jnp.dot(a, b, preferred_element_type=jnp.float32)  35.7 us
  transfers between devices with their start and end apart: 8, of which 3 were waited for; matrix products, arithmetic and copies ran while one was open for 20% of the time, Pallas kernels for 2%

profile of v3, /device:TPU:0, one launch (start us, length us, event | category | flops | bytes accessed | tf_op | source)
XLA Modules:
  0.0 782.0 jit_solution(5350348818498584322)
XLA Ops:
  29.4 104.5 %weight_gather.1 = (bf16[4,2,2,2,64,3200]{5,4,3,2,1,0:T(8,128)(2,1)S(1)}, bf16[4,2,2,2,64,2688]{5,4,3,2,1,0:T(8,128)(2,1)S(1)}) custom-call(bf16[64,3200]{1,0:T(8,128)(2,1)S(1)} %pad_maximum_fusion.2.refs_0_, bf16[64,2688]{1,0:T(8,128)(2,1)S(1)} %pad_maximum_fusion.3.refs_1_, bf16[2,2,2,64,2048]{4,3,2,1,0:T(8,128)(2,1)S(1)} %bitcast.206, ...), custom_call_target="tpu_custom_call" | custom-call | bytes 48234496 | tf_op jit(solution)/shard_map/weight_gather/pallas_call | solution.py:437
  133.9 4.0 copy-done.6
  140.3 2.3 copy-done.7
  156.3 15.8 %sequence_gather.1 = bf16[2,2,2,128,1024]{4,3,2,1,0:T(8,128)(2,1)S(1)} custom-call(bf16[128,1024]{1,0:T(8,128)(2,1)S(1)} %pad_maximum_fusion.4.own), custom_call_target="tpu_custom_call" | custom-call | bytes 4194304 | tf_op jit(solution)/shard_map/sequence_gather/pallas_call | solution.py:483
  176.1 2.6 copy.161
  178.7 2.8 copy.128
  183.4 2.7 fusion.60
  187.9 5.5 fusion.106
  198.6 5.0 multiply_reduce_fusion.10
  206.8 45.2 %all-gather.5.cloned.1.call-done = bf16[512,2048]{1,0:T(8,128)(2,1)} async-done(((bf16[128,2048]{1,0:T(8,128)(2,1)}), bf16[512,2048]{1,0:T(8,128)(2,1)}) %all-gather.5.cloned.1.call-update) | async-done | bytes 2097168 | tf_op jit(solution)/shard_map/all_gather | solution.py:63
  252.1 8.7 %fusion.108 = f32[512,2048]{1,0:T(8,128)S(1)} fusion(bf16[512,2048]{1,0:T(8,128)(2,1)} %all-gather.5.cloned.1.call-done, bf16[2048,2048]{1,0:T(8,128)(2,1)} %param.33), kind=kOutput, calls=%fused_computation.257 | convolution fusion | flops 4294967296 | bytes 14680064 | tf_op jit(solution)/shard_map/dot_general | solution.py:43
  260.8 11.6 %multiply_convert_fusion.2 = (bf16[512,2048]{1,0:T(8,128)(2,1)S(1)}, f32[512,2048]{1,0:T(8,128)}) fusion(f32[512,2048]{1,0:T(8,128)S(1)} %fusion.108, bf16[512,2048]{1,0:T(8,128)(2,1)S(1)} %copy-done.94, bf16[2048,2048]{1,0:T(8,128)(2,1)} %param.34), kind=kOutput, calls=%fused_computation.24 | convolution fusion | flops 4305453056 | bytes 20971520 | tf_op jit(solution)/shard_map/dot_general | solution.py:43
  273.7 5.7 convolution_convert_fusion.5
  279.4 2.3 slice.164
  281.7 2.3 reshape.544
  284.0 38.1 %reduce-scatter.3.cloned.1.call-done = bf16[128,2048]{1,0:T(8,128)(2,1)} async-done(((bf16[512,2048]{1,0:T(8,128)(2,1)}), bf16[128,2048]{1,0:T(8,128)(2,1)}) %reduce-scatter.3.cloned.1.call-update) | async-done | bytes 524304 | tf_op jit(solution)/shard_map/reduce_scatter | solution.py:67
  331.2 2.5 fusion.39
  335.8 45.4 %all-gather.7.cloned.1.call-done = bf16[512,2048]{1,0:T(8,128)(2,1)} async-done(((bf16[128,2048]{1,0:T(8,128)(2,1)}), bf16[512,2048]{1,0:T(8,128)(2,1)}) %all-gather.7.cloned.1.call-update) | async-done | bytes 2097168 | tf_op jit(solution)/shard_map/all_gather | solution.py:63
  381.2 12.2 %multiply_convert_fusion.1 = (bf16[512,2048]{1,0:T(8,128)(2,1)S(1)}, bf16[512,2048]{1,0:T(8,128)(2,1)S(1)}) fusion(f32[512,2048]{1,0:T(8,128)} %copy-done.98, f32[512,2048]{1,0:T(8,128)} %get-tuple-element.198, bf16[512,2048]{1,0:T(8,128)(2,1)} %all-gather.7.cloned.1.call-done, bf16[2048,2048]{1,0:T(8,128)(2,1)} %param.35), kind=kOutput, calls=%fused_computation.23 | convolution fusion | flops 4320133120 | bytes 23068672 | tf_op jit(solution)/shard_map/dot_general | solution.py:47
  393.4 8.5 %fusion.109 = f32[512,2048]{1,0:T(8,128)S(1)} fusion(bf16[512,2048]{1,0:T(8,128)(2,1)S(1)} %get-tuple-element.148, bf16[2048,2048]{1,0:T(8,128)(2,1)} %param.33), kind=kOutput, calls=%fused_computation.258 | convolution fusion | flops 4294967296 | bytes 14680064 | tf_op jit(solution)/shard_map/dot_general | solution.py:47
  401.9 9.4 %add_convert_fusion = bf16[512,2048]{1,0:T(8,128)(2,1)} fusion(f32[512,2048]{1,0:T(8,128)S(1)} %fusion.109, bf16[512,2048]{1,0:T(8,128)(2,1)S(1)} %get-tuple-element.147, bf16[2048,2048]{1,0:T(8,128)(2,1)} %param.34), kind=kOutput, calls=%fused_computation.22 | convolution fusion | flops 4297064448 | bytes 16777216 | tf_op jit(solution)/shard_map/dot_general | solution.py:47
  413.8 2.5 convolution_convert_fusion.7
  416.3 2.7 convolution_convert_fusion.6
  419.0 2.7 copy.150
  421.6 2.5 copy.178
  424.1 2.9 copy.151
  427.1 3.7 convert_element_type.363
  430.8 2.6 convert_element_type.365
  439.2 10.2 %convolution_convert_fusion.2.refs_0_ = bf16[2048,2048]{1,0:T(8,128)(2,1)} fusion(bf16[512,2048]{1,0:T(8,128)(2,1)} %all-gather.7.cloned.1.call-done, bf16[512,2048]{1,0:T(8,128)(2,1)} %copy-done.99), kind=kOutput, calls=%fused_computation.7 | convolution fusion | flops 4299161600 | bytes 12582912 | tf_op jit(solution)/shard_map/dot_general | solution.py:51
  449.4 6.8 convolution_convert_fusion.1.refs_1_
  456.2 6.9 convolution_convert_fusion.refs_2_
  463.3 2.1 fusion.43
  466.1 3.4 multiply_reduce_fusion.1
  471.6 7.3 fusion.20
  478.9 2.2 reshape.545
  489.0 2.6 copy.158.refs_0_
  491.5 18.0 %owner_sums.2 = bf16[128,1024]{1,0:T(8,128)(2,1)} custom-call(bf16[1024,1024]{1,0:T(8,128)(2,1)} %copy.158.refs_0_), custom_call_target="tpu_custom_call" | custom-call | flops 1048576 | bytes 4194304 | tf_op jit(solution)/shard_map/owner_sums/pallas_call | solution.py:233
  530.5 4.1 all-to-all-start
  537.6 2.2 convert_element_type.357
  543.5 2.2 convert_element_type.359
  551.0 9.9 %fusion.1 = f32[128,2048]{1,0:T(8,128)} fusion(bf16[128,3072]{1,0:T(8,128)(2,1)S(1)} %add_convert_fusion.1, bf16[2048,3200]{1,0:T(8,128)(2,1)} %bitcast.220), kind=kOutput, calls=%fused_computation.1 | convolution fusion | flops 1610612736 | bytes 14417920 | tf_op jit(solution)/shard_map/dot_general | solution.py:47
  560.9 5.4 all-to-all-start.1
  580.2 3.4 pad.42
  583.6 4.6 reshape.560.refs_5_
  589.4 4.2 convolution_convert_fusion.4.refs_3_
  593.6 5.1 convolution_convert_fusion.3.refs_4_
  598.7 157.2 %owner_sums.3 = (bf16[256,2048]{1,0:T(8,128)(2,1)}, bf16[256,2048]{1,0:T(8,128)(2,1)}, bf16[256,2048]{1,0:T(8,128)(2,1)}, bf16[256,512]{1,0:T(8,128)(2,1)}, bf16...) custom-call(bf16[2048,2048]{1,0:T(8,128)(2,1)} %convolution_convert_fusion.2.refs_0_, ...), custom_call_target="tpu_custom_call" | custom-call | flops 16580608 | bytes 66322432 | tf_op jit(solution)/shard_map/owner_sums/pallas_call | solution.py:233
  766.9 2.8 convert_element_type.389
  (400 shorter events, 148.7 us)
Async XLA Ops:
  7.2 18.8 %copy-start.2 = (bf16[512,512]{1,0:T(8,128)(2,1)S(1)}, bf16[512,512]{1,0:T(8,128)(2,1)}, u32[]{:S(2)}) copy-start(bf16[512,512]{1,0:T(8,128)(2,1)} %param.29) | copy-start | bytes 1572868
  7.2 18.7 %copy-start.3 = (bf16[512,512]{1,0:T(8,128)(2,1)S(1)}, bf16[512,512]{1,0:T(8,128)(2,1)}, u32[]{:S(2)}) copy-start(bf16[512,512]{1,0:T(8,128)(2,1)} %param.28) | copy-start | bytes 1572868
  7.2 18.7 %copy-start = (bf16[512,2048]{1,0:T(8,128)(2,1)S(1)}, bf16[512,2048]{1,0:T(8,128)(2,1)}, u32[]{:S(2)}) copy-start(bf16[512,2048]{1,0:T(8,128)(2,1)} %param.30) | copy-start | bytes 6291460
  7.2 244.8 %all-gather.5.cloned.1.call-start = ((), (), s32[]{:S(2)}) async-start(), calls=%async_computation.4 | async-start | bytes 2621440 | tf_op jit(solution)/shard_map/all_gather | solution.py:63
  23.8 114.1 %copy-start.19 = (bf16[128,2048]{1,0:T(8,128)(2,1)S(1)}, bf16[128,2048]{1,0:T(8,128)(2,1)}, u32[]{:S(2)}) copy-start(bf16[128,2048]{1,0:T(8,128)(2,1)} %fusion.35) | copy-start | bytes 1572868
  151.4 20.7 %copy-start.36 = (f32[128,2,256]{2,1,0:T(2,128)}, f32[128,2,256]{2,1,0:T(2,128)S(1)}, u32[]{:S(2)}) copy-start(f32[128,2,256]{2,1,0:T(2,128)S(1)} %reshape.537) | copy-start | bytes 786436
  152.7 19.4 %copy-start.37 = (f32[16,8,2,256]{3,1,2,0:T(8,128)}, f32[16,8,2,256]{3,1,2,0:T(8,128)S(1)}, u32[]{:S(2)}) copy-start(f32[16,8,2,256]{3,1,2,0:T(8,128)S(1)} %copy.173) | copy-start | bytes 786436
  155.1 17.1 %copy-start.50 = (f32[128,2]{1,0:T(8,128)}, f32[128,2]{1,0:T(8,128)S(1)}, u32[]{:S(2)}) copy-start(f32[128,2]{1,0:T(8,128)S(1)} %copy.122) | copy-start | bytes 3076
  176.1 10.1 %copy-start.16 = (bf16[1024,2,256]{2,0,1:T(8,128)(2,1)}, bf16[1024,2,256]{2,0,1:T(8,128)(2,1)S(1)}, u32[]{:S(2)}) copy-start(bf16[1024,2,256]{2,0,1:T(8,128)(2,1)S(1)} %copy.126) | copy-start | bytes 3145732
  198.6 7.2 copy-start.59
  206.8 115.3 %reduce-scatter.3.cloned.1.call-start = ((), (), s32[]{:S(2)}) async-start(), calls=%async_computation.5 | async-start | bytes 2621440 | tf_op jit(solution)/shard_map/reduce_scatter | solution.py:67
  252.0 8.7 %copy-start.94 = (bf16[512,2048]{1,0:T(8,128)(2,1)S(1)}, bf16[512,2048]{1,0:T(8,128)(2,1)}, u32[]{:S(2)}) copy-start(bf16[512,2048]{1,0:T(8,128)(2,1)} %all-gather.5.cloned.1.call-done) | copy-start | bytes 6291460
  252.0 21.6 %slice-start.1 = ((s8[8388608]{0:T(1024)(128)(4,1)}), s8[4194304]{0:T(1024)(128)(4,1)S(1)}, s32[]{:S(2)}) async-start(s8[8388608]{0:T(1024)(128)(4,1)} %bitcast.269), calls=%async_computation.11 | async-start | bytes 8388608
  260.7 11.6 %copy-start.98 = (f32[512,2048]{1,0:T(8,128)}, f32[512,2048]{1,0:T(8,128)S(1)}, u32[]{:S(2)}) copy-start(f32[512,2048]{1,0:T(8,128)S(1)} %fusion.108) | copy-start | bytes 12582916
  260.7 12.9 %slice-start.2 = ((s8[8388608]{0:T(1024)(128)(4,1)}), s8[4194304]{0:T(1024)(128)(4,1)S(1)}, s32[]{:S(2)}) async-start(s8[8388608]{0:T(1024)(128)(4,1)} %bitcast.269), calls=%async_computation.12 | async-start | bytes 8388608
  279.4 101.8 %all-gather.7.cloned.1.call-start = ((), (), s32[]{:S(2)}) async-start(), calls=%async_computation.6 | async-start | bytes 2621440 | tf_op jit(solution)/shard_map/all_gather | solution.py:63
  322.1 6.5 copy-start.18
  335.8 127.4 %reduce-scatter.5.cloned.1.call-start = ((), (), s32[]{:S(2)}) async-start(), calls=%async_computation.7 | async-start | bytes 2621440 | tf_op jit(solution)/shard_map/reduce_scatter | solution.py:67
  393.4 8.5 %copy-start.102 = (bf16[512,2048]{1,0:T(8,128)(2,1)}, bf16[512,2048]{1,0:T(8,128)(2,1)S(1)}, u32[]{:S(2)}) copy-start(bf16[512,2048]{1,0:T(8,128)(2,1)S(1)} %get-tuple-element.148) | copy-start | bytes 6291460
  393.4 8.5 %copy-start.100 = (bf16[512,2048]{1,0:T(8,128)(2,1)}, bf16[512,2048]{1,0:T(8,128)(2,1)S(1)}, u32[]{:S(2)}) copy-start(bf16[512,2048]{1,0:T(8,128)(2,1)S(1)} %get-tuple-element.147) | copy-start | bytes 6291460
  411.3 178.1 %all-gather.9.cloned.1.call-start = ((), (), s32[]{:S(2)}) async-start(), calls=%async_computation.8 | async-start | bytes 2621440 | tf_op jit(solution)/shard_map/all_gather | solution.py:63
  411.9 181.7 %all-gather.11.cloned.1.call-start = ((), (), s32[]{:S(2)}) async-start(), calls=%async_computation.9 | async-start | bytes 2621440 | tf_op jit(solution)/shard_map/all_gather | solution.py:63
  439.2 10.2 %copy-start.95 = (bf16[512,2048]{1,0:T(8,128)(2,1)S(1)}, bf16[512,2048]{1,0:T(8,128)(2,1)}, u32[]{:S(2)}) copy-start(bf16[512,2048]{1,0:T(8,128)(2,1)} %all-gather.5.cloned.1.call-done) | copy-start | bytes 6291460
  439.2 10.2 %copy-start.103 = (bf16[512,2048]{1,0:T(8,128)(2,1)S(1)}, bf16[512,2048]{1,0:T(8,128)(2,1)}, u32[]{:S(2)}) copy-start(bf16[512,2048]{1,0:T(8,128)(2,1)} %copy-done.102) | copy-start | bytes 6291460
  449.4 6.8 copy-start.101
  471.6 12.7 %copy-start.9 = (bf16[2,512,1024]{2,1,0:T(8,128)(2,1)S(1)}, bf16[2,512,1024]{2,1,0:T(8,128)(2,1)}, u32[]{:S(2)}) copy-start(bf16[2,512,1024]{2,1,0:T(8,128)(2,1)} %copy-done.8) | copy-start | bytes 6291460
  491.5 22.3 %copy-start.23 = (bf16[128,2048]{1,0:T(8,128)(2,1)S(1)}, bf16[128,2048]{1,0:T(8,128)(2,1)}, u32[]{:S(2)}) copy-start(bf16[128,2048]{1,0:T(8,128)(2,1)} %get-tuple-element.161) | copy-start | bytes 1572868
  491.5 25.1 %copy-start.31 = (f32[2,512,256]{2,1,0:T(8,128)S(1)}, f32[2,512,256]{2,1,0:T(8,128)}, u32[]{:S(2)}) copy-start(f32[2,512,256]{2,1,0:T(8,128)} %fusion.58) | copy-start | bytes 3145732
  520.3 9.3 %copy-start.44 = (bf16[128,2048]{1,0:T(8,128)(2,1)S(1)}, bf16[128,2048]{1,0:T(8,128)(2,1)}, u32[]{:S(2)}) copy-start(bf16[128,2048]{1,0:T(8,128)(2,1)} %copy-done.43) | copy-start | bytes 1572868
  520.3 14.3 %copy-start.20 = (bf16[128,2048]{1,0:T(8,128)(2,1)S(1)}, bf16[128,2048]{1,0:T(8,128)(2,1)}, u32[]{:S(2)}) copy-start(bf16[128,2048]{1,0:T(8,128)(2,1)} %fusion.35) | copy-start | bytes 1572868
  520.3 14.3 %copy-start.55 = (bf16[128,64]{0,1:T(8,128)(2,1)S(1)}, bf16[128,64]{0,1:T(8,128)(2,1)}, u32[]{:S(2)}) copy-start(bf16[128,64]{0,1:T(8,128)(2,1)} %convolution_convert_fusion.12) | copy-start | bytes 49156
  527.0 20.5 %copy-start.24 = (bf16[32,16384]{1,0:T(8,128)(2,1)S(1)}, bf16[32,16384]{1,0:T(8,128)(2,1)}, u32[]{:S(2)}) copy-start(bf16[32,16384]{1,0:T(8,128)(2,1)} %convert_element_type.363) | copy-start | bytes 3145732
  530.5 30.5 %all-to-all-start = ((bf16[4,128,512]{2,1,0:T(8,128)(2,1)}), bf16[4,128,512]{2,1,0:T(8,128)(2,1)}, u32[]{:S(2)}, u32[]{:S(2)}) async-start(bf16[4,128,512]{2,1,0:T(8,128)(2,1)} %bitcast.201), calls=%async_computation.2 | async-start | bytes 1048576 | tf_op jit(solution)/shard_map/all_to_all | solution.py:729
  535.5 13.0 %copy-start.28 = (bf16[4,8,32,512]{3,1,2,0:T(8,128)(2,1)S(1)}, bf16[4,8,32,512]{3,1,2,0:T(8,128)(2,1)}, u32[]{:S(2)}) copy-start(bf16[4,8,32,512]{3,1,2,0:T(8,128)(2,1)} %copy.179) | copy-start | bytes 3145732
  551.0 15.4 %copy-start.11 = (f32[128,2048]{1,0:T(8,128)S(1)}, f32[128,2048]{1,0:T(8,128)}, u32[]{:S(2)}) copy-start(f32[128,2048]{1,0:T(8,128)} %copy-done.10) | copy-start | bytes 3145732
  551.0 15.4 %copy-start.13 = (bf16[1,128,2048]{2,1,0:T(8,128)(2,1)S(1)}, bf16[1,128,2048]{2,1,0:T(8,128)(2,1)}, u32[]{:S(2)}) copy-start(bf16[1,128,2048]{2,1,0:T(8,128)(2,1)} %param.23) | copy-start | bytes 1572868
  551.0 15.4 %copy-start.57 = (f32[2048]{0:T(1024)S(1)}, f32[2048]{0:T(1024)}, u32[]{:S(2)}) copy-start(f32[2048]{0:T(1024)} %param.38) | copy-start | bytes 24580
  551.0 15.4 %copy-start.80 = (f32[128]{0:T(128)S(1)}, f32[128]{0:T(128)}, u32[]{:S(2)}) copy-start(f32[128]{0:T(128)} %copy-done.78) | copy-start | bytes 1540
  560.9 7.6 copy-start.72
  560.9 7.7 copy-start.71
  560.9 7.8 copy-start.70
  560.9 7.9 %copy-start.88 = (bf16[256]{0:T(256)(128)(2,1)S(1)}, bf16[256]{0:T(256)(128)(2,1)}, u32[]{:S(2)}) copy-start(bf16[256]{0:T(256)(128)(2,1)} %get-tuple-element.138) | copy-start | bytes 1540
  560.9 13.7 %copy-start.69 = (bf16[32,64]{1,0:T(8,128)(2,1)S(1)}, bf16[32,64]{1,0:T(8,128)(2,1)}, u32[]{:S(2)}) copy-start(bf16[32,64]{1,0:T(8,128)(2,1)} %convert_element_type.377) | copy-start | bytes 12292
  560.9 15.1 %copy-start.68 = (bf16[32,64]{1,0:T(8,128)(2,1)S(1)}, bf16[32,64]{1,0:T(8,128)(2,1)}, u32[]{:S(2)}) copy-start(bf16[32,64]{1,0:T(8,128)(2,1)} %convert_element_type.379) | copy-start | bytes 12292
  560.9 32.7 %all-to-all-start.1 = ((bf16[4,128,768]{2,1,0:T(8,128)(2,1)}), bf16[4,128,768]{2,1,0:T(8,128)(2,1)S(1)}, u32[]{:S(2)}, u32[]{:S(2)}) async-start(bf16[4,128,768]{2,1,0:T(8,128)(2,1)} %maximum_bitcast_fusion), calls=%async_computation.3 | async-start | bytes 1572864 | tf_op jit(solution)/shard_map/all_to_all | solution.py:729
  580.2 8.0 %copy-start.92 = (f32[128]{0:T(128)S(1)}, f32[128]{0:T(128)}, u32[]{:S(2)}) copy-start(f32[128]{0:T(128)} %copy-done.91) | copy-start | bytes 1540
  755.9 13.8 %copy-start.47 = (bf16[256,2048]{1,0:T(8,128)(2,1)S(1)}, bf16[256,2048]{1,0:T(8,128)(2,1)}, u32[]{:S(2)}) copy-start(bf16[256,2048]{1,0:T(8,128)(2,1)} %get-tuple-element.36) | copy-start | bytes 3145732
  757.8 13.4 %copy-start.46 = (bf16[256,2048]{1,0:T(8,128)(2,1)S(1)}, bf16[256,2048]{1,0:T(8,128)(2,1)}, u32[]{:S(2)}) copy-start(bf16[256,2048]{1,0:T(8,128)(2,1)} %get-tuple-element.37) | copy-start | bytes 3145732
  (67 other events, 221.6 us)
Sparse Core Ops, SparseCore 0:
  206.9 45.0 all-gather.4
  279.5 42.5 reduce-scatter.2
  335.9 45.2 all-gather.6
  411.5 42.5 reduce-scatter.4
  455.5 45.4 all-gather.8
  503.0 54.5 all-gather.10

commit v4 on v1

v4 whole, which is shorter than its diff:
```python
import functools
import math

import jax
import jax.numpy as jnp
from jax import lax
from jax.experimental import pallas as pl
from jax.experimental.pallas import tpu as pltpu
from jax.sharding import PartitionSpec as P

HEADS = 8
KV_HEADS = 2
HD = 256
MESH = pl.DeviceIdType.MESH


epsilon = 1e-06
rope_theta = 1000000.0
masked_score = -1e30
inverse_root = 1.0 / math.sqrt(2.0)


def rms_norm(v, factor):
    return v * lax.rsqrt(jnp.mean(v * v, axis=-1, keepdims=True) + epsilon) * factor


def forward_product(a, b):
    return jnp.dot(a, b, preferred_element_type=jnp.float32)


def across(a, b):
    return lax.dot_general(a, b, (((1,), (1,)), ((), ())), preferred_element_type=jnp.float32)


def over_rows(a, b):
    return lax.dot_general(a, b, (((0,), (0,)), ((), ())), preferred_element_type=jnp.float32)


def hidden_piece(gate_in, up_in):
    return jax.nn.gelu(gate_in, approximate=True) * up_in


def middle_piece(mixed_in, ffn_in_rows, factor):
    return mixed_in + rms_norm(ffn_in_rows, factor)


def gather(x, axis):
    return lax.all_gather(x, axis, axis=0, tiled=True)


def scatter_sum(x, axis):
    return lax.psum_scatter(x, axis, scatter_dimension=0, tiled=True)


def partner_barrier(partners):
    barrier = pltpu.get_barrier_semaphore()
    for partner in partners:
        pl.semaphore_signal(barrier, inc=1, device_id=partner, device_id_type=MESH)
    pl.semaphore_wait(barrier, len(partners))


def add_rows(target, source, first, rows):
    tile = 16

    def one(step, carry):
        at = pl.ds(pl.multiple_of(first + step * tile, tile), tile)
        from_at = pl.ds(pl.multiple_of(step * tile, tile), tile)
        total = target[at].astype(jnp.float32) + source[from_at].astype(jnp.float32)
        target[at] = total.astype(target.dtype)
        return carry

    lax.fori_loop(0, rows // tile, one, 0)


def held_index(mine, done, bits):
    return tuple(slice(None) if t in done else mine[t] for t in reversed(range(bits)))


def ctx_position(ctx_count):
    bits = ctx_count.bit_length() - 1
    place = lax.axis_index("ctx")
    along = lax.axis_index("fsdp")
    mine = [lax.rem(place // (1 << t), 2) for t in range(bits)]
    partners = [(place + (1 - 2 * mine[t]) * (1 << t), along) for t in range(bits)]
    orders = [list(range(1, bits)), list(range(bits - 1, 0, -1))]
    return bits, place, along, mine, partners, orders


def spread_copy(out, lead, half, stage, position, send_sem, recv_sem):
    bits, _, _, mine, partners, orders = position
    order = orders[half]
    rows = out.shape[-2] // 2
    at = lead + held_index(mine, order[:stage], bits) + (pl.ds(half * rows, rows),)
    return pltpu.make_async_remote_copy(
        src_ref=out.at[at],
        dst_ref=out.at[at],
        send_sem=send_sem.at[half, stage],
        recv_sem=recv_sem.at[half, stage],
        device_id=partners[order[stage]],
        device_id_type=MESH,
    )


def sibling_copy(out, lead, position, send_sem, recv_sem):
    bits, _, _, mine, partners, orders = position
    at = lead + held_index(mine, orders[0], bits)
    return pltpu.make_async_remote_copy(
        src_ref=out.at[at],
        dst_ref=out.at[at],
        send_sem=send_sem,
        recv_sem=recv_sem,
        device_id=partners[0],
        device_id_type=MESH,
    )


def weight_gather_kernel(ctx_count, fsdp_count, members, lines, *refs):
    sets = len(members)
    own_count = sum(members)
    own, line_own = refs[:own_count], refs[own_count : own_count + lines]
    rest = refs[own_count + lines :]
    outs, line_outs = rest[:sets], rest[sets : sets + lines]
    rest = rest[sets + lines :]
    passing, pieces = rest[: own_count + lines], rest[own_count + lines : own_count + lines + sets]
    own_sem, line_send, line_recv, send_sem, recv_sem, core_send, core_recv = rest[
        own_count + lines + sets :
    ]
    position = ctx_position(ctx_count)
    bits, place, along, mine, partners, _ = position
    steps = fsdp_count - 1
    here = held_index(mine, (), bits)
    columns = []
    for i in range(sets):
        start = 0
        for _ in range(members[i]):
            wide = own[len(columns)].shape[-1]
            columns.append((i, pl.ds(start, wide)))
            start += wide
    piece_loads = [
        pltpu.make_async_copy(own[n].at[here], pieces[i].at[:, at], own_sem.at[0, n])
        for n, (i, at) in enumerate(columns)
    ]
    for load in piece_loads:
        load.start()
    loads = [
        pltpu.make_async_copy(source, passing[n], own_sem.at[1, n])
        for n, source in enumerate(own + line_own)
    ]
    for load in loads:
        load.start()
    partner_barrier(
        partners
        + [(place, lax.rem(along + 1, fsdp_count)), (place, lax.rem(along + steps, fsdp_count))]
    )

    def line_copy(i, way, step, origin):
        toward = along + 1 if way == 0 else along - 1
        if i < sets:
            first, target = pieces[i], outs[i].at[(origin,) + here]
        else:
            first, target = line_own[i - sets], line_outs[i - sets].at[origin]
        return pltpu.make_async_remote_copy(
            src_ref=first if step == 1 else target,
            dst_ref=target,
            send_sem=line_send.at[i, way, step - 1],
            recv_sem=line_recv.at[i, way, step - 1],
            device_id=(place, toward),
            device_id_type=MESH,
        )

    def comes(way, step):
        return along >= step if way == 0 else along + step < fsdp_count

    def goes(way, step):
        if way == 0:
            return (along + 1 < fsdp_count) & (along >= step - 1)
        return (along >= 1) & (along + step - 1 < fsdp_count)

    def origin_of(way, step):
        return along - step if way == 0 else along + step

    def each(flag, action):
        pl.when(flag)(action)

    def forward(i, step):
        for way in range(2):
            each(goes(way, step), lambda: line_copy(i, way, step, origin_of(way, step - 1)).start())

    for load in piece_loads:
        load.wait()
    for i in range(sets):
        forward(i, 1)
    stores = []
    for n, load in enumerate(loads):
        load.wait()
        if n < own_count:
            i, at = columns[n]
            target = outs[i].at[(along,) + (slice(None),) * (bits + 1) + (at,)]
        else:
            target = line_outs[n - own_count].at[along]
        stores.append(pltpu.make_async_copy(passing[n], target, own_sem.at[2, n]))
        stores[-1].start()

    def stage_copies(i, way, step, stage):
        lead = (origin_of(way, step),)
        at = (i, way, step - 1)
        return [
            spread_copy(outs[i], lead, half, stage, position, send_sem.at[at], recv_sem.at[at])
            for half in range(2)
        ]

    def core_copy(i, way, step):
        at = (i, way, step - 1)
        return sibling_copy(
            outs[i], (origin_of(way, step),), position, core_send.at[at], core_recv.at[at]
        )

    def arrive(i, step):
        for way in range(2):

            def landed():
                line_copy(i, way, step, origin_of(way, step)).wait_recv()

            each(comes(way, step), landed)
        if step < steps:
            forward(i, step + 1)
        if i >= sets:
            return
        for way in range(2):

            def begin():
                for copy in stage_copies(i, way, step, 0):
                    copy.start()

            each(comes(way, step), begin)

    def advance(i, step, stage):
        if i >= sets:
            return
        for way in range(2):

            def proceed():
                for copy in stage_copies(i, way, step, stage):
                    copy.wait_recv()
                if stage < bits - 2:
                    for copy in stage_copies(i, way, step, stage + 1):
                        copy.start()
                else:
                    core_copy(i, way, step).start()

            each(comes(way, step), proceed)

    order = [(i, step) for i in range(sets + lines) for step in range(1, steps + 1)]
    for tick in range(len(order) + bits - 1):
        if tick < len(order):
            if order[tick] == (sets - 1, 1):
                for i in range(sets, sets + lines):
                    forward(i, 1)
            arrive(*order[tick])
        for stage in range(bits - 1):
            at = tick - 1 - stage
            if 0 <= at < len(order):
                advance(*order[at], stage)
    for copy in stores:
        copy.wait()
    for i, step in order:
        for way in range(2):

            def leave():
                line_copy(i, way, step, origin_of(way, step - 1)).wait_send()

            def finish():
                for stage in range(bits - 1):
                    for copy in stage_copies(i, way, step, stage):
                        copy.wait_send()
                core_copy(i, way, step).wait()

            each(goes(way, step), leave)
            if i < sets:
                each(comes(way, step), finish)


def weight_gather(own, lines):
    ctx_count = lax.axis_size("ctx")
    fsdp_count = lax.axis_size("fsdp")
    bits = ctx_count.bit_length() - 1
    steps = fsdp_count - 1
    sets = len(own)
    cut = (2,) * bits
    low = jnp.bfloat16
    flat = [w.reshape(cut + (w.shape[0] // ctx_count, w.shape[1])) for group in own for w in group]
    pieces = [(g[0].shape[0] // ctx_count, sum(w.shape[1] for w in g)) for g in own]
    out_shapes = [(fsdp_count,) + cut + p for p in pieces]
    out_shapes += [(fsdp_count,) + w.shape for w in lines]
    total = sum(rows * columns for rows, columns in pieces) * ctx_count * fsdp_count
    outs = pl.pallas_call(
        functools.partial(
            weight_gather_kernel, ctx_count, fsdp_count, [len(g) for g in own], len(lines)
        ),
        out_shape=[jax.ShapeDtypeStruct(s, low) for s in out_shapes],
        in_specs=[pl.BlockSpec(memory_space=pltpu.HBM)] * (len(flat) + len(lines)),
        out_specs=[pl.BlockSpec(memory_space=pltpu.HBM)] * len(out_shapes),
        scratch_shapes=[pltpu.VMEM(w.shape, low) for w in flat + list(lines)]
        + [pltpu.VMEM(p, low) for p in pieces]
        + [
            pltpu.SemaphoreType.DMA((3, len(flat) + len(lines))),
            pltpu.SemaphoreType.DMA((sets + len(lines), 2, steps)),
            pltpu.SemaphoreType.DMA((sets + len(lines), 2, steps)),
            pltpu.SemaphoreType.DMA((sets, 2, steps, 2, bits - 1)),
            pltpu.SemaphoreType.DMA((sets, 2, steps, 2, bits - 1)),
            pltpu.SemaphoreType.DMA((sets, 2, steps)),
            pltpu.SemaphoreType.DMA((sets, 2, steps)),
        ],
        compiler_params=pltpu.CompilerParams(
            collective_id=1, has_side_effects=True, vmem_limit_bytes=60 << 20
        ),
        cost_estimate=pl.CostEstimate(flops=0, bytes_accessed=4 * total, transcendentals=0),
        name="weight_gather",
    )(*flat, *lines)
    return [o.reshape(-1, o.shape[-1]) for o in outs[:sets]] + list(outs[sets:])


class Halving:
    def __init__(self, position, rows, give, held, first_in, later_in, sems):
        self.bits, self.place, self.along, self.mine, self.partners, self.orders = position
        self.rows, self.give, self.held = rows, give, held
        self.first_in, self.later_in = first_in, later_in
        self.send_zero, self.recv_zero, self.send_sem, self.recv_sem = sems
        self.pairs = 1 << (self.bits - 1)

    def first_copy(self, b):
        return pltpu.make_async_remote_copy(
            src_ref=self.give(b),
            dst_ref=self.first_in.at[b],
            send_sem=self.send_zero.at[b],
            recv_sem=self.recv_zero.at[b],
            device_id=self.partners[0],
            device_id_type=MESH,
        )

    def start_first(self):
        for b in range(self.pairs):
            self.first_copy(b).start()

    def end_first(self, b):
        self.first_copy(b).wait()
        add_rows(self.held(b), self.first_in.at[b], 0, self.rows)

    def slot_of(self, stage):
        return sum(1 << (self.bits - 2 - s) for s in range(stage))

    def block_sets(self, half, stage):
        order = self.orders[half]
        bit = order[stage]
        free = order[stage + 1 :]
        fixed = sum(self.mine[t] * (1 << (t - 1)) for t in order[:stage])
        sent, kept = [], []
        for combo in range(1 << len(free)):
            value = sum(((combo >> n) & 1) << (t - 1) for n, t in enumerate(free))
            sent.append(fixed + (1 - self.mine[bit]) * (1 << (bit - 1)) + value)
            kept.append(fixed + self.mine[bit] * (1 << (bit - 1)) + value)
        return bit, sent, kept

    def stage_copies(self, stage):
        rows = self.rows // 2
        copies = []
        for half in range(2):
            bit, sent, _ = self.block_sets(half, stage)
            for n, block in enumerate(sent):
                at = (half, self.slot_of(stage) + n)
                copies.append(
                    pltpu.make_async_remote_copy(
                        src_ref=self.held(block).at[pl.ds(half * rows, rows)],
                        dst_ref=self.later_in.at[at],
                        send_sem=self.send_sem.at[at],
                        recv_sem=self.recv_sem.at[at],
                        device_id=self.partners[bit],
                        device_id_type=MESH,
                    )
                )
        return copies

    def start(self, stage):
        for copy in self.stage_copies(stage):
            copy.start()

    def end(self, stage):
        for copy in self.stage_copies(stage):
            copy.wait()
        rows = self.rows // 2
        for half in range(2):
            _, _, kept = self.block_sets(half, stage)
            for n, block in enumerate(kept):
                at = (half, self.slot_of(stage) + n)
                add_rows(self.held(block), self.later_in.at[at], half * rows, rows)

    def mine_now(self):
        return self.held(self.place // 2)


def halving_scratch(ctx_count, rows, columns):
    pairs = ctx_count // 2
    return [
        pltpu.VMEM((pairs, rows, columns), jnp.bfloat16),
        pltpu.VMEM((2, pairs - 1, rows // 2, columns), jnp.bfloat16),
        pltpu.SemaphoreType.DMA((pairs,)),
        pltpu.SemaphoreType.DMA((pairs,)),
        pltpu.SemaphoreType.DMA((2, pairs - 1)),
        pltpu.SemaphoreType.DMA((2, pairs - 1)),
    ]


def unit_rows(v):
    scale = lax.rsqrt(jnp.mean(v * v, axis=-1, keepdims=True) + epsilon)
    return v * scale, scale


def turned(v, cosine, sine_part):
    halfway = v.shape[-1] // 2
    leading, trailing = v[:, :halfway], v[:, halfway:]
    return jnp.concatenate(
        [leading * cosine - trailing * sine_part, trailing * cosine + leading * sine_part], axis=-1
    )


def unit_rows_pull(v, grad, gain):
    unit, scale = unit_rows(v)
    gain_grad = jnp.sum(grad * unit, axis=0, keepdims=True)
    scaled = grad * gain
    return scale * (scaled - unit * jnp.mean(unit * scaled, axis=-1, keepdims=True)), gain_grad


def head_at(h):
    return pl.ds(pl.multiple_of(h * HD, HD), HD)


def attention_forward_kernel(
    ctx_count,
    raw,
    cosine_ref,
    sine_ref,
    query_gain,
    key_gain,
    row_ids,
    key_ids,
    kv,
    query_low,
    attended_low,
    log_totals,
    bias,
    send_sem,
    recv_sem,
    core_send,
    core_recv,
):
    position = ctx_position(ctx_count)
    bits, place, _, mine, partners, _ = position
    rows = raw.shape[0]
    groups = HEADS // KV_HEADS
    length = ctx_count * rows
    here = held_index(mine, (), bits)
    cosine, sine_part = cosine_ref[...], sine_ref[...]
    for k in range(KV_HEADS):
        unit, _ = unit_rows(raw[:, pl.ds((HEADS + k) * HD, HD)])
        key = turned(unit * key_gain[...], cosine, sine_part)
        kv[here + (slice(None), pl.ds(k * HD, HD))] = key.astype(kv.dtype)
        value, _ = unit_rows(raw[:, pl.ds((HEADS + KV_HEADS + k) * HD, HD)])
        kv[here + (slice(None), pl.ds((KV_HEADS + k) * HD, HD))] = value.astype(kv.dtype)
    partner_barrier(partners)

    def copies_of(stage):
        return [spread_copy(kv, (), h, stage, position, send_sem, recv_sem) for h in range(2)]

    for copy in copies_of(0):
        copy.start()
    allowed = (row_ids[...] == key_ids[...]) & (
        lax.broadcasted_iota(jnp.int32, (rows, length), 1)
        <= lax.broadcasted_iota(jnp.int32, (rows, length), 0) + place * rows
    )
    bias[...] = jnp.where(allowed, 0.0, masked_score)

    def one_query(h, carry):
        unit, _ = unit_rows(raw[:, head_at(h)])
        query = turned(unit * query_gain[...], cosine, sine_part)
        query_low[:, head_at(h)] = query.astype(query_low.dtype)
        return carry

    lax.fori_loop(0, HEADS, one_query, 0)
    for stage in range(1, bits - 1):
        for copy in copies_of(stage - 1):
            copy.wait()
        for copy in copies_of(stage):
            copy.start()
    for copy in copies_of(bits - 2):
        copy.wait()
    last = sibling_copy(kv, (), position, core_send, core_recv)
    last.start()
    last.wait()
    everywhere = (slice(None),) * (bits + 1)
    for k in range(KV_HEADS):
        key = kv[everywhere + (pl.ds(k * HD, HD),)].reshape(length, HD)
        value = kv[everywhere + (pl.ds((KV_HEADS + k) * HD, HD),)].reshape(length, HD)

        def one_head(g, carry, k=k, key=key, value=value):
            h = k * groups + g
            scores = across(query_low[:, head_at(h)], key) + bias[...]
            row_max = jnp.max(scores, axis=-1, keepdims=True)
            weights = jnp.exp(scores - row_max)
            row_total = jnp.sum(weights, axis=-1, keepdims=True)
            weights = (weights * (1.0 / row_total)).astype(value.dtype)
            attended_low[:, head_at(h)] = forward_product(weights, value).astype(attended_low.dtype)
            log_total = jnp.broadcast_to(row_max + jnp.log(row_total), (rows, rows))
            log_totals[h] = log_total.T[:8]
            return carry

        lax.fori_loop(0, groups, one_head, 0)


def attention_forward(raw, cosine, sine_part, query_gain, key_gain, row_ids, key_ids):
    ctx_count = lax.axis_size("ctx")
    bits = ctx_count.bit_length() - 1
    rows = raw.shape[0]
    length = ctx_count * rows
    low = jnp.bfloat16
    vmem = pl.BlockSpec(memory_space=pltpu.VMEM)
    return pl.pallas_call(
        functools.partial(attention_forward_kernel, ctx_count),
        out_shape=[
            jax.ShapeDtypeStruct((2,) * bits + (rows, 2 * KV_HEADS * HD), low),
            jax.ShapeDtypeStruct((rows, HEADS * HD), low),
            jax.ShapeDtypeStruct((rows, HEADS * HD), low),
            jax.ShapeDtypeStruct((HEADS, 8, rows), jnp.float32),
        ],
        in_specs=[vmem] * 7,
        out_specs=[vmem] * 4,
        scratch_shapes=[
            pltpu.VMEM((rows, length), jnp.float32),
            pltpu.SemaphoreType.DMA((2, bits - 1)),
            pltpu.SemaphoreType.DMA((2, bits - 1)),
            pltpu.SemaphoreType.DMA,
            pltpu.SemaphoreType.DMA,
        ],
        compiler_params=pltpu.CompilerParams(
            collective_id=2, has_side_effects=True, vmem_limit_bytes=40 << 20
        ),
        cost_estimate=pl.CostEstimate(
            flops=4 * HEADS * HD * rows * length,
            bytes_accessed=8 << 20,
            transcendentals=HEADS * rows * length,
        ),
        name="attention_forward",
    )(raw, cosine, sine_part, query_gain[None], key_gain[None], row_ids[:, None], key_ids[None])


def attention_backward_kernel(ctx_count, extra, *refs):
    (
        grads,
        query_low,
        kv,
        log_totals,
        raw,
        cosine_ref,
        sine_ref,
        query_gain,
        key_gain,
        row_ids,
        key_ids,
    ) = refs[:11]
    many = len(extra)
    extra_in = refs[11 : 11 + many]
    back, gain_grads = refs[11 + many : 13 + many]
    extra_out = refs[13 + many : 13 + 2 * many]
    rest = refs[13 + 2 * many :]
    bias, score_grads, weights_low, query_grads, kv_grads = rest[:5]
    kv_parts = rest[5:11]
    extra_parts = [rest[11 + 8 * i : 19 + 8 * i] for i in range(many)]
    position = ctx_position(ctx_count)
    bits, place, _, mine, partners, _ = position
    pairs = ctx_count // 2
    rows = raw.shape[0]
    groups = HEADS // KV_HEADS
    length = ctx_count * rows
    low = jnp.bfloat16

    kv_sum = Halving(
        position,
        rows,
        lambda b: kv_grads.at[2 * b + 1 - mine[0]],
        lambda b: kv_grads.at[2 * b + mine[0]],
        kv_parts[0],
        kv_parts[1],
        kv_parts[2:6],
    )
    sums, own_copies = [], []
    for i, (block, _) in enumerate(extra):
        held, first_in, later_in, own_sem = extra_parts[i][:4]

        def give(b, i=i, block=block):
            at = pl.multiple_of((2 * b + 1 - mine[0]) * block, 16)
            return extra_in[i].at[pl.ds(at, block)]

        sums.append(
            Halving(
                position,
                block,
                give,
                lambda b, held=held: held.at[b],
                first_in,
                later_in,
                extra_parts[i][4:8],
            )
        )
        copies = []
        for b in range(pairs):
            at = pl.multiple_of((2 * b + mine[0]) * block, 16)
            copies.append(
                pltpu.make_async_copy(
                    extra_in[i].at[pl.ds(at, block)], held.at[b], own_sem.at[b]
                )
            )
            copies[-1].start()
        own_copies.append(copies)

    partner_barrier(partners)
    for one in sums:
        one.start_first()

    def open_extra(i):
        for b in range(pairs):
            own_copies[i][b].wait()
            sums[i].end_first(b)
        sums[i].start(0)

    allowed = (key_ids[...] == row_ids[...]) & (
        lax.broadcasted_iota(jnp.int32, (length, rows), 0)
        <= lax.broadcasted_iota(jnp.int32, (length, rows), 1) + place * rows
    )
    bias[...] = jnp.where(allowed, 0.0, masked_score)
    everywhere = (slice(None),) * (bits + 1)
    for k in range(KV_HEADS):
        if k < many:
            open_extra(k)
        key = kv[everywhere + (pl.ds(k * HD, HD),)].reshape(length, HD)
        value = kv[everywhere + (pl.ds((KV_HEADS + k) * HD, HD),)].reshape(length, HD)

        def one_head(g, carry, k=k, key=key, value=value):
            h = k * groups + g
            columns = pl.ds(pl.multiple_of(g * rows, rows), rows)
            scores = across(key, query_low[:, head_at(h)]) + bias[...]
            weights = jnp.exp(scores - log_totals[h][:1])
            weight_grad = across(value, grads[:, head_at(h)])
            delta = jnp.sum(weights * weight_grad, axis=0, keepdims=True)
            score_grads[:, columns] = (weights * (weight_grad - delta)).astype(low)
            weights_low[:, columns] = weights.astype(low)
            return carry

        lax.fori_loop(0, groups, one_head, 0)
        heads = [pl.ds((k * groups + g) * HD, HD) for g in range(groups)]
        query_stack = jnp.concatenate([query_low[:, at] for at in heads], axis=0)
        grad_stack = jnp.concatenate([grads[:, at] for at in heads], axis=0)
        key_grad = forward_product(score_grads[...], query_stack).astype(low)
        value_grad = forward_product(weights_low[...], grad_stack).astype(low)
        kv_grads[:, :, pl.ds(k * HD, HD)] = key_grad.reshape(ctx_count, rows, HD)
        kv_grads[:, :, pl.ds((KV_HEADS + k) * HD, HD)] = value_grad.reshape(ctx_count, rows, HD)
        query_grad = over_rows(key, score_grads[...])
        for g, at in enumerate(heads):
            query_grads[:, at] = query_grad[:, g * rows : (g + 1) * rows].T

    kv_sum.start_first()
    for b in range(pairs):
        kv_sum.end_first(b)
    kv_sum.start(0)
    for i in range(KV_HEADS, many):
        open_extra(i)
    cosine, sine_part = cosine_ref[...], sine_ref[...]

    def one_query(h, gain_grad):
        grad = turned(query_grads[:, head_at(h)], cosine, -sine_part)
        pulled, more = unit_rows_pull(raw[:, head_at(h)], grad, query_gain[...])
        back[:, head_at(h)] = pulled.astype(low)
        return gain_grad + more

    gain_grads[0:1] = lax.fori_loop(0, HEADS, one_query, jnp.zeros((1, HD), jnp.float32))
    for stage in range(1, bits - 1):
        kv_sum.end(stage - 1)
        kv_sum.start(stage)
    kv_sum.end(bits - 2)
    summed = kv_sum.mine_now()
    key_gain_grad = jnp.zeros((1, HD), jnp.float32)
    for k in range(KV_HEADS):
        grad = summed[:, pl.ds(k * HD, HD)].astype(jnp.float32)
        grad = turned(grad, cosine, -sine_part)
        at = pl.ds((HEADS + k) * HD, HD)
        pulled, more = unit_rows_pull(raw[:, at], grad, key_gain[...])
        back[:, at] = pulled.astype(low)
        key_gain_grad = key_gain_grad + more
        grad = summed[:, pl.ds((KV_HEADS + k) * HD, HD)].astype(jnp.float32)
        at = pl.ds((HEADS + KV_HEADS + k) * HD, HD)
        pulled, _ = unit_rows_pull(raw[:, at], grad, 1.0)
        back[:, at] = pulled.astype(low)
    gain_grads[1:2] = key_gain_grad
    for stage in range(1, bits - 1):
        for one in sums:
            one.end(stage - 1)
            one.start(stage)
    for i in range(many):
        sums[i].end(bits - 2)
        extra_out[i][...] = sums[i].mine_now()[...]


def attention_backward(
    grads, query_low, kv, log_totals, raw, cosine, sine_part, query_gain, key_gain, row_ids, key_ids, extra
):
    ctx_count = lax.axis_size("ctx")
    rows = raw.shape[0]
    length = ctx_count * rows
    pairs = ctx_count // 2
    groups = HEADS // KV_HEADS
    low = jnp.bfloat16
    vmem = pl.BlockSpec(memory_space=pltpu.VMEM)
    shapes = [(a.shape[0] // ctx_count, a.shape[1]) for a in extra]
    scratch = [
        pltpu.VMEM((length, rows), jnp.float32),
        pltpu.VMEM((length, groups * rows), low),
        pltpu.VMEM((length, groups * rows), low),
        pltpu.VMEM((rows, HEADS * HD), jnp.float32),
        pltpu.VMEM((ctx_count, rows, 2 * KV_HEADS * HD), low),
    ]
    scratch += halving_scratch(ctx_count, rows, 2 * KV_HEADS * HD)
    for shape in shapes:
        parts = halving_scratch(ctx_count, *shape)
        scratch += [pltpu.VMEM((pairs,) + shape, low)] + parts[:2]
        scratch += [pltpu.SemaphoreType.DMA((pairs,))] + parts[2:]
    outs = pl.pallas_call(
        functools.partial(attention_backward_kernel, ctx_count, shapes),
        out_shape=[
            jax.ShapeDtypeStruct(raw.shape, low),
            jax.ShapeDtypeStruct((8, HD), jnp.float32),
        ]
        + [jax.ShapeDtypeStruct(s, low) for s in shapes],
        in_specs=[vmem] * 11 + [pl.BlockSpec(memory_space=pl.ANY)] * len(extra),
        out_specs=[vmem] * (2 + len(extra)),
        scratch_shapes=scratch,
        compiler_params=pltpu.CompilerParams(
            collective_id=3, has_side_effects=True, vmem_limit_bytes=60 << 20
        ),
        cost_estimate=pl.CostEstimate(
            flops=10 * HEADS * HD * rows * length,
            bytes_accessed=64 << 20,
            transcendentals=HEADS * rows * length,
        ),
        name="attention_backward",
    )(
        grads,
        query_low,
        kv,
        log_totals,
        raw,
        cosine,
        sine_part,
        query_gain[None],
        key_gain[None],
        row_ids[None],
        key_ids[:, None],
        *extra,
    )
    return outs[0], outs[1][0], outs[1][1], outs[2:]


def owner_sum_kernel(ctx_count, fsdp_count, shapes, shared, *refs):
    many = len(shapes)
    whole = many - shared
    ins, outs = refs[:many], refs[many : 2 * many]
    rest = refs[2 * many :]
    parts = [rest[8 * i : 8 * i + 8] for i in range(many)]
    shares = rest[8 * many : 8 * many + shared]
    send_z, recv_z = rest[8 * many + shared :]
    position = ctx_position(ctx_count)
    bits, place, along, mine, partners, _ = position
    pairs = ctx_count // 2
    across_line = [(place, lax.rem(along + d, fsdp_count)) for d in range(1, fsdp_count)]
    partner_barrier(partners + across_line)
    sums, own_copies = [], []
    for i, (block, _) in enumerate(shapes):
        held, first_in, later_in, own_sem = parts[i][:4]

        def give(b, i=i, block=block):
            at = pl.multiple_of((2 * b + 1 - mine[0]) * block, 16)
            return ins[i].at[pl.ds(at, block)]

        sums.append(
            Halving(
                position,
                block,
                give,
                lambda b, held=held: held.at[b],
                first_in,
                later_in,
                parts[i][4:8],
            )
        )
        sums[i].start_first()
        copies = []
        for b in range(pairs):
            at = pl.multiple_of((2 * b + mine[0]) * block, 16)
            copies.append(
                pltpu.make_async_copy(ins[i].at[pl.ds(at, block)], held.at[b], own_sem.at[b])
            )
            copies[-1].start()
        own_copies.append(copies)
    order = list(range(whole, many)) + list(range(whole))
    for i in order:
        for b in range(pairs):
            own_copies[i][b].wait()
            sums[i].end_first(b)
        sums[i].start(0)
    for stage in range(1, bits - 1):
        for i in order:
            sums[i].end(stage - 1)
            sums[i].start(stage)

    def share_copies(i):
        size = shapes[i][0] // fsdp_count
        return [
            pltpu.make_async_remote_copy(
                src_ref=sums[i].mine_now().at[pl.ds(pl.multiple_of(peer[1] * size, 16), size)],
                dst_ref=shares[i - whole].at[d],
                send_sem=send_z.at[i - whole, d],
                recv_sem=recv_z.at[i - whole, d],
                device_id=peer,
                device_id_type=MESH,
            )
            for d, peer in enumerate(across_line)
        ]

    for i in range(whole, many):
        sums[i].end(bits - 2)
        for copy in share_copies(i):
            copy.start()
    for i in range(whole):
        sums[i].end(bits - 2)
        outs[i][...] = sums[i].mine_now()[...]
    for i in range(whole, many):
        for copy in share_copies(i):
            copy.wait()
        size = shapes[i][0] // fsdp_count
        own = sums[i].mine_now()[pl.ds(pl.multiple_of(along * size, 16), size)]
        total = own.astype(jnp.float32)
        for d in range(fsdp_count - 1):
            total = total + shares[i - whole][d].astype(jnp.float32)
        outs[i][...] = total.astype(outs[i].dtype)


def owner_sums(arrays, shared):
    ctx_count = lax.axis_size("ctx")
    fsdp_count = lax.axis_size("fsdp")
    pairs = ctx_count // 2
    many = len(arrays)
    whole = many - shared
    low = jnp.bfloat16
    shapes = [(a.shape[0] // ctx_count, a.shape[1]) for a in arrays]
    share_shapes = [(s[0] // fsdp_count, s[1]) for s in shapes[whole:]]
    scratch = []
    for shape in shapes:
        parts = halving_scratch(ctx_count, *shape)
        scratch += [pltpu.VMEM((pairs,) + shape, low)] + parts[:2]
        scratch += [pltpu.SemaphoreType.DMA((pairs,))] + parts[2:]
    scratch += [pltpu.VMEM((fsdp_count - 1,) + s, low) for s in share_shapes]
    scratch += [pltpu.SemaphoreType.DMA((shared, fsdp_count - 1))] * 2
    total = sum(a.size for a in arrays)
    return pl.pallas_call(
        functools.partial(owner_sum_kernel, ctx_count, fsdp_count, shapes, shared),
        out_shape=[jax.ShapeDtypeStruct(s, low) for s in shapes[:whole] + share_shapes],
        in_specs=[pl.BlockSpec(memory_space=pl.ANY)] * many,
        out_specs=[pl.BlockSpec(memory_space=pltpu.VMEM)] * many,
        scratch_shapes=scratch,
        compiler_params=pltpu.CompilerParams(
            collective_id=0, has_side_effects=True, vmem_limit_bytes=48 << 20
        ),
        cost_estimate=pl.CostEstimate(flops=total, bytes_accessed=4 * total, transcendentals=0),
        name="owner_sums",
    )(*arrays)


def body(
    tokens,
    per_layer,
    out_grad,
    segment_ids,
    query_weight,
    key_weight,
    value_weight,
    out_weight,
    left_weight,
    right_weight,
    gate_weight,
    up_weight,
    down_weight,
    side_gate,
    side_out,
    input_gain,
    laurel_gain,
    attn_gain,
    pre_gain,
    post_gain,
    side_gain,
    query_gain,
    key_gain,
):
    low = jnp.bfloat16
    inputs = tokens[0].astype(jnp.float32)
    extra_rows = per_layer[0].astype(jnp.float32)
    cotangent = out_grad[0].astype(jnp.float32)
    sequence_ids = segment_ids[0]
    rows_here, width = inputs.shape
    ctx_count = lax.axis_size("ctx")
    fsdp_count = lax.axis_size("fsdp")
    count = ctx_count * fsdp_count
    ctx_place = lax.axis_index("ctx")
    rank = left_weight.shape[1]
    side = side_gate.shape[1]
    query_width = HEADS * HD
    kv_width = KV_HEADS * HD
    query_pos = ctx_place * rows_here + jnp.arange(rows_here, dtype=jnp.int32)

    piece = width // count

    qkv_width = query_width + 2 * kv_width
    full_qkv, full_second, full_left, full_right, full_side_out = weight_gather(
        [[query_weight, key_weight, value_weight], [out_weight, side_gate]],
        [left_weight, right_weight, side_out],
    )
    full_out = full_second[:, :width]
    full_side_gate = full_second[:, width:]
    full_left = full_left.reshape(width, rank)
    full_right = full_right.transpose(1, 0, 2).reshape(rank, width)
    full_side_out = full_side_out.reshape(side, width)

    normed, input_pull = jax.vjp(rms_norm, inputs, input_gain)
    normed_low = normed.astype(low)
    qkv_raw = forward_product(normed_low, full_qkv)
    left_low = forward_product(normed_low, full_left).astype(low)
    right_out = forward_product(left_low, full_right)

    frequency = jnp.exp(
        jnp.arange(HD // 2).astype(jnp.float32) * (-2.0 * math.log(rope_theta) / HD)
    )
    angles = query_pos.astype(jnp.float32)[:, None] * frequency[None, :]
    cosine, sine_part = jnp.cos(angles), jnp.sin(angles)
    query_ids = lax.dynamic_slice_in_dim(sequence_ids, ctx_place * rows_here, rows_here)
    kv_all, query_low, attended_low, log_totals = attention_forward(
        qkv_raw, cosine, sine_part, query_gain, key_gain, query_ids, sequence_ids
    )
    attn_raw = forward_product(attended_low, full_out)

    def mix_piece(x, normed_in, attn_in, right_in, gain_one, gain_two, gain_three):
        mixed = (
            x + rms_norm(attn_in, gain_one) + normed_in + rms_norm(right_in, gain_two)
        ) * inverse_root
        return (mixed, rms_norm(mixed, gain_three))

    (mixed, ffn_in), mix_pull = jax.vjp(
        mix_piece, inputs, normed, attn_raw, right_out, attn_gain, laurel_gain, pre_gain
    )

    ffn_all = gather(ffn_in.astype(low), "fsdp")
    gate_raw = forward_product(ffn_all, gate_weight)
    up_raw = forward_product(ffn_all, up_weight)
    hidden, hidden_pull = jax.vjp(hidden_piece, gate_raw, up_raw)
    hidden_low = hidden.astype(low)
    ffn_out = scatter_sum(forward_product(hidden_low, down_weight).astype(low), "fsdp")
    ffn_out = ffn_out.astype(jnp.float32)
    middle, middle_pull = jax.vjp(middle_piece, mixed, ffn_out, post_gain)
    middle_low = middle.astype(low)
    layer_gate = forward_product(middle_low, full_side_gate)
    layer_act, extra_pull = jax.vjp(hidden_piece, layer_gate, extra_rows)
    layer_low = layer_act.astype(low)
    layer_out = forward_product(layer_low, full_side_out)
    result, out_pull = jax.vjp(middle_piece, middle, layer_out, side_gain)

    middle_grad_one, layer_out_grad, side_gain_grad = out_pull(cotangent)
    layer_grad_low = layer_out_grad.astype(low)
    side_out_grad = over_rows(layer_low, layer_grad_low)
    layer_gate_grad, extra_grad = extra_pull(across(layer_grad_low, full_side_out))
    gate_grad_low = layer_gate_grad.astype(low)
    side_gate_grad = over_rows(gate_grad_low, middle_low)
    mixed_grad_one, ffn_out_grad, post_gain_grad = middle_pull(
        middle_grad_one + across(gate_grad_low, full_side_gate)
    )
    ffn_grad_all = gather(ffn_out_grad.astype(low), "fsdp")
    down_weight_grad = over_rows(ffn_grad_all, hidden_low)
    gate_raw_grad, up_raw_grad = hidden_pull(across(ffn_grad_all, down_weight))
    gate_back_low = gate_raw_grad.astype(low)
    up_back_low = up_raw_grad.astype(low)
    ffn_in_grad = scatter_sum(
        (across(gate_back_low, gate_weight) + across(up_back_low, up_weight)).astype(low), "fsdp"
    )
    gate_weight_grad = over_rows(ffn_all, gate_back_low)
    up_weight_grad = over_rows(ffn_all, up_back_low)
    ffn_in_grad, ffn_weight_grads, late_low = lax.optimization_barrier(
        (
            ffn_in_grad,
            [g.astype(low) for g in (down_weight_grad, gate_weight_grad, up_weight_grad)],
            (attended_low, normed_low),
        )
    )
    down_weight_grad, gate_weight_grad, up_weight_grad = ffn_weight_grads
    attended_all, normed_all = (gather(part, "fsdp") for part in late_low)
    (
        inputs_grad_one,
        normed_grad_one,
        attn_raw_grad,
        right_out_grad,
        attn_gain_grad,
        laurel_gain_grad,
        pre_gain_grad,
    ) = mix_pull((mixed_grad_one, ffn_in_grad.astype(jnp.float32)))
    attn_grad_low = attn_raw_grad.astype(low)
    attended_grad_low = across(attn_grad_low, full_out).astype(low)
    right_grad_low = right_out_grad.astype(low)
    right_weight_grad = over_rows(right_grad_low, left_low)
    left_grad_low = across(right_grad_low, full_right).astype(low)
    left_weight_grad = over_rows(normed_low, left_grad_low)
    qkv_back_low, query_gain_grad, key_gain_grad, ffn_sums = attention_backward(
        attended_grad_low,
        query_low,
        kv_all,
        log_totals,
        qkv_raw,
        cosine,
        sine_part,
        query_gain,
        key_gain,
        query_ids,
        sequence_ids,
        [g.astype(low) for g in (gate_weight_grad, up_weight_grad)],
    )
    down_low, qkv_back_low = lax.optimization_barrier((down_weight_grad.astype(low), qkv_back_low))
    down_weight_grad = scatter_sum(down_low, "ctx")
    normed_grad_two = across(qkv_back_low, full_qkv) + across(left_grad_low, full_left)
    inputs_grad_two, input_gain_grad = input_pull(normed_grad_one + normed_grad_two)
    block_out = result.astype(low)[None]
    tokens_grad = (inputs_grad_one + inputs_grad_two).astype(low)[None]
    per_layer_grad = extra_grad.astype(low)[None]

    def columns_to_owner(x):
        parts = x.reshape(rows_here, fsdp_count, -1).transpose(1, 0, 2)
        return lax.all_to_all(parts, "fsdp", 0, 0, tiled=True).reshape(fsdp_count * rows_here, -1)

    out_columns = columns_to_owner(attn_grad_low)
    out_weight_grad = over_rows(attended_all, out_columns)
    qkv_parts = jnp.concatenate(
        [
            part.reshape(rows_here, fsdp_count, -1)
            for part in (
                qkv_back_low[:, :query_width],
                qkv_back_low[:, query_width : query_width + kv_width],
                qkv_back_low[:, query_width + kv_width :],
            )
        ],
        axis=2,
    )
    qkv_columns = columns_to_owner(qkv_parts.reshape(rows_here, -1))
    qkv_weight_grad = over_rows(normed_all, qkv_columns)

    small_gains = [
        jnp.pad(g.reshape(count, -1), ((0, 0), (0, piece - g.shape[0] // count))).reshape(-1)
        for g in (query_gain_grad, key_gain_grad)
    ]
    gains = jnp.stack(
        [
            input_gain_grad,
            laurel_gain_grad,
            attn_gain_grad,
            pre_gain_grad,
            post_gain_grad,
            side_gain_grad,
            *small_gains,
        ]
    )
    gate_blocks = side_gate_grad.astype(low).reshape(side, ctx_count, -1).transpose(1, 0, 2)
    gate_columns = width // ctx_count
    tall = jnp.concatenate(
        [
            left_weight_grad.astype(low),
            right_weight_grad.astype(low),
            jnp.pad(gains.astype(low).T, ((0, 0), (0, 128 - gains.shape[0]))),
        ],
        axis=1,
    )
    out_blocks = side_out_grad.astype(low).reshape(
        ctx_count, side // ctx_count, fsdp_count, width // fsdp_count
    )
    out_blocks = out_blocks.transpose(0, 2, 1, 3).reshape(-1, width // fsdp_count)
    out_weight_grad, qkv_weight_grad, tall, gate_blocks, side_out_grad = owner_sums(
        [
            out_weight_grad.astype(low),
            qkv_weight_grad.astype(low),
            tall,
            gate_blocks.reshape(-1, gate_columns),
            out_blocks,
        ],
        3,
    )
    gate_weight_grad, up_weight_grad = ffn_sums
    down_weight_grad = down_weight_grad.T
    query_part = query_width // fsdp_count
    kv_part = kv_width // fsdp_count
    query_weight_grad = qkv_weight_grad[:, :query_part]
    key_weight_grad = qkv_weight_grad[:, query_part : query_part + kv_part]
    value_weight_grad = qkv_weight_grad[:, query_part + kv_part :]
    wide = jnp.float32
    tall = tall.astype(wide)
    left_weight_grad = tall[:, :rank]
    right_weight_grad = tall[:, rank : 2 * rank].T
    gains = tall[:, 2 * rank : 2 * rank + 8].T
    small_part = query_gain.shape[0] // count
    side_gate_grad = gate_blocks.astype(wide).T
    side_out_grad = side_out_grad.astype(wide)
    return (
        block_out,
        tokens_grad,
        per_layer_grad,
        query_weight_grad.astype(wide),
        key_weight_grad.astype(wide),
        value_weight_grad.astype(wide),
        out_weight_grad.astype(wide),
        left_weight_grad,
        right_weight_grad,
        gate_weight_grad.astype(wide),
        up_weight_grad.astype(wide),
        down_weight_grad.astype(wide),
        side_gate_grad,
        side_out_grad,
        *(gains[n] for n in range(6)),
        gains[6, :small_part],
        gains[7, :small_part],
    )


def solution(mesh):
    placed = (
        P("fsdp", "ctx", None),
        P("fsdp", "ctx", None),
        P("fsdp", "ctx", None),
        P("fsdp", None),
        P("fsdp", None),
        P("fsdp", None),
        P("fsdp", None),
        P("fsdp", None),
        P("fsdp", None),
        P(None, "fsdp"),
        P(None, "fsdp"),
        P(None, "fsdp"),
        P("fsdp", None),
        P("fsdp", None),
        P("fsdp", None),
        P(),
        P(),
        P(),
        P(),
        P(),
        P(),
        P(),
        P(),
    )
    return jax.shard_map(
        body,
        mesh=mesh,
        in_specs=placed,
        out_specs=(
            P("fsdp", "ctx", None),
            P("fsdp", "ctx", None),
            P("fsdp", "ctx", None),
            P("ctx", "fsdp"),
            P("ctx", "fsdp"),
            P("ctx", "fsdp"),
            P("ctx", "fsdp"),
            P(("ctx", "fsdp"), None),
            P(None, ("ctx", "fsdp")),
            P("ctx", "fsdp"),
            P("ctx", "fsdp"),
            P("fsdp", "ctx"),
            P("ctx", "fsdp"),
            P("ctx", "fsdp"),
            P(("ctx", "fsdp")),
            P(("ctx", "fsdp")),
            P(("ctx", "fsdp")),
            P(("ctx", "fsdp")),
            P(("ctx", "fsdp")),
            P(("ctx", "fsdp")),
            P(("ctx", "fsdp")),
            P(("ctx", "fsdp")),
        ),
        check_vma=False,
    )
```

time: 1110 us -> 657 us (0.59)
  waiting for transfers between devices: 781 us -> 152 us
  Pallas kernels: 0 us -> 274 us
  local copies, waits for them, and re-layouts: 97 us -> 26.9 us
  other arithmetic: 52.3 us -> 35.7 us
  matrix products: 148 us -> 135 us
    reduce_scatter x7 -> x3, waiting for transfers between devices: 335 us -> 57.9 us  [scatter_sum(): return lax.psum_scatter(x, axis, scatter_dimension=0, tiled=True)]
    pallas_call x0 -> x4, Pallas kernels: none -> 274 us  [the longest x1 108 us: weight_gather(): pl.pallas_call(functools.partial(weight_gather_kernel, ctx_count, fsdp_co...]
    all_gather x7 -> x4, waiting for transfers between devices: 287 us -> 89.5 us  [gather(): return lax.all_gather(x, axis, axis=0, tiled=True)]
    unnamed x18 -> x7, waiting for transfers between devices: 139 us -> 0.62 us
    unnamed x244 -> x128, local copies, waits for them, and re-layouts: 38.4 us -> 11.4 us
    convert_element_type x22 -> x2, local copies, waits for them, and re-layouts: 24.8 us -> 2 us  [the longest x1 1 us: body(): right_weight_grad.astype(low)]
    all_to_all x2, waiting for transfers between devices: 19.8 us -> 3.94 us  [columns_to_owner(): lax.all_to_all(parts, 'fsdp', 0, 0, tiled=True)]
  transfers between devices with their start and end apart: 18 -> 9, of which waited for: 14 -> 5; matrix products, arithmetic and copies ran while one was open for 18% -> 15% of each run, Pallas kernels for 0% -> 22%
where the time goes in v4:
time: 657 us; the launch traced here: 649 us
  Pallas kernels  274 us (42%)
  waiting for transfers between devices  152 us (23%)
  matrix products  135 us (21%)
  other arithmetic  35.7 us (5%)
  local copies, waits for them, and re-layouts  26.9 us (4%)
  between operations  15.5 us (2%)
  starting transfers between devices  10.8 us (2%)
    pallas_call x1, Pallas kernels, weight_gather(): pl.pallas_call(functools.partial(weight_gather_kernel, ctx_count, fsdp_co...  108 us
    pallas_call x1, Pallas kernels, attention_backward(): pl.pallas_call(functools.partial(attention_backward_kernel, ctx_count, sh...  96.7 us
    all_gather x4, waiting for transfers between devices, gather(): return lax.all_gather(x, axis, axis=0, tiled=True)  89.5 us
    reduce_scatter x3, waiting for transfers between devices, scatter_sum(): return lax.psum_scatter(x, axis, scatter_dimension=0, tiled=True)  57.9 us
    dot_general x9, matrix products, across(): lax.dot_general(a, b, (((1,), (1,)), ((), ())), preferred_element_type=jn...  52.1 us
    pallas_call x1, Pallas kernels, owner_sums(): pl.pallas_call(functools.partial(owner_sum_kernel, ctx_count, fsdp_count,...  46.7 us
    dot_general x9, matrix products, forward_product(): return jnp.dot(a, b, preferred_element_type=jnp.float32)  43.4 us
    dot_general x9, matrix products, over_rows(): lax.dot_general(a, b, (((0,), (0,)), ((), ())), preferred_element_type=jn...  39.4 us
  transfers between devices with their start and end apart: 9, of which 5 were waited for; matrix products, arithmetic and copies ran while one was open for 15% of the time, Pallas kernels for 22%

profile of v4, /device:TPU:0, one launch (start us, length us, event | category | flops | bytes accessed | tf_op | source)
XLA Modules:
  0.0 649.3 jit_solution(11145425019070699363)
XLA Ops:
  7.3 1.6 copy.90.refs_5_
  10.2 108.2 %weight_gather.1 = (bf16[4,2,2,2,64,3072]{5,4,3,2,1,0:T(8,128)(2,1)}, bf16[4,2,2,2,64,2304]{5,4,3,2,1,0:T(8,128)(2,1)}, bf16[4,512,64]{2,1,0:T(8,128)(2,1)}, bf1...) custom-call(bf16[2,2,2,64,2048]{4,3,2,1,0:T(8,128)(2,1)} %bitcast.182, bf16[2,2,2,64,512]{4,3,2,1,0:T(8,128)(2,1)} %bitcast.191, ...), custom_call_target="tpu_custom_call" | custom-call | bytes 44040192 | tf_op jit(solution)/shard_map/weight_gather/pallas_call | solution.py:296
  118.4 1.7 copy.110
  120.0 1.4 convolution_convert_fusion.11
  121.5 6.5 %fusion.61.raw.refs_4_ = f32[128,3072]{1,0:T(8,128)S(1)} fusion(bf16[2048,3072]{1,0:T(8,128)(2,1)} %bitcast.177, bf16[1,128,2048]{2,1,0:T(8,128)(2,1)S(1)} %copy-done.15, f32[2048]{0:T(1024)S(1)} %copy-done.34, f32[128]{0:T(128)S(1)} %fusion.72), kind=kOutput, calls=%fused_computation.115 | convolution fusion | flops 1611661312 | bytes 14688768 | tf_op jit(solution)/shard_map/dot_general | solution.py:28
  128.2 1.5 multiply_reduce_fusion.6
  130.1 22.0 %attention_forward.1 = (bf16[2,2,2,128,1024]{4,3,2,1,0:T(8,128)(2,1)S(1)}, bf16[128,2048]{1,0:T(8,128)(2,1)S(1)}, bf16[128,2048]{1,0:T(8,128)(2,1)}, f32[8,8,128]{2,1,0:T(8,128)S(1)}) custom-call(f32[128,3072]{1,0:T(8,128)S(1)} %fusion.61.raw.refs_4_, f32[128,128]{1,0:T(8,128)S(1)} %get-tuple-element.203.cosine_ref.refs_5_, ...), custom_call_target="tpu_custom_call" | custom-call | flops 1073741824 | bytes 8388608 | tf_op jit(solution)/shard_map/attention_forward/pallas_call | solution.py:526
  154.9 5.9 multiply_reduce_fusion.7
  160.8 2.6 multiply_reduce_fusion.5
  164.6 44.5 %all-gather.5.cloned.1.call-done = bf16[512,2048]{1,0:T(8,128)(2,1)} async-done(((bf16[128,2048]{1,0:T(8,128)(2,1)}), bf16[512,2048]{1,0:T(8,128)(2,1)}) %all-gather.5.cloned.1.call-update) | async-done | bytes 2097168 | tf_op jit(solution)/shard_map/all_gather | solution.py:48
  209.2 8.5 %fusion.82 = f32[512,2048]{1,0:T(8,128)S(1)} fusion(bf16[512,2048]{1,0:T(8,128)(2,1)} %all-gather.5.cloned.1.call-done, bf16[2048,2048]{1,0:T(8,128)(2,1)} %param.33), kind=kOutput, calls=%fused_computation.173 | convolution fusion | flops 4294967296 | bytes 14680064 | tf_op jit(solution)/shard_map/dot_general | solution.py:28
  217.7 11.6 %multiply_convert_fusion.1 = (bf16[512,2048]{1,0:T(8,128)(2,1)S(1)}, f32[512,2048]{1,0:T(8,128)}) fusion(f32[512,2048]{1,0:T(8,128)S(1)} %fusion.82, bf16[512,2048]{1,0:T(8,128)(2,1)S(1)} %copy-done.53, bf16[2048,2048]{1,0:T(8,128)(2,1)} %param.34), kind=kOutput, calls=%fused_computation.18 | convolution fusion | flops 4305453056 | bytes 20971520 | tf_op jit(solution)/shard_map/dot_general | solution.py:28
  230.7 5.7 convolution_convert_fusion.5
  236.5 42.7 %reduce-scatter.4.cloned.1.call-done = bf16[128,2048]{1,0:T(8,128)(2,1)} async-done(((bf16[512,2048]{1,0:T(8,128)(2,1)}), bf16[128,2048]{1,0:T(8,128)(2,1)}) %reduce-scatter.4.cloned.1.call-update) | async-done | bytes 524304 | tf_op jit(solution)/shard_map/reduce_scatter | solution.py:52
  281.9 1.7 fusion.54
  284.1 1.5 fusion.49
  285.6 2.5 fusion.43
  289.2 1.9 fusion.33
  293.7 45.0 %all-gather.7.cloned.1.call-done = bf16[512,2048]{1,0:T(8,128)(2,1)} async-done(((bf16[128,2048]{1,0:T(8,128)(2,1)}), bf16[512,2048]{1,0:T(8,128)(2,1)}) %all-gather.7.cloned.1.call-update) | async-done | bytes 2097168 | tf_op jit(solution)/shard_map/all_gather | solution.py:48
  338.6 12.0 %multiply_convert_fusion = (bf16[512,2048]{1,0:T(8,128)(2,1)S(1)}, bf16[512,2048]{1,0:T(8,128)(2,1)S(1)}) fusion(f32[512,2048]{1,0:T(8,128)} %copy-done.55, f32[512,2048]{1,0:T(8,128)} %get-tuple-element.211, bf16[512,2048]{1,0:T(8,128)(2,1)} %all-gather.7.cloned.1.call-done, bf16[2048,2048]{1,0:T(8,128)(2,1)} %param.35), kind=kOutput, calls=%fused_computation.17 | convolution fusion | flops 4320133120 | bytes 23068672 | tf_op jit(solution)/shard_map/dot_general | solution.py:32
  350.7 8.5 %fusion.83 = f32[512,2048]{1,0:T(8,128)S(1)} fusion(bf16[512,2048]{1,0:T(8,128)(2,1)S(1)} %get-tuple-element.190, bf16[2048,2048]{1,0:T(8,128)(2,1)} %param.33), kind=kOutput, calls=%fused_computation.174 | convolution fusion | flops 4294967296 | bytes 14680064 | tf_op jit(solution)/shard_map/dot_general | solution.py:32
  359.1 9.4 %add_convert_fusion = bf16[512,2048]{1,0:T(8,128)(2,1)} fusion(f32[512,2048]{1,0:T(8,128)S(1)} %fusion.83, bf16[512,2048]{1,0:T(8,128)(2,1)S(1)} %get-tuple-element.189, bf16[2048,2048]{1,0:T(8,128)(2,1)} %param.34), kind=kOutput, calls=%fused_computation.16 | convolution fusion | flops 4297064448 | bytes 16777216 | tf_op jit(solution)/shard_map/dot_general | solution.py:32
  368.8 10.1 %convolution_convert_fusion.2 = bf16[2048,2048]{1,0:T(8,128)(2,1)} fusion(bf16[512,2048]{1,0:T(8,128)(2,1)} %all-gather.7.cloned.1.call-done, bf16[512,2048]{1,0:T(8,128)(2,1)} %copy-done.56), kind=kOutput, calls=%fused_computation.2 | convolution fusion | flops 4299161600 | bytes 12582912 | tf_op jit(solution)/shard_map/dot_general | solution.py:36
  379.0 10.3 %convolution_convert_fusion.1.refs_11_ = bf16[2048,2048]{1,0:T(8,128)(2,1)} fusion(bf16[512,2048]{1,0:T(8,128)(2,1)} %all-gather.5.cloned.1.call-done, bf16[512,2048]{1,0:T(8,128)(2,1)} %copy-done.59), kind=kOutput, calls=%fused_computation.1 | convolution fusion | flops 4299161600 | bytes 12582912 | tf_op jit(solution)/shard_map/dot_general | solution.py:36
  389.3 6.8 %convolution_convert_fusion.refs_12_ = bf16[2048,2048]{1,0:T(8,128)(2,1)} fusion(bf16[512,2048]{1,0:T(8,128)(2,1)S(1)} %copy-done.54, bf16[512,2048]{1,0:T(8,128)(2,1)S(1)} %copy-done.58), kind=kOutput, calls=%fused_computation | convolution fusion | flops 4299161600 | bytes 12582912 | tf_op jit(solution)/shard_map/dot_general | solution.py:36
  396.1 15.2 %reduce-scatter.6.cloned.1.call-done = bf16[128,2048]{1,0:T(8,128)(2,1)} async-done(((bf16[512,2048]{1,0:T(8,128)(2,1)}), bf16[128,2048]{1,0:T(8,128)(2,1)}) %reduce-scatter.6.cloned.1.call-update) | async-done | bytes 524304 | tf_op jit(solution)/shard_map/reduce_scatter | solution.py:52
  413.7 1.5 fusion.38
  415.2 3.4 multiply_reduce_fusion
  418.7 2.8 fusion.46
  421.5 7.3 %fusion.12.refs_0_ = bf16[128,2048]{1,0:T(8,128)(2,1)} fusion(bf16[128,2048]{1,0:T(8,128)(2,1)S(1)} %get-tuple-element.194, bf16[2048,2304]{1,0:T(8,128)(2,1)} %bitcast.202), kind=kOutput, calls=%fused_computation.28 | convolution fusion | flops 1074003968 | bytes 9437184 | tf_op jit(solution)/shard_map/dot_general | solution.py:32
  428.8 96.7 %attention_backward.1 = (bf16[128,3072]{1,0:T(8,128)(2,1)}, f32[8,256]{1,0:T(8,128)}, bf16[256,2048]{1,0:T(8,128)(2,1)}, bf16[256,2048]{1,0:T(8,128)(2,1)}) custom-call(bf16[128,2048]{1,0:T(8,128)(2,1)} %fusion.12.refs_0_, bf16[128,2048]{1,0:T(8,128)(2,1)} %copy-done.3, bf16[2,2,2,128,1024]{4,3,2,1,0:T(8,128)(2,1)} %copy-done.1, f32[8,8,128]{2,1,0:T(8,128)} %copy-done.6, ...), custom_call_target="tpu_custom_call" | custom-call | flops 2684354560 | bytes 67108864 | tf_op jit(solution)/shard_map/attention_backward/pallas_call | solution.py:734
  527.1 1.5 convolution_convert_fusion.6
  528.6 1.6 reshape.307
  530.2 1.5 copy.102
  531.8 1.9 copy.118
  533.7 4.4 all-to-all-start
  541.8 9.0 %fusion.84 = f32[128,2048]{1,0:T(8,128)S(1)} fusion(bf16[128,3072]{1,0:T(8,128)(2,1)S(1)} %copy-done.23, bf16[2048,3072]{1,0:T(8,128)(2,1)} %bitcast.178), kind=kOutput, calls=%fused_computation.175 | convolution fusion | flops 1610612736 | bytes 14417920 | tf_op jit(solution)/shard_map/dot_general | solution.py:32
  550.9 1.6 fusion.35
  554.0 5.1 all-to-all-start.1
  562.7 2.9 convert_element_type.219
  565.6 2.8 convert_element_type.220
  570.3 4.3 convolution_convert_fusion.4.refs_0_
  574.5 3.9 all-to-all-done.1
  578.5 5.4 convolution_convert_fusion.3.refs_1_
  583.9 46.7 %owner_sums.1 = (bf16[256,512]{1,0:T(8,128)(2,1)S(1)}, bf16[256,768]{1,0:T(8,128)(2,1)S(1)}, bf16[64,256]{1,0:T(8,128)(2,1)S(1)}, bf16[64,256]{1,0:T(8,128)(2,1)S(1)}, bf16[32,512]{1,0:T(8,128)(2,1)S(1)}) custom-call(bf16[2048,512]{1,0:T(8,128)(2,1)S(1)} %copy-done.2, bf16[2048,768]{1,0:T(8,128)(2,1)} %convolution_convert_fusion.3.refs_1_, ...), custom_call_target="tpu_custom_call" | custom-call | flops 4194304 | bytes 16777216 | tf_op jit(solution)/shard_map/owner_sums/pallas_call | solution.py:871
  632.9 1.4 convert_element_type.223
  638.7 1.5 convert_bitcast_fusion
  640.2 1.8 copy.104
  (211 shorter events, 35.3 us)
Async XLA Ops:
  7.2 112.8 %copy-start.15 = (bf16[1,128,2048]{2,1,0:T(8,128)(2,1)S(1)}, bf16[1,128,2048]{2,1,0:T(8,128)(2,1)}, u32[]{:S(2)}) copy-start(bf16[1,128,2048]{2,1,0:T(8,128)(2,1)} %param.23) | copy-start | bytes 1572868
  7.2 112.8 %copy-start.34 = (f32[2048]{0:T(1024)S(1)}, f32[2048]{0:T(1024)}, u32[]{:S(2)}) copy-start(f32[2048]{0:T(1024)} %param.38) | copy-start | bytes 24580
  7.2 201.9 %all-gather.5.cloned.1.call-start = ((), (), s32[]{:S(2)}) async-start(), calls=%async_computation.5 | async-start | bytes 2621440 | tf_op jit(solution)/shard_map/all_gather | solution.py:48
  10.1 117.8 %copy-start.51 = (f32[128]{0:T(128)}, f32[128]{0:T(128)S(1)}, u32[]{:S(2)}) copy-start(f32[128]{0:T(128)S(1)} %fusion.39) | copy-start | bytes 1540
  10.2 150.6 %copy-start.45 = (f32[128]{0:T(128)}, f32[128]{0:T(128)S(1)}, u32[]{:S(2)}) copy-start(f32[128]{0:T(128)S(1)} %fusion.72) | copy-start | bytes 1540
  121.5 6.6 %copy-start.9 = (s32[1,1024]{1,0:T(1,128)S(1)}, s32[1,1024]{1,0:T(1,128)}, u32[]{:S(2)}) copy-start(s32[1,1024]{1,0:T(1,128)} %key_ids.1) | copy-start | bytes 12292
  121.5 8.6 %copy-start.10 = (f32[256]{0:T(256)S(1)}, f32[256]{0:T(256)}, u32[]{:S(2)}) copy-start(f32[256]{0:T(256)} %param.44) | copy-start | bytes 3076
  121.5 8.6 %copy-start.11 = (f32[256]{0:T(256)S(1)}, f32[256]{0:T(256)}, u32[]{:S(2)}) copy-start(f32[256]{0:T(256)} %param.45) | copy-start | bytes 3076
  128.0 32.7 %copy-start = (f32[128,3072]{1,0:T(8,128)}, f32[128,3072]{1,0:T(8,128)S(1)}, u32[]{:S(2)}) copy-start(f32[128,3072]{1,0:T(8,128)S(1)} %fusion.61.raw.refs_4_) | copy-start | bytes 4718596
  129.7 31.0 %copy-start.49 = (f32[128]{0:T(128)}, f32[128]{0:T(128)S(1)}, u32[]{:S(2)}) copy-start(f32[128]{0:T(128)S(1)} %get-tuple-element.206) | copy-start | bytes 1540
  130.0 30.7 %copy-start.4 = (f32[128,128]{1,0:T(8,128)}, f32[128,128]{1,0:T(8,128)S(1)}, u32[]{:S(2)}) copy-start(f32[128,128]{1,0:T(8,128)S(1)} %get-tuple-element.202.sine_ref.refs_6_) | copy-start | bytes 196612
  130.0 30.7 %copy-start.5 = (f32[128,128]{1,0:T(8,128)}, f32[128,128]{1,0:T(8,128)S(1)}, u32[]{:S(2)}) copy-start(f32[128,128]{1,0:T(8,128)S(1)} %get-tuple-element.203.cosine_ref.refs_5_) | copy-start | bytes 196612
  154.9 5.9 copy-start.42
  154.9 5.9 copy-start.43
  164.4 114.8 %reduce-scatter.4.cloned.1.call-start = ((), (), s32[]{:S(2)}) async-start(), calls=%async_computation.6 | async-start | bytes 2621440 | tf_op jit(solution)/shard_map/reduce_scatter | solution.py:52
  209.2 8.6 %copy-start.53 = (bf16[512,2048]{1,0:T(8,128)(2,1)S(1)}, bf16[512,2048]{1,0:T(8,128)(2,1)}, u32[]{:S(2)}) copy-start(bf16[512,2048]{1,0:T(8,128)(2,1)} %all-gather.5.cloned.1.call-done) | copy-start | bytes 6291460
  209.2 21.5 %slice-start = ((s8[8388608]{0:T(1024)(128)(4,1)}), s8[4194304]{0:T(1024)(128)(4,1)S(1)}, s32[]{:S(2)}) async-start(s8[8388608]{0:T(1024)(128)(4,1)} %bitcast.203), calls=%async_computation.12 | async-start | bytes 8388608
  217.7 11.7 %copy-start.55 = (f32[512,2048]{1,0:T(8,128)}, f32[512,2048]{1,0:T(8,128)S(1)}, u32[]{:S(2)}) copy-start(f32[512,2048]{1,0:T(8,128)S(1)} %fusion.82) | copy-start | bytes 12582916
  217.7 13.0 %slice-start.1 = ((s8[8388608]{0:T(1024)(128)(4,1)}), s8[4194304]{0:T(1024)(128)(4,1)S(1)}, s32[]{:S(2)}) async-start(s8[8388608]{0:T(1024)(128)(4,1)} %bitcast.203), calls=%async_computation.13 | async-start | bytes 8388608
  230.7 49.9 %copy-start.37 = (f32[2048]{0:T(1024)S(1)}, f32[2048]{0:T(1024)}, u32[]{:S(2)}) copy-start(f32[2048]{0:T(1024)} %param.42) | copy-start | bytes 24580
  236.4 47.2 %copy-start.35 = (bf16[1,128,256]{2,1,0:T(8,128)(2,1)S(1)}, bf16[1,128,256]{2,1,0:T(8,128)(2,1)}, u32[]{:S(2)}) copy-start(bf16[1,128,256]{2,1,0:T(8,128)(2,1)} %param.24) | copy-start | bytes 196612
  236.4 47.7 %copy-start.41 = (f32[2048]{0:T(1024)S(1)}, f32[2048]{0:T(1024)}, u32[]{:S(2)}) copy-start(f32[2048]{0:T(1024)} %param.43) | copy-start | bytes 24580
  236.5 102.2 %all-gather.7.cloned.1.call-start = ((), (), s32[]{:S(2)}) async-start(), calls=%async_computation.7 | async-start | bytes 2621440 | tf_op jit(solution)/shard_map/all_gather | solution.py:48
  279.2 6.4 copy-start.17
  289.2 61.4 %copy-start.39 = (bf16[128,256]{1,0:T(8,128)(2,1)}, bf16[128,256]{1,0:T(8,128)(2,1)S(1)}, u32[]{:S(2)}) copy-start(bf16[128,256]{1,0:T(8,128)(2,1)S(1)} %get-tuple-element.201) | copy-start | bytes 196612
  293.2 118.1 %reduce-scatter.6.cloned.1.call-start = ((), (), s32[]{:S(2)}) async-start(), calls=%async_computation.8 | async-start | bytes 2621440 | tf_op jit(solution)/shard_map/reduce_scatter | solution.py:52
  350.6 8.5 %copy-start.59 = (bf16[512,2048]{1,0:T(8,128)(2,1)}, bf16[512,2048]{1,0:T(8,128)(2,1)S(1)}, u32[]{:S(2)}) copy-start(bf16[512,2048]{1,0:T(8,128)(2,1)S(1)} %get-tuple-element.190) | copy-start | bytes 6291460
  350.6 8.5 %copy-start.57 = (bf16[512,2048]{1,0:T(8,128)(2,1)}, bf16[512,2048]{1,0:T(8,128)(2,1)S(1)}, u32[]{:S(2)}) copy-start(bf16[512,2048]{1,0:T(8,128)(2,1)S(1)} %get-tuple-element.189) | copy-start | bytes 6291460
  368.6 201.7 %all-gather.9.cloned.1.call-start = ((), (), s32[]{:S(2)}) async-start(), calls=%async_computation.9 | async-start | bytes 2621440 | tf_op jit(solution)/shard_map/all_gather | solution.py:48
  379.0 10.3 %copy-start.54 = (bf16[512,2048]{1,0:T(8,128)(2,1)S(1)}, bf16[512,2048]{1,0:T(8,128)(2,1)}, u32[]{:S(2)}) copy-start(bf16[512,2048]{1,0:T(8,128)(2,1)} %all-gather.5.cloned.1.call-done) | copy-start | bytes 6291460
  379.0 10.3 %copy-start.58 = (bf16[512,2048]{1,0:T(8,128)(2,1)S(1)}, bf16[512,2048]{1,0:T(8,128)(2,1)}, u32[]{:S(2)}) copy-start(bf16[512,2048]{1,0:T(8,128)(2,1)} %copy-done.57) | copy-start | bytes 6291460
  411.4 7.3 %copy-start.50 = (f32[128]{0:T(128)S(1)}, f32[128]{0:T(128)}, u32[]{:S(2)}) copy-start(f32[128]{0:T(128)} %copy-done.49) | copy-start | bytes 1540
  411.4 167.1 %all-gather.11.cloned.1.call-start = ((), (), s32[]{:S(2)}) async-start(), calls=%async_computation.10 | async-start | bytes 2621440 | tf_op jit(solution)/shard_map/all_gather | solution.py:48
  411.9 226.8 %reduce-scatter.8.cloned.1.call-start = ((), (), s32[]{:S(2)}) async-start(), calls=%async_computation.11 | async-start | bytes 9437184 | tf_op jit(solution)/shard_map/reduce_scatter | solution.py:52
  421.5 7.3 %copy-start.31 = (bf16[128,2048]{1,0:T(8,128)(2,1)}, bf16[128,2048]{1,0:T(8,128)(2,1)S(1)}, u32[]{:S(2)}) copy-start(bf16[128,2048]{1,0:T(8,128)(2,1)S(1)} %get-tuple-element.194) | copy-start | bytes 1572868
  530.2 10.3 %copy-start.19 = (bf16[128,2048]{1,0:T(8,128)(2,1)S(1)}, bf16[128,2048]{1,0:T(8,128)(2,1)}, u32[]{:S(2)}) copy-start(bf16[128,2048]{1,0:T(8,128)(2,1)} %get-tuple-element.193) | copy-start | bytes 1572868
  533.7 20.3 %all-to-all-start = ((bf16[4,128,512]{2,1,0:T(8,128)(2,1)}), bf16[4,128,512]{2,1,0:T(8,128)(2,1)}, u32[]{:S(2)}, u32[]{:S(2)}) async-start(bf16[4,128,512]{2,1,0:T(8,128)(2,1)} %bitcast.186), calls=%async_computation.2 | async-start | bytes 1048576 | tf_op jit(solution)/shard_map/all_to_all | solution.py:1048
  541.8 9.0 %copy-start.13 = (f32[128,2048]{1,0:T(8,128)S(1)}, f32[128,2048]{1,0:T(8,128)}, u32[]{:S(2)}) copy-start(f32[128,2048]{1,0:T(8,128)} %copy-done.12) | copy-start | bytes 3145732
  541.8 9.0 %copy-start.33 = (bf16[4,512,64]{2,1,0:T(8,128)(2,1)S(1)}, bf16[4,512,64]{2,1,0:T(8,128)(2,1)}, u32[]{:S(2)}) copy-start(bf16[4,512,64]{2,1,0:T(8,128)(2,1)} %get-tuple-element.51) | copy-start | bytes 786436
  541.8 9.0 %copy-start.46 = (f32[128]{0:T(128)S(1)}, f32[128]{0:T(128)}, u32[]{:S(2)}) copy-start(f32[128]{0:T(128)} %copy-done.45) | copy-start | bytes 1540
  554.0 24.4 %all-to-all-start.1 = ((bf16[4,128,768]{2,1,0:T(8,128)(2,1)}), bf16[4,128,768]{2,1,0:T(8,128)(2,1)}, u32[]{:S(2)}, u32[]{:S(2)}) async-start(bf16[4,128,768]{2,1,0:T(8,128)(2,1)} %maximum_bitcast_fusion), calls=%async_computation.3 | async-start | bytes 1572864 | tf_op jit(solution)/shard_map/all_to_all | solution.py:1048
  562.6 5.8 copy-start.27
  562.6 5.8 copy-start.28
  562.6 5.8 copy-start.29
  562.6 6.3 copy-start.14
  562.6 6.3 copy-start.16
  562.7 6.3 copy-start.21
  562.7 6.3 copy-start.47
  (23 other events, 50.2 us)
Sparse Core Ops, SparseCore 0:
  164.5 44.6 all-gather.4
  236.6 42.5 reduce-scatter.3
  293.3 45.2 all-gather.6
  368.7 42.5 reduce-scatter.5
  412.7 45.2 all-gather.8
  460.1 44.6 all-gather.10
  525.7 71.5 reduce-scatter.7

commit v5 on v4

--- a/solution.py
+++ b/solution.py
@@ -12,6 +12,9 @@
 KV_HEADS = 2
 HD = 256
 MESH = pl.DeviceIdType.MESH
+FF_TILE = 512
+BACK_TILE = 512
+GRAD_TILE = 256
 
 
 epsilon = 1e-06
@@ -882,6 +885,465 @@
     )(*arrays)
 
 
+def line_comes(along, count, way, step):
+    return along >= step if way == 0 else along + step < count
+
+
+def line_goes(along, count, way, step):
+    if way == 0:
+        return (along + 1 < count) & (along >= step - 1)
+    return (along >= 1) & (along + step - 1 < count)
+
+
+def line_origin(along, way, step):
+    return along - step if way == 0 else along + step
+
+
+class LineExchange:
+    def __init__(self, count, own, gathered, outgoing, incoming, sems):
+        self.count, self.steps = count, count - 1
+        self.own, self.gathered = own, gathered
+        self.outgoing, self.incoming = outgoing, incoming
+        self.line_send, self.line_recv, self.back_send, self.back_recv = sems
+        self.place = lax.axis_index("ctx")
+        self.along = lax.axis_index("fsdp")
+        self.width = outgoing.shape[-1]
+        self.chunks = self.width // BACK_TILE
+
+    def barrier(self):
+        partner_barrier(
+            [
+                (self.place, lax.rem(self.along + d, self.count))
+                for d in sorted({1, self.count - 1})
+            ]
+        )
+
+    def line_copy(self, way, step, origin):
+        toward = self.along + 1 if way == 0 else self.along - 1
+        return pltpu.make_async_remote_copy(
+            src_ref=self.own if step == 1 else self.gathered.at[origin],
+            dst_ref=self.gathered.at[origin],
+            send_sem=self.line_send.at[way, step - 1],
+            recv_sem=self.line_recv.at[way, step - 1],
+            device_id=(self.place, toward),
+            device_id_type=MESH,
+        )
+
+    def forward(self, step):
+        for way in range(2):
+            origin = line_origin(self.along, way, step - 1)
+            pl.when(line_goes(self.along, self.count, way, step))(
+                lambda way=way, origin=origin: self.line_copy(way, step, origin).start()
+            )
+
+    def arrive(self, step):
+        for way in range(2):
+            origin = line_origin(self.along, way, step)
+            pl.when(line_comes(self.along, self.count, way, step))(
+                lambda way=way, origin=origin: self.line_copy(way, step, origin).wait_recv()
+            )
+        if step < self.steps:
+            self.forward(step + 1)
+
+    def back_copy(self, way, owner, chunk):
+        toward = self.along + 1 if way == 0 else self.along - 1
+        columns = pl.ds(chunk * BACK_TILE, BACK_TILE)
+        landing = owner if way == 0 else jnp.where(owner == toward, self.count, owner)
+        return pltpu.make_async_remote_copy(
+            src_ref=self.outgoing.at[owner, :, columns],
+            dst_ref=self.incoming.at[landing, :, columns],
+            send_sem=self.back_send.at[way, owner, chunk],
+            recv_sem=self.back_recv.at[way, owner, chunk],
+            device_id=(self.place, toward),
+            device_id_type=MESH,
+        )
+
+    def landed(self, way, owner, chunk, landing):
+        columns = pl.ds(chunk * BACK_TILE, BACK_TILE)
+        pltpu.make_async_remote_copy(
+            src_ref=self.outgoing.at[owner, :, columns],
+            dst_ref=self.incoming.at[landing, :, columns],
+            send_sem=self.back_send.at[way, owner, chunk],
+            recv_sem=self.back_recv.at[way, owner, chunk],
+            device_id=(self.place, self.along),
+            device_id_type=MESH,
+        ).wait_recv()
+        return self.incoming[landing, :, columns].astype(jnp.float32)
+
+    def relays(self, way):
+        return self.along >= 1 if way == 0 else self.along + 1 < self.count
+
+    def run(self, compute, before_last):
+
+        def one(way, step):
+            back = 1 - way
+            origin = line_origin(self.along, way, step)
+
+            def work():
+                def write(columns, tile):
+                    self.outgoing[origin, :, columns] = tile.astype(self.outgoing.dtype)
+
+                compute(origin, write)
+
+                def begin():
+                    for chunk in range(self.chunks):
+                        self.back_copy(back, origin, chunk).start()
+
+                pl.when(jnp.logical_not(self.relays(back)))(begin)
+
+            pl.when(line_comes(self.along, self.count, way, step))(work)
+
+        def relay(way, step):
+            owner = step if way == 0 else self.steps - step
+            passes = owner > self.along if way == 0 else owner < self.along
+
+            def work():
+                for chunk in range(self.chunks):
+                    more = self.landed(way, owner, chunk, owner)
+                    columns = pl.ds(chunk * BACK_TILE, BACK_TILE)
+                    mine = self.outgoing[owner, :, columns].astype(jnp.float32)
+                    self.outgoing[owner, :, columns] = (mine + more).astype(self.outgoing.dtype)
+                    self.back_copy(way, owner, chunk).start()
+
+            pl.when(self.relays(way) & passes)(work)
+
+        for step in range(1, self.steps + 1):
+            self.arrive(step)
+            for way in range(2):
+                one(way, step)
+            if step == self.steps:
+                before_last()
+            for way in range(2):
+                relay(way, step)
+
+    def finish(self, total):
+        for way in range(2):
+
+            def receive(way=way):
+                landing = self.along if way == 0 else self.count
+                for chunk in range(self.chunks):
+                    columns = pl.ds(chunk * BACK_TILE, BACK_TILE)
+                    more = self.landed(way, self.along, chunk, landing)
+                    total[:, columns] = total[:, columns] + more
+
+            pl.when(self.relays(way))(receive)
+        for step in range(1, self.steps + 1):
+            for way in range(2):
+                origin = line_origin(self.along, way, step - 1)
+
+                def left(way=way, step=step, origin=origin):
+                    self.line_copy(way, step, origin).wait_send()
+
+                def returned(way=way, step=step):
+                    for chunk in range(self.chunks):
+                        self.back_copy(1 - way, line_origin(self.along, way, step), chunk).wait_send()
+
+                pl.when(line_goes(self.along, self.count, way, step))(left)
+                pl.when(line_comes(self.along, self.count, way, step))(returned)
+
+
+def line_scratch(count, rows, columns):
+    steps = count - 1
+    chunks = columns // BACK_TILE
+    return [
+        pltpu.VMEM((count, rows, columns), jnp.bfloat16),
+        pltpu.VMEM((count + 1, rows, columns), jnp.bfloat16),
+        pltpu.SemaphoreType.DMA((2, steps)),
+        pltpu.SemaphoreType.DMA((2, steps)),
+        pltpu.SemaphoreType.DMA((2, count, chunks)),
+        pltpu.SemaphoreType.DMA((2, count, chunks)),
+    ]
+
+
+def tile_at(t, size):
+    return pl.ds(pl.multiple_of(t * size, size), size)
+
+
+def feed_forward_kernel(
+    count,
+    rows_in,
+    gate_hbm,
+    up_hbm,
+    down_hbm,
+    total,
+    gathered,
+    gate_keep,
+    up_keep,
+    hidden_keep,
+    gate_w,
+    up_w,
+    down_w,
+    weight_sem,
+    *parts,
+):
+    rows, width = rows_in.shape
+    units = gate_w.shape[1]
+    tile = FF_TILE
+    line = LineExchange(count, rows_in, gathered, parts[0], parts[1], parts[2:])
+    loads = []
+    for n, (source, target) in enumerate(((gate_hbm, gate_w), (up_hbm, up_w), (down_hbm, down_w))):
+        group = []
+        for t in range(target.shape[1] // tile):
+            at = (slice(None), pl.ds(t * tile, tile))
+            group.append(pltpu.make_async_copy(source.at[at], target.at[at], weight_sem.at[n, t]))
+        loads.append(group)
+    for t in range(units // tile):
+        loads[0][t].start()
+        loads[1][t].start()
+    for load in loads[2]:
+        load.start()
+    line.barrier()
+    line.forward(1)
+    gathered[line.along] = rows_in[...]
+
+    def hidden_tile(origin, columns):
+        at = pl.ds(pl.multiple_of(origin * rows, rows), rows)
+        gate = forward_product(gathered[origin], gate_w[:, columns])
+        up = forward_product(gathered[origin], up_w[:, columns])
+        gate_keep[at, columns] = gate.astype(gate_keep.dtype)
+        up_keep[at, columns] = up.astype(up_keep.dtype)
+        hidden_keep[at, columns] = hidden_piece(gate, up).astype(hidden_keep.dtype)
+
+    def out_tile(origin, columns):
+        at = pl.ds(pl.multiple_of(origin * rows, rows), rows)
+        return forward_product(hidden_keep[at], down_w[:, columns])
+
+    for t in range(units // tile):
+        loads[0][t].wait()
+        loads[1][t].wait()
+        hidden_tile(line.along, pl.ds(t * tile, tile))
+    for t in range(width // tile):
+        loads[2][t].wait()
+        columns = pl.ds(t * tile, tile)
+        total[:, columns] = out_tile(line.along, columns)
+
+    def compute(origin, write):
+        def hidden_step(t, carry):
+            hidden_tile(origin, tile_at(t, tile))
+            return carry
+
+        def out_step(t, carry):
+            columns = tile_at(t, tile)
+            write(columns, out_tile(origin, columns))
+            return carry
+
+        lax.fori_loop(0, units // tile, hidden_step, 0)
+        lax.fori_loop(0, width // tile, out_step, 0)
+
+    line.run(compute, lambda: None)
+    line.finish(total)
+
+
+def feed_forward(rows_in, gate_weight, up_weight, down_weight):
+    count = lax.axis_size("fsdp")
+    rows, width = rows_in.shape
+    units = gate_weight.shape[1]
+    low = jnp.bfloat16
+    vmem = pl.BlockSpec(memory_space=pltpu.VMEM)
+    hbm = pl.BlockSpec(memory_space=pltpu.HBM)
+    kept = jax.ShapeDtypeStruct((count * rows, units), low)
+    out, gathered, gate, up, hidden = pl.pallas_call(
+        functools.partial(feed_forward_kernel, count),
+        out_shape=[
+            jax.ShapeDtypeStruct((rows, width), jnp.float32),
+            jax.ShapeDtypeStruct((count, rows, width), low),
+            kept,
+            kept,
+            kept,
+        ],
+        in_specs=[vmem, hbm, hbm, hbm],
+        out_specs=[vmem] * 5,
+        scratch_shapes=[
+            pltpu.VMEM((width, units), low),
+            pltpu.VMEM((width, units), low),
+            pltpu.VMEM((units, width), low),
+            pltpu.SemaphoreType.DMA((3, max(width, units) // FF_TILE)),
+        ]
+        + line_scratch(count, rows, width),
+        compiler_params=pltpu.CompilerParams(
+            collective_id=4, has_side_effects=True, vmem_limit_bytes=56 << 20
+        ),
+        cost_estimate=pl.CostEstimate(
+            flops=6 * count * rows * width * units,
+            bytes_accessed=6 * width * units,
+            transcendentals=count * rows * units,
+        ),
+        name="feed_forward",
+    )(rows_in, gate_weight, up_weight, down_weight)
+    return out, gathered.reshape(count * rows, width), gate, up, hidden
+
+
+def hidden_pull_tile(grad, gate, up):
+    slope = math.sqrt(2.0 / math.pi)
+    square = gate * gate
+    curve = jnp.tanh(slope * gate * (1.0 + 0.044715 * square))
+    bend = 0.5 * (1.0 + curve)
+    steep = bend + 0.5 * gate * (1.0 - curve * curve) * slope * (1.0 + 3.0 * 0.044715 * square)
+    return grad * up * steep, grad * gate * bend
+
+
+def feed_forward_backward_kernel(
+    count,
+    grads_in,
+    gate_keep,
+    up_keep,
+    hidden_keep,
+    tokens,
+    gate_hbm,
+    up_hbm,
+    down_hbm,
+    total,
+    down_grad,
+    gate_grad,
+    up_grad,
+    gathered,
+    gate_back,
+    up_back,
+    gate_w,
+    up_w,
+    down_w,
+    weight_sem,
+    staged,
+    staged_sem,
+    *parts,
+):
+    rows, width = grads_in.shape
+    units = gate_w.shape[1]
+    tile = FF_TILE
+    line = LineExchange(count, grads_in, gathered, parts[0], parts[1], parts[2:])
+    loads = []
+    for n, (source, target) in enumerate(((gate_hbm, gate_w), (up_hbm, up_w), (down_hbm, down_w))):
+        group = []
+        for t in range(target.shape[0] // tile):
+            at = pl.ds(t * tile, tile)
+            group.append(pltpu.make_async_copy(source.at[at], target.at[at], weight_sem.at[n, t]))
+        loads.append(group)
+    for load in loads[2]:
+        load.start()
+    for t in range(width // tile):
+        loads[0][t].start()
+        loads[1][t].start()
+    line.barrier()
+    line.forward(1)
+    gathered[line.along] = grads_in[...]
+
+    def hidden_tile(origin, columns):
+        at = pl.ds(pl.multiple_of(origin * rows, rows), rows)
+        grad = across(gathered[origin], down_w[columns])
+        gate = gate_keep[at, columns].astype(jnp.float32)
+        up = up_keep[at, columns].astype(jnp.float32)
+        gate_pull, up_pull = hidden_pull_tile(grad, gate, up)
+        gate_back[at, columns] = gate_pull.astype(gate_back.dtype)
+        up_back[at, columns] = up_pull.astype(up_back.dtype)
+
+    def out_tile(origin, columns):
+        at = pl.ds(pl.multiple_of(origin * rows, rows), rows)
+        return across(gate_back[at], gate_w[columns]) + across(up_back[at], up_w[columns])
+
+    for t in range(units // tile):
+        loads[2][t].wait()
+        hidden_tile(line.along, pl.ds(t * tile, tile))
+    for t in range(width // tile):
+        loads[0][t].wait()
+        loads[1][t].wait()
+        columns = pl.ds(t * tile, tile)
+        total[:, columns] = out_tile(line.along, columns)
+
+    def compute(origin, write):
+        def hidden_step(t, carry):
+            hidden_tile(origin, tile_at(t, tile))
+            return carry
+
+        def out_step(t, carry):
+            columns = tile_at(t, tile)
+            write(columns, out_tile(origin, columns))
+            return carry
+
+        lax.fori_loop(0, units // tile, hidden_step, 0)
+        lax.fori_loop(0, width // tile, out_step, 0)
+
+    band = GRAD_TILE
+    bands = width // band
+
+    def stage(slot, which, t, target):
+        return pltpu.make_async_copy(
+            staged.at[slot, which], target.at[tile_at(t, band)], staged_sem.at[slot, which]
+        )
+
+    def grad_bands(jobs):
+        def step(t, carry):
+            slot = lax.rem(t, 2)
+            for left, right, target, which in jobs:
+
+                @pl.when(t >= 2)
+                def _(target=target, which=which):
+                    stage(slot, which, t, target).wait()
+
+                product = over_rows(left(tile_at(t, band)), right[...])
+                staged[slot, which] = product.astype(staged.dtype)
+                stage(slot, which, t, target).start()
+            return carry
+
+        lax.fori_loop(0, bands, step, 0)
+        for back in range(2):
+            t = bands - 2 + back
+            for _, _, target, which in jobs:
+                stage(t % 2, which, t, target).wait()
+
+    def grads_at(columns):
+        return gathered[:, :, columns].reshape(count * rows, band)
+
+    line.run(
+        compute, lambda: grad_bands([(grads_at, hidden_keep, down_grad, 0)])
+    )
+    grad_bands(
+        [
+            (lambda columns: tokens[:, columns], gate_back, gate_grad, 0),
+            (lambda columns: tokens[:, columns], up_back, up_grad, 1),
+        ]
+    )
+    line.finish(total)
+
+
+def feed_forward_backward(
+    grads_in, gate_keep, up_keep, hidden_keep, tokens, gate_weight, up_weight, down_weight
+):
+    count = lax.axis_size("fsdp")
+    rows, width = grads_in.shape
+    units = gate_weight.shape[1]
+    low = jnp.bfloat16
+    vmem = pl.BlockSpec(memory_space=pltpu.VMEM)
+    hbm = pl.BlockSpec(memory_space=pltpu.HBM)
+    grad_shape = jax.ShapeDtypeStruct((width, units), low)
+    return pl.pallas_call(
+        functools.partial(feed_forward_backward_kernel, count),
+        out_shape=[jax.ShapeDtypeStruct((rows, width), jnp.float32)] + [grad_shape] * 3,
+        in_specs=[vmem] * 5 + [hbm] * 3,
+        out_specs=[vmem] + [hbm] * 3,
+        scratch_shapes=[
+            pltpu.VMEM((count, rows, width), low),
+            pltpu.VMEM((count * rows, units), low),
+            pltpu.VMEM((count * rows, units), low),
+            pltpu.VMEM((width, units), low),
+            pltpu.VMEM((width, units), low),
+            pltpu.VMEM((units, width), low),
+            pltpu.SemaphoreType.DMA((3, max(width, units) // FF_TILE)),
+            pltpu.VMEM((2, 2, GRAD_TILE, units), low),
+            pltpu.SemaphoreType.DMA((2, 2)),
+        ]
+        + line_scratch(count, rows, width),
+        compiler_params=pltpu.CompilerParams(
+            collective_id=5, has_side_effects=True, vmem_limit_bytes=60 << 20
+        ),
+        cost_estimate=pl.CostEstimate(
+            flops=12 * count * rows * width * units,
+            bytes_accessed=12 * width * units,
+            transcendentals=count * rows * units,
+        ),
+        name="feed_forward_backward",
+    )(grads_in, gate_keep, up_keep, hidden_keep, tokens, gate_weight, up_weight, down_weight)
+
+
 def body(
     tokens,
     per_layer,
@@ -963,13 +1425,9 @@
         mix_piece, inputs, normed, attn_raw, right_out, attn_gain, laurel_gain, pre_gain
     )
 
-    ffn_all = gather(ffn_in.astype(low), "fsdp")
-    gate_raw = forward_product(ffn_all, gate_weight)
-    up_raw = forward_product(ffn_all, up_weight)
-    hidden, hidden_pull = jax.vjp(hidden_piece, gate_raw, up_raw)
-    hidden_low = hidden.astype(low)
-    ffn_out = scatter_sum(forward_product(hidden_low, down_weight).astype(low), "fsdp")
-    ffn_out = ffn_out.astype(jnp.float32)
+    ffn_out, ffn_all, gate_raw, up_raw, hidden_low = feed_forward(
+        ffn_in.astype(low), gate_weight, up_weight, down_weight
+    )
     middle, middle_pull = jax.vjp(middle_piece, mixed, ffn_out, post_gain)
     middle_low = middle.astype(low)
     layer_gate = forward_product(middle_low, full_side_gate)
@@ -987,24 +1445,17 @@
     mixed_grad_one, ffn_out_grad, post_gain_grad = middle_pull(
         middle_grad_one + across(gate_grad_low, full_side_gate)
     )
-    ffn_grad_all = gather(ffn_out_grad.astype(low), "fsdp")
-    down_weight_grad = over_rows(ffn_grad_all, hidden_low)
-    gate_raw_grad, up_raw_grad = hidden_pull(across(ffn_grad_all, down_weight))
-    gate_back_low = gate_raw_grad.astype(low)
-    up_back_low = up_raw_grad.astype(low)
-    ffn_in_grad = scatter_sum(
-        (across(gate_back_low, gate_weight) + across(up_back_low, up_weight)).astype(low), "fsdp"
-    )
-    gate_weight_grad = over_rows(ffn_all, gate_back_low)
-    up_weight_grad = over_rows(ffn_all, up_back_low)
-    ffn_in_grad, ffn_weight_grads, late_low = lax.optimization_barrier(
-        (
-            ffn_in_grad,
-            [g.astype(low) for g in (down_weight_grad, gate_weight_grad, up_weight_grad)],
-            (attended_low, normed_low),
-        )
-    )
-    down_weight_grad, gate_weight_grad, up_weight_grad = ffn_weight_grads
+    ffn_in_grad, down_weight_grad, gate_weight_grad, up_weight_grad = feed_forward_backward(
+        ffn_out_grad.astype(low),
+        gate_raw,
+        up_raw,
+        hidden_low,
+        ffn_all,
+        gate_weight,
+        up_weight,
+        down_weight,
+    )
+    ffn_in_grad, late_low = lax.optimization_barrier((ffn_in_grad, (attended_low, normed_low)))
     attended_all, normed_all = (gather(part, "fsdp") for part in late_low)
     (
         inputs_grad_one,
@@ -1014,7 +1465,7 @@
         attn_gain_grad,
         laurel_gain_grad,
         pre_gain_grad,
-    ) = mix_pull((mixed_grad_one, ffn_in_grad.astype(jnp.float32)))
+    ) = mix_pull((mixed_grad_one, ffn_in_grad))
     attn_grad_low = attn_raw_grad.astype(low)
     attended_grad_low = across(attn_grad_low, full_out).astype(low)
     right_grad_low = right_out_grad.astype(low)
@@ -1033,9 +1484,9 @@
         key_gain,
         query_ids,
         sequence_ids,
-        [g.astype(low) for g in (gate_weight_grad, up_weight_grad)],
-    )
-    down_low, qkv_back_low = lax.optimization_barrier((down_weight_grad.astype(low), qkv_back_low))
+        [gate_weight_grad, up_weight_grad],
+    )
+    down_low, qkv_back_low = lax.optimization_barrier((down_weight_grad, qkv_back_low))
     down_weight_grad = scatter_sum(down_low, "ctx")
     normed_grad_two = across(qkv_back_low, full_qkv) + across(left_grad_low, full_left)
     inputs_grad_two, input_gain_grad = input_pull(normed_grad_one + normed_grad_two)

time: 657 us -> 587 us (0.89)
  Pallas kernels: 274 us -> 439 us
  waiting for transfers between devices: 152 us -> 3.52 us
  matrix products: 135 us -> 52.5 us
    pallas_call x0 -> x2, Pallas kernels: none -> 162 us  [the longest x1 81.9 us: feed_forward(): pl.pallas_call(functools.partial(feed_forward_kernel, count), out_shape=[...]
    all_gather x4 -> x2, waiting for transfers between devices: 89.5 us -> 0.01 us  [gather(): return lax.all_gather(x, axis, axis=0, tiled=True)]
    reduce_scatter x3 -> x1, waiting for transfers between devices: 57.9 us -> 0.01 us  [scatter_sum(): return lax.psum_scatter(x, axis, scatter_dimension=0, tiled=True)]
    dot_general x9 -> x6, matrix products: 39.4 us -> 11.8 us  [over_rows(): lax.dot_general(a, b, (((0,), (0,)), ((), ())), preferred_element_type=jn...]
    dot_general x9 -> x6, matrix products: 52.1 us -> 24.5 us  [across(): lax.dot_general(a, b, (((1,), (1,)), ((), ())), preferred_element_type=jn...]
    dot_general x9 -> x6, matrix products: 43.4 us -> 16.2 us  [forward_product(): return jnp.dot(a, b, preferred_element_type=jnp.float32)]
    all_to_all x2, starting transfers between devices: 9.47 us -> 16.9 us  [columns_to_owner(): lax.all_to_all(parts, 'fsdp', 0, 0, tiled=True)]
  transfers between devices with their start and end apart: 9 -> 5, of which waited for: 5 -> 1; matrix products, arithmetic and copies ran while one was open for 15% -> 11% of each run, Pallas kernels for 22% -> 25%
where the time goes in v5:
time: 587 us; the launch traced here: 582 us
  Pallas kernels  439 us (75%)
  matrix products  52.5 us (9%)
  other arithmetic  29.5 us (5%)
  local copies, waits for them, and re-layouts  23 us (4%)
  starting transfers between devices  17.1 us (3%)
  between operations  17.1 us (3%)
    pallas_call x1, Pallas kernels, weight_gather(): pl.pallas_call(functools.partial(weight_gather_kernel, ctx_count, fsdp_co...  108 us
    pallas_call x1, Pallas kernels, attention_backward(): pl.pallas_call(functools.partial(attention_backward_kernel, ctx_count, sh...  95.9 us
    pallas_call x1, Pallas kernels, feed_forward(): pl.pallas_call(functools.partial(feed_forward_kernel, count), out_shape=[...  81.9 us
    pallas_call x1, Pallas kernels, feed_forward_backward(): pl.pallas_call(functools.partial(feed_forward_backward_kernel, count), ou...  80.3 us
    pallas_call x1, Pallas kernels, owner_sums(): pl.pallas_call(functools.partial(owner_sum_kernel, ctx_count, fsdp_count,...  50.8 us
    dot_general x6, matrix products, across(): lax.dot_general(a, b, (((1,), (1,)), ((), ())), preferred_element_type=jn...  24.5 us
    pallas_call x1, Pallas kernels, attention_forward(): pl.pallas_call(functools.partial(attention_forward_kernel, ctx_count), ou...  22.1 us
    all_to_all x2, starting transfers between devices, columns_to_owner(): lax.all_to_all(parts, 'fsdp', 0, 0, tiled=True)  16.9 us
  transfers between devices with their start and end apart: 5, of which 1 were waited for; matrix products, arithmetic and copies ran while one was open for 11% of the time, Pallas kernels for 25%

profile of v5, /device:TPU:0, one launch (start us, length us, event | category | flops | bytes accessed | tf_op | source)
XLA Modules:
  0.0 581.7 jit_solution(11111166789198664943)
XLA Ops:
  8.1 1.6 copy.90.refs_5_
  9.7 1.2 fusion.23
  11.5 108.1 %weight_gather.1 = (bf16[4,2,2,2,64,3072]{5,4,3,2,1,0:T(8,128)(2,1)}, bf16[4,2,2,2,64,2304]{5,4,3,2,1,0:T(8,128)(2,1)}, bf16[4,512,64]{2,1,0:T(8,128)(2,1)}, bf1...) custom-call(bf16[2,2,2,64,2048]{4,3,2,1,0:T(8,128)(2,1)} %bitcast.163, bf16[2,2,2,64,512]{4,3,2,1,0:T(8,128)(2,1)} %bitcast.171, ...), custom_call_target="tpu_custom_call" | custom-call | bytes 44040192 | tf_op jit(solution)/shard_map/weight_gather/pallas_call | solution.py:299
  119.6 1.0 copy.110
  120.6 1.4 convolution_convert_fusion.7
  122.1 6.5 %fusion.44.raw.refs_4_ = f32[128,3072]{1,0:T(8,128)S(1)} fusion(bf16[2048,3072]{1,0:T(8,128)(2,1)} %bitcast.158, bf16[1,128,2048]{2,1,0:T(8,128)(2,1)S(1)} %copy-done.17, f32[2048]{0:T(1024)S(1)} %copy-done.41, f32[128]{0:T(128)S(1)} %fusion.55), kind=kOutput, calls=%fused_computation.88 | convolution fusion | flops 1611661312 | bytes 14688768 | tf_op jit(solution)/shard_map/dot_general | solution.py:31
  128.7 1.3 multiply_reduce_fusion.11
  130.4 22.1 %attention_forward.1 = (bf16[2,2,2,128,1024]{4,3,2,1,0:T(8,128)(2,1)S(1)}, bf16[128,2048]{1,0:T(8,128)(2,1)S(1)}, bf16[128,2048]{1,0:T(8,128)(2,1)}, f32[8,8,128]{2,1,0:T(8,128)S(1)}) custom-call(f32[128,3072]{1,0:T(8,128)S(1)} %fusion.44.raw.refs_4_, f32[128,128]{1,0:T(8,128)S(1)} %get-tuple-element.213.cosine_ref.refs_5_, ...), custom_call_target="tpu_custom_call" | custom-call | flops 1073741824 | bytes 8388608 | tf_op jit(solution)/shard_map/attention_forward/pallas_call | solution.py:529
  152.5 1.3 copy-done.1
  155.2 5.0 multiply_reduce_fusion.12
  160.8 1.3 multiply_reduce_fusion.10
  162.7 0.9 multiply_convert_fusion.rows_in
  163.6 81.9 %feed_forward.1 = (f32[128,2048]{1,0:T(8,128)}, bf16[4,128,2048]{2,1,0:T(8,128)(2,1)}, bf16[512,2048]{1,0:T(8,128)(2,1)}, bf16[512,2048]{1,0:T(8,128)(2,1)}, bf16[512,2048]{1,0:T(8,128)(2,1)}) custom-call(bf16[128,2048]{1,0:T(8,128)(2,1)} %multiply_convert_fusion.rows_in, bf16[2048,2048]{1,0:T(8,128)(2,1)} %gate_hbm.3, bf16[2048,2048]{1,0:T(8,128)(2,1)} %up_hbm.3, ...), custom_call_target="tpu_custom_call" | custom-call | flops 12884901888 | bytes 25165824 | tf_op jit(solution)/shard_map/feed_forward/pallas_call | solution.py:1145
  245.6 1.4 multiply_reduce_fusion.9
  247.0 1.5 multiply_add_fusion
  248.5 1.6 fusion.36
  251.0 1.2 fusion.27
  252.2 1.2 fusion.54
  253.3 2.5 multiply_reduce_fusion
  255.9 1.1 fusion.28.grads_in
  257.0 80.3 %feed_forward_backward.1 = (f32[128,2048]{1,0:T(8,128)}, bf16[2048,2048]{1,0:T(8,128)(2,1)}, bf16[2048,2048]{1,0:T(8,128)(2,1)}, bf16[2048,2048]{1,0:T(8,128)(2,1)}) custom-call(bf16[128,2048]{1,0:T(8,128)(2,1)} %fusion.28.grads_in, bf16[512,2048]{1,0:T(8,128)(2,1)} %get-tuple-element.61.gate_keep, bf16[512,2048]{1,0:T(8,128)(2,1)} %get-tuple-element.62.up_keep, ...), custom_call_target="tpu_custom_call" | custom-call | flops 25769803776 | bytes 50331648 | tf_op jit(solution)/shard_map/feed_forward_backward/pallas_call | solution.py:1318
  338.2 1.0 copy.93.refs_10_
  339.9 1.6 multiply_reduce_fusion.1
  341.6 3.7 multiply_reduce_fusion.2
  345.9 7.3 %fusion.5.refs_0_ = bf16[128,2048]{1,0:T(8,128)(2,1)} fusion(bf16[128,2048]{1,0:T(8,128)(2,1)S(1)} %get-tuple-element.204, bf16[2048,2304]{1,0:T(8,128)(2,1)} %bitcast.180), kind=kOutput, calls=%fused_computation.11 | convolution fusion | flops 1074003968 | bytes 9437184 | tf_op jit(solution)/shard_map/dot_general | solution.py:35
  353.1 95.9 %attention_backward.1 = (bf16[128,3072]{1,0:T(8,128)(2,1)}, f32[8,256]{1,0:T(8,128)}, bf16[256,2048]{1,0:T(8,128)(2,1)}, bf16[256,2048]{1,0:T(8,128)(2,1)}) custom-call(bf16[128,2048]{1,0:T(8,128)(2,1)} %fusion.5.refs_0_, bf16[128,2048]{1,0:T(8,128)(2,1)} %copy-done.3, bf16[2,2,2,128,1024]{4,3,2,1,0:T(8,128)(2,1)} %copy-done.1, f32[8,8,128]{2,1,0:T(8,128)} %copy-done.6, ...), custom_call_target="tpu_custom_call" | custom-call | flops 2684354560 | bytes 67108864 | tf_op jit(solution)/shard_map/attention_backward/pallas_call | solution.py:737
  449.9 11.5 %all-to-all-start = ((bf16[4,128,512]{2,1,0:T(8,128)(2,1)}), bf16[4,128,512]{2,1,0:T(8,128)(2,1)}, u32[]{:S(2)}, u32[]{:S(2)}) async-start(bf16[4,128,512]{2,1,0:T(8,128)(2,1)} %bitcast.148), calls=%async_computation | async-start | bytes 1048576 | tf_op jit(solution)/shard_map/all_to_all | solution.py:1499
  461.4 1.1 slice.67
  462.5 1.0 slice_bitcast_fusion.1
  464.3 1.0 maximum_bitcast_fusion
  465.6 11.1 %fusion.65 = f32[128,2048]{1,0:T(8,128)S(1)} fusion(bf16[128,3072]{1,0:T(8,128)(2,1)S(1)} %copy-done.30, bf16[2048,3072]{1,0:T(8,128)(2,1)} %bitcast.159), kind=kOutput, calls=%fused_computation.146 | convolution fusion | flops 1610612736 | bytes 14417920 | tf_op jit(solution)/shard_map/dot_general | solution.py:35
  476.8 2.2 fusion.22
  481.7 5.4 all-to-all-start.1
  487.8 1.0 copy.98
  488.8 1.0 copy.100
  489.8 1.0 copy.99
  492.0 1.0 copy-done.37
  492.9 1.6 convert_element_type.179
  494.5 1.6 convert_element_type.180
  497.9 1.2 fusion.39
  499.1 4.3 convolution_convert_fusion.1.refs_0_
  503.4 2.8 all-to-all-done.1
  506.2 5.5 convolution_convert_fusion.refs_1_
  511.6 50.8 %owner_sums.1 = (bf16[256,512]{1,0:T(8,128)(2,1)S(1)}, bf16[256,768]{1,0:T(8,128)(2,1)S(1)}, bf16[64,256]{1,0:T(8,128)(2,1)S(1)}, bf16[64,256]{1,0:T(8,128)(2,1)S(1)}, bf16[32,512]{1,0:T(8,128)(2,1)S(1)}) custom-call(bf16[2048,512]{1,0:T(8,128)(2,1)S(1)} %copy-done.2, bf16[2048,768]{1,0:T(8,128)(2,1)} %convolution_convert_fusion.refs_1_, ...), custom_call_target="tpu_custom_call" | custom-call | flops 4194304 | bytes 16777216 | tf_op jit(solution)/shard_map/owner_sums/pallas_call | solution.py:874
  564.7 1.4 convert_element_type.183
  567.6 1.4 convert_bitcast_fusion.2
  570.6 1.5 convert_bitcast_fusion
  572.1 1.8 copy.104
  (229 shorter events, 19.7 us)
Async XLA Ops:
  8.0 491.1 %all-gather.3.cloned.1.call-start = ((), (), s32[]{:S(2)}) async-start(), calls=%async_computation.3 | async-start | bytes 2621440 | tf_op jit(solution)/shard_map/all_gather | solution.py:51
  10.9 149.8 %copy-start.61 = (f32[128]{0:T(128)}, f32[128]{0:T(128)S(1)}, u32[]{:S(2)}) copy-start(f32[128]{0:T(128)S(1)} %fusion.55) | copy-start | bytes 1540
  11.5 109.1 %copy-start.17 = (bf16[1,128,2048]{2,1,0:T(8,128)(2,1)S(1)}, bf16[1,128,2048]{2,1,0:T(8,128)(2,1)}, u32[]{:S(2)}) copy-start(bf16[1,128,2048]{2,1,0:T(8,128)(2,1)} %param.23) | copy-start | bytes 1572868
  11.5 109.1 %copy-start.41 = (f32[2048]{0:T(1024)S(1)}, f32[2048]{0:T(1024)}, u32[]{:S(2)}) copy-start(f32[2048]{0:T(1024)} %param.38) | copy-start | bytes 24580
  122.0 6.7 %copy-start.49 = (bf16[128,64]{0,1:T(8,128)(2,1)}, bf16[128,64]{0,1:T(8,128)(2,1)S(1)}, u32[]{:S(2)}) copy-start(bf16[128,64]{0,1:T(8,128)(2,1)S(1)} %convolution_convert_fusion.7) | copy-start | bytes 49156
  122.0 6.6 %copy-start.9 = (s32[1,1024]{1,0:T(1,128)S(1)}, s32[1,1024]{1,0:T(1,128)}, u32[]{:S(2)}) copy-start(s32[1,1024]{1,0:T(1,128)} %key_ids.1) | copy-start | bytes 12292
  122.0 8.4 %copy-start.10 = (f32[256]{0:T(256)S(1)}, f32[256]{0:T(256)}, u32[]{:S(2)}) copy-start(f32[256]{0:T(256)} %param.44) | copy-start | bytes 3076
  122.1 8.4 %copy-start.11 = (f32[256]{0:T(256)S(1)}, f32[256]{0:T(256)}, u32[]{:S(2)}) copy-start(f32[256]{0:T(256)} %param.45) | copy-start | bytes 3076
  128.6 23.9 %copy-start = (f32[128,3072]{1,0:T(8,128)}, f32[128,3072]{1,0:T(8,128)S(1)}, u32[]{:S(2)}) copy-start(f32[128,3072]{1,0:T(8,128)S(1)} %fusion.44.raw.refs_4_) | copy-start | bytes 4718596
  130.1 30.2 %copy-start.70 = (f32[128]{0:T(128)}, f32[128]{0:T(128)S(1)}, u32[]{:S(2)}) copy-start(f32[128]{0:T(128)S(1)} %get-tuple-element.216) | copy-start | bytes 1540
  130.4 29.9 %copy-start.4 = (f32[128,128]{1,0:T(8,128)}, f32[128,128]{1,0:T(8,128)S(1)}, u32[]{:S(2)}) copy-start(f32[128,128]{1,0:T(8,128)S(1)} %get-tuple-element.212.sine_ref.refs_6_) | copy-start | bytes 196612
  130.4 29.8 %copy-start.5 = (f32[128,128]{1,0:T(8,128)}, f32[128,128]{1,0:T(8,128)S(1)}, u32[]{:S(2)}) copy-start(f32[128,128]{1,0:T(8,128)S(1)} %get-tuple-element.213.cosine_ref.refs_5_) | copy-start | bytes 196612
  155.2 5.5 copy-start.15
  155.2 5.5 copy-start.52
  155.2 5.5 copy-start.54
  162.1 83.4 %copy-start.79 = (f32[128]{0:T(128)}, f32[128]{0:T(128)S(1)}, u32[]{:S(2)}) copy-start(f32[128]{0:T(128)S(1)} %get-tuple-element.199) | copy-start | bytes 1540
  162.7 82.9 %copy-start.72 = (f32[128]{0:T(128)}, f32[128]{0:T(128)S(1)}, u32[]{:S(2)}) copy-start(f32[128]{0:T(128)S(1)} %get-tuple-element.215) | copy-start | bytes 1540
  163.6 83.3 %copy-start.46 = (f32[2048]{0:T(1024)S(1)}, f32[2048]{0:T(1024)}, u32[]{:S(2)}) copy-start(f32[2048]{0:T(1024)} %param.42) | copy-start | bytes 24580
  246.9 3.2 copy-start.39
  247.0 3.2 copy-start.44
  252.2 3.7 copy-start.34
  253.3 3.7 copy-start.42
  337.4 168.8 %all-gather.5.cloned.1.call-start = ((), (), s32[]{:S(2)}) async-start(), calls=%async_computation.4 | async-start | bytes 2621440 | tf_op jit(solution)/shard_map/all_gather | solution.py:51
  338.1 232.4 %reduce-scatter.2.cloned.1.call-start = ((), (), s32[]{:S(2)}) async-start(), calls=%async_computation.5 | async-start | bytes 9437184 | tf_op jit(solution)/shard_map/reduce_scatter | solution.py:55
  341.6 3.8 copy-start.71
  341.6 3.8 copy-start.78
  341.6 3.8 copy-start.16
  341.6 3.8 copy-start.22
  345.3 131.3 %copy-start.13 = (f32[128,2048]{1,0:T(8,128)}, f32[128,2048]{1,0:T(8,128)S(1)}, u32[]{:S(2)}) copy-start(f32[128,2048]{1,0:T(8,128)S(1)} %get-tuple-element.198) | copy-start | bytes 3145732
  345.9 119.3 %copy-start.25 = (bf16[128,2048]{1,0:T(8,128)(2,1)}, bf16[128,2048]{1,0:T(8,128)(2,1)S(1)}, u32[]{:S(2)}) copy-start(bf16[128,2048]{1,0:T(8,128)(2,1)S(1)} %get-tuple-element.203) | copy-start | bytes 1572868
  449.9 31.8 %all-to-all-start = ((bf16[4,128,512]{2,1,0:T(8,128)(2,1)}), bf16[4,128,512]{2,1,0:T(8,128)(2,1)}, u32[]{:S(2)}, u32[]{:S(2)}) async-start(bf16[4,128,512]{2,1,0:T(8,128)(2,1)} %bitcast.148), calls=%async_computation | async-start | bytes 1048576 | tf_op jit(solution)/shard_map/all_to_all | solution.py:1499
  465.6 11.1 %copy-start.18 = (bf16[1,128,2048]{2,1,0:T(8,128)(2,1)S(1)}, bf16[1,128,2048]{2,1,0:T(8,128)(2,1)}, u32[]{:S(2)}) copy-start(bf16[1,128,2048]{2,1,0:T(8,128)(2,1)} %param.23) | copy-start | bytes 1572868
  465.6 11.1 %copy-start.40 = (bf16[4,512,64]{2,1,0:T(8,128)(2,1)S(1)}, bf16[4,512,64]{2,1,0:T(8,128)(2,1)}, u32[]{:S(2)}) copy-start(bf16[4,512,64]{2,1,0:T(8,128)(2,1)} %get-tuple-element.57) | copy-start | bytes 786436
  465.6 11.1 %copy-start.62 = (f32[128]{0:T(128)S(1)}, f32[128]{0:T(128)}, u32[]{:S(2)}) copy-start(f32[128]{0:T(128)} %copy-done.61) | copy-start | bytes 1540
  476.7 2.7 copy-start.26
  476.7 2.7 copy-start.50
  476.8 3.0 copy-start.24
  476.8 3.9 copy-start.35
  476.8 3.9 copy-start.45
  481.1 6.0 %copy-start.64 = (bf16[8,256]{1,0:T(8,128)(2,1)S(1)}, bf16[8,256]{1,0:T(8,128)(2,1)}, u32[]{:S(2)}) copy-start(bf16[8,256]{1,0:T(8,128)(2,1)} %convert.49) | copy-start | bytes 12292
  481.2 6.0 %copy-start.60 = (bf16[2048]{0:T(1024)(128)(2,1)S(1)}, bf16[2048]{0:T(1024)(128)(2,1)}, u32[]{:S(2)}) copy-start(bf16[2048]{0:T(1024)(128)(2,1)} %get-tuple-element.184) | copy-start | bytes 12292
  481.2 6.0 %copy-start.59 = (bf16[2048]{0:T(1024)(128)(2,1)S(1)}, bf16[2048]{0:T(1024)(128)(2,1)}, u32[]{:S(2)}) copy-start(bf16[2048]{0:T(1024)(128)(2,1)} %get-tuple-element.187) | copy-start | bytes 12292
  481.2 6.0 %copy-start.58 = (bf16[2048]{0:T(1024)(128)(2,1)S(1)}, bf16[2048]{0:T(1024)(128)(2,1)}, u32[]{:S(2)}) copy-start(bf16[2048]{0:T(1024)(128)(2,1)} %get-tuple-element.178) | copy-start | bytes 12292
  481.2 6.0 %copy-start.57 = (bf16[2048]{0:T(1024)(128)(2,1)S(1)}, bf16[2048]{0:T(1024)(128)(2,1)}, u32[]{:S(2)}) copy-start(bf16[2048]{0:T(1024)(128)(2,1)} %get-tuple-element.176) | copy-start | bytes 12292
  481.2 6.1 %copy-start.56 = (bf16[2048]{0:T(1024)(128)(2,1)S(1)}, bf16[2048]{0:T(1024)(128)(2,1)}, u32[]{:S(2)}) copy-start(bf16[2048]{0:T(1024)(128)(2,1)} %get-tuple-element.174) | copy-start | bytes 12292
  481.7 8.1 %copy-start.38 = (bf16[2048,64]{0,1:T(8,128)(2,1)S(1)}, bf16[2048,64]{0,1:T(8,128)(2,1)}, u32[]{:S(2)}) copy-start(bf16[2048,64]{0,1:T(8,128)(2,1)} %convolution_convert_fusion.5) | copy-start | bytes 786436
  481.7 24.5 %all-to-all-start.1 = ((bf16[4,128,768]{2,1,0:T(8,128)(2,1)}), bf16[4,128,768]{2,1,0:T(8,128)(2,1)}, u32[]{:S(2)}, u32[]{:S(2)}) async-start(bf16[4,128,768]{2,1,0:T(8,128)(2,1)} %maximum_bitcast_fusion), calls=%async_computation.1 | async-start | bytes 1572864 | tf_op jit(solution)/shard_map/all_to_all | solution.py:1499
  506.2 5.5 copy-start.2
  (38 other events, 68.5 us)
Sparse Core Ops, SparseCore 0:
  337.5 52.7 all-gather.2
  392.4 44.6 all-gather.4
Sparse Core Ops, SparseCore 1:
  449.1 82.5 reduce-scatter.1

commit v6 on v5

--- a/solution.py
+++ b/solution.py
@@ -117,16 +117,14 @@
     )
 
 
-def weight_gather_kernel(ctx_count, fsdp_count, members, lines, *refs):
+def weight_gather_kernel(ctx_count, fsdp_count, members, spread, *refs):
     sets = len(members)
     own_count = sum(members)
-    own, line_own = refs[:own_count], refs[own_count : own_count + lines]
-    rest = refs[own_count + lines :]
-    outs, line_outs = rest[:sets], rest[sets : sets + lines]
-    rest = rest[sets + lines :]
-    passing, pieces = rest[: own_count + lines], rest[own_count + lines : own_count + lines + sets]
+    own, outs = refs[:own_count], refs[own_count : own_count + sets]
+    rest = refs[own_count + sets :]
+    passing, pieces = rest[:own_count], rest[own_count : own_count + sets]
     own_sem, line_send, line_recv, send_sem, recv_sem, core_send, core_recv = rest[
-        own_count + lines + sets :
+        own_count + sets :
     ]
     position = ctx_position(ctx_count)
     bits, place, along, mine, partners, _ = position
@@ -147,7 +145,7 @@
         load.start()
     loads = [
         pltpu.make_async_copy(source, passing[n], own_sem.at[1, n])
-        for n, source in enumerate(own + line_own)
+        for n, source in enumerate(own)
     ]
     for load in loads:
         load.start()
@@ -158,10 +156,7 @@
 
     def line_copy(i, way, step, origin):
         toward = along + 1 if way == 0 else along - 1
-        if i < sets:
-            first, target = pieces[i], outs[i].at[(origin,) + here]
-        else:
-            first, target = line_own[i - sets], line_outs[i - sets].at[origin]
+        first, target = pieces[i], outs[i].at[(origin,) + here]
         return pltpu.make_async_remote_copy(
             src_ref=first if step == 1 else target,
             dst_ref=target,
@@ -196,11 +191,8 @@
     stores = []
     for n, load in enumerate(loads):
         load.wait()
-        if n < own_count:
-            i, at = columns[n]
-            target = outs[i].at[(along,) + (slice(None),) * (bits + 1) + (at,)]
-        else:
-            target = line_outs[n - own_count].at[along]
+        i, at = columns[n]
+        target = outs[i].at[(along,) + (slice(None),) * (bits + 1) + (at,)]
         stores.append(pltpu.make_async_copy(passing[n], target, own_sem.at[2, n]))
         stores[-1].start()
 
@@ -227,7 +219,7 @@
             each(comes(way, step), landed)
         if step < steps:
             forward(i, step + 1)
-        if i >= sets:
+        if i >= spread:
             return
         for way in range(2):
 
@@ -238,7 +230,7 @@
             each(comes(way, step), begin)
 
     def advance(i, step, stage):
-        if i >= sets:
+        if i >= spread:
             return
         for way in range(2):
 
@@ -253,12 +245,9 @@
 
             each(comes(way, step), proceed)
 
-    order = [(i, step) for i in range(sets + lines) for step in range(1, steps + 1)]
+    order = [(i, step) for i in range(sets) for step in range(1, steps + 1)]
     for tick in range(len(order) + bits - 1):
         if tick < len(order):
-            if order[tick] == (sets - 1, 1):
-                for i in range(sets, sets + lines):
-                    forward(i, 1)
             arrive(*order[tick])
         for stage in range(bits - 1):
             at = tick - 1 - stage
@@ -279,11 +268,11 @@
                 core_copy(i, way, step).wait()
 
             each(goes(way, step), leave)
-            if i < sets:
+            if i < spread:
                 each(comes(way, step), finish)
 
 
-def weight_gather(own, lines):
+def weight_gather(own, spread):
     ctx_count = lax.axis_size("ctx")
     fsdp_count = lax.axis_size("fsdp")
     bits = ctx_count.bit_length() - 1
@@ -294,33 +283,126 @@
     flat = [w.reshape(cut + (w.shape[0] // ctx_count, w.shape[1])) for group in own for w in group]
     pieces = [(g[0].shape[0] // ctx_count, sum(w.shape[1] for w in g)) for g in own]
     out_shapes = [(fsdp_count,) + cut + p for p in pieces]
-    out_shapes += [(fsdp_count,) + w.shape for w in lines]
     total = sum(rows * columns for rows, columns in pieces) * ctx_count * fsdp_count
     outs = pl.pallas_call(
         functools.partial(
-            weight_gather_kernel, ctx_count, fsdp_count, [len(g) for g in own], len(lines)
+            weight_gather_kernel, ctx_count, fsdp_count, [len(g) for g in own], spread
         ),
         out_shape=[jax.ShapeDtypeStruct(s, low) for s in out_shapes],
-        in_specs=[pl.BlockSpec(memory_space=pltpu.HBM)] * (len(flat) + len(lines)),
+        in_specs=[pl.BlockSpec(memory_space=pltpu.HBM)] * len(flat),
         out_specs=[pl.BlockSpec(memory_space=pltpu.HBM)] * len(out_shapes),
-        scratch_shapes=[pltpu.VMEM(w.shape, low) for w in flat + list(lines)]
+        scratch_shapes=[pltpu.VMEM(w.shape, low) for w in flat]
         + [pltpu.VMEM(p, low) for p in pieces]
         + [
-            pltpu.SemaphoreType.DMA((3, len(flat) + len(lines))),
-            pltpu.SemaphoreType.DMA((sets + len(lines), 2, steps)),
-            pltpu.SemaphoreType.DMA((sets + len(lines), 2, steps)),
-            pltpu.SemaphoreType.DMA((sets, 2, steps, 2, bits - 1)),
-            pltpu.SemaphoreType.DMA((sets, 2, steps, 2, bits - 1)),
+            pltpu.SemaphoreType.DMA((3, len(flat))),
             pltpu.SemaphoreType.DMA((sets, 2, steps)),
             pltpu.SemaphoreType.DMA((sets, 2, steps)),
+            pltpu.SemaphoreType.DMA((spread, 2, steps, 2, bits - 1)),
+            pltpu.SemaphoreType.DMA((spread, 2, steps, 2, bits - 1)),
+            pltpu.SemaphoreType.DMA((spread, 2, steps)),
+            pltpu.SemaphoreType.DMA((spread, 2, steps)),
         ],
         compiler_params=pltpu.CompilerParams(
             collective_id=1, has_side_effects=True, vmem_limit_bytes=60 << 20
         ),
         cost_estimate=pl.CostEstimate(flops=0, bytes_accessed=4 * total, transcendentals=0),
         name="weight_gather",
-    )(*flat, *lines)
-    return [o.reshape(-1, o.shape[-1]) for o in outs[:sets]] + list(outs[sets:])
+    )(*flat)
+    return [o.reshape(-1, o.shape[-1]) for o in outs[:spread]] + list(outs[spread:])
+
+
+def line_comes(along, count, way, step):
+    return along >= step if way == 0 else along + step < count
+
+
+def line_goes(along, count, way, step):
+    if way == 0:
+        return (along + 1 < count) & (along >= step - 1)
+    return (along >= 1) & (along + step - 1 < count)
+
+
+def line_origin(along, way, step):
+    return along - step if way == 0 else along + step
+
+
+class LineGather:
+    def __init__(self, count, owns, outs, passing, own_sems, send_sems, recv_sems):
+        self.count, self.steps = count, count - 1
+        self.owns, self.outs, self.passing = owns, outs, passing
+        self.own_sems, self.send_sems, self.recv_sems = own_sems, send_sems, recv_sems
+        self.place = lax.axis_index("ctx")
+        self.along = lax.axis_index("fsdp")
+        self.done = 0
+
+    def partners(self):
+        return [(self.place, lax.rem(self.along + d, self.count)) for d in sorted({1, self.steps})]
+
+    def own_copies(self, n):
+        return (
+            pltpu.make_async_copy(self.owns[n], self.passing[n], self.own_sems.at[0, n]),
+            pltpu.make_async_copy(self.passing[n], self.outs[n].at[self.along], self.own_sems.at[1, n]),
+        )
+
+    def copies(self, way, step, origin):
+        toward = self.along + 1 if way == 0 else self.along - 1
+        return [
+            pltpu.make_async_remote_copy(
+                src_ref=self.owns[n] if step == 1 else self.outs[n].at[origin],
+                dst_ref=self.outs[n].at[origin],
+                send_sem=self.send_sems.at[n, way, step - 1],
+                recv_sem=self.recv_sems.at[n, way, step - 1],
+                device_id=(self.place, toward),
+                device_id_type=MESH,
+            )
+            for n in range(len(self.owns))
+        ]
+
+    def forward(self, step):
+        for way in range(2):
+
+            def go(way=way):
+                for copy in self.copies(way, step, line_origin(self.along, way, step - 1)):
+                    copy.start()
+
+            pl.when(line_goes(self.along, self.count, way, step))(go)
+
+    def load(self):
+        for n in range(len(self.owns)):
+            self.own_copies(n)[0].start()
+
+    def store(self):
+        for n in range(len(self.owns)):
+            self.own_copies(n)[0].wait()
+            self.own_copies(n)[1].start()
+
+    def arrive(self):
+        if self.done == self.steps:
+            return
+        self.done += 1
+        step = self.done
+        for way in range(2):
+
+            def land(way=way):
+                for copy in self.copies(way, step, line_origin(self.along, way, step)):
+                    copy.wait_recv()
+
+            pl.when(line_comes(self.along, self.count, way, step))(land)
+        if step < self.steps:
+            self.forward(step + 1)
+
+    def finish(self):
+        while self.done < self.steps:
+            self.arrive()
+        for n in range(len(self.owns)):
+            self.own_copies(n)[1].wait()
+        for step in range(1, self.steps + 1):
+            for way in range(2):
+
+                def leave(way=way, step=step):
+                    for copy in self.copies(way, step, line_origin(self.along, way, step - 1)):
+                        copy.wait_send()
+
+                pl.when(line_goes(self.along, self.count, way, step))(leave)
 
 
 class Halving:
@@ -439,6 +521,7 @@
 
 def attention_forward_kernel(
     ctx_count,
+    lines,
     raw,
     cosine_ref,
     sine_ref,
@@ -446,36 +529,87 @@
     key_gain,
     row_ids,
     key_ids,
-    kv,
-    query_low,
-    attended_low,
-    log_totals,
-    bias,
-    send_sem,
-    recv_sem,
-    core_send,
-    core_recv,
+    _,
+    *refs,
 ):
+    line_owns, refs = refs[:lines], refs[lines:]
+    kv, query_low, attended_low, log_totals, weights_out = refs[:5]
+    line_outs, refs = refs[5 : 5 + lines], refs[5 + lines :]
+    bias, send_sem, recv_sem, core_send, core_recv, weight_sems, weight_core_sems = refs[:7]
+    line = LineGather(
+        weights_out.shape[0], line_owns, line_outs, refs[7 : 7 + lines], *refs[7 + lines :]
+    )
+    line.load()
     position = ctx_position(ctx_count)
-    bits, place, _, mine, partners, _ = position
+    bits, place, along, mine, partners, _ = position
+    count = weights_out.shape[0]
+    units = [(way, step) for step in range(1, count) for way in range(2)]
+
+    def weight_copies(way, step, stage):
+        lead = (line_origin(along, way, step),)
+        at = (way, step - 1)
+        return [
+            spread_copy(
+                weights_out,
+                lead,
+                half,
+                stage,
+                position,
+                weight_sems.at[(0,) + at],
+                weight_sems.at[(1,) + at],
+            )
+            for half in range(2)
+        ]
+
+    def weight_core_copy(way, step):
+        at = (way, step - 1)
+        return sibling_copy(
+            weights_out,
+            (line_origin(along, way, step),),
+            position,
+            weight_core_sems.at[(0,) + at],
+            weight_core_sems.at[(1,) + at],
+        )
+
+    def each_unit(action):
+        for way, step in units:
+            pl.when(line_comes(along, count, way, step))(functools.partial(action, way, step))
+
+    def start_weights(stage):
+        def action(way, step):
+            for copy in weight_copies(way, step, stage):
+                copy.start()
+
+        each_unit(action)
+
+    def land_weights(stage):
+        def action(way, step):
+            for copy in weight_copies(way, step, stage):
+                copy.wait_recv()
+
+        each_unit(action)
+
     rows = raw.shape[0]
     groups = HEADS // KV_HEADS
     length = ctx_count * rows
     here = held_index(mine, (), bits)
     cosine, sine_part = cosine_ref[...], sine_ref[...]
+    partner_barrier(partners + line.partners())
+    start_weights(0)
+    line.forward(1)
     for k in range(KV_HEADS):
         unit, _ = unit_rows(raw[:, pl.ds((HEADS + k) * HD, HD)])
         key = turned(unit * key_gain[...], cosine, sine_part)
         kv[here + (slice(None), pl.ds(k * HD, HD))] = key.astype(kv.dtype)
         value, _ = unit_rows(raw[:, pl.ds((HEADS + KV_HEADS + k) * HD, HD)])
         kv[here + (slice(None), pl.ds((KV_HEADS + k) * HD, HD))] = value.astype(kv.dtype)
-    partner_barrier(partners)
 
     def copies_of(stage):
         return [spread_copy(kv, (), h, stage, position, send_sem, recv_sem) for h in range(2)]
 
     for copy in copies_of(0):
         copy.start()
+    line.store()
     allowed = (row_ids[...] == key_ids[...]) & (
         lax.broadcasted_iota(jnp.int32, (rows, length), 1)
         <= lax.broadcasted_iota(jnp.int32, (rows, length), 0) + place * rows
@@ -494,6 +628,9 @@
             copy.wait()
         for copy in copies_of(stage):
             copy.start()
+        land_weights(stage - 1)
+        start_weights(stage)
+        line.arrive()
     for copy in copies_of(bits - 2):
         copy.wait()
     last = sibling_copy(kv, (), position, core_send, core_recv)
@@ -517,34 +654,60 @@
             return carry
 
         lax.fori_loop(0, groups, one_head, 0)
-
-
-def attention_forward(raw, cosine, sine_part, query_gain, key_gain, row_ids, key_ids):
+        line.arrive()
+        if k == KV_HEADS - 2:
+            land_weights(bits - 2)
+            each_unit(lambda way, step: weight_core_copy(way, step).start())
+
+    def finish(way, step):
+        for stage in range(bits - 1):
+            for copy in weight_copies(way, step, stage):
+                copy.wait_send()
+        weight_core_copy(way, step).wait()
+
+    each_unit(finish)
+    line.finish()
+
+
+def attention_forward(raw, cosine, sine_part, query_gain, key_gain, row_ids, key_ids, weights, lines):
     ctx_count = lax.axis_size("ctx")
+    steps = lax.axis_size("fsdp") - 1
+    hbm = pl.BlockSpec(memory_space=pltpu.HBM)
     bits = ctx_count.bit_length() - 1
     rows = raw.shape[0]
     length = ctx_count * rows
     low = jnp.bfloat16
     vmem = pl.BlockSpec(memory_space=pltpu.VMEM)
     return pl.pallas_call(
-        functools.partial(attention_forward_kernel, ctx_count),
+        functools.partial(attention_forward_kernel, ctx_count, len(lines)),
         out_shape=[
             jax.ShapeDtypeStruct((2,) * bits + (rows, 2 * KV_HEADS * HD), low),
             jax.ShapeDtypeStruct((rows, HEADS * HD), low),
             jax.ShapeDtypeStruct((rows, HEADS * HD), low),
             jax.ShapeDtypeStruct((HEADS, 8, rows), jnp.float32),
-        ],
-        in_specs=[vmem] * 7,
-        out_specs=[vmem] * 4,
+            jax.ShapeDtypeStruct(weights.shape, low),
+        ]
+        + [jax.ShapeDtypeStruct((steps + 1,) + w.shape, low) for w in lines],
+        in_specs=[vmem] * 7 + [hbm] * (1 + len(lines)),
+        out_specs=[vmem] * 4 + [hbm] * (1 + len(lines)),
+        input_output_aliases={7: 4},
         scratch_shapes=[
             pltpu.VMEM((rows, length), jnp.float32),
             pltpu.SemaphoreType.DMA((2, bits - 1)),
             pltpu.SemaphoreType.DMA((2, bits - 1)),
             pltpu.SemaphoreType.DMA,
             pltpu.SemaphoreType.DMA,
+            pltpu.SemaphoreType.DMA((2, 2, steps, 2, bits - 1)),
+            pltpu.SemaphoreType.DMA((2, 2, steps)),
+        ]
+        + [pltpu.VMEM(w.shape, low) for w in lines]
+        + [
+            pltpu.SemaphoreType.DMA((2, len(lines))),
+            pltpu.SemaphoreType.DMA((len(lines), 2, steps)),
+            pltpu.SemaphoreType.DMA((len(lines), 2, steps)),
         ],
         compiler_params=pltpu.CompilerParams(
-            collective_id=2, has_side_effects=True, vmem_limit_bytes=40 << 20
+            collective_id=2, has_side_effects=True, vmem_limit_bytes=56 << 20
         ),
         cost_estimate=pl.CostEstimate(
             flops=4 * HEADS * HD * rows * length,
@@ -552,12 +715,21 @@
             transcendentals=HEADS * rows * length,
         ),
         name="attention_forward",
-    )(raw, cosine, sine_part, query_gain[None], key_gain[None], row_ids[:, None], key_ids[None])
-
-
-def attention_backward_kernel(ctx_count, extra, *refs):
+    )(
+        raw,
+        cosine,
+        sine_part,
+        query_gain[None],
+        key_gain[None],
+        row_ids[:, None],
+        key_ids[None],
+        weights,
+        *lines,
+    )
+
+
+def attention_backward_kernel(ctx_count, fsdp_count, extra, *refs):
     (
-        grads,
         query_low,
         kv,
         log_totals,
@@ -568,19 +740,55 @@
         key_gain,
         row_ids,
         key_ids,
-    ) = refs[:11]
+        row_grads,
+        out_weight,
+        qkv_weight,
+    ) = refs[:13]
     many = len(extra)
-    extra_in = refs[11 : 11 + many]
-    back, gain_grads = refs[11 + many : 13 + many]
-    extra_out = refs[13 + many : 13 + 2 * many]
-    rest = refs[13 + 2 * many :]
+    extra_in = refs[13 : 13 + many]
+    back, gain_grads, column_grads, normed_grads = refs[13 + many : 17 + many]
+    extra_out = refs[17 + many : 17 + 2 * many]
+    rest = refs[17 + 2 * many :]
     bias, score_grads, weights_low, query_grads, kv_grads = rest[:5]
     kv_parts = rest[5:11]
     extra_parts = [rest[11 + 8 * i : 19 + 8 * i] for i in range(many)]
     position = ctx_position(ctx_count)
-    bits, place, _, mine, partners, _ = position
+    bits, place, along, mine, partners, _ = position
     pairs = ctx_count // 2
     rows = raw.shape[0]
+    column_send, column_recv, grads, streamed, stream_sem = rest[11 + 8 * many :]
+    tile = streamed.shape[1]
+
+    def stream(weight, columns, use):
+        tiles = weight.shape[0] // tile
+
+        def copy(t):
+            return pltpu.make_async_copy(
+                weight.at[pl.ds(t * tile, tile), pl.ds(0, columns)],
+                streamed.at[t % 2, :, pl.ds(0, columns)],
+                stream_sem.at[t % 2],
+            )
+
+        copy(0).start()
+        for t in range(tiles):
+            if t + 1 < tiles:
+                copy(t + 1).start()
+            copy(t).wait()
+            use(pl.ds(t * tile, tile), streamed[t % 2, :, :columns])
+
+    peers = [lax.rem(along + d, fsdp_count) for d in range(1, fsdp_count)]
+    wide = column_grads.shape[-1]
+    column_copies = [
+        pltpu.make_async_remote_copy(
+            src_ref=row_grads.at[:, pl.ds(pl.multiple_of(peer * wide, wide), wide)],
+            dst_ref=column_grads.at[along],
+            send_sem=column_send.at[d],
+            recv_sem=column_recv.at[d],
+            device_id=(place, peer),
+            device_id_type=MESH,
+        )
+        for d, peer in enumerate(peers)
+    ]
     groups = HEADS // KV_HEADS
     length = ctx_count * rows
     low = jnp.bfloat16
@@ -624,9 +832,17 @@
             copies[-1].start()
         own_copies.append(copies)
 
-    partner_barrier(partners)
+    partner_barrier(partners + [(place, peer) for peer in peers])
     for one in sums:
         one.start_first()
+    for copy in column_copies:
+        copy.start()
+    column_grads[along] = row_grads[:, pl.ds(pl.multiple_of(along * wide, wide), wide)]
+
+    def attended_tile(columns, weight):
+        grads[:, columns] = across(row_grads[...], weight).astype(low)
+
+    stream(out_weight, row_grads.shape[1], attended_tile)
 
     def open_extra(i):
         for b in range(pairs):
@@ -675,6 +891,11 @@
     kv_sum.start(0)
     for i in range(KV_HEADS, many):
         open_extra(i)
+
+    def step_extra(i, stage):
+        sums[i].end(stage - 1)
+        sums[i].start(stage)
+
     cosine, sine_part = cosine_ref[...], sine_ref[...]
 
     def one_query(h, gain_grad):
@@ -688,6 +909,8 @@
         kv_sum.end(stage - 1)
         kv_sum.start(stage)
     kv_sum.end(bits - 2)
+    for i in range(many):
+        step_extra(i, 1)
     summed = kv_sum.mine_now()
     key_gain_grad = jnp.zeros((1, HD), jnp.float32)
     for k in range(KV_HEADS):
@@ -702,18 +925,39 @@
         pulled, _ = unit_rows_pull(raw[:, at], grad, 1.0)
         back[:, at] = pulled.astype(low)
     gain_grads[1:2] = key_gain_grad
-    for stage in range(1, bits - 1):
-        for one in sums:
-            one.end(stage - 1)
-            one.start(stage)
+
+    def normed_tile(columns, weight):
+        normed_grads[:, columns] = across(back[...], weight)
+
+    stream(qkv_weight, back.shape[1], normed_tile)
+    for stage in range(2, bits - 1):
+        for i in range(many):
+            step_extra(i, stage)
+    for copy in column_copies:
+        copy.wait()
     for i in range(many):
         sums[i].end(bits - 2)
         extra_out[i][...] = sums[i].mine_now()[...]
 
 
 def attention_backward(
-    grads, query_low, kv, log_totals, raw, cosine, sine_part, query_gain, key_gain, row_ids, key_ids, extra
+    query_low,
+    kv,
+    log_totals,
+    raw,
+    cosine,
+    sine_part,
+    query_gain,
+    key_gain,
+    row_ids,
+    key_ids,
+    row_grads,
+    out_weight,
+    qkv_weight,
+    extra,
 ):
+    fsdp_count = lax.axis_size("fsdp")
+    hbm = pl.BlockSpec(memory_space=pltpu.HBM)
     ctx_count = lax.axis_size("ctx")
     rows = raw.shape[0]
     length = ctx_count * rows
@@ -734,15 +978,24 @@
         parts = halving_scratch(ctx_count, *shape)
         scratch += [pltpu.VMEM((pairs,) + shape, low)] + parts[:2]
         scratch += [pltpu.SemaphoreType.DMA((pairs,))] + parts[2:]
+    scratch += [pltpu.SemaphoreType.DMA((fsdp_count - 1,))] * 2
+    scratch += [
+        pltpu.VMEM((rows, HEADS * HD), low),
+        pltpu.VMEM((2, FF_TILE, qkv_weight.shape[1]), low),
+        pltpu.SemaphoreType.DMA((2,)),
+    ]
+    columns_shape = (fsdp_count, rows, row_grads.shape[1] // fsdp_count)
     outs = pl.pallas_call(
-        functools.partial(attention_backward_kernel, ctx_count, shapes),
+        functools.partial(attention_backward_kernel, ctx_count, fsdp_count, shapes),
         out_shape=[
             jax.ShapeDtypeStruct(raw.shape, low),
             jax.ShapeDtypeStruct((8, HD), jnp.float32),
+            jax.ShapeDtypeStruct(columns_shape, low),
+            jax.ShapeDtypeStruct((rows, qkv_weight.shape[0]), jnp.float32),
         ]
         + [jax.ShapeDtypeStruct(s, low) for s in shapes],
-        in_specs=[vmem] * 11 + [pl.BlockSpec(memory_space=pl.ANY)] * len(extra),
-        out_specs=[vmem] * (2 + len(extra)),
+        in_specs=[vmem] * 11 + [hbm] * (2 + len(extra)),
+        out_specs=[vmem] * (4 + len(extra)),
         scratch_shapes=scratch,
         compiler_params=pltpu.CompilerParams(
             collective_id=3, has_side_effects=True, vmem_limit_bytes=60 << 20
@@ -754,7 +1007,6 @@
         ),
         name="attention_backward",
     )(
-        grads,
         query_low,
         kv,
         log_totals,
@@ -765,9 +1017,13 @@
         key_gain[None],
         row_ids[None],
         key_ids[:, None],
+        row_grads,
+        out_weight,
+        qkv_weight,
         *extra,
     )
-    return outs[0], outs[1][0], outs[1][1], outs[2:]
+    columns = outs[2].reshape(-1, outs[2].shape[-1])
+    return outs[0], outs[1][0], outs[1][1], columns, outs[3], outs[4:]
 
 
 def owner_sum_kernel(ctx_count, fsdp_count, shapes, shared, *refs):
@@ -883,20 +1139,6 @@
         cost_estimate=pl.CostEstimate(flops=total, bytes_accessed=4 * total, transcendentals=0),
         name="owner_sums",
     )(*arrays)
-
-
-def line_comes(along, count, way, step):
-    return along >= step if way == 0 else along + step < count
-
-
-def line_goes(along, count, way, step):
-    if way == 0:
-        return (along + 1 < count) & (along >= step - 1)
-    return (along >= 1) & (along + step - 1 < count)
-
-
-def line_origin(along, way, step):
-    return along - step if way == 0 else along + step
 
 
 class LineExchange:
@@ -1388,31 +1630,39 @@
     piece = width // count
 
     qkv_width = query_width + 2 * kv_width
-    full_qkv, full_second, full_left, full_right, full_side_out = weight_gather(
-        [[query_weight, key_weight, value_weight], [out_weight, side_gate]],
+    full_qkv, second_line = weight_gather(
+        [[query_weight, key_weight, value_weight], [out_weight, side_gate]], 1
+    )
+
+    normed, input_pull = jax.vjp(rms_norm, inputs, input_gain)
+    normed_low = normed.astype(low)
+    qkv_raw = forward_product(normed_low, full_qkv)
+    frequency = jnp.exp(
+        jnp.arange(HD // 2).astype(jnp.float32) * (-2.0 * math.log(rope_theta) / HD)
+    )
+    angles = query_pos.astype(jnp.float32)[:, None] * frequency[None, :]
+    cosine, sine_part = jnp.cos(angles), jnp.sin(angles)
+    query_ids = lax.dynamic_slice_in_dim(sequence_ids, ctx_place * rows_here, rows_here)
+    kv_all, query_low, attended_low, log_totals, full_second, *full_small = attention_forward(
+        qkv_raw,
+        cosine,
+        sine_part,
+        query_gain,
+        key_gain,
+        query_ids,
+        sequence_ids,
+        second_line,
         [left_weight, right_weight, side_out],
     )
-    full_out = full_second[:, :width]
-    full_side_gate = full_second[:, width:]
+    full_left, full_right, full_side_out = full_small
     full_left = full_left.reshape(width, rank)
     full_right = full_right.transpose(1, 0, 2).reshape(rank, width)
     full_side_out = full_side_out.reshape(side, width)
-
-    normed, input_pull = jax.vjp(rms_norm, inputs, input_gain)
-    normed_low = normed.astype(low)
-    qkv_raw = forward_product(normed_low, full_qkv)
+    full_second = full_second.reshape(width, -1)
+    full_out = full_second[:, :width]
+    full_side_gate = full_second[:, width:]
     left_low = forward_product(normed_low, full_left).astype(low)
     right_out = forward_product(left_low, full_right)
-
-    frequency = jnp.exp(
-        jnp.arange(HD // 2).astype(jnp.float32) * (-2.0 * math.log(rope_theta) / HD)
-    )
-    angles = query_pos.astype(jnp.float32)[:, None] * frequency[None, :]
-    cosine, sine_part = jnp.cos(angles), jnp.sin(angles)
-    query_ids = lax.dynamic_slice_in_dim(sequence_ids, ctx_place * rows_here, rows_here)
-    kv_all, query_low, attended_low, log_totals = attention_forward(
-        qkv_raw, cosine, sine_part, query_gain, key_gain, query_ids, sequence_ids
-    )
     attn_raw = forward_product(attended_low, full_out)
 
     def mix_piece(x, normed_in, attn_in, right_in, gain_one, gain_two, gain_three):
@@ -1467,13 +1717,18 @@
         pre_gain_grad,
     ) = mix_pull((mixed_grad_one, ffn_in_grad))
     attn_grad_low = attn_raw_grad.astype(low)
-    attended_grad_low = across(attn_grad_low, full_out).astype(low)
     right_grad_low = right_out_grad.astype(low)
     right_weight_grad = over_rows(right_grad_low, left_low)
     left_grad_low = across(right_grad_low, full_right).astype(low)
     left_weight_grad = over_rows(normed_low, left_grad_low)
-    qkv_back_low, query_gain_grad, key_gain_grad, ffn_sums = attention_backward(
-        attended_grad_low,
+    (
+        qkv_back_low,
+        query_gain_grad,
+        key_gain_grad,
+        out_columns,
+        normed_grad_two,
+        ffn_sums,
+    ) = attention_backward(
         query_low,
         kv_all,
         log_totals,
@@ -1484,11 +1739,14 @@
         key_gain,
         query_ids,
         sequence_ids,
+        attn_grad_low,
+        full_second,
+        full_qkv,
         [gate_weight_grad, up_weight_grad],
     )
     down_low, qkv_back_low = lax.optimization_barrier((down_weight_grad, qkv_back_low))
     down_weight_grad = scatter_sum(down_low, "ctx")
-    normed_grad_two = across(qkv_back_low, full_qkv) + across(left_grad_low, full_left)
+    normed_grad_two = normed_grad_two + across(left_grad_low, full_left)
     inputs_grad_two, input_gain_grad = input_pull(normed_grad_one + normed_grad_two)
     block_out = result.astype(low)[None]
     tokens_grad = (inputs_grad_one + inputs_grad_two).astype(low)[None]
@@ -1498,7 +1756,6 @@
         parts = x.reshape(rows_here, fsdp_count, -1).transpose(1, 0, 2)
         return lax.all_to_all(parts, "fsdp", 0, 0, tiled=True).reshape(fsdp_count * rows_here, -1)
 
-    out_columns = columns_to_owner(attn_grad_low)
     out_weight_grad = over_rows(attended_all, out_columns)
     qkv_parts = jnp.concatenate(
         [

time: 587 us -> 566 us (0.964)
  matrix products: 52.5 us -> 36 us
  starting transfers between devices: 17.1 us -> 4.56 us
  Pallas kernels: 439 us -> 447 us
    pallas_call x2, Pallas kernels: 118 us -> 160 us  [the longest x1 106 us: attention_backward(): pl.pallas_call(functools.partial(attention_backward_kernel, ctx_count, fs...]
    pallas_call x1, Pallas kernels: 108 us -> 68 us  [weight_gather(): pl.pallas_call(functools.partial(weight_gather_kernel, ctx_count, fsdp_co...]
    dot_general x6 -> x4, matrix products: 24.5 us -> 7.34 us  [across(): lax.dot_general(a, b, (((1,), (1,)), ((), ())), preferred_element_type=jn...]
    all_to_all x2 -> x1, starting transfers between devices: 16.9 us -> 4.44 us  [columns_to_owner(): lax.all_to_all(parts, 'fsdp', 0, 0, tiled=True)]
    pallas_call x1, Pallas kernels: 50.8 us -> 57.1 us  [owner_sums(): pl.pallas_call(functools.partial(owner_sum_kernel, ctx_count, fsdp_count,...]
  transfers between devices with their start and end apart: 5 -> 4, of which waited for: 1 -> 0; matrix products, arithmetic and copies ran while one was open for 11% -> 9% of each run, Pallas kernels for 25% -> 29%
where the time goes in v6:
time: 566 us; the launch traced here: 561 us
  Pallas kernels  447 us (79%)
  matrix products  36 us (6%)
  other arithmetic  32.7 us (6%)
  local copies, waits for them, and re-layouts  23.4 us (4%)
  between operations  16.9 us (3%)
    pallas_call x1, Pallas kernels, attention_backward(): pl.pallas_call(functools.partial(attention_backward_kernel, ctx_count, fs...  106 us
    pallas_call x1, Pallas kernels, feed_forward(): pl.pallas_call(functools.partial(feed_forward_kernel, count), out_shape=[...  81.6 us
    pallas_call x1, Pallas kernels, feed_forward_backward(): pl.pallas_call(functools.partial(feed_forward_backward_kernel, count), ou...  80.2 us
    pallas_call x1, Pallas kernels, weight_gather(): pl.pallas_call(functools.partial(weight_gather_kernel, ctx_count, fsdp_co...  68 us
    pallas_call x1, Pallas kernels, owner_sums(): pl.pallas_call(functools.partial(owner_sum_kernel, ctx_count, fsdp_count,...  57.1 us
    pallas_call x1, Pallas kernels, attention_forward(): pl.pallas_call(functools.partial(attention_forward_kernel, ctx_count, len...  53.6 us
    dot_general x6, matrix products, forward_product(): return jnp.dot(a, b, preferred_element_type=jnp.float32)  16.6 us
    dot_general x6, matrix products, over_rows(): lax.dot_general(a, b, (((0,), (0,)), ((), ())), preferred_element_type=jn...  12 us
  transfers between devices with their start and end apart: 4, of which 0 were waited for; matrix products, arithmetic and copies ran while one was open for 9% of the time, Pallas kernels for 29%

profile of v6, /device:TPU:0, one launch (start us, length us, event | category | flops | bytes accessed | tf_op | source)
XLA Modules:
  0.0 561.0 jit_solution(13477557109903698105)
XLA Ops:
  9.5 1.2 fusion.18
  11.2 1.6 copy.90.refs_0_
  12.9 1.0 multiply_sine_fusion
  13.8 68.0 %weight_gather.1 = (bf16[4,2,2,2,64,3072]{5,4,3,2,1,0:T(8,128)(2,1)}, bf16[4,2,2,2,64,2304]{5,4,3,2,1,0:T(8,128)(2,1)}) custom-call(bf16[2,2,2,64,2048]{4,3,2,1,0:T(8,128)(2,1)} %bitcast.154, bf16[2,2,2,64,512]{4,3,2,1,0:T(8,128)(2,1)} %bitcast.161, bf16[2,2,2,64,512]{4,3,2,1,0:T(8,128)(2,1)} %bitcast.162, bf16[2,2,2,64,2048]{4,3,2,1,0:T(8,128)(2,1)} %bitcast.155, ...), custom_call_target="tpu_custom_call" | custom-call | bytes 44040192 | tf_op jit(solution)/shard_map/weight_gather/pallas_call | solution.py:287
  81.8 7.6 %fusion.39.raw.refs_3_ = f32[128,3072]{1,0:T(8,128)} fusion(bf16[2048,3072]{1,0:T(8,128)(2,1)} %bitcast.143, bf16[1,128,2048]{2,1,0:T(8,128)(2,1)S(1)} %copy-done.8, f32[2048]{0:T(1024)S(1)} %copy-done.29, f32[128]{0:T(128)S(1)} %fusion.50), kind=kOutput, calls=%fused_computation.84 | convolution fusion | flops 1611661312 | bytes 14688768 | tf_op jit(solution)/shard_map/dot_general | solution.py:31
  89.5 53.6 %attention_forward.1 = (bf16[2,2,2,128,1024]{4,3,2,1,0:T(8,128)(2,1)}, bf16[128,2048]{1,0:T(8,128)(2,1)}, bf16[128,2048]{1,0:T(8,128)(2,1)}, f32[8,8,128]{2,1,0:...) custom-call(f32[128,3072]{1,0:T(8,128)} %fusion.39.raw.refs_3_, ...), custom_call_target="tpu_custom_call", output_to_operand_aliasing={{4}: (7, {})} | custom-call | flops 1073741824 | bytes 8388608 | tf_op jit(solution)/shard_map/attention_forward/pallas_call | solution.py:681
  143.1 1.5 convolution_convert_fusion.7
  144.6 1.0 copy.107
  146.0 5.1 multiply_reduce_fusion.12
  151.3 1.3 multiply_reduce_fusion.10
  153.2 1.0 multiply_convert_fusion.rows_in
  154.1 81.6 %feed_forward.1 = (f32[128,2048]{1,0:T(8,128)}, bf16[4,128,2048]{2,1,0:T(8,128)(2,1)}, bf16[512,2048]{1,0:T(8,128)(2,1)}, bf16[512,2048]{1,0:T(8,128)(2,1)}, bf16[512,2048]{1,0:T(8,128)(2,1)}) custom-call(bf16[128,2048]{1,0:T(8,128)(2,1)} %multiply_convert_fusion.rows_in, bf16[2048,2048]{1,0:T(8,128)(2,1)} %gate_hbm.3, bf16[2048,2048]{1,0:T(8,128)(2,1)} %up_hbm.3, ...), custom_call_target="tpu_custom_call" | custom-call | flops 12884901888 | bytes 25165824 | tf_op jit(solution)/shard_map/feed_forward/pallas_call | solution.py:1387
  235.7 1.4 multiply_reduce_fusion.9
  237.1 1.5 multiply_add_fusion
  238.7 1.6 fusion.31
  240.8 0.9 fusion.28
  241.7 1.2 fusion.22
  242.9 1.2 fusion.49
  244.1 2.5 multiply_reduce_fusion
  246.6 1.1 fusion.23.grads_in
  247.8 80.2 %feed_forward_backward.1 = (f32[128,2048]{1,0:T(8,128)}, bf16[2048,2048]{1,0:T(8,128)(2,1)}, bf16[2048,2048]{1,0:T(8,128)(2,1)}, bf16[2048,2048]{1,0:T(8,128)(2,1)}) custom-call(bf16[128,2048]{1,0:T(8,128)(2,1)} %fusion.23.grads_in, bf16[512,2048]{1,0:T(8,128)(2,1)} %get-tuple-element.65.gate_keep, bf16[512,2048]{1,0:T(8,128)(2,1)} %get-tuple-element.66.up_keep, ...), custom_call_target="tpu_custom_call" | custom-call | flops 25769803776 | bytes 50331648 | tf_op jit(solution)/shard_map/feed_forward_backward/pallas_call | solution.py:1560
  328.9 1.7 copy.92.refs_9_
  330.6 1.3 constant_dynamic-slice_fusion.refs_8_
  331.9 1.5 multiply_reduce_fusion.1
  333.5 3.7 multiply_reduce_fusion.2
  337.3 1.3 fusion.25
  338.6 106.1 %attention_backward.1 = (bf16[128,3072]{1,0:T(8,128)(2,1)}, f32[8,256]{1,0:T(8,128)}, bf16[4,128,512]{2,1,0:T(8,128)(2,1)}, f32[128,2048]{1,0:T(8,128)}, bf16[25...) custom-call(bf16[128,2048]{1,0:T(8,128)(2,1)} %get-tuple-element.71.refs_0_, ...), custom_call_target="tpu_custom_call" | custom-call | flops 2684354560 | bytes 67108864 | tf_op jit(solution)/shard_map/attention_backward/pallas_call | solution.py:988
  444.7 1.1 slice.67
  445.8 1.0 slice_bitcast_fusion.1
  446.9 1.0 maximum_bitcast_fusion
  447.8 4.4 all-to-all-start
  453.4 3.3 fusion.17
  457.5 0.9 convolution_convert_fusion.4
  459.4 1.6 reshape.307
  461.0 1.5 copy.100
  462.6 1.0 copy.97
  463.6 2.0 copy.98
  466.2 1.0 copy.96
  467.2 2.8 convert_element_type.175
  470.0 1.6 convert_element_type.176
  473.3 1.2 fusion.34
  474.6 4.6 convolution_convert_fusion.1.refs_0_
  479.1 5.4 convolution_convert_fusion.refs_1_
  484.5 57.1 %owner_sums.1 = (bf16[256,512]{1,0:T(8,128)(2,1)S(1)}, bf16[256,768]{1,0:T(8,128)(2,1)S(1)}, bf16[64,256]{1,0:T(8,128)(2,1)S(1)}, bf16[64,256]{1,0:T(8,128)(2,1)S(1)}, bf16[32,512]{1,0:T(8,128)(2,1)S(1)}) custom-call(bf16[2048,512]{1,0:T(8,128)(2,1)S(1)} %copy-done, bf16[2048,768]{1,0:T(8,128)(2,1)} %convolution_convert_fusion.refs_1_, ...), custom_call_target="tpu_custom_call" | custom-call | flops 4194304 | bytes 16777216 | tf_op jit(solution)/shard_map/owner_sums/pallas_call | solution.py:1130
  543.9 1.4 convert_element_type.179
  546.9 1.4 convert_bitcast_fusion.2
  549.8 1.5 convert_bitcast_fusion
  551.3 1.8 copy.102
  (192 shorter events, 15.0 us)
Async XLA Ops:
  8.0 466.5 %all-gather.3.cloned.1.call-start = ((), (), s32[]{:S(2)}) async-start(), calls=%async_computation.2 | async-start | bytes 2621440 | tf_op jit(solution)/shard_map/all_gather | solution.py:51
  11.2 140.0 %copy-start.48 = (f32[128]{0:T(128)}, f32[128]{0:T(128)S(1)}, u32[]{:S(2)}) copy-start(f32[128]{0:T(128)S(1)} %fusion.50) | copy-start | bytes 1540
  13.8 68.0 %copy-start.8 = (bf16[1,128,2048]{2,1,0:T(8,128)(2,1)S(1)}, bf16[1,128,2048]{2,1,0:T(8,128)(2,1)}, u32[]{:S(2)}) copy-start(bf16[1,128,2048]{2,1,0:T(8,128)(2,1)} %param.23) | copy-start | bytes 1572868
  13.8 68.0 %copy-start.29 = (f32[2048]{0:T(1024)S(1)}, f32[2048]{0:T(1024)}, u32[]{:S(2)}) copy-start(f32[2048]{0:T(1024)} %param.38) | copy-start | bytes 24580
  143.1 2.9 copy-start.28
  144.6 6.6 %copy-start.36 = (bf16[128,64]{0,1:T(8,128)(2,1)}, bf16[128,64]{0,1:T(8,128)(2,1)S(1)}, u32[]{:S(2)}) copy-start(bf16[128,64]{0,1:T(8,128)(2,1)S(1)} %convolution_convert_fusion.7) | copy-start | bytes 49156
  146.0 5.2 copy-start.54
  146.0 5.3 copy-start.6
  146.0 5.2 copy-start.39
  146.0 5.2 copy-start.41
  152.6 83.1 %copy-start.63 = (f32[128]{0:T(128)}, f32[128]{0:T(128)S(1)}, u32[]{:S(2)}) copy-start(f32[128]{0:T(128)S(1)} %get-tuple-element.205) | copy-start | bytes 1540
  153.2 82.5 %copy-start.56 = (f32[128]{0:T(128)}, f32[128]{0:T(128)S(1)}, u32[]{:S(2)}) copy-start(f32[128]{0:T(128)S(1)} %get-tuple-element.221) | copy-start | bytes 1540
  154.1 83.0 %copy-start.34 = (f32[2048]{0:T(1024)S(1)}, f32[2048]{0:T(1024)}, u32[]{:S(2)}) copy-start(f32[2048]{0:T(1024)} %param.42) | copy-start | bytes 24580
  237.1 3.2 copy-start.27
  237.1 3.2 copy-start.32
  242.9 3.7 copy-start.24
  244.1 3.7 copy-start.30
  328.0 3.9 copy-start.18
  328.0 151.1 %all-gather.5.cloned.1.call-start = ((), (), s32[]{:S(2)}) async-start(), calls=%async_computation.3 | async-start | bytes 2621440 | tf_op jit(solution)/shard_map/all_gather | solution.py:51
  328.8 221.0 %reduce-scatter.2.cloned.1.call-start = ((), (), s32[]{:S(2)}) async-start(), calls=%async_computation.4 | async-start | bytes 9437184 | tf_op jit(solution)/shard_map/reduce_scatter | solution.py:55
  330.6 2.8 copy-start.40
  330.6 2.8 copy-start.42
  330.6 2.9 copy-start.19
  330.6 2.9 copy-start.51
  330.6 2.9 copy-start.53
  330.6 2.9 copy-start.59
  333.5 3.8 copy-start.62
  333.5 3.8 copy-start.55
  333.5 3.8 copy-start.7
  333.5 3.8 copy-start.13
  337.2 116.1 %copy-start.4 = (f32[128,2048]{1,0:T(8,128)}, f32[128,2048]{1,0:T(8,128)S(1)}, u32[]{:S(2)}) copy-start(f32[128,2048]{1,0:T(8,128)S(1)} %get-tuple-element.204) | copy-start | bytes 3145732
  338.6 114.5 %copy-start.16 = (bf16[128,2048]{1,0:T(8,128)(2,1)}, bf16[128,2048]{1,0:T(8,128)(2,1)S(1)}, u32[]{:S(2)}) copy-start(bf16[128,2048]{1,0:T(8,128)(2,1)S(1)} %get-tuple-element.209) | copy-start | bytes 1572868
  446.8 6.5 %copy-start.9 = (bf16[1,128,2048]{2,1,0:T(8,128)(2,1)S(1)}, bf16[1,128,2048]{2,1,0:T(8,128)(2,1)}, u32[]{:S(2)}) copy-start(bf16[1,128,2048]{2,1,0:T(8,128)(2,1)} %param.23) | copy-start | bytes 1572868
  446.8 6.5 %copy-start.49 = (f32[128]{0:T(128)S(1)}, f32[128]{0:T(128)}, u32[]{:S(2)}) copy-start(f32[128]{0:T(128)} %copy-done.48) | copy-start | bytes 1540
  447.8 31.3 %all-to-all-start = ((bf16[4,128,768]{2,1,0:T(8,128)(2,1)}), bf16[4,128,768]{2,1,0:T(8,128)(2,1)}, u32[]{:S(2)}, u32[]{:S(2)}) async-start(bf16[4,128,768]{2,1,0:T(8,128)(2,1)} %maximum_bitcast_fusion), calls=%async_computation | async-start | bytes 1572864 | tf_op jit(solution)/shard_map/all_to_all | solution.py:1757
  453.3 3.4 copy-start.58
  453.3 3.9 copy-start.15
  453.4 4.2 copy-start.17
  453.4 4.2 copy-start.37
  453.4 5.1 copy-start.25
  453.4 5.1 copy-start.33
  462.5 3.5 copy-start.47
  462.5 3.5 copy-start.46
  462.5 3.5 copy-start.45
  462.5 3.5 copy-start.44
  462.5 3.6 copy-start.43
  465.6 4.4 copy-start.26
  479.1 5.4 copy-start
  (21 other events, 35.1 us)
Sparse Core Ops, SparseCore 0:
  328.2 63.9 all-gather.2
  394.3 44.6 all-gather.4
Sparse Core Ops, SparseCore 1:
  444.8 82.6 reduce-scatter.1

commit v7 on v6

--- a/solution.py
+++ b/solution.py
@@ -13,7 +13,7 @@
 HD = 256
 MESH = pl.DeviceIdType.MESH
 FF_TILE = 512
-BACK_TILE = 512
+BACK_TILE = FF_TILE
 GRAD_TILE = 256
 
 
@@ -728,7 +728,7 @@
     )
 
 
-def attention_backward_kernel(ctx_count, fsdp_count, extra, *refs):
+def attention_backward_kernel(ctx_count, fsdp_count, extra, exchange, *refs):
     (
         query_low,
         kv,
@@ -749,6 +749,9 @@
     back, gain_grads, column_grads, normed_grads = refs[13 + many : 17 + many]
     extra_out = refs[17 + many : 17 + 2 * many]
     rest = refs[17 + 2 * many :]
+    if exchange:
+        back_columns, rest = rest[0], rest[1:]
+        *rest, back_send, back_recv = rest
     bias, score_grads, weights_low, query_grads, kv_grads = rest[:5]
     kv_parts = rest[5:11]
     extra_parts = [rest[11 + 8 * i : 19 + 8 * i] for i in range(many)]
@@ -758,6 +761,37 @@
     rows = raw.shape[0]
     column_send, column_recv, grads, streamed, stream_sem = rest[11 + 8 * many :]
     tile = streamed.shape[1]
+
+    head_parts = [(0, HEADS), (HEADS, KV_HEADS), (HEADS + KV_HEADS, KV_HEADS)]
+
+    def back_span(part, owner):
+        first, heads = head_parts[part]
+        size = heads * HD // fsdp_count
+        start = pl.multiple_of(first * HD + owner * size, size)
+        return pl.ds(start, size), pl.ds(first * HD // fsdp_count, size)
+
+    def back_copies(part):
+        copies = []
+        for d, peer in enumerate(peers):
+            source, target = back_span(part, peer)
+            copies.append(
+                pltpu.make_async_remote_copy(
+                    src_ref=back.at[:, source],
+                    dst_ref=back_columns.at[along, :, target],
+                    send_sem=back_send.at[part, d],
+                    recv_sem=back_recv.at[part, d],
+                    device_id=(place, peer),
+                    device_id_type=MESH,
+                )
+            )
+        return copies
+
+    def start_back(part):
+        if exchange:
+            for copy in back_copies(part):
+                copy.start()
+            source, target = back_span(part, along)
+            back_columns[along, :, target] = back[:, source]
 
     def stream(weight, columns, use):
         tiles = weight.shape[0] // tile
@@ -905,6 +939,7 @@
         return gain_grad + more
 
     gain_grads[0:1] = lax.fori_loop(0, HEADS, one_query, jnp.zeros((1, HD), jnp.float32))
+    start_back(0)
     for stage in range(1, bits - 1):
         kv_sum.end(stage - 1)
         kv_sum.start(stage)
@@ -925,6 +960,8 @@
         pulled, _ = unit_rows_pull(raw[:, at], grad, 1.0)
         back[:, at] = pulled.astype(low)
     gain_grads[1:2] = key_gain_grad
+    start_back(1)
+    start_back(2)
 
     def normed_tile(columns, weight):
         normed_grads[:, columns] = across(back[...], weight)
@@ -935,6 +972,10 @@
             step_extra(i, stage)
     for copy in column_copies:
         copy.wait()
+    if exchange:
+        for part in range(3):
+            for copy in back_copies(part):
+                copy.wait()
     for i in range(many):
         sums[i].end(bits - 2)
         extra_out[i][...] = sums[i].mine_now()[...]
@@ -984,18 +1025,24 @@
         pltpu.VMEM((2, FF_TILE, qkv_weight.shape[1]), low),
         pltpu.SemaphoreType.DMA((2,)),
     ]
+    exchange = KV_HEADS * HD // fsdp_count % 128 == 0
+    back_out = []
+    if exchange:
+        scratch += [pltpu.SemaphoreType.DMA((3, fsdp_count - 1))] * 2
+        back_out = [jax.ShapeDtypeStruct((fsdp_count, rows, raw.shape[1] // fsdp_count), low)]
     columns_shape = (fsdp_count, rows, row_grads.shape[1] // fsdp_count)
     outs = pl.pallas_call(
-        functools.partial(attention_backward_kernel, ctx_count, fsdp_count, shapes),
+        functools.partial(attention_backward_kernel, ctx_count, fsdp_count, shapes, exchange),
         out_shape=[
             jax.ShapeDtypeStruct(raw.shape, low),
             jax.ShapeDtypeStruct((8, HD), jnp.float32),
             jax.ShapeDtypeStruct(columns_shape, low),
             jax.ShapeDtypeStruct((rows, qkv_weight.shape[0]), jnp.float32),
         ]
-        + [jax.ShapeDtypeStruct(s, low) for s in shapes],
+        + [jax.ShapeDtypeStruct(s, low) for s in shapes]
+        + back_out,
         in_specs=[vmem] * 11 + [hbm] * (2 + len(extra)),
-        out_specs=[vmem] * (4 + len(extra)),
+        out_specs=[vmem] * (4 + len(extra) + len(back_out)),
         scratch_shapes=scratch,
         compiler_params=pltpu.CompilerParams(
             collective_id=3, has_side_effects=True, vmem_limit_bytes=60 << 20
@@ -1023,7 +1070,11 @@
         *extra,
     )
     columns = outs[2].reshape(-1, outs[2].shape[-1])
-    return outs[0], outs[1][0], outs[1][1], columns, outs[3], outs[4:]
+    back_columns = None
+    if exchange:
+        back_columns = outs[-1].reshape(-1, outs[-1].shape[-1])
+    sums = outs[4 : 4 + len(extra)]
+    return outs[0], outs[1][0], outs[1][1], columns, outs[3], sums, back_columns
 
 
 def owner_sum_kernel(ctx_count, fsdp_count, shapes, shared, *refs):
@@ -1189,7 +1240,7 @@
 
     def back_copy(self, way, owner, chunk):
         toward = self.along + 1 if way == 0 else self.along - 1
-        columns = pl.ds(chunk * BACK_TILE, BACK_TILE)
+        columns = tile_at(chunk, BACK_TILE)
         landing = owner if way == 0 else jnp.where(owner == toward, self.count, owner)
         return pltpu.make_async_remote_copy(
             src_ref=self.outgoing.at[owner, :, columns],
@@ -1222,20 +1273,20 @@
             origin = line_origin(self.along, way, step)
 
             def work():
-                def write(columns, tile):
+                def write(chunk, tile):
+                    columns = tile_at(chunk, BACK_TILE)
                     self.outgoing[origin, :, columns] = tile.astype(self.outgoing.dtype)
+                    pl.when(jnp.logical_not(self.relays(back)))(
+                        lambda: self.back_copy(back, origin, chunk).start()
+                    )
 
                 compute(origin, write)
 
-                def begin():
-                    for chunk in range(self.chunks):
-                        self.back_copy(back, origin, chunk).start()
-
-                pl.when(jnp.logical_not(self.relays(back)))(begin)
-
             pl.when(line_comes(self.along, self.count, way, step))(work)
 
-        def relay(way, step):
+        near_start = 2 * self.along < self.steps
+
+        def relay(way, step, turn):
             owner = step if way == 0 else self.steps - step
             passes = owner > self.along if way == 0 else owner < self.along
 
@@ -1247,7 +1298,7 @@
                     self.outgoing[owner, :, columns] = (mine + more).astype(self.outgoing.dtype)
                     self.back_copy(way, owner, chunk).start()
 
-            pl.when(self.relays(way) & passes)(work)
+            pl.when(self.relays(way) & passes & turn)(work)
 
         for step in range(1, self.steps + 1):
             self.arrive(step)
@@ -1255,8 +1306,9 @@
                 one(way, step)
             if step == self.steps:
                 before_last()
-            for way in range(2):
-                relay(way, step)
+            relay(0, step, near_start)
+            relay(1, step, True)
+            relay(0, step, jnp.logical_not(near_start))
 
     def finish(self, total):
         for way in range(2):
@@ -1365,8 +1417,7 @@
             return carry
 
         def out_step(t, carry):
-            columns = tile_at(t, tile)
-            write(columns, out_tile(origin, columns))
+            write(t, out_tile(origin, tile_at(t, tile)))
             return carry
 
         lax.fori_loop(0, units // tile, hidden_step, 0)
@@ -1497,8 +1548,7 @@
             return carry
 
         def out_step(t, carry):
-            columns = tile_at(t, tile)
-            write(columns, out_tile(origin, columns))
+            write(t, out_tile(origin, tile_at(t, tile)))
             return carry
 
         lax.fori_loop(0, units // tile, hidden_step, 0)
@@ -1728,6 +1778,7 @@
         out_columns,
         normed_grad_two,
         ffn_sums,
+        qkv_columns,
     ) = attention_backward(
         query_low,
         kv_all,
@@ -1744,7 +1795,7 @@
         full_qkv,
         [gate_weight_grad, up_weight_grad],
     )
-    down_low, qkv_back_low = lax.optimization_barrier((down_weight_grad, qkv_back_low))
+    down_low, normed_grad_two = lax.optimization_barrier((down_weight_grad, normed_grad_two))
     down_weight_grad = scatter_sum(down_low, "ctx")
     normed_grad_two = normed_grad_two + across(left_grad_low, full_left)
     inputs_grad_two, input_gain_grad = input_pull(normed_grad_one + normed_grad_two)
@@ -1757,18 +1808,19 @@
         return lax.all_to_all(parts, "fsdp", 0, 0, tiled=True).reshape(fsdp_count * rows_here, -1)
 
     out_weight_grad = over_rows(attended_all, out_columns)
-    qkv_parts = jnp.concatenate(
-        [
-            part.reshape(rows_here, fsdp_count, -1)
-            for part in (
-                qkv_back_low[:, :query_width],
-                qkv_back_low[:, query_width : query_width + kv_width],
-                qkv_back_low[:, query_width + kv_width :],
-            )
-        ],
-        axis=2,
-    )
-    qkv_columns = columns_to_owner(qkv_parts.reshape(rows_here, -1))
+    if qkv_columns is None:
+        qkv_parts = jnp.concatenate(
+            [
+                part.reshape(rows_here, fsdp_count, -1)
+                for part in (
+                    qkv_back_low[:, :query_width],
+                    qkv_back_low[:, query_width : query_width + kv_width],
+                    qkv_back_low[:, query_width + kv_width :],
+                )
+            ],
+            axis=2,
+        )
+        qkv_columns = columns_to_owner(qkv_parts.reshape(rows_here, -1))
     qkv_weight_grad = over_rows(normed_all, qkv_columns)
 
     small_gains = [

time: 566 us -> 545 us (0.963)
  Pallas kernels: 447 us -> 438 us
    pallas_call x1, Pallas kernels: 81.6 us -> 71.4 us  [feed_forward(): pl.pallas_call(functools.partial(feed_forward_kernel, count), out_shape=[...]
    pallas_call x1, Pallas kernels: 57.1 us -> 65.7 us  [owner_sums(): pl.pallas_call(functools.partial(owner_sum_kernel, ctx_count, fsdp_count,...]
  transfers between devices with their start and end apart: 4 -> 3, of which waited for: 0 -> 0; matrix products, arithmetic and copies ran while one was open for 9% -> 8% of each run, Pallas kernels for 29% -> 31%
where the time goes in v7:
time: 545 us; the launch traced here: 541 us
  Pallas kernels  438 us (80%)
  matrix products  35.1 us (6%)
  other arithmetic  29.3 us (5%)
  local copies, waits for them, and re-layouts  21 us (4%)
  between operations  16.8 us (3%)
    pallas_call x1, Pallas kernels, attention_backward(): pl.pallas_call(functools.partial(attention_backward_kernel, ctx_count, fs...  101 us
    pallas_call x1, Pallas kernels, feed_forward_backward(): pl.pallas_call(functools.partial(feed_forward_backward_kernel, count), ou...  78.1 us
    pallas_call x1, Pallas kernels, feed_forward(): pl.pallas_call(functools.partial(feed_forward_kernel, count), out_shape=[...  71.4 us
    pallas_call x1, Pallas kernels, weight_gather(): pl.pallas_call(functools.partial(weight_gather_kernel, ctx_count, fsdp_co...  68 us
    pallas_call x1, Pallas kernels, owner_sums(): pl.pallas_call(functools.partial(owner_sum_kernel, ctx_count, fsdp_count,...  65.7 us
    pallas_call x1, Pallas kernels, attention_forward(): pl.pallas_call(functools.partial(attention_forward_kernel, ctx_count, len...  53.6 us
    dot_general x6, matrix products, forward_product(): return jnp.dot(a, b, preferred_element_type=jnp.float32)  16.7 us
    dot_general x6, matrix products, over_rows(): lax.dot_general(a, b, (((0,), (0,)), ((), ())), preferred_element_type=jn...  11.5 us
  transfers between devices with their start and end apart: 3, of which 0 were waited for; matrix products, arithmetic and copies ran while one was open for 8% of the time, Pallas kernels for 31%

profile of v7, /device:TPU:0, one launch (start us, length us, event | category | flops | bytes accessed | tf_op | source)
XLA Modules:
  0.0 540.9 jit_solution(16856616048902123007)
XLA Ops:
  8.1 1.2 fusion.18
  10.6 0.7 copy.83.row_ids
  11.3 1.6 copy.84.refs_0_
  12.9 1.0 multiply_sine_fusion
  13.9 68.0 %weight_gather.1 = (bf16[4,2,2,2,64,3072]{5,4,3,2,1,0:T(8,128)(2,1)}, bf16[4,2,2,2,64,2304]{5,4,3,2,1,0:T(8,128)(2,1)}) custom-call(bf16[2,2,2,64,2048]{4,3,2,1,0:T(8,128)(2,1)} %bitcast.137, bf16[2,2,2,64,512]{4,3,2,1,0:T(8,128)(2,1)} %bitcast.141, bf16[2,2,2,64,512]{4,3,2,1,0:T(8,128)(2,1)} %bitcast.142, bf16[2,2,2,64,2048]{4,3,2,1,0:T(8,128)(2,1)} %bitcast.138, ...), custom_call_target="tpu_custom_call" | custom-call | bytes 44040192 | tf_op jit(solution)/shard_map/weight_gather/pallas_call | solution.py:287
  81.9 7.7 %fusion.39.raw.refs_3_ = f32[128,3072]{1,0:T(8,128)} fusion(bf16[2048,3072]{1,0:T(8,128)(2,1)} %bitcast.127, bf16[1,128,2048]{2,1,0:T(8,128)(2,1)S(1)} %copy-done.8, f32[2048]{0:T(1024)S(1)} %copy-done.28, f32[128]{0:T(128)S(1)} %fusion.50), kind=kOutput, calls=%fused_computation.82 | convolution fusion | flops 1611661312 | bytes 14688768 | tf_op jit(solution)/shard_map/dot_general | solution.py:31
  89.5 53.6 %attention_forward.1 = (bf16[2,2,2,128,1024]{4,3,2,1,0:T(8,128)(2,1)}, bf16[128,2048]{1,0:T(8,128)(2,1)}, bf16[128,2048]{1,0:T(8,128)(2,1)}, f32[8,8,128]{2,1,0:...) custom-call(f32[128,3072]{1,0:T(8,128)} %fusion.39.raw.refs_3_, ...), custom_call_target="tpu_custom_call", output_to_operand_aliasing={{4}: (7, {})} | custom-call | flops 1073741824 | bytes 8388608 | tf_op jit(solution)/shard_map/attention_forward/pallas_call | solution.py:681
  143.2 1.5 convolution_convert_fusion.7
  144.7 1.0 copy.95
  146.1 5.1 multiply_reduce_fusion.12
  151.3 1.3 multiply_reduce_fusion.10
  153.2 1.0 multiply_convert_fusion.rows_in
  154.2 71.4 %feed_forward.1 = (f32[128,2048]{1,0:T(8,128)}, bf16[4,128,2048]{2,1,0:T(8,128)(2,1)}, bf16[512,2048]{1,0:T(8,128)(2,1)}, bf16[512,2048]{1,0:T(8,128)(2,1)}, bf16[512,2048]{1,0:T(8,128)(2,1)}) custom-call(bf16[128,2048]{1,0:T(8,128)(2,1)} %multiply_convert_fusion.rows_in, bf16[2048,2048]{1,0:T(8,128)(2,1)} %gate_hbm.3, bf16[2048,2048]{1,0:T(8,128)(2,1)} %up_hbm.3, ...), custom_call_target="tpu_custom_call" | custom-call | flops 12884901888 | bytes 25165824 | tf_op jit(solution)/shard_map/feed_forward/pallas_call | solution.py:1438
  225.6 1.4 multiply_reduce_fusion.9
  227.0 1.5 multiply_add_fusion
  228.6 1.6 fusion.31
  230.7 0.9 fusion.28
  231.6 1.2 fusion.22
  232.8 1.2 fusion.49
  234.0 2.5 multiply_reduce_fusion
  236.5 1.1 fusion.23.grads_in
  237.7 78.1 %feed_forward_backward.1 = (f32[128,2048]{1,0:T(8,128)}, bf16[2048,2048]{1,0:T(8,128)(2,1)}, bf16[2048,2048]{1,0:T(8,128)(2,1)}, bf16[2048,2048]{1,0:T(8,128)(2,1)}) custom-call(bf16[128,2048]{1,0:T(8,128)(2,1)} %fusion.23.grads_in, bf16[512,2048]{1,0:T(8,128)(2,1)} %get-tuple-element.65.gate_keep, bf16[512,2048]{1,0:T(8,128)(2,1)} %get-tuple-element.66.up_keep, ...), custom_call_target="tpu_custom_call" | custom-call | flops 25769803776 | bytes 50331648 | tf_op jit(solution)/shard_map/feed_forward_backward/pallas_call | solution.py:1610
  316.8 1.7 copy.86.refs_9_
  318.6 1.3 constant_dynamic-slice_fusion.refs_8_
  319.9 1.5 multiply_reduce_fusion.1
  321.5 3.7 multiply_reduce_fusion.2
  325.3 1.3 fusion.25
  326.5 100.8 %attention_backward.1 = (bf16[128,3072]{1,0:T(8,128)(2,1)}, f32[8,256]{1,0:T(8,128)}, bf16[4,128,512]{2,1,0:T(8,128)(2,1)}, f32[128,2048]{1,0:T(8,128)}, bf16[25...) custom-call(bf16[128,2048]{1,0:T(8,128)(2,1)} %get-tuple-element.72.refs_0_, ...), custom_call_target="tpu_custom_call" | custom-call | flops 2684354560 | bytes 67108864 | tf_op jit(solution)/shard_map/attention_backward/pallas_call | solution.py:1034
  428.5 2.9 fusion.17
  432.1 1.0 copy.87
  433.3 1.0 copy.89
  434.6 1.0 copy.88
  437.2 1.0 reshape.295
  438.5 1.1 copy-done.25
  439.6 1.6 convert_element_type.175
  441.2 1.6 convert_element_type.176
  444.5 1.2 fusion.34
  445.7 4.3 convolution_convert_fusion.1.refs_0_
  450.0 5.8 %convolution_convert_fusion.refs_1_ = bf16[2048,768]{1,0:T(8,128)(2,1)} fusion(bf16[512,2048]{1,0:T(8,128)(2,1)} %all-gather.5.cloned.1.call-done, bf16[512,768]{1,0:T(8,128)(2,1)} %bitcast.152), kind=kOutput, calls=%fused_computation.2 | convolution fusion | flops 1612185600 | bytes 6029312 | tf_op jit(solution)/shard_map/dot_general | solution.py:39
  455.9 65.7 %owner_sums.1 = (bf16[256,512]{1,0:T(8,128)(2,1)S(1)}, bf16[256,768]{1,0:T(8,128)(2,1)S(1)}, bf16[64,256]{1,0:T(8,128)(2,1)S(1)}, bf16[64,256]{1,0:T(8,128)(2,1)S(1)}, bf16[32,512]{1,0:T(8,128)(2,1)S(1)}) custom-call(bf16[2048,512]{1,0:T(8,128)(2,1)S(1)} %copy-done, bf16[2048,768]{1,0:T(8,128)(2,1)} %convolution_convert_fusion.refs_1_, ...), custom_call_target="tpu_custom_call" | custom-call | flops 4194304 | bytes 16777216 | tf_op jit(solution)/shard_map/owner_sums/pallas_call | solution.py:1181
  522.3 0.9 convert_element_type.173
  523.9 1.4 convert_element_type.179
  525.3 0.7 slice_reduce_fusion.6
  526.0 0.8 slice_reduce_fusion
  526.8 1.4 convert_bitcast_fusion.2
  528.9 0.9 slice_convert_fusion
  529.8 1.5 convert_bitcast_fusion
  531.2 1.8 copy.93
  (186 shorter events, 11.6 us)
Async XLA Ops:
  8.0 437.7 %all-gather.3.cloned.1.call-start = ((), (), s32[]{:S(2)}) async-start(), calls=%async_computation.1 | async-start | bytes 2621440 | tf_op jit(solution)/shard_map/all_gather | solution.py:51
  9.9 141.4 %copy-start.49 = (f32[128]{0:T(128)}, f32[128]{0:T(128)S(1)}, u32[]{:S(2)}) copy-start(f32[128]{0:T(128)S(1)} %fusion.50) | copy-start | bytes 1540
  13.9 68.0 %copy-start.8 = (bf16[1,128,2048]{2,1,0:T(8,128)(2,1)S(1)}, bf16[1,128,2048]{2,1,0:T(8,128)(2,1)}, u32[]{:S(2)}) copy-start(bf16[1,128,2048]{2,1,0:T(8,128)(2,1)} %param.23) | copy-start | bytes 1572868
  13.9 68.0 %copy-start.28 = (f32[2048]{0:T(1024)S(1)}, f32[2048]{0:T(1024)}, u32[]{:S(2)}) copy-start(f32[2048]{0:T(1024)} %param.38) | copy-start | bytes 24580
  143.2 2.9 copy-start.27
  144.6 6.6 %copy-start.37 = (bf16[128,64]{0,1:T(8,128)(2,1)}, bf16[128,64]{0,1:T(8,128)(2,1)S(1)}, u32[]{:S(2)}) copy-start(bf16[128,64]{0,1:T(8,128)(2,1)S(1)} %convolution_convert_fusion.7) | copy-start | bytes 49156
  146.0 5.2 copy-start.56
  146.0 5.3 copy-start.6
  146.1 5.2 copy-start.40
  146.1 5.2 copy-start.42
  152.7 72.9 %copy-start.64 = (f32[128]{0:T(128)}, f32[128]{0:T(128)S(1)}, u32[]{:S(2)}) copy-start(f32[128]{0:T(128)S(1)} %get-tuple-element.205) | copy-start | bytes 1540
  153.2 72.4 %copy-start.58 = (f32[128]{0:T(128)}, f32[128]{0:T(128)S(1)}, u32[]{:S(2)}) copy-start(f32[128]{0:T(128)S(1)} %get-tuple-element.219) | copy-start | bytes 1540
  154.2 72.8 %copy-start.35 = (f32[2048]{0:T(1024)S(1)}, f32[2048]{0:T(1024)}, u32[]{:S(2)}) copy-start(f32[2048]{0:T(1024)} %param.42) | copy-start | bytes 24580
  227.0 3.2 copy-start.26
  227.0 3.2 copy-start.31
  228.5 2.1 copy-start.14
  228.6 2.1 copy-start.39
  231.6 2.4 copy-start.3
  232.8 3.7 copy-start.22
  234.0 3.7 copy-start.29
  315.8 4.1 copy-start.16
  315.8 134.2 %all-gather.5.cloned.1.call-start = ((), (), s32[]{:S(2)}) async-start(), calls=%async_computation.2 | async-start | bytes 2621440 | tf_op jit(solution)/shard_map/all_gather | solution.py:51
  316.6 213.2 %reduce-scatter.2.cloned.1.call-start = ((), (), s32[]{:S(2)}) async-start(), calls=%async_computation.3 | async-start | bytes 9437184 | tf_op jit(solution)/shard_map/reduce_scatter | solution.py:55
  318.5 2.8 copy-start.65
  318.5 2.8 copy-start.41
  318.5 2.8 copy-start.43
  318.5 2.9 copy-start.17
  318.6 2.9 copy-start.53
  318.6 2.9 copy-start.55
  318.6 2.9 copy-start.61
  321.5 3.8 copy-start.57
  321.5 3.8 copy-start.63
  321.5 3.8 copy-start.7
  321.5 3.8 copy-start.13
  325.2 102.5 %copy-start.4 = (f32[128,2048]{1,0:T(8,128)}, f32[128,2048]{1,0:T(8,128)S(1)}, u32[]{:S(2)}) copy-start(f32[128,2048]{1,0:T(8,128)S(1)} %get-tuple-element.204) | copy-start | bytes 3145732
  428.4 3.0 copy-start.33
  428.4 3.0 copy-start.48
  428.4 3.1 copy-start.47
  428.4 3.1 copy-start.46
  428.4 3.1 copy-start.45
  428.4 3.1 copy-start.44
  428.4 3.1 copy-start.51
  428.4 4.7 copy-start.38
  431.4 3.0 copy-start.15
  431.4 4.2 copy-start.30
  431.4 2.9 copy-start.34
  438.5 2.7 copy-start.24
  450.0 5.8 %copy-start = (bf16[2048,512]{1,0:T(8,128)(2,1)S(1)}, bf16[2048,512]{1,0:T(8,128)(2,1)}, u32[]{:S(2)}) copy-start(bf16[2048,512]{1,0:T(8,128)(2,1)} %convolution_convert_fusion.1.refs_0_) | copy-start | bytes 6291460
  (21 other events, 29.3 us)
Sparse Core Ops, SparseCore 0:
  315.9 69.8 all-gather.2
  388.0 50.2 all-gather.4
Sparse Core Ops, SparseCore 1:
  427.5 92.4 reduce-scatter.1

commit v8 on v7

--- a/solution.py
+++ b/solution.py
@@ -14,7 +14,6 @@
 MESH = pl.DeviceIdType.MESH
 FF_TILE = 512
 BACK_TILE = FF_TILE
-GRAD_TILE = 256
 
 
 epsilon = 1e-06
@@ -1203,13 +1202,10 @@
         self.width = outgoing.shape[-1]
         self.chunks = self.width // BACK_TILE
 
-    def barrier(self):
-        partner_barrier(
-            [
-                (self.place, lax.rem(self.along + d, self.count))
-                for d in sorted({1, self.count - 1})
-            ]
-        )
+    def partners(self):
+        return [
+            (self.place, lax.rem(self.along + d, self.count)) for d in sorted({1, self.count - 1})
+        ]
 
     def line_copy(self, way, step, origin):
         toward = self.along + 1 if way == 0 else self.along - 1
@@ -1386,7 +1382,7 @@
         loads[1][t].start()
     for load in loads[2]:
         load.start()
-    line.barrier()
+    partner_barrier(line.partners())
     line.forward(1)
     gathered[line.along] = rows_in[...]
 
@@ -1486,7 +1482,8 @@
     up_hbm,
     down_hbm,
     total,
-    down_grad,
+    down_sum,
+    down_rest,
     gate_grad,
     up_grad,
     gathered,
@@ -1498,17 +1495,29 @@
     weight_sem,
     staged,
     staged_sem,
+    later_in,
+    send_zero,
+    recv_zero,
+    send_sem,
+    recv_sem,
+    ready_sem,
+    rest_sem,
     *parts,
 ):
     rows, width = grads_in.shape
-    units = gate_w.shape[1]
+    ctx_count, block, units = gate_w.shape
+    pairs = ctx_count // 2
+    position = ctx_position(ctx_count)
+    bits, _, _, mine, partners, _ = position
     tile = FF_TILE
+    blocks = tile // block
     line = LineExchange(count, grads_in, gathered, parts[0], parts[1], parts[2:])
     loads = []
     for n, (source, target) in enumerate(((gate_hbm, gate_w), (up_hbm, up_w), (down_hbm, down_w))):
         group = []
-        for t in range(target.shape[0] // tile):
-            at = pl.ds(t * tile, tile)
+        size = tile if n else blocks
+        for t in range(target.shape[0] // size):
+            at = pl.ds(t * size, size)
             group.append(pltpu.make_async_copy(source.at[at], target.at[at], weight_sem.at[n, t]))
         loads.append(group)
     for load in loads[2]:
@@ -1516,7 +1525,7 @@
     for t in range(width // tile):
         loads[0][t].start()
         loads[1][t].start()
-    line.barrier()
+    partner_barrier(partners + line.partners())
     line.forward(1)
     gathered[line.along] = grads_in[...]
 
@@ -1529,9 +1538,10 @@
         gate_back[at, columns] = gate_pull.astype(gate_back.dtype)
         up_back[at, columns] = up_pull.astype(up_back.dtype)
 
-    def out_tile(origin, columns):
+    def out_tile(origin, t):
         at = pl.ds(pl.multiple_of(origin * rows, rows), rows)
-        return across(gate_back[at], gate_w[columns]) + across(up_back[at], up_w[columns])
+        gate_rows = gate_w[pl.ds(t * blocks, blocks)].reshape(tile, units)
+        return across(gate_back[at], gate_rows) + across(up_back[at], up_w[tile_at(t, tile)])
 
     for t in range(units // tile):
         loads[2][t].wait()
@@ -1539,8 +1549,7 @@
     for t in range(width // tile):
         loads[0][t].wait()
         loads[1][t].wait()
-        columns = pl.ds(t * tile, tile)
-        total[:, columns] = out_tile(line.along, columns)
+        total[:, pl.ds(t * tile, tile)] = out_tile(line.along, t)
 
     def compute(origin, write):
         def hidden_step(t, carry):
@@ -1548,60 +1557,107 @@
             return carry
 
         def out_step(t, carry):
-            write(t, out_tile(origin, tile_at(t, tile)))
+            write(t, out_tile(origin, t))
             return carry
 
         lax.fori_loop(0, units // tile, hidden_step, 0)
         lax.fori_loop(0, width // tile, out_step, 0)
 
-    band = GRAD_TILE
-    bands = width // band
+    half = down_sum.shape[1]
+    here, there = pl.ds(0, half), pl.ds(half, units - half)
+    down = Halving(
+        position,
+        block,
+        lambda b: staged.at[b // 2 % 2, b % 2, :, here],
+        lambda b: gate_w.at[b, :, here],
+        gate_w.at[pl.ds(pairs, pairs), :, here],
+        later_in,
+        (send_zero, recv_zero, send_sem, recv_sem),
+    )
+
+    def down_block(c):
+        left = gathered[:, :, tile_at(c, block)].reshape(count * rows, block)
+        return over_rows(left, hidden_keep[...]).astype(gate_w.dtype)
+
+    def rest_copy(source, c):
+        return pltpu.make_async_copy(
+            source.at[:, there], down_rest.at[tile_at(c, block)], rest_sem.at[c]
+        )
+
+    def given(b):
+        return rest_copy(staged.at[b // 2 % 2, b % 2], 2 * b + 1 - mine[0])
+
+    def kept(b):
+        return rest_copy(gate_w.at[b], 2 * b + mine[0])
+
+    def start_down():
+        pl.semaphore_signal(ready_sem, inc=1, device_id=partners[0], device_id_type=MESH)
+        pl.semaphore_wait(ready_sem, 1)
+        for b in range(pairs):
+            if b >= 4:
+                down.first_copy(b - 4).wait_send()
+                given(b - 4).wait()
+            staged[b // 2 % 2, b % 2] = down_block(2 * b + 1 - mine[0])
+            down.first_copy(b).start()
+            given(b).start()
+        for b in range(pairs):
+            gate_w[b] = down_block(2 * b + mine[0])
+            kept(b).start()
+        for b in range(pairs):
+            copy = down.first_copy(b)
+            if b >= pairs - 4:
+                copy.wait_send()
+                given(b).wait()
+            copy.wait_recv()
+            add_rows(down.held(b), down.first_in.at[b], 0, block)
+        down.start(0)
 
     def stage(slot, which, t, target):
         return pltpu.make_async_copy(
-            staged.at[slot, which], target.at[tile_at(t, band)], staged_sem.at[slot, which]
+            staged.at[slot, which], target.at[tile_at(t, block)], staged_sem.at[slot, which]
         )
 
-    def grad_bands(jobs):
+    def grad_bands(first, last):
         def step(t, carry):
             slot = lax.rem(t, 2)
-            for left, right, target, which in jobs:
+            left = tokens[:, tile_at(t, block)]
+            for which, (right, target) in enumerate(((gate_back, gate_grad), (up_back, up_grad))):
 
                 @pl.when(t >= 2)
                 def _(target=target, which=which):
                     stage(slot, which, t, target).wait()
 
-                product = over_rows(left(tile_at(t, band)), right[...])
-                staged[slot, which] = product.astype(staged.dtype)
+                staged[slot, which] = over_rows(left, right[...]).astype(staged.dtype)
                 stage(slot, which, t, target).start()
             return carry
 
-        lax.fori_loop(0, bands, step, 0)
-        for back in range(2):
-            t = bands - 2 + back
-            for _, _, target, which in jobs:
-                stage(t % 2, which, t, target).wait()
-
-    def grads_at(columns):
-        return gathered[:, :, columns].reshape(count * rows, band)
-
-    line.run(
-        compute, lambda: grad_bands([(grads_at, hidden_keep, down_grad, 0)])
-    )
-    grad_bands(
-        [
-            (lambda columns: tokens[:, columns], gate_back, gate_grad, 0),
-            (lambda columns: tokens[:, columns], up_back, up_grad, 1),
-        ]
-    )
+        lax.fori_loop(first, last, step, 0)
+
+    line.run(compute, start_down)
+    grad_bands(0, ctx_count * 3 // 4)
+    for step in range(1, bits - 1):
+        down.end(step - 1)
+        down.start(step)
+    grad_bands(ctx_count * 3 // 4, ctx_count)
     line.finish(total)
+    for t in (ctx_count - 2, ctx_count - 1):
+        for which, target in enumerate((gate_grad, up_grad)):
+            stage(t % 2, which, t, target).wait()
+    for b in range(pairs):
+        kept(b).wait()
+    down.end(bits - 2)
+    down_sum[...] = down.mine_now()[...]
 
 
 def feed_forward_backward(
     grads_in, gate_keep, up_keep, hidden_keep, tokens, gate_weight, up_weight, down_weight
 ):
     count = lax.axis_size("fsdp")
+    ctx_count = lax.axis_size("ctx")
+    pairs = ctx_count // 2
     rows, width = grads_in.shape
+    block = width // ctx_count
+    half = gate_weight.shape[1] // 2
     units = gate_weight.shape[1]
     low = jnp.bfloat16
     vmem = pl.BlockSpec(memory_space=pltpu.VMEM)
@@ -1609,19 +1665,28 @@
     grad_shape = jax.ShapeDtypeStruct((width, units), low)
     return pl.pallas_call(
         functools.partial(feed_forward_backward_kernel, count),
-        out_shape=[jax.ShapeDtypeStruct((rows, width), jnp.float32)] + [grad_shape] * 3,
+        out_shape=[
+            jax.ShapeDtypeStruct((rows, width), jnp.float32),
+            jax.ShapeDtypeStruct((block, half), low),
+            jax.ShapeDtypeStruct((width, units - half), low),
+            grad_shape,
+            grad_shape,
+        ],
         in_specs=[vmem] * 5 + [hbm] * 3,
-        out_specs=[vmem] + [hbm] * 3,
+        out_specs=[vmem, vmem, hbm, hbm, hbm],
         scratch_shapes=[
             pltpu.VMEM((count, rows, width), low),
             pltpu.VMEM((count * rows, units), low),
             pltpu.VMEM((count * rows, units), low),
-            pltpu.VMEM((width, units), low),
+            pltpu.VMEM((ctx_count, block, units), low),
             pltpu.VMEM((width, units), low),
             pltpu.VMEM((units, width), low),
             pltpu.SemaphoreType.DMA((3, max(width, units) // FF_TILE)),
-            pltpu.VMEM((2, 2, GRAD_TILE, units), low),
+            pltpu.VMEM((2, 2, block, units), low),
             pltpu.SemaphoreType.DMA((2, 2)),
+            *halving_scratch(ctx_count, block, half)[1:],
+            pltpu.SemaphoreType.REGULAR,
+            pltpu.SemaphoreType.DMA((ctx_count,)),
         ]
         + line_scratch(count, rows, width),
         compiler_params=pltpu.CompilerParams(
@@ -1633,7 +1698,16 @@
             transcendentals=count * rows * units,
         ),
         name="feed_forward_backward",
-    )(grads_in, gate_keep, up_keep, hidden_keep, tokens, gate_weight, up_weight, down_weight)
+    )(
+        grads_in,
+        gate_keep,
+        up_keep,
+        hidden_keep,
+        tokens,
+        gate_weight.reshape(ctx_count, block, units),
+        up_weight,
+        down_weight,
+    )
 
 
 def body(
@@ -1745,7 +1819,7 @@
     mixed_grad_one, ffn_out_grad, post_gain_grad = middle_pull(
         middle_grad_one + across(gate_grad_low, full_side_gate)
     )
-    ffn_in_grad, down_weight_grad, gate_weight_grad, up_weight_grad = feed_forward_backward(
+    ffn_in_grad, down_sum, down_rest, gate_weight_grad, up_weight_grad = feed_forward_backward(
         ffn_out_grad.astype(low),
         gate_raw,
         up_raw,
@@ -1795,8 +1869,8 @@
         full_qkv,
         [gate_weight_grad, up_weight_grad],
     )
-    down_low, normed_grad_two = lax.optimization_barrier((down_weight_grad, normed_grad_two))
-    down_weight_grad = scatter_sum(down_low, "ctx")
+    down_rest, normed_grad_two = lax.optimization_barrier((down_rest, normed_grad_two))
+    down_rest = scatter_sum(down_rest, "ctx")
     normed_grad_two = normed_grad_two + across(left_grad_low, full_left)
     inputs_grad_two, input_gain_grad = input_pull(normed_grad_one + normed_grad_two)
     block_out = result.astype(low)[None]
@@ -1863,7 +1937,7 @@
         3,
     )
     gate_weight_grad, up_weight_grad = ffn_sums
-    down_weight_grad = down_weight_grad.T
+    down_weight_grad = jnp.concatenate([down_sum.T, down_rest.T], axis=0)
     query_part = query_width // fsdp_count
     kv_part = kv_width // fsdp_count
     query_weight_grad = qkv_weight_grad[:, :query_part]

time: 545 us -> 535 us (0.982)
  Pallas kernels: 438 us -> 428 us
    pallas_call x1, Pallas kernels: 65.7 us -> 49.1 us  [owner_sums(): pl.pallas_call(functools.partial(owner_sum_kernel, ctx_count, fsdp_count,...]
    pallas_call x1, Pallas kernels: 78.1 us -> 88.6 us  [feed_forward_backward(): pl.pallas_call(functools.partial(feed_forward_backward_kernel, count), ou...]
  transfers between devices with their start and end apart: 3 -> 3, of which waited for: 0 -> 0; matrix products, arithmetic and copies ran while one was open for 8% -> 8% of each run, Pallas kernels for 31% -> 28%
where the time goes in v8:
time: 535 us; the launch traced here: 531 us
  Pallas kernels  428 us (80%)
  matrix products  34.8 us (7%)
  other arithmetic  29.4 us (5%)
  local copies, waits for them, and re-layouts  20.8 us (4%)
  between operations  16.6 us (3%)
    pallas_call x1, Pallas kernels, attention_backward(): pl.pallas_call(functools.partial(attention_backward_kernel, ctx_count, fs...  98.1 us
    pallas_call x1, Pallas kernels, feed_forward_backward(): pl.pallas_call(functools.partial(feed_forward_backward_kernel, count), ou...  88.6 us
    pallas_call x1, Pallas kernels, feed_forward(): pl.pallas_call(functools.partial(feed_forward_kernel, count), out_shape=[...  71.2 us
    pallas_call x1, Pallas kernels, weight_gather(): pl.pallas_call(functools.partial(weight_gather_kernel, ctx_count, fsdp_co...  68 us
    pallas_call x1, Pallas kernels, attention_forward(): pl.pallas_call(functools.partial(attention_forward_kernel, ctx_count, len...  53.5 us
    pallas_call x1, Pallas kernels, owner_sums(): pl.pallas_call(functools.partial(owner_sum_kernel, ctx_count, fsdp_count,...  49.1 us
    dot_general x6, matrix products, forward_product(): return jnp.dot(a, b, preferred_element_type=jnp.float32)  16.6 us
    dot_general x6, matrix products, over_rows(): lax.dot_general(a, b, (((0,), (0,)), ((), ())), preferred_element_type=jn...  11.2 us
  transfers between devices with their start and end apart: 3, of which 0 were waited for; matrix products, arithmetic and copies ran while one was open for 8% of the time, Pallas kernels for 28%

profile of v8, /device:TPU:0, one launch (start us, length us, event | category | flops | bytes accessed | tf_op | source)
XLA Modules:
  0.0 530.9 jit_solution(9718857526733940862)
XLA Ops:
  8.1 1.2 fusion.18
  10.5 0.7 copy.83.row_ids
  11.3 1.6 copy.84.refs_0_
  12.9 1.0 multiply_sine_fusion
  13.8 68.0 %weight_gather.1 = (bf16[4,2,2,2,64,3072]{5,4,3,2,1,0:T(8,128)(2,1)}, bf16[4,2,2,2,64,2304]{5,4,3,2,1,0:T(8,128)(2,1)}) custom-call(bf16[2,2,2,64,2048]{4,3,2,1,0:T(8,128)(2,1)} %bitcast.138, bf16[2,2,2,64,512]{4,3,2,1,0:T(8,128)(2,1)} %bitcast.144, bf16[2,2,2,64,512]{4,3,2,1,0:T(8,128)(2,1)} %bitcast.145, bf16[2,2,2,64,2048]{4,3,2,1,0:T(8,128)(2,1)} %bitcast.139, ...), custom_call_target="tpu_custom_call" | custom-call | bytes 44040192 | tf_op jit(solution)/shard_map/weight_gather/pallas_call | solution.py:286
  81.8 7.6 %fusion.39.raw.refs_3_ = f32[128,3072]{1,0:T(8,128)} fusion(bf16[2048,3072]{1,0:T(8,128)(2,1)} %bitcast.128, bf16[1,128,2048]{2,1,0:T(8,128)(2,1)S(1)} %copy-done.8, f32[2048]{0:T(1024)S(1)} %copy-done.29, f32[128]{0:T(128)S(1)} %fusion.50), kind=kOutput, calls=%fused_computation.82 | convolution fusion | flops 1611661312 | bytes 14688768 | tf_op jit(solution)/shard_map/dot_general | solution.py:30
  89.5 53.5 %attention_forward.1 = (bf16[2,2,2,128,1024]{4,3,2,1,0:T(8,128)(2,1)}, bf16[128,2048]{1,0:T(8,128)(2,1)}, bf16[128,2048]{1,0:T(8,128)(2,1)}, f32[8,8,128]{2,1,0:...) custom-call(f32[128,3072]{1,0:T(8,128)} %fusion.39.raw.refs_3_, ...), custom_call_target="tpu_custom_call", output_to_operand_aliasing={{4}: (7, {})} | custom-call | flops 1073741824 | bytes 8388608 | tf_op jit(solution)/shard_map/attention_forward/pallas_call | solution.py:680
  143.0 1.5 convolution_convert_fusion.7
  144.4 1.0 copy.95
  145.9 5.1 multiply_reduce_fusion.12
  151.1 1.3 multiply_reduce_fusion.10
  153.0 1.0 multiply_convert_fusion.rows_in
  154.0 71.2 %feed_forward.1 = (f32[128,2048]{1,0:T(8,128)}, bf16[4,128,2048]{2,1,0:T(8,128)(2,1)}, bf16[512,2048]{1,0:T(8,128)(2,1)}, bf16[512,2048]{1,0:T(8,128)(2,1)}, bf16[512,2048]{1,0:T(8,128)(2,1)}) custom-call(bf16[128,2048]{1,0:T(8,128)(2,1)} %multiply_convert_fusion.rows_in, bf16[2048,2048]{1,0:T(8,128)(2,1)} %gate_hbm.1, bf16[2048,2048]{1,0:T(8,128)(2,1)} %up_hbm.3, ...), custom_call_target="tpu_custom_call" | custom-call | flops 12884901888 | bytes 25165824 | tf_op jit(solution)/shard_map/feed_forward/pallas_call | solution.py:1434
  225.2 1.4 multiply_reduce_fusion.9
  226.7 1.5 multiply_add_fusion
  228.2 1.6 fusion.31
  230.3 0.9 fusion.28
  231.2 1.2 fusion.22
  232.4 1.2 fusion.49
  233.6 2.5 multiply_reduce_fusion
  236.2 1.1 fusion.23.grads_in
  237.3 88.6 %feed_forward_backward.1 = (f32[128,2048]{1,0:T(8,128)}, bf16[256,1024]{1,0:T(8,128)(2,1)}, bf16[2048,1024]{1,0:T(8,128)(2,1)}, bf16[2048,2048]{1,0:T(8,128)(2,1)}, bf16[2048,2048]{1,0:T(8,128)(2,1)}) custom-call(bf16[128,2048]{1,0:T(8,128)(2,1)} %fusion.23.grads_in, bf16[512,2048]{1,0:T(8,128)(2,1)} %get-tuple-element.66.gate_keep, ...), custom_call_target="tpu_custom_call" | custom-call | flops 25769803776 | bytes 50331648 | tf_op jit(solution)/shard_map/feed_forward_backward/pallas_call | solution.py:1666
  326.8 1.7 copy.86.refs_9_
  328.5 1.3 constant_dynamic-slice_fusion.refs_8_
  329.8 1.5 multiply_reduce_fusion.1
  331.4 3.9 multiply_reduce_fusion.2
  335.4 1.3 fusion.25
  336.7 98.1 %attention_backward.1 = (bf16[128,3072]{1,0:T(8,128)(2,1)}, f32[8,256]{1,0:T(8,128)}, bf16[4,128,512]{2,1,0:T(8,128)(2,1)}, f32[128,2048]{1,0:T(8,128)}, bf16[25...) custom-call(bf16[128,2048]{1,0:T(8,128)(2,1)} %get-tuple-element.73.refs_0_, ...), custom_call_target="tpu_custom_call" | custom-call | flops 2684354560 | bytes 67108864 | tf_op jit(solution)/shard_map/attention_backward/pallas_call | solution.py:1033
  435.9 2.9 fusion.17
  439.5 1.0 copy.87
  440.7 1.0 copy.89
  442.0 1.0 copy.88
  444.6 1.0 reshape.299
  445.9 1.0 copy-done.25
  446.9 1.6 convert_element_type.172
  448.4 1.6 convert_element_type.173
  451.7 1.2 fusion.34
  453.0 4.5 convolution_convert_fusion.1.refs_0_
  457.5 5.4 %convolution_convert_fusion.refs_1_ = bf16[2048,768]{1,0:T(8,128)(2,1)} fusion(bf16[512,2048]{1,0:T(8,128)(2,1)} %all-gather.5.cloned.1.call-done, bf16[512,768]{1,0:T(8,128)(2,1)} %bitcast.156), kind=kOutput, calls=%fused_computation.2 | convolution fusion | flops 1612185600 | bytes 6029312 | tf_op jit(solution)/shard_map/dot_general | solution.py:38
  462.8 49.1 %owner_sums.1 = (bf16[256,512]{1,0:T(8,128)(2,1)S(1)}, bf16[256,768]{1,0:T(8,128)(2,1)S(1)}, bf16[64,256]{1,0:T(8,128)(2,1)S(1)}, bf16[64,256]{1,0:T(8,128)(2,1)S(1)}, bf16[32,512]{1,0:T(8,128)(2,1)S(1)}) custom-call(bf16[2048,512]{1,0:T(8,128)(2,1)S(1)} %copy-done, bf16[2048,768]{1,0:T(8,128)(2,1)} %convolution_convert_fusion.refs_1_, ...), custom_call_target="tpu_custom_call" | custom-call | flops 4194304 | bytes 16777216 | tf_op jit(solution)/shard_map/owner_sums/pallas_call | solution.py:1180
  512.6 0.9 convert_element_type.170
  514.3 1.4 convert_element_type.175
  515.7 0.7 slice_reduce_fusion.6
  516.4 0.8 slice_reduce_fusion
  517.2 1.4 convert_bitcast_fusion.1
  519.3 0.9 slice_convert_fusion
  520.2 1.3 maximum_convert_fusion
  521.4 1.8 copy.93
  (188 shorter events, 11.4 us)
Async XLA Ops:
  8.0 445.0 %all-gather.3.cloned.1.call-start = ((), (), s32[]{:S(2)}) async-start(), calls=%async_computation.1 | async-start | bytes 2621440 | tf_op jit(solution)/shard_map/all_gather | solution.py:50
  9.9 141.2 %copy-start.50 = (f32[128]{0:T(128)}, f32[128]{0:T(128)S(1)}, u32[]{:S(2)}) copy-start(f32[128]{0:T(128)S(1)} %fusion.50) | copy-start | bytes 1540
  13.8 68.0 %copy-start.8 = (bf16[1,128,2048]{2,1,0:T(8,128)(2,1)S(1)}, bf16[1,128,2048]{2,1,0:T(8,128)(2,1)}, u32[]{:S(2)}) copy-start(bf16[1,128,2048]{2,1,0:T(8,128)(2,1)} %param.23) | copy-start | bytes 1572868
  13.8 68.0 %copy-start.29 = (f32[2048]{0:T(1024)S(1)}, f32[2048]{0:T(1024)}, u32[]{:S(2)}) copy-start(f32[2048]{0:T(1024)} %param.38) | copy-start | bytes 24580
  142.9 2.9 copy-start.27
  144.4 6.6 %copy-start.38 = (bf16[128,64]{0,1:T(8,128)(2,1)}, bf16[128,64]{0,1:T(8,128)(2,1)S(1)}, u32[]{:S(2)}) copy-start(bf16[128,64]{0,1:T(8,128)(2,1)S(1)} %convolution_convert_fusion.7) | copy-start | bytes 49156
  145.8 5.2 copy-start.57
  145.8 5.3 copy-start.6
  145.9 5.2 copy-start.41
  145.9 5.2 copy-start.43
  152.5 72.7 %copy-start.65 = (f32[128]{0:T(128)}, f32[128]{0:T(128)S(1)}, u32[]{:S(2)}) copy-start(f32[128]{0:T(128)S(1)} %get-tuple-element.207) | copy-start | bytes 1540
  153.0 72.2 %copy-start.59 = (f32[128]{0:T(128)}, f32[128]{0:T(128)S(1)}, u32[]{:S(2)}) copy-start(f32[128]{0:T(128)S(1)} %get-tuple-element.221) | copy-start | bytes 1540
  154.0 72.7 %copy-start.36 = (f32[2048]{0:T(1024)S(1)}, f32[2048]{0:T(1024)}, u32[]{:S(2)}) copy-start(f32[2048]{0:T(1024)} %param.42) | copy-start | bytes 24580
  226.6 3.2 copy-start.26
  226.6 3.2 copy-start.32
  228.2 2.1 copy-start.14
  231.2 2.4 copy-start.3
  232.4 3.7 copy-start.22
  233.6 3.7 copy-start.30
  325.9 3.9 copy-start.16
  326.0 131.5 %all-gather.5.cloned.1.call-start = ((), (), s32[]{:S(2)}) async-start(), calls=%async_computation.2 | async-start | bytes 2621440 | tf_op jit(solution)/shard_map/all_gather | solution.py:50
  326.7 193.4 %reduce-scatter.2.cloned.1.call-start = ((), (), s32[]{:S(2)}) async-start(), calls=%async_computation.3 | async-start | bytes 4718592 | tf_op jit(solution)/shard_map/reduce_scatter | solution.py:54
  328.5 2.8 copy-start.66
  328.5 2.8 copy-start.42
  328.5 2.9 copy-start.44
  328.5 2.9 copy-start.17
  328.5 2.9 copy-start.54
  328.5 2.9 copy-start.56
  328.5 2.9 copy-start.62
  331.4 4.0 copy-start.58
  331.4 4.0 copy-start.64
  331.4 4.0 copy-start.7
  331.4 4.0 copy-start.13
  335.3 99.8 %copy-start.4 = (f32[128,2048]{1,0:T(8,128)}, f32[128,2048]{1,0:T(8,128)S(1)}, u32[]{:S(2)}) copy-start(f32[128,2048]{1,0:T(8,128)S(1)} %get-tuple-element.206) | copy-start | bytes 3145732
  435.8 3.0 copy-start.34
  435.8 3.0 copy-start.49
  435.8 3.0 copy-start.48
  435.8 3.1 copy-start.47
  435.8 3.1 copy-start.46
  435.8 3.1 copy-start.45
  435.8 3.1 copy-start.52
  435.9 4.7 copy-start.39
  438.8 3.0 copy-start.15
  438.8 4.2 copy-start.31
  438.8 2.9 copy-start.35
  445.9 2.6 copy-start.24
  457.4 5.4 %copy-start = (bf16[2048,512]{1,0:T(8,128)(2,1)S(1)}, bf16[2048,512]{1,0:T(8,128)(2,1)}, u32[]{:S(2)}) copy-start(bf16[2048,512]{1,0:T(8,128)(2,1)} %convolution_convert_fusion.1.refs_0_) | copy-start | bytes 6291460
  512.0 8.2 %copy-start.28 = (bf16[256,1024]{1,0:T(8,128)(2,1)S(1)}, bf16[256,1024]{1,0:T(8,128)(2,1)}, u32[]{:S(2)}) copy-start(bf16[256,1024]{1,0:T(8,128)(2,1)} %get-tuple-element.90) | copy-start | bytes 1572868
  (22 other events, 31.0 us)
Sparse Core Ops, SparseCore 0:
  326.1 67.3 all-gather.2
  395.6 50.1 all-gather.4
Sparse Core Ops, SparseCore 1:
  434.9 54.1 reduce-scatter.1

commit v9 on v8

--- a/solution.py
+++ b/solution.py
@@ -246,9 +246,11 @@
 
     order = [(i, step) for i in range(sets) for step in range(1, steps + 1)]
     for tick in range(len(order) + bits - 1):
+        if 1 <= tick <= len(order):
+            advance(*order[tick - 1], 0)
         if tick < len(order):
             arrive(*order[tick])
-        for stage in range(bits - 1):
+        for stage in range(1, bits - 1):
             at = tick - 1 - stage
             if 0 <= at < len(order):
                 advance(*order[at], stage)

time: 535 us -> 528 us (0.987)
  Pallas kernels: 428 us -> 421 us
    pallas_call x1, Pallas kernels: 68 us -> 61.8 us  [weight_gather(): pl.pallas_call(functools.partial(weight_gather_kernel, ctx_count, fsdp_co...]
where the time goes in v9:
time: 528 us; the launch traced here: 524 us
  Pallas kernels  421 us (80%)
  matrix products  34.6 us (7%)
  other arithmetic  29.3 us (6%)
  local copies, waits for them, and re-layouts  20.9 us (4%)
  between operations  16.6 us (3%)
    pallas_call x1, Pallas kernels, attention_backward(): pl.pallas_call(functools.partial(attention_backward_kernel, ctx_count, fs...  97.1 us
    pallas_call x1, Pallas kernels, feed_forward_backward(): pl.pallas_call(functools.partial(feed_forward_backward_kernel, count), ou...  88.3 us
    pallas_call x1, Pallas kernels, feed_forward(): pl.pallas_call(functools.partial(feed_forward_kernel, count), out_shape=[...  71.2 us
    pallas_call x1, Pallas kernels, weight_gather(): pl.pallas_call(functools.partial(weight_gather_kernel, ctx_count, fsdp_co...  61.8 us
    pallas_call x1, Pallas kernels, owner_sums(): pl.pallas_call(functools.partial(owner_sum_kernel, ctx_count, fsdp_count,...  51.4 us
    pallas_call x1, Pallas kernels, attention_forward(): pl.pallas_call(functools.partial(attention_forward_kernel, ctx_count, len...  51.4 us
    dot_general x6, matrix products, forward_product(): return jnp.dot(a, b, preferred_element_type=jnp.float32)  16.6 us
    dot_general x6, matrix products, over_rows(): lax.dot_general(a, b, (((0,), (0,)), ((), ())), preferred_element_type=jn...  11 us
  transfers between devices with their start and end apart: 3, of which 0 were waited for; matrix products, arithmetic and copies ran while one was open for 8% of the time, Pallas kernels for 28%

profile of v9, /device:TPU:0, one launch (start us, length us, event | category | flops | bytes accessed | tf_op | source)
XLA Modules:
  0.0 523.6 jit_solution(6947311966827533848)
XLA Ops:
  8.1 1.2 fusion.18
  10.5 0.7 copy.83.row_ids
  11.3 1.6 copy.84.refs_0_
  12.9 1.0 multiply_sine_fusion
  13.8 61.8 %weight_gather.1 = (bf16[4,2,2,2,64,3072]{5,4,3,2,1,0:T(8,128)(2,1)}, bf16[4,2,2,2,64,2304]{5,4,3,2,1,0:T(8,128)(2,1)}) custom-call(bf16[2,2,2,64,2048]{4,3,2,1,0:T(8,128)(2,1)} %bitcast.138, bf16[2,2,2,64,512]{4,3,2,1,0:T(8,128)(2,1)} %bitcast.144, bf16[2,2,2,64,512]{4,3,2,1,0:T(8,128)(2,1)} %bitcast.145, bf16[2,2,2,64,2048]{4,3,2,1,0:T(8,128)(2,1)} %bitcast.139, ...), custom_call_target="tpu_custom_call" | custom-call | bytes 44040192 | tf_op jit(solution)/shard_map/weight_gather/pallas_call | solution.py:288
  75.7 7.6 %fusion.39.raw.refs_3_ = f32[128,3072]{1,0:T(8,128)} fusion(bf16[2048,3072]{1,0:T(8,128)(2,1)} %bitcast.128, bf16[1,128,2048]{2,1,0:T(8,128)(2,1)S(1)} %copy-done.8, f32[2048]{0:T(1024)S(1)} %copy-done.29, f32[128]{0:T(128)S(1)} %fusion.50), kind=kOutput, calls=%fused_computation.82 | convolution fusion | flops 1611661312 | bytes 14688768 | tf_op jit(solution)/shard_map/dot_general | solution.py:30
  83.3 51.4 %attention_forward.1 = (bf16[2,2,2,128,1024]{4,3,2,1,0:T(8,128)(2,1)}, bf16[128,2048]{1,0:T(8,128)(2,1)}, bf16[128,2048]{1,0:T(8,128)(2,1)}, f32[8,8,128]{2,1,0:...) custom-call(f32[128,3072]{1,0:T(8,128)} %fusion.39.raw.refs_3_, ...), custom_call_target="tpu_custom_call", output_to_operand_aliasing={{4}: (7, {})} | custom-call | flops 1073741824 | bytes 8388608 | tf_op jit(solution)/shard_map/attention_forward/pallas_call | solution.py:682
  134.8 1.5 convolution_convert_fusion.7
  136.2 1.0 copy.95
  137.7 5.1 multiply_reduce_fusion.12
  142.9 1.3 multiply_reduce_fusion.10
  144.8 1.0 multiply_convert_fusion.rows_in
  145.8 71.2 %feed_forward.1 = (f32[128,2048]{1,0:T(8,128)}, bf16[4,128,2048]{2,1,0:T(8,128)(2,1)}, bf16[512,2048]{1,0:T(8,128)(2,1)}, bf16[512,2048]{1,0:T(8,128)(2,1)}, bf16[512,2048]{1,0:T(8,128)(2,1)}) custom-call(bf16[128,2048]{1,0:T(8,128)(2,1)} %multiply_convert_fusion.rows_in, bf16[2048,2048]{1,0:T(8,128)(2,1)} %gate_hbm.1, bf16[2048,2048]{1,0:T(8,128)(2,1)} %up_hbm.3, ...), custom_call_target="tpu_custom_call" | custom-call | flops 12884901888 | bytes 25165824 | tf_op jit(solution)/shard_map/feed_forward/pallas_call | solution.py:1436
  217.0 1.4 multiply_reduce_fusion.9
  218.4 1.5 multiply_add_fusion
  220.0 1.6 fusion.31
  222.0 0.9 fusion.28
  223.0 1.2 fusion.22
  224.2 1.2 fusion.49
  225.4 2.5 multiply_reduce_fusion
  227.9 1.1 fusion.23.grads_in
  229.1 88.3 %feed_forward_backward.1 = (f32[128,2048]{1,0:T(8,128)}, bf16[256,1024]{1,0:T(8,128)(2,1)}, bf16[2048,1024]{1,0:T(8,128)(2,1)}, bf16[2048,2048]{1,0:T(8,128)(2,1)}, bf16[2048,2048]{1,0:T(8,128)(2,1)}) custom-call(bf16[128,2048]{1,0:T(8,128)(2,1)} %fusion.23.grads_in, bf16[512,2048]{1,0:T(8,128)(2,1)} %get-tuple-element.66.gate_keep, ...), custom_call_target="tpu_custom_call" | custom-call | flops 25769803776 | bytes 50331648 | tf_op jit(solution)/shard_map/feed_forward_backward/pallas_call | solution.py:1668
  318.2 1.7 copy.86.refs_9_
  319.9 1.3 constant_dynamic-slice_fusion.refs_8_
  321.2 1.5 multiply_reduce_fusion.1
  322.9 3.9 multiply_reduce_fusion.2
  326.8 1.3 fusion.25
  328.1 97.1 %attention_backward.1 = (bf16[128,3072]{1,0:T(8,128)(2,1)}, f32[8,256]{1,0:T(8,128)}, bf16[4,128,512]{2,1,0:T(8,128)(2,1)}, f32[128,2048]{1,0:T(8,128)}, bf16[25...) custom-call(bf16[128,2048]{1,0:T(8,128)(2,1)} %get-tuple-element.73.refs_0_, ...), custom_call_target="tpu_custom_call" | custom-call | flops 2684354560 | bytes 67108864 | tf_op jit(solution)/shard_map/attention_backward/pallas_call | solution.py:1035
  426.3 2.9 fusion.17
  429.9 1.0 copy.87
  431.2 1.0 copy.89
  432.4 1.0 copy.88
  435.0 1.0 reshape.299
  436.3 1.1 copy-done.25
  437.4 1.6 convert_element_type.172
  438.9 1.6 convert_element_type.173
  442.2 1.2 fusion.34
  443.5 4.3 convolution_convert_fusion.1.refs_0_
  447.8 5.4 %convolution_convert_fusion.refs_1_ = bf16[2048,768]{1,0:T(8,128)(2,1)} fusion(bf16[512,2048]{1,0:T(8,128)(2,1)} %all-gather.5.cloned.1.call-done, bf16[512,768]{1,0:T(8,128)(2,1)} %bitcast.156), kind=kOutput, calls=%fused_computation.2 | convolution fusion | flops 1612185600 | bytes 6029312 | tf_op jit(solution)/shard_map/dot_general | solution.py:38
  453.2 51.4 %owner_sums.1 = (bf16[256,512]{1,0:T(8,128)(2,1)S(1)}, bf16[256,768]{1,0:T(8,128)(2,1)S(1)}, bf16[64,256]{1,0:T(8,128)(2,1)S(1)}, bf16[64,256]{1,0:T(8,128)(2,1)S(1)}, bf16[32,512]{1,0:T(8,128)(2,1)S(1)}) custom-call(bf16[2048,512]{1,0:T(8,128)(2,1)S(1)} %copy-done, bf16[2048,768]{1,0:T(8,128)(2,1)} %convolution_convert_fusion.refs_1_, ...), custom_call_target="tpu_custom_call" | custom-call | flops 4194304 | bytes 16777216 | tf_op jit(solution)/shard_map/owner_sums/pallas_call | solution.py:1182
  505.3 0.9 convert_element_type.170
  506.9 1.4 convert_element_type.175
  508.3 0.7 slice_reduce_fusion.6
  509.0 0.8 slice_reduce_fusion
  509.8 1.4 convert_bitcast_fusion.1
  511.9 0.9 slice_convert_fusion
  512.8 1.3 maximum_convert_fusion
  514.1 1.8 copy.93
  (188 shorter events, 11.4 us)
Async XLA Ops:
  8.0 435.5 %all-gather.3.cloned.1.call-start = ((), (), s32[]{:S(2)}) async-start(), calls=%async_computation.1 | async-start | bytes 2621440 | tf_op jit(solution)/shard_map/all_gather | solution.py:50
  9.9 133.0 %copy-start.50 = (f32[128]{0:T(128)}, f32[128]{0:T(128)S(1)}, u32[]{:S(2)}) copy-start(f32[128]{0:T(128)S(1)} %fusion.50) | copy-start | bytes 1540
  13.8 61.8 %copy-start.8 = (bf16[1,128,2048]{2,1,0:T(8,128)(2,1)S(1)}, bf16[1,128,2048]{2,1,0:T(8,128)(2,1)}, u32[]{:S(2)}) copy-start(bf16[1,128,2048]{2,1,0:T(8,128)(2,1)} %param.23) | copy-start | bytes 1572868
  13.8 61.8 %copy-start.29 = (f32[2048]{0:T(1024)S(1)}, f32[2048]{0:T(1024)}, u32[]{:S(2)}) copy-start(f32[2048]{0:T(1024)} %param.38) | copy-start | bytes 24580
  134.8 2.9 copy-start.27
  136.2 6.6 %copy-start.38 = (bf16[128,64]{0,1:T(8,128)(2,1)}, bf16[128,64]{0,1:T(8,128)(2,1)S(1)}, u32[]{:S(2)}) copy-start(bf16[128,64]{0,1:T(8,128)(2,1)S(1)} %convolution_convert_fusion.7) | copy-start | bytes 49156
  137.6 5.2 copy-start.57
  137.6 5.3 %copy-start.6 = (f32[128,2048]{1,0:T(8,128)}, f32[128,2048]{1,0:T(8,128)S(1)}, u32[]{:S(2)}) copy-start(f32[128,2048]{1,0:T(8,128)S(1)} %get-tuple-element.223) | copy-start | bytes 3145732
  137.7 5.2 %copy-start.41 = (f32[2048]{0:T(1024)S(1)}, f32[2048]{0:T(1024)}, u32[]{:S(2)}) copy-start(f32[2048]{0:T(1024)} %param.39) | copy-start | bytes 24580
  137.7 5.2 %copy-start.43 = (f32[2048]{0:T(1024)S(1)}, f32[2048]{0:T(1024)}, u32[]{:S(2)}) copy-start(f32[2048]{0:T(1024)} %param.40) | copy-start | bytes 24580
  144.3 72.7 %copy-start.65 = (f32[128]{0:T(128)}, f32[128]{0:T(128)S(1)}, u32[]{:S(2)}) copy-start(f32[128]{0:T(128)S(1)} %get-tuple-element.207) | copy-start | bytes 1540
  144.8 72.2 %copy-start.59 = (f32[128]{0:T(128)}, f32[128]{0:T(128)S(1)}, u32[]{:S(2)}) copy-start(f32[128]{0:T(128)S(1)} %get-tuple-element.221) | copy-start | bytes 1540
  145.8 72.6 %copy-start.36 = (f32[2048]{0:T(1024)S(1)}, f32[2048]{0:T(1024)}, u32[]{:S(2)}) copy-start(f32[2048]{0:T(1024)} %param.42) | copy-start | bytes 24580
  218.4 3.2 copy-start.26
  218.4 3.2 copy-start.32
  219.9 2.1 copy-start.14
  223.0 2.4 copy-start.3
  224.2 3.7 copy-start.22
  225.4 3.7 copy-start.30
  317.3 3.9 copy-start.16
  317.4 130.4 %all-gather.5.cloned.1.call-start = ((), (), s32[]{:S(2)}) async-start(), calls=%async_computation.2 | async-start | bytes 2621440 | tf_op jit(solution)/shard_map/all_gather | solution.py:50
  318.1 194.7 %reduce-scatter.2.cloned.1.call-start = ((), (), s32[]{:S(2)}) async-start(), calls=%async_computation.3 | async-start | bytes 4718592 | tf_op jit(solution)/shard_map/reduce_scatter | solution.py:54
  319.9 2.8 copy-start.66
  319.9 2.8 copy-start.42
  319.9 2.9 copy-start.44
  319.9 2.9 copy-start.17
  319.9 2.9 copy-start.54
  319.9 2.9 copy-start.56
  319.9 2.9 copy-start.62
  322.8 3.9 copy-start.58
  322.8 3.9 copy-start.64
  322.8 4.0 copy-start.7
  322.8 4.0 copy-start.13
  326.7 98.8 %copy-start.4 = (f32[128,2048]{1,0:T(8,128)}, f32[128,2048]{1,0:T(8,128)S(1)}, u32[]{:S(2)}) copy-start(f32[128,2048]{1,0:T(8,128)S(1)} %get-tuple-element.206) | copy-start | bytes 3145732
  426.2 3.0 copy-start.34
  426.2 3.0 copy-start.49
  426.2 3.1 copy-start.48
  426.2 3.1 copy-start.47
  426.2 3.1 copy-start.46
  426.2 3.1 copy-start.45
  426.3 3.1 copy-start.52
  426.3 4.7 copy-start.39
  429.2 3.0 copy-start.15
  429.2 4.2 copy-start.31
  429.2 2.9 copy-start.35
  436.3 2.7 copy-start.24
  447.8 5.4 %copy-start = (bf16[2048,512]{1,0:T(8,128)(2,1)S(1)}, bf16[2048,512]{1,0:T(8,128)(2,1)}, u32[]{:S(2)}) copy-start(bf16[2048,512]{1,0:T(8,128)(2,1)} %convolution_convert_fusion.1.refs_0_) | copy-start | bytes 6291460
  504.6 8.2 %copy-start.28 = (bf16[256,1024]{1,0:T(8,128)(2,1)S(1)}, bf16[256,1024]{1,0:T(8,128)(2,1)}, u32[]{:S(2)}) copy-start(bf16[256,1024]{1,0:T(8,128)(2,1)} %get-tuple-element.90) | copy-start | bytes 1572868
  (22 other events, 31.1 us)
Sparse Core Ops, SparseCore 0:
  317.5 68.1 all-gather.2
  387.8 50.1 all-gather.4
Sparse Core Ops, SparseCore 1:
  425.3 56.1 reduce-scatter.1
